TPU v7x, 32 devices: a whole 2x2x4 slice. The times are simulated.
32 devices in a mesh: grp: 2 (over core), wide: 8 (over z, x), narrow: 2 (over y).
Axes of the slice: x: 2, y: 2, z: 4, core: 2. Of those that a mesh axis runs over, the one named last changes fastest.
Arguments:
- tokens: bfloat16 [8192, 2048], P(('grp', 'wide', 'narrow')), parts along dimension 0, may hold values from -12 to 12
- cotangent: bfloat16 [8192, 2048], P(('grp', 'wide', 'narrow')), parts along dimension 0, may hold values from -6 to 6
- valid: int32 [8192], P(('grp', 'wide', 'narrow')), parts along dimension 0, may hold values from 0 to 1
- routes: int32 [8192, 8], P(('grp', 'wide', 'narrow')), parts along dimension 0, may hold values from 0 to 15, all different within a row; in each aligned block of 256 rows (0 to 255, 256 to 511, ...) at most 160 rows name the same one
- w_query: bfloat16 [2048, 2048], P(None, 'wide'), may hold values from -0.125 to 0.125
- w_key: bfloat16 [2048, 2048], P(None, 'wide'), may hold values from -0.125 to 0.125
- w_value: bfloat16 [2048, 2048], P(None, 'wide'), may hold values from -0.125 to 0.125
- w_out: bfloat16 [2048, 2048], P('wide'), may hold values from -2 to 2
- norm_attn: bfloat16 [2048], replicated, may hold values from 0.25 to 1.75
- norm_query: bfloat16 [2048], P('wide'), may hold values from 0.25 to 1.75
- norm_key: bfloat16 [2048], P('wide'), may hold values from 0.25 to 1.75
- norm_moe: bfloat16 [2048], replicated, may hold values from 0.25 to 1.75
- w_router: bfloat16 [2048, 16], replicated, may hold values from -0.0625 to 0.0625
- w_gate: bfloat16 [16, 2048, 1024], P(('wide', 'narrow')), may hold values from -0.125 to 0.125
- w_up: bfloat16 [16, 2048, 1024], P(('wide', 'narrow')), may hold values from -0.125 to 0.125
- w_down: bfloat16 [16, 1024, 2048], P(('wide', 'narrow')), may hold values from -1.5 to 1.5
Outputs:
- output: bfloat16 [8192, 2048], P(('grp', 'wide', 'narrow')), parts along dimension 0
- grad_input: float32 [8192, 2048], P(('grp', 'wide', 'narrow')), parts along dimension 0
- grad_query: float32 [4096, 2048], P('grp', 'wide'), parts along dimension 0
- grad_key: float32 [4096, 2048], P('grp', 'wide'), parts along dimension 0
- grad_value: float32 [4096, 2048], P('grp', 'wide'), parts along dimension 0
- grad_out: float32 [4096, 2048], P(('grp', 'wide')), parts along dimension 0
- grad_norm_attn: float32 [4096], P('grp'), parts along dimension 0
- grad_norm_query: float32 [4096], P(('grp', 'wide')), parts along dimension 0
- grad_norm_key: float32 [4096], P(('grp', 'wide')), parts along dimension 0
- grad_norm_moe: float32 [4096], P('grp'), parts along dimension 0
- grad_router: float32 [4096, 16], P('grp'), parts along dimension 0
- grad_gate: float32 [32, 2048, 1024], P(('grp', 'wide', 'narrow')), parts along dimension 0
- grad_up: float32 [32, 2048, 1024], P(('grp', 'wide', 'narrow')), parts along dimension 0
- grad_down: float32 [32, 1024, 2048], P(('grp', 'wide', 'narrow')), parts along dimension 0
- rms: float32 [10], P('grp'), parts along dimension 0
There are 2 independent parts, one for each index of `grp`. A program takes and returns all parts, laid end to end along the dimension named above; an argument that names none is the same for every part. Nothing has to cross between parts.
Inputs may be any that keep to these rules, and one draw needn't show every extreme that they name: `routes`: in the rows of one device no expert is named by more than 160 rows, and in every draw some expert is named by exactly 160 rows of some device; each row names 8 different experts.
All inputs are finite; a program needn't handle non-finite values.
Results may differ from a plain program's by a relative error of at most 0.028.
Values may be sent and summed in bfloat16 or wider, within the bound.
A program may use at most 320 MiB of HBM per device.

v0:
```python
import jax
import jax.numpy as jnp
from jax import lax
from jax.sharding import PartitionSpec as P

D = 2048
HD = 128
TOP = 8
EXP_DEV = 1
PROMPT = 2048
CONT = 256
NCONT = 8
QB = 512


EPSILON = 1e-05
THETA = 10000.0
NEGATIVE = -1e30


def token_info(token_ids):
    span = PROMPT + NCONT * CONT
    local = token_ids % span
    group = token_ids // span
    branch = jnp.where(local < PROMPT, -1, (local - PROMPT) // CONT)
    place = jnp.where(local < PROMPT, local, PROMPT + (local - PROMPT) % CONT)
    return (group, local, branch, place)


def allowed(query_ids, key_ids):
    query_group, query_local, query_branch, query_place = token_info(query_ids)
    key_group, key_local, key_branch, key_place = token_info(key_ids)
    same = query_group[:, None] == key_group[None, :]
    earlier = key_local[None, :] <= query_local[:, None]
    prompt_key = (key_branch[None, :] < 0) & ((query_branch[:, None] >= 0) | earlier)
    own_key = (key_branch[None, :] >= 0) & (key_branch[None, :] == query_branch[:, None]) & earlier
    return same & (prompt_key | own_key)


def rotation(place):
    frequency = THETA ** (-2.0 * jnp.arange(HD // 2, dtype=jnp.float32) / HD)
    angle = place.astype(jnp.float32)[:, None] * frequency[None, :]
    return (jnp.cos(angle), jnp.sin(angle))


def rotate(values, cosine, sine):
    first = values[..., : HD // 2]
    second = values[..., HD // 2 :]
    cos_row = cosine[:, None, :]
    sin_row = sine[:, None, :]
    return jnp.concatenate(
        [first * cos_row - second * sin_row, second * cos_row + first * sin_row], -1
    )


def rotate_back(values, cosine, sine):
    first = values[..., : HD // 2]
    second = values[..., HD // 2 :]
    cos_row = cosine[:, None, :]
    sin_row = sine[:, None, :]
    return jnp.concatenate(
        [first * cos_row + second * sin_row, second * cos_row - first * sin_row], -1
    )


def add_slice(total, values, start):
    current = lax.dynamic_slice_in_dim(total, start, values.shape[0], 0)
    return lax.dynamic_update_slice_in_dim(total, current + values, start, 0)


def shards(
    tokens,
    cotangent,
    valid,
    routes,
    w_query,
    w_key,
    w_value,
    w_out,
    norm_attn,
    norm_query,
    norm_key,
    norm_moe,
    w_router,
    w_gate,
    w_up,
    w_down,
):
    wide_count = lax.axis_size("wide")
    narrow_count = lax.axis_size("narrow")
    rows = tokens.shape[0]
    devices_part = wide_count * narrow_count
    all_rows = rows * devices_part
    half = all_rows // narrow_count
    columns = w_query.shape[1]
    heads_local = columns // HD
    experts = w_router.shape[1]
    capacity = min(max(rows * TOP * 5 // (4 * experts), 2), rows)
    side = lax.axis_index("narrow")
    scale = HD ** (-0.5)
    blocks = half // QB
    span = PROMPT + NCONT * CONT
    window = QB * narrow_count + CONT
    prompt_offsets = jnp.arange(PROMPT, dtype=jnp.int32)
    window_offsets = jnp.arange(window, dtype=jnp.int32)
    stream = tokens.astype(jnp.float32)
    inv_one = lax.rsqrt(jnp.mean(stream * stream, -1, keepdims=True) + EPSILON)
    gain_one = norm_attn.astype(jnp.float32)
    normed = (stream * inv_one * gain_one).astype(jnp.bfloat16)
    normed_all = lax.all_gather(normed, ("wide", "narrow"), axis=0, tiled=True)
    normed_own = lax.dynamic_index_in_dim(
        normed_all.reshape(wide_count, narrow_count, rows, D), side, 1, keepdims=False
    ).reshape(half, D)
    query_ids = (
        (jnp.arange(wide_count, dtype=jnp.int32)[:, None] * narrow_count + side) * rows
        + jnp.arange(rows, dtype=jnp.int32)[None, :]
    ).reshape(half)
    key_ids = jnp.arange(all_rows, dtype=jnp.int32)
    query_raw = jnp.dot(normed_own, w_query, preferred_element_type=jnp.float32)
    key_value = jnp.dot(
        normed_all, jnp.concatenate([w_key, w_value], 1), preferred_element_type=jnp.float32
    )
    key_raw = key_value[:, :columns]
    value_raw = key_value[:, columns:]
    query_sum, key_sum = lax.psum(
        (jnp.sum(query_raw * query_raw, -1), jnp.sum(key_raw * key_raw, -1)), "wide"
    )
    inv_query = lax.rsqrt(query_sum / D + EPSILON)[:, None]
    inv_key = lax.rsqrt(key_sum / D + EPSILON)[:, None]
    gain_query = norm_query.astype(jnp.float32)
    gain_key = norm_key.astype(jnp.float32)
    query_cos, query_sin = rotation(token_info(query_ids)[3])
    key_cos, key_sin = rotation(token_info(key_ids)[3])
    query_rot = rotate(
        (query_raw * inv_query * gain_query).reshape(half, heads_local, HD), query_cos, query_sin
    ).astype(jnp.bfloat16)
    key_rot = rotate(
        (key_raw * inv_key * gain_key).reshape(all_rows, heads_local, HD), key_cos, key_sin
    ).astype(jnp.bfloat16)
    value_b = value_raw.reshape(all_rows, heads_local, HD).astype(jnp.bfloat16)
    query_blocks = query_rot.reshape(blocks, QB, heads_local, HD)
    id_blocks = query_ids.reshape(blocks, QB)

    def key_span(block_ids):
        lowest = block_ids[0]
        group_start = lowest // span * span
        window_start = jnp.clip(lowest - CONT, 0, all_rows - window)
        prompt_ids = group_start + prompt_offsets
        window_ids = window_start + window_offsets
        later = (token_info(window_ids)[1] >= PROMPT)[None, :]
        mask = jnp.concatenate(
            [allowed(block_ids, prompt_ids), allowed(block_ids, window_ids) & later], 1
        )
        keys = jnp.concatenate(
            [
                lax.dynamic_slice_in_dim(key_rot, group_start, PROMPT, 0),
                lax.dynamic_slice_in_dim(key_rot, window_start, window, 0),
            ],
            0,
        )
        values = jnp.concatenate(
            [
                lax.dynamic_slice_in_dim(value_b, group_start, PROMPT, 0),
                lax.dynamic_slice_in_dim(value_b, window_start, window, 0),
            ],
            0,
        )
        return (group_start, window_start, mask, keys, values)

    def attend(operands):
        query_block, block_ids = operands
        group_start, window_start, mask, keys, values = key_span(block_ids)
        scores = (
            jnp.einsum("qhd,khd->hqk", query_block, keys, preferred_element_type=jnp.float32)
            * scale
        )
        scores = jnp.where(mask[None], scores, NEGATIVE)
        largest = jnp.max(scores, -1, keepdims=True)
        weights = jnp.exp(scores - largest)
        weight_sum = jnp.sum(weights, -1, keepdims=True)
        weights = weights / weight_sum
        mixed = jnp.einsum(
            "hqk,khd->qhd", weights.astype(jnp.bfloat16), values, preferred_element_type=jnp.float32
        ).astype(jnp.bfloat16)
        return (mixed, (largest + jnp.log(weight_sum))[..., 0])

    attended, log_totals = lax.map(attend, (query_blocks, id_blocks))
    attended_flat = attended.reshape(half, columns)
    piece = attended_flat
    branch = lax.psum_scatter(
        jnp.dot(piece, w_out, preferred_element_type=jnp.float32).astype(jnp.bfloat16),
        "wide",
        scatter_dimension=0,
        tiled=True,
    ).astype(jnp.float32)
    hidden = stream + branch
    inv_two = lax.rsqrt(jnp.mean(hidden * hidden, -1, keepdims=True) + EPSILON)
    gain_two = norm_moe.astype(jnp.float32)
    moe_in = (hidden * inv_two * gain_two).astype(jnp.bfloat16)
    logits = jnp.dot(moe_in, w_router, preferred_element_type=jnp.float32)
    router_probs = jax.nn.softmax(logits, -1)
    route_table = (
        routes[:, :, None] == jnp.arange(experts, dtype=jnp.int32)[None, None, :]
    ).astype(jnp.float32)
    gates = jnp.sum(route_table * router_probs[:, None, :], -1)
    flat = routes.reshape(-1)
    token_of = jnp.arange(rows * TOP, dtype=jnp.int32) // TOP
    onehot = (flat[:, None] == jnp.arange(experts, dtype=jnp.int32)[None, :]).astype(jnp.int32)
    rank = jnp.sum((jnp.cumsum(onehot, 0) - onehot) * onehot, -1)
    slot = flat * capacity + rank
    slot_token = jnp.full((experts * capacity,), rows, jnp.int32).at[slot].set(token_of)
    padded = jnp.concatenate([moe_in, jnp.zeros((1, D), jnp.bfloat16)], 0)
    send = jnp.take(padded, slot_token, axis=0).reshape(devices_part, EXP_DEV * capacity, D)
    received = lax.all_to_all(
        send, ("wide", "narrow"), split_axis=0, concat_axis=0, tiled=True
    ).reshape(devices_part, EXP_DEV, capacity, D)
    gate_pre = jnp.einsum("sjcd,jdf->sjcf", received, w_gate, preferred_element_type=jnp.float32)
    up_pre = jnp.einsum("sjcd,jdf->sjcf", received, w_up, preferred_element_type=jnp.float32)
    sigmoid_gate = jax.nn.sigmoid(gate_pre)
    silu_gate = gate_pre * sigmoid_gate
    inner = (silu_gate * up_pre).astype(jnp.bfloat16)
    expert_out = jnp.einsum(
        "sjcf,jfd->sjcd", inner, w_down, preferred_element_type=jnp.float32
    ).astype(jnp.bfloat16)
    returned = lax.all_to_all(
        expert_out.reshape(devices_part, EXP_DEV * capacity, D),
        ("wide", "narrow"),
        split_axis=0,
        concat_axis=0,
        tiled=True,
    ).reshape(experts * capacity, D)
    routed = jnp.take(returned, slot, axis=0).reshape(rows, TOP, D).astype(jnp.float32)
    moe = jnp.sum(gates[:, :, None] * routed, 1)
    final = hidden + moe
    output = final.astype(jnp.bfloat16)
    mask = valid.astype(jnp.float32)[:, None]
    grad_final = cotangent.astype(jnp.float32) * mask
    grad_gates = jnp.sum(grad_final[:, None, :] * routed, -1)
    grad_routed = (
        (gates[:, :, None] * grad_final[:, None, :]).astype(jnp.bfloat16).reshape(rows * TOP, D)
    )
    grad_slots = jnp.zeros((experts * capacity, D), jnp.bfloat16).at[slot].set(grad_routed)
    grad_expert = lax.all_to_all(
        grad_slots.reshape(devices_part, EXP_DEV * capacity, D),
        ("wide", "narrow"),
        split_axis=0,
        concat_axis=0,
        tiled=True,
    ).reshape(devices_part, EXP_DEV, capacity, D)
    grad_inner = jnp.einsum(
        "sjcd,jfd->sjcf", grad_expert, w_down, preferred_element_type=jnp.float32
    )
    grad_down = jnp.einsum("sjcf,sjcd->jfd", inner, grad_expert, preferred_element_type=jnp.float32)
    grad_gate_pre = (
        grad_inner * up_pre * sigmoid_gate * (1.0 + gate_pre * (1.0 - sigmoid_gate))
    ).astype(jnp.bfloat16)
    grad_up_pre = (grad_inner * silu_gate).astype(jnp.bfloat16)
    grad_gate = jnp.einsum(
        "sjcd,sjcf->jdf", received, grad_gate_pre, preferred_element_type=jnp.float32
    )
    grad_up = jnp.einsum(
        "sjcd,sjcf->jdf", received, grad_up_pre, preferred_element_type=jnp.float32
    )
    grad_route_in = (
        jnp.einsum("sjcf,jdf->sjcd", grad_gate_pre, w_gate, preferred_element_type=jnp.float32)
        + jnp.einsum("sjcf,jdf->sjcd", grad_up_pre, w_up, preferred_element_type=jnp.float32)
    ).astype(jnp.bfloat16)
    grad_back = lax.all_to_all(
        grad_route_in.reshape(devices_part, EXP_DEV * capacity, D),
        ("wide", "narrow"),
        split_axis=0,
        concat_axis=0,
        tiled=True,
    ).reshape(experts * capacity, D)
    grad_moe_in = jnp.sum(
        jnp.take(grad_back, slot, axis=0).reshape(rows, TOP, D).astype(jnp.float32), 1
    )
    grad_probs = jnp.sum(grad_gates[:, :, None] * route_table, 1)
    grad_logits = (
        router_probs * (grad_probs - jnp.sum(router_probs * grad_probs, -1, keepdims=True))
    ).astype(jnp.bfloat16)
    grad_router = jnp.einsum("td,te->de", moe_in, grad_logits, preferred_element_type=jnp.float32)
    grad_moe_in = grad_moe_in + jnp.einsum(
        "te,de->td", grad_logits, w_router, preferred_element_type=jnp.float32
    )
    grad_gain_two = jnp.sum(grad_moe_in * hidden * inv_two, 0)
    grad_hidden = (
        grad_final
        + inv_two * gain_two * grad_moe_in
        - hidden * inv_two**3 * jnp.sum(grad_moe_in * gain_two * hidden, -1, keepdims=True) / D
    )
    grad_branch = grad_hidden.astype(jnp.bfloat16)
    piece = lax.all_gather(grad_branch, "wide", axis=0, tiled=True)
    weight_acc = jnp.einsum("tc,td->cd", attended_flat, piece, preferred_element_type=jnp.float32)
    part = jnp.einsum("td,cd->tc", piece, w_out, preferred_element_type=jnp.float32).astype(
        jnp.bfloat16
    )

    def attend_back(carry, operands):
        key_acc, value_acc = carry
        query_block, block_ids, grad_block, log_block = operands
        group_start, window_start, mask, keys, values = key_span(block_ids)
        scores = (
            jnp.einsum("qhd,khd->hqk", query_block, keys, preferred_element_type=jnp.float32)
            * scale
        )
        weights = jnp.where(mask[None], jnp.exp(scores - log_block[..., None]), 0.0)
        weights_b = weights.astype(jnp.bfloat16)
        grad_weights = jnp.einsum(
            "qhd,khd->hqk", grad_block, values, preferred_element_type=jnp.float32
        )
        row_dot = jnp.sum(weights * grad_weights, -1, keepdims=True)
        grad_scores = (weights * (grad_weights - row_dot)).astype(jnp.bfloat16)
        grad_query_block = (
            jnp.einsum("hqk,khd->qhd", grad_scores, keys, preferred_element_type=jnp.float32)
            * scale
        )
        key_part = (
            jnp.einsum("hqk,qhd->khd", grad_scores, query_block, preferred_element_type=jnp.float32)
            * scale
        )
        value_part = jnp.einsum(
            "hqk,qhd->khd", weights_b, grad_block, preferred_element_type=jnp.float32
        )
        key_acc = add_slice(
            add_slice(key_acc, key_part[:PROMPT], group_start), key_part[PROMPT:], window_start
        )
        value_acc = add_slice(
            add_slice(value_acc, value_part[:PROMPT], group_start),
            value_part[PROMPT:],
            window_start,
        )
        return ((key_acc, value_acc), grad_query_block)

    zero_keys = jnp.zeros((all_rows, heads_local, HD), jnp.float32)
    grad_blocks = part.reshape(blocks, QB, heads_local, HD)
    (grad_key_rot, grad_values), grad_query_rot = lax.scan(
        attend_back, (zero_keys, zero_keys), (query_blocks, id_blocks, grad_blocks, log_totals)
    )
    grad_query_normed = rotate_back(
        grad_query_rot.reshape(half, heads_local, HD), query_cos, query_sin
    ).reshape(half, columns)
    grad_key_normed = rotate_back(grad_key_rot, key_cos, key_sin).reshape(all_rows, columns)
    query_dot, key_dot = lax.psum(
        (
            jnp.sum(grad_query_normed * gain_query * query_raw, -1),
            jnp.sum(grad_key_normed * gain_key * key_raw, -1),
        ),
        "wide",
    )
    grad_gain_query = jnp.sum(grad_query_normed * query_raw * inv_query, 0)
    grad_gain_key = jnp.sum(grad_key_normed * key_raw * inv_key, 0)
    grad_query_raw = (
        inv_query * gain_query * grad_query_normed
        - query_raw * inv_query**3 * query_dot[:, None] / D
    ).astype(jnp.bfloat16)
    grad_key_part = (
        inv_key * gain_key * grad_key_normed - key_raw * inv_key**3 * key_dot[:, None] / D
    )
    grad_value_part = grad_values.reshape(all_rows, columns)
    weights_joined = jnp.concatenate([w_query, w_key, w_value], 1)
    key_halves, value_halves = (
        lax.psum_scatter(
            grad_key_part.reshape(wide_count, narrow_count, rows, columns).astype(jnp.bfloat16),
            "narrow",
            scatter_dimension=1,
            tiled=True,
        ).astype(jnp.float32),
        lax.psum_scatter(
            grad_value_part.reshape(wide_count, narrow_count, rows, columns).astype(jnp.bfloat16),
            "narrow",
            scatter_dimension=1,
            tiled=True,
        ).astype(jnp.float32),
    )
    grad_key_raw = key_halves.reshape(half, columns).astype(jnp.bfloat16)
    grad_value_raw = value_halves.reshape(half, columns).astype(jnp.bfloat16)
    grads_joined = jnp.concatenate([grad_query_raw, grad_key_raw, grad_value_raw], 1)
    grad_weights = jnp.einsum(
        "td,tc->dc", normed_own, grads_joined, preferred_element_type=jnp.float32
    )
    piece = grads_joined
    grad_normed = lax.psum_scatter(
        jnp.einsum("tc,dc->td", piece, weights_joined, preferred_element_type=jnp.float32).astype(
            jnp.bfloat16
        ),
        "wide",
        scatter_dimension=0,
        tiled=True,
    ).astype(jnp.float32)
    grad_query_w = grad_weights[:, :columns]
    grad_key_w = grad_weights[:, columns : 2 * columns]
    grad_value_w = grad_weights[:, 2 * columns :]
    summed = (
        lax.psum(grad_query_w.astype(jnp.bfloat16), "narrow").astype(jnp.float32),
        lax.psum(grad_key_w.astype(jnp.bfloat16), "narrow").astype(jnp.float32),
        lax.psum(grad_value_w.astype(jnp.bfloat16), "narrow").astype(jnp.float32),
        lax.psum(weight_acc.astype(jnp.bfloat16), "narrow").astype(jnp.float32),
        lax.psum(grad_gain_query.astype(jnp.bfloat16), "narrow").astype(jnp.float32),
        lax.psum(grad_gain_key.astype(jnp.bfloat16), "narrow").astype(jnp.float32),
    )
    grad_gain_one = jnp.sum(grad_normed * stream * inv_one, 0)
    grad_input = (
        grad_hidden
        + inv_one * gain_one * grad_normed
        - stream * inv_one**3 * jnp.sum(grad_normed * gain_one * stream, -1, keepdims=True) / D
    )

    def square_sum(values):
        return jnp.sum(values * values * mask)

    stat_sums = jnp.stack(
        [
            square_sum(stream),
            square_sum(branch),
            square_sum(hidden),
            square_sum(moe),
            square_sum(final),
        ]
    )
    count_local = jnp.sum(mask)
    replicated = (
        lax.psum(grad_router.astype(jnp.bfloat16), ("wide", "narrow")).astype(jnp.float32),
        lax.psum(grad_gain_one.astype(jnp.bfloat16), ("wide", "narrow")).astype(jnp.float32),
        lax.psum(grad_gain_two.astype(jnp.bfloat16), ("wide", "narrow")).astype(jnp.float32),
        lax.psum(stat_sums.astype(jnp.bfloat16), ("wide", "narrow")).astype(jnp.float32),
        lax.psum(count_local.astype(jnp.bfloat16), ("wide", "narrow")).astype(jnp.float32),
    )
    rms = jnp.sqrt(replicated[3] / (jnp.maximum(replicated[4], 1.0) * D))
    return (
        output,
        grad_input,
        summed[0],
        summed[1],
        summed[2],
        summed[3],
        replicated[1],
        summed[4],
        summed[5],
        replicated[2],
        replicated[0],
        grad_gate,
        grad_up,
        grad_down,
        rms,
    )


def solution(mesh):
    return jax.shard_map(
        shards,
        mesh=mesh,
        in_specs=(
            P(("grp", "wide", "narrow"), None),
            P(("grp", "wide", "narrow"), None),
            P(("grp", "wide", "narrow")),
            P(("grp", "wide", "narrow"), None),
            P(None, "wide"),
            P(None, "wide"),
            P(None, "wide"),
            P("wide", None),
            P(),
            P("wide"),
            P("wide"),
            P(),
            P(),
            P(("wide", "narrow"), None, None),
            P(("wide", "narrow"), None, None),
            P(("wide", "narrow"), None, None),
        ),
        out_specs=(
            P(("grp", "wide", "narrow"), None),
            P(("grp", "wide", "narrow"), None),
            P("grp", "wide"),
            P("grp", "wide"),
            P("grp", "wide"),
            P(("grp", "wide"), None),
            P("grp"),
            P(("grp", "wide")),
            P(("grp", "wide")),
            P("grp"),
            P("grp", None),
            P(("grp", "wide", "narrow"), None, None),
            P(("grp", "wide", "narrow"), None, None),
            P(("grp", "wide", "narrow"), None, None),
            P("grp"),
        ),
        check_vma=False,
    )
```

profile of v0, /device:TPU:0, one launch (start us, length us, event | category | flops | bytes accessed | tf_op | source)
XLA Modules:
  0.0 2783.2 jit_solution(83446065345228138)
XLA Ops:
  24.1 183.7 %all-gather.3.cloned.1.call-done = bf16[4096,2048]{1,0:T(8,128)(2,1)} async-done(((bf16[256,2048]{1,0:T(8,128)(2,1)}), bf16[4096,2048]{1,0:T(8,128)(2,1)}) %all-gather.3.cloned.1.call-update) | async-done | bytes 16777232 | tf_op jit(solution)/shard_map/all_gather | solution.py:110
  243.0 35.5 %all-reduce.2 = (f32[2048]{0:T(1024)S(1)}, f32[4096]{0:T(1024)S(1)}) all-reduce(f32[2048]{0:T(1024)S(1)} %get-tuple-element.602, f32[4096]{0:T(1024)S(1)} %multiply_reduce_fusion.1), channel_id=1, replica_groups=mesh['grp'=2,'wide'=8,'narrow'=2] {'wide'}, use_global_device_ids=true, to_apply=%region_2.3 | all-reduce | flops 6144 | bytes 49152 | tf_op jit(solution)/shard_map/psum | solution.py:125
  305.8 106.0 %while.34 = (s32[]{:T(128)}, bf16[4,512,2,128]{3,2,1,0:T(2,128)(2,1)}, f32[4,2,512]{2,1,0:T(2,128)S(1)}, s32[4,512]{1,0:T(4,128)S(1)}, bf16[4096,2,128]{0,2,1:T(...) while((s32[]{:T(128)}, ...), condition=%wide.region_8.9_spmd.clone, body=%wide.region_5.8_spmd.clone.sunk | while | flops 1810701056 | bytes 74081776 | solution.py:187
  434.5 130.6 %reduce-scatter.5.cloned.1.call-done = bf16[256,2048]{1,0:T(8,128)(2,1)} async-done(((bf16[2048,2048]{1,0:T(8,128)(2,1)}), bf16[256,2048]{1,0:T(8,128)(2,1)}) %reduce-scatter.5.cloned.1.call-update) | async-done | bytes 1048592 | tf_op jit(solution)/shard_map/reduce_scatter | solution.py:190
  587.4 233.7 %all_to_all.20 = bf16[16,160,2048]{2,1,0:T(8,128)(2,1)S(1)} all-to-all(bf16[16,160,2048]{2,1,0:T(8,128)(2,1)S(1)} %broadcast_select_fusion), channel_id=1, replica_groups=mesh['grp'=2,'wide'=8,'narrow'=2] {'wide','narrow'}, dimensions={0} | all-to-all | bytes 20971520 | tf_op jit(solution)/shard_map/all_to_all | solution.py:214
  861.7 16.6 convolution_convert_fusion.2
  886.8 195.5 %all-to-all-done.1 = bf16[16,160,2048]{2,1,0:T(8,128)(2,1)} async-done(((bf16[16,160,2048]{2,1,0:T(8,128)(2,1)}), bf16[16,160,2048]{2,1,0:T(8,128)(2,1)}, u32[]{:S(2)}, u32[]{:S(2)}) %all-to-all-start.1) | async-done | bytes 10485792 | tf_op jit(solution)/shard_map/all_to_all | solution.py:225
  1082.3 21.6 gather_fusion.1
  1110.3 19.0 scatter_custom_fusion.1
  1129.2 294.2 %all_to_all.21 = bf16[16,160,2048]{2,1,0:T(8,128)(2,1)} all-to-all(bf16[16,160,2048]{2,1,0:T(8,128)(2,1)} %bitcast.307), channel_id=1, replica_groups=mesh['grp'=2,'wide'=8,'narrow'=2] {'wide','narrow'}, dimensions={0} | all-to-all | bytes 20971520 | tf_op jit(solution)/shard_map/all_to_all | solution.py:243
  1423.5 23.5 fusion.141
  1447.0 18.2 fusion.144
  1465.2 20.0 add_convert_fusion
  1490.1 198.6 %all-to-all-done.3 = bf16[16,160,2048]{2,1,0:T(8,128)(2,1)} async-done(((bf16[16,160,2048]{2,1,0:T(8,128)(2,1)}), bf16[16,160,2048]{2,1,0:T(8,128)(2,1)}, u32[]{:S(2)}, u32[]{:S(2)}) %all-to-all-start.3) | async-done | bytes 10485792 | tf_op jit(solution)/shard_map/all_to_all | solution.py:268
  1688.7 22.1 gather_fusion.2
  1710.8 17.4 convert_reduce_fusion
  1737.1 182.9 %all-gather.5.cloned.1.call-done = bf16[2048,2048]{1,0:T(8,128)(2,1)} async-done(((bf16[256,2048]{1,0:T(8,128)(2,1)}), bf16[2048,2048]{1,0:T(8,128)(2,1)}) %all-gather.5.cloned.1.call-update) | async-done | bytes 8388624 | tf_op jit(solution)/shard_map/all_gather | solution.py:293
  1931.9 316.8 %while.35 = (s32[]{:T(128)}, f32[4096,2,128]{0,2,1:T(8,128)}, f32[4096,2,128]{0,2,1:T(8,128)}, f32[4,512,2,128]{3,1,0,2:T(8,128)}, s32[4,512]{1,0:T(4,128)}, /*i...) while((s32[]{:T(128)}, f32[4096,2,128]{0,2,1:T(8,128)}, ...), condition=%wide.region_27.29_spmd.clone, body=%wide.region_25.28_spmd.clone.sunk | while | flops 4423790592 | bytes 250623584 | solution.py:337
  2273.3 34.2 %all-reduce.1 = (f32[4096]{0:T(1024)S(1)}, f32[2048]{0:T(1024)S(1)}) all-reduce(f32[4096]{0:T(1024)S(1)} %get-tuple-element.486, f32[2048]{0:T(1024)S(1)} %get-tuple-element.490), channel_id=1, replica_groups=mesh['grp'=2,'wide'=8,'narrow'=2] {'wide'}, use_global_device_ids=true, to_apply=%region_31.33 | all-reduce | flops 6144 | bytes 49152 | tf_op jit(solution)/shard_map/psum | solution.py:344
  2378.2 83.8 %all-reduce.9.cloned.1.call-done = bf16[2048,16]{0,1:T(8,128)(2,1)} async-done(((bf16[2048,16]{0,1:T(8,128)(2,1)}), bf16[2048,16]{0,1:T(8,128)(2,1)}) %all-reduce.9.cloned.1.call-update) | async-done | bytes 65552 | tf_op jit(solution)/shard_map/psum | solution.py:423
  2463.5 17.5 convolution_bitcast_fusion
  2519.4 53.9 %all-reduce.11.cloned.1.call-done = (bf16[2048,256]{1,0:T(8,128)(2,1)}, bf16[2048,256]{1,0:T(8,128)(2,1)}, bf16[2048,256]{1,0:T(8,128)(2,1)}, bf16[256,2048]{1,0:T(8,128)(2,1)}) async-done(((bf16[2048,256]{1,0:T(8,128)(2,1)}, bf16[2048,256]{1,0:T(8,128)(2,1)}, bf16[2048,256]{1,0:T(8,128)(2,1)}, bf16[256,2048]{1,0:T(8,128)(2,1)}), (bf16[2048,256]{1,0:T(8,128)(2,1)}, bf16[2048,256]{1,0:T(8,128)(2,1)}, ...) | async-done | bytes 4194320 | tf_op jit(solution)/shard_map/psum | solution.py:395
  2582.0 144.4 %reduce-scatter.11.cloned.1.call-done = bf16[256,2048]{1,0:T(8,128)(2,1)} async-done(((bf16[2048,2048]{1,0:T(8,128)(2,1)}), bf16[256,2048]{1,0:T(8,128)(2,1)}) %reduce-scatter.11.cloned.1.call-update) | async-done | bytes 1048592 | tf_op jit(solution)/shard_map/reduce_scatter | solution.py:383
  2728.2 41.4 %all-reduce.3 = (bf16[2048]{0:T(1024)(128)(2,1)S(1)}, bf16[2048]{0:T(1024)(128)(2,1)S(1)}, bf16[5]{0:T(256)(128)(2,1)S(1)}, bf16[]{:T(256)}) all-reduce(bf16[2048]{0:T(1024)(128)(2,1)S(1)} %get-tuple-element.496, bf16[2048]{0:T(1024)(128)(2,1)S(1)} %copy-done.58, ...), channel_id=1, replica_groups=mesh['grp'=2,'wide'=8,'narrow'=2] {'wide','narrow'}, use_global_device_ids=true, to_apply=%region_41.43 | all-reduce | flops 4102 | bytes 16408 | tf_op jit(solution)/shard_map/psum | solution.py:424
  (586 shorter events, 750.7 us)
Async XLA Ops:
  7.2 404.7 %copy-start = (bf16[256,2048]{1,0:T(8,128)(2,1)S(1)}, bf16[256,2048]{1,0:T(8,128)(2,1)}, u32[]{:S(2)}) copy-start(bf16[256,2048]{1,0:T(8,128)(2,1)} %param.29) | copy-start | bytes 3145732
  7.2 200.5 %copy-start.63 = (bf16[2048,256]{1,0:T(8,128)(2,1)S(1)}, bf16[2048,256]{1,0:T(8,128)(2,1)}, u32[]{:S(2)}) copy-start(bf16[2048,256]{1,0:T(8,128)(2,1)} %param.28) | copy-start | bytes 3145732
  7.2 200.5 %copy-start.64 = (bf16[2048,256]{1,0:T(8,128)(2,1)S(1)}, bf16[2048,256]{1,0:T(8,128)(2,1)}, u32[]{:S(2)}) copy-start(bf16[2048,256]{1,0:T(8,128)(2,1)} %param.27) | copy-start | bytes 3145732
  7.2 200.5 %all-gather.3.cloned.1.call-start = ((), (), s32[]{:S(2)}) async-start(), calls=%async_computation.8 | async-start | bytes 17825792 | tf_op jit(solution)/shard_map/all_gather | solution.py:110
  13.3 551.8 %reduce-scatter.5.cloned.1.call-start = ((), (), s32[]{:S(2)}) async-start(), calls=%async_computation.9 | async-start | bytes 9437184 | tf_op jit(solution)/shard_map/reduce_scatter | solution.py:190
  13.4 266.3 %copy-start.51 = (f32[256]{0:T(256)}, f32[256]{0:T(256)S(1)}, u32[]{:S(2)}) copy-start(f32[256]{0:T(256)S(1)} %convert_element_type.252) | copy-start | bytes 3076
  13.4 284.1 %copy-start.53 = (f32[256]{0:T(256)}, f32[256]{0:T(256)S(1)}, u32[]{:S(2)}) copy-start(f32[256]{0:T(256)S(1)} %convert_element_type.254) | copy-start | bytes 3076
  411.8 155.2 %copy-start.3 = (bf16[4096,2,128]{2,0,1:T(8,128)(2,1)}, bf16[4096,2,128]{2,0,1:T(8,128)(2,1)S(1)}, u32[]{:S(2)}) copy-start(bf16[4096,2,128]{2,0,1:T(8,128)(2,1)S(1)} %get-tuple-element.865) | copy-start | bytes 6291460
  420.7 150.1 %copy-start.35 = (f32[2048]{0:T(1024)}, f32[2048]{0:T(1024)S(1)}, u32[]{:S(2)}) copy-start(f32[2048]{0:T(1024)S(1)} %convert_element_type.258) | copy-start | bytes 24580
  587.4 233.7 %copy-start.62 = (bf16[1,2048,1024]{2,1,0:T(8,128)(2,1)S(1)}, bf16[1,2048,1024]{2,1,0:T(8,128)(2,1)}, u32[]{:S(2)}) copy-start(bf16[1,2048,1024]{2,1,0:T(8,128)(2,1)} %param.36) | copy-start | bytes 12582916
  878.3 204.1 %all-to-all-start.1 = ((bf16[16,160,2048]{2,1,0:T(8,128)(2,1)}), bf16[16,160,2048]{2,1,0:T(8,128)(2,1)}, u32[]{:S(2)}, u32[]{:S(2)}) async-start(bf16[16,160,2048]{2,1,0:T(8,128)(2,1)} %convolution_convert_fusion.2), calls=%async_computation.2 | async-start | bytes 20971520 | tf_op jit(solution)/shard_map/all_to_all | solution.py:225
  1485.2 203.5 %all-to-all-start.3 = ((bf16[16,160,2048]{2,1,0:T(8,128)(2,1)}), bf16[16,160,2048]{2,1,0:T(8,128)(2,1)}, u32[]{:S(2)}, u32[]{:S(2)}) async-start(bf16[16,160,2048]{2,1,0:T(8,128)(2,1)} %add_convert_fusion), calls=%async_computation.4 | async-start | bytes 20971520 | tf_op jit(solution)/shard_map/all_to_all | solution.py:268
  1490.0 430.0 %all-gather.5.cloned.1.call-start = ((), (), s32[]{:S(2)}) async-start(), calls=%async_computation.10 | async-start | bytes 9437184 | tf_op jit(solution)/shard_map/all_gather | solution.py:293
  1490.1 238.1 %copy-start.42 = (bf16[256,16]{0,1:T(8,128)(2,1)}, bf16[256,16]{0,1:T(8,128)(2,1)S(1)}, u32[]{:S(2)}) copy-start(bf16[256,16]{0,1:T(8,128)(2,1)S(1)} %multiply_convert_fusion.2) | copy-start | bytes 24580
  1734.6 602.1 %reduce-scatter.9.cloned.1.call-start = ((), (), s32[]{:S(2)}) async-start(), calls=%async_computation.12 | async-start | bytes 3145728 | tf_op jit(solution)/shard_map/reduce_scatter | solution.py:369
  2257.3 95.9 %reduce-scatter.7.cloned.1.call-start = ((), (), s32[]{:S(2)}) async-start(), calls=%async_computation.11 | async-start | bytes 3145728 | tf_op jit(solution)/shard_map/reduce_scatter | solution.py:363
  2324.0 138.0 %all-reduce.9.cloned.1.call-start = ((), (), s32[]{:S(2)}) async-start(), calls=%async_computation.14 | async-start | bytes 131072 | tf_op jit(solution)/shard_map/psum | solution.py:423
  2326.2 247.1 %all-reduce.11.cloned.1.call-start = ((), (), s32[]{:S(2)}) async-start(), calls=%async_computation.15 | async-start | bytes 8388608 | tf_op jit(solution)/shard_map/psum | solution.py:395
  2366.1 360.2 %reduce-scatter.11.cloned.1.call-start = ((), (), s32[]{:S(2)}) async-start(), calls=%async_computation.13 | async-start | bytes 9437184 | tf_op jit(solution)/shard_map/reduce_scatter | solution.py:383
  2576.1 150.2 %copy-start.10 = (bf16[256,2048]{1,0:T(8,128)(2,1)S(1)}, bf16[256,2048]{1,0:T(8,128)(2,1)}, u32[]{:S(2)}) copy-start(bf16[256,2048]{1,0:T(8,128)(2,1)} %param.22) | copy-start | bytes 3145732
  2576.1 150.2 %copy-start.33 = (f32[2048]{0:T(1024)S(1)}, f32[2048]{0:T(1024)}, u32[]{:S(2)}) copy-start(f32[2048]{0:T(1024)} %copy-done.32) | copy-start | bytes 24580
  2576.1 150.2 %copy-start.46 = (f32[256]{0:T(256)S(1)}, f32[256]{0:T(256)}, u32[]{:S(2)}) copy-start(f32[256]{0:T(256)} %copy-done.45) | copy-start | bytes 3076
  2578.9 149.3 %copy-start.58 = (bf16[2048]{0:T(1024)(128)(2,1)S(1)}, bf16[2048]{0:T(1024)(128)(2,1)}, u32[]{:S(2)}) copy-start(bf16[2048]{0:T(1024)(128)(2,1)} %get-tuple-element.495) | copy-start | bytes 12292
  2578.9 193.1 %copy-start.55 = (f32[256]{0:T(256)S(1)}, f32[256]{0:T(256)}, u32[]{:S(2)}) copy-start(f32[256]{0:T(256)} %get-tuple-element.598) | copy-start | bytes 3076
  (79 other events, 734.4 us)
Sparse Core Ops, SparseCore 0:
  13.4 194.2 all-gather.2
  419.8 145.2 reduce-scatter.4
  1734.7 185.2 all-gather.4
  2257.4 29.8 reduce-scatter.8
  2324.1 29.0 reduce-scatter.6
  2360.0 101.9 all-reduce.8
  2465.2 108.0 all-reduce.10
  2577.3 148.9 reduce-scatter.10
where the time goes:
time: 2800 us; the launch traced here: 2780 us
  waiting for transfers between devices  1190 us (42%)
  blocking collectives  644 us (23%)
  matrix products  344 us (12%)
  other arithmetic  279 us (10%)
  local copies, waits for them, and re-layouts  272 us (10%)
  loops' own time  28.2 us (1%)
    all_to_all x1, blocking collectives, shards(): lax.all_to_all(grad_slots.reshape(devices_part, EXP_DEV * capacity, D), (...  294 us
    all_to_all x1, blocking collectives, shards(): lax.all_to_all(send, ('wide', 'narrow'), split_axis=0, concat_axis=0, til...  234 us
    all_to_all x1, waiting for transfers between devices, shards(): lax.all_to_all(grad_route_in.reshape(devices_part, EXP_DEV * capacity, D)...  199 us
    all_to_all x1, waiting for transfers between devices, shards(): lax.all_to_all(expert_out.reshape(devices_part, EXP_DEV * capacity, D), (...  196 us
    all_gather x1, waiting for transfers between devices, shards(): normed_all = lax.all_gather(normed, ('wide', 'narrow'), axis=0, tiled=True)  184 us
    all_gather x1, waiting for transfers between devices, shards(): piece = lax.all_gather(grad_branch, 'wide', axis=0, tiled=True)  183 us
    reduce_scatter x1, waiting for transfers between devices, shards(): lax.psum_scatter(jnp.einsum('tc,dc->td', piece, weights_joined, preferred...  144 us
    reduce_scatter x1, waiting for transfers between devices, shards(): lax.psum_scatter(jnp.dot(piece, w_out, preferred_element_type=jnp.float32...  131 us
  transfers between devices with their start and end apart: 10, of which 9 were waited for; matrix products, arithmetic and copies ran while one was open for 6% of the time, Pallas kernels for 0%

commit v1 on v0

v1 whole, which is shorter than its diff:
```python
import functools

import jax
import jax.numpy as jnp
from jax import lax
from jax.experimental import pallas as pl
from jax.experimental.pallas import tpu as pltpu
from jax.sharding import PartitionSpec as P

D = 2048
HD = 128
TOP = 8
PROMPT = 2048
CONT = 256
NCONT = 8

EPSILON = 1e-05
THETA = 10000.0
NEGATIVE = -1e30


LOG2E = 1.4426950408889634
NT = (((1,), (1,)), ((), ()))


def block_parts(w, rows, prompt_blocks, paired, limit):
    def cut(plane, count):
        return [
            (plane, first, min(limit, count - first), None) for first in range(0, count, limit)
        ]

    if w is None:
        parts = cut(0, prompt_blocks * rows) + cut(1, prompt_blocks * rows)
        own = None
        if paired:
            parts.append((1, None, rows, "side"))
    else:
        own = w * rows
        parts = cut(0, own) + cut(1, own) + [(1, own, rows, "side")]
    return parts + [(0, own, rows, "causal")]


def for_blocks(blocks, prompt_blocks, one):
    for w in range(prompt_blocks):
        one(w, w)

    def body(w, carry):
        one(None, w)
        return carry

    lax.fori_loop(prompt_blocks, blocks, body, 0)


def masked_scores(score, mask, side, rows):
    if mask == "causal":
        key = lax.broadcasted_iota(jnp.int32, (rows, rows), 0)
        query = lax.broadcasted_iota(jnp.int32, (rows, rows), 1)
        return jnp.where(key <= query, score, NEGATIVE)
    if mask == "side":
        return jnp.where(side == 1, score, NEGATIVE)
    return score


def attend_kernel(rows, prompt_blocks, paired, side_ref, q_ref, k_ref, v_ref, ko_ref, vo_ref, o_ref, lse_ref, vt_ref):
    half, columns = q_ref.shape
    side = side_ref[0]
    for h in range(columns // HD):
        hs = slice(h * HD, (h + 1) * HD)
        for plane, ref in enumerate((v_ref, vo_ref)):
            vt_ref[plane, hs, :] = ref[:, hs].T

    def one(w, w_index):
        start = w_index * rows if w is not None else pl.multiple_of(w_index * rows, rows)
        for h in range(columns // HD):
            hs = slice(h * HD, (h + 1) * HD)
            query = q_ref[pl.ds(start, rows), hs]
            scores = []
            for plane, first, count, mask in block_parts(w, rows, prompt_blocks, paired, 512):
                at = pl.ds(start if first is None else first, count)
                key = (k_ref, ko_ref)[plane][at, hs]
                score = lax.dot_general(key, query, NT, preferred_element_type=jnp.float32)
                score = score * (HD**-0.5 * LOG2E)
                scores.append((plane, at, masked_scores(score, mask, side, rows)))
            largest = functools.reduce(
                jnp.maximum, [jnp.max(score, 0, keepdims=True) for _, _, score in scores]
            )
            total = jnp.zeros((1, rows), jnp.float32)
            mixed = jnp.zeros((HD, rows), jnp.float32)
            for plane, at, score in scores:
                weight = jnp.exp2(score - largest)
                total = total + jnp.sum(weight, 0, keepdims=True)
                mixed = mixed + jnp.dot(
                    vt_ref[plane, hs, at], weight.astype(jnp.bfloat16), preferred_element_type=jnp.float32
                )
            o_ref[pl.ds(start, rows), hs] = (mixed / total).T.astype(jnp.bfloat16)
            lse_ref[h : h + 1, pl.ds(start, rows)] = largest + jnp.log(total) * LOG2E

    for_blocks(half // rows, prompt_blocks, one)


def attend_back_kernel(
    rows, prompt_blocks, paired, side_ref, q_ref, k_ref, v_ref, ko_ref, vo_ref, do_ref, o_ref, lse_ref,
    dq_ref, dk_ref, dv_ref, dko_ref, dvo_ref, kt_ref,
):
    half, columns = q_ref.shape
    side = side_ref[0]
    for ref in (dk_ref, dv_ref, dko_ref, dvo_ref):
        ref[...] = jnp.zeros_like(ref)
    for h in range(columns // HD):
        hs = slice(h * HD, (h + 1) * HD)
        for plane, ref in enumerate((k_ref, ko_ref)):
            kt_ref[plane, hs, :] = ref[:, hs].T

    def one(w, w_index):
        start = w_index * rows if w is not None else pl.multiple_of(w_index * rows, rows)
        for h in range(columns // HD):
            hs = slice(h * HD, (h + 1) * HD)
            query = q_ref[pl.ds(start, rows), hs]
            grad = do_ref[pl.ds(start, rows), hs]
            product = grad.astype(jnp.float32) * o_ref[pl.ds(start, rows), hs].astype(jnp.float32)
            delta = jnp.sum(product.T, 0, keepdims=True)
            lse = lse_ref[h : h + 1, pl.ds(start, rows)]
            back = jnp.zeros((HD, rows), jnp.float32)
            for plane, first, count, mask in block_parts(w, rows, prompt_blocks, paired, 512):
                at = pl.ds(start if first is None else first, count)
                key = (k_ref, ko_ref)[plane][at, hs]
                value = (v_ref, vo_ref)[plane][at, hs]
                score = lax.dot_general(key, query, NT, preferred_element_type=jnp.float32)
                score = masked_scores(score * (HD**-0.5 * LOG2E), mask, side, rows)
                weight = jnp.exp2(score - lse)
                grad_weight = lax.dot_general(value, grad, NT, preferred_element_type=jnp.float32)
                grad_score = (weight * (grad_weight - delta)).astype(jnp.bfloat16)
                dv = (dv_ref, dvo_ref)[plane]
                dv[at, hs] += jnp.dot(weight.astype(jnp.bfloat16), grad, preferred_element_type=jnp.float32)
                dk = (dk_ref, dko_ref)[plane]
                dk[at, hs] += jnp.dot(grad_score, query, preferred_element_type=jnp.float32) * HD**-0.5
                back = back + jnp.dot(kt_ref[plane, hs, at], grad_score, preferred_element_type=jnp.float32)
            dq_ref[pl.ds(start, rows), hs] = back.T * HD**-0.5

    for_blocks(half // rows, prompt_blocks, one)


def attention_calls(rows, half, columns, prompt_blocks, paired):
    smem = pl.BlockSpec(memory_space=pltpu.SMEM)
    vmem = pl.BlockSpec(memory_space=pltpu.VMEM)
    heads = columns // HD
    params = pltpu.CompilerParams(vmem_limit_bytes=60 * 2**20)
    wide16 = jax.ShapeDtypeStruct((half, columns), jnp.bfloat16)
    wide32 = jax.ShapeDtypeStruct((half, columns), jnp.float32)
    work = half * half * columns * 2
    forward = pl.pallas_call(
        functools.partial(attend_kernel, rows, prompt_blocks, paired),
        out_shape=(wide16, jax.ShapeDtypeStruct((heads, half), jnp.float32)),
        in_specs=[smem] + [vmem] * 5,
        out_specs=(vmem, vmem),
        scratch_shapes=[pltpu.VMEM((2, columns, half), jnp.bfloat16)],
        compiler_params=params,
        cost_estimate=pl.CostEstimate(flops=2 * work, bytes_accessed=half * columns * 12, transcendentals=0),
    )
    backward = pl.pallas_call(
        functools.partial(attend_back_kernel, rows, prompt_blocks, paired),
        out_shape=(wide32,) * 5,
        in_specs=[smem] + [vmem] * 8,
        out_specs=(vmem,) * 5,
        scratch_shapes=[pltpu.VMEM((2, columns, half), jnp.bfloat16)],
        compiler_params=params,
        cost_estimate=pl.CostEstimate(flops=5 * work, bytes_accessed=half * columns * 40, transcendentals=0),
    )
    return forward, backward


def positions(token_ids):
    local = token_ids % (PROMPT + NCONT * CONT)
    return jnp.where(local < PROMPT, local, PROMPT + (local - PROMPT) % CONT)


def rotation(place):
    frequency = THETA ** (-2.0 * jnp.arange(HD // 2, dtype=jnp.float32) / HD)
    angle = place.astype(jnp.float32)[:, None] * frequency[None, :]
    cosine, sine = jnp.cos(angle), jnp.sin(angle)
    return jnp.concatenate([cosine, cosine], 1), jnp.concatenate([-sine, sine], 1)


def swap_halves(values):
    return jnp.concatenate([values[..., HD // 2 :], values[..., : HD // 2]], -1)


def rotate(values, cosine, sine):
    rows, columns = values.shape
    heads = values.reshape(rows, columns // HD, HD)
    turned = heads * cosine[:, None, :] + swap_halves(heads) * sine[:, None, :]
    return turned.reshape(rows, columns)


def dot(a, b):
    return jnp.dot(a, b, preferred_element_type=jnp.float32)


def dot_nt(a, b):
    return lax.dot_general(a, b, (((1,), (1,)), ((), ())), preferred_element_type=jnp.float32)


def dot_tn(a, b):
    return lax.dot_general(a, b, (((0,), (0,)), ((), ())), preferred_element_type=jnp.float32)


def shards(
    tokens,
    cotangent,
    valid,
    routes,
    w_query,
    w_key,
    w_value,
    w_out,
    norm_attn,
    norm_query,
    norm_key,
    norm_moe,
    w_router,
    w_gate,
    w_up,
    w_down,
):
    bf16, f32 = jnp.bfloat16, jnp.float32
    wide_count = lax.axis_size("wide")
    narrow_count = lax.axis_size("narrow")
    rows = tokens.shape[0]
    half = rows * wide_count
    columns = w_query.shape[1]
    experts = w_router.shape[1]
    capacity = min(max(rows * TOP * 5 // (4 * experts), 2), rows)
    assert narrow_count == 2 and CONT in (rows, 2 * rows)
    side = lax.axis_index("narrow")
    place = lax.axis_index("wide")
    swap = [(0, 1), (1, 0)]
    prompt_blocks = PROMPT // (rows * narrow_count)
    attend, attend_back = attention_calls(rows, half, columns, prompt_blocks, CONT == 2 * rows)
    side_array = side.astype(jnp.int32).reshape(1)

    stream = tokens.astype(f32)
    inv_one = lax.rsqrt(jnp.mean(stream * stream, -1, keepdims=True) + EPSILON)
    gain_one = norm_attn.astype(f32)
    normed = (stream * inv_one * gain_one).astype(bf16)
    normed_plane = lax.all_gather(normed, "wide", axis=0, tiled=True)
    mask = valid.astype(f32)[:, None]
    grad_final = cotangent.astype(f32) * mask
    routes_plane = lax.all_gather(routes, "wide", axis=0, tiled=True)
    w_out_all = lax.all_gather(w_out, "wide", axis=0, tiled=True)
    grad_plane = lax.all_gather(grad_final.astype(bf16), "wide", axis=0, tiled=True)
    other_weights = [lax.ppermute(w, "narrow", swap) for w in (w_gate[0], w_up[0], w_down[0])]

    joined = jnp.concatenate([w_query, w_key, w_value], 1)
    raw = dot(normed_plane, joined)
    query_raw, key_raw, value_raw = (raw[:, i * columns : (i + 1) * columns] for i in range(3))
    sums = lax.psum(jnp.stack([jnp.sum(query_raw * query_raw, -1), jnp.sum(key_raw * key_raw, -1)]), "wide")
    inv_query, inv_key = lax.rsqrt(sums / D + EPSILON)[:, :, None]
    gain_query = norm_query.astype(f32)
    gain_key = norm_key.astype(f32)
    plane_ids = (
        (jnp.arange(wide_count, dtype=jnp.int32)[:, None] * narrow_count + side) * rows
        + jnp.arange(rows, dtype=jnp.int32)[None, :]
    ).reshape(half)
    cosine, sine = rotation(positions(plane_ids))
    query_rot = rotate(query_raw * inv_query * gain_query, cosine, sine).astype(bf16)
    key_rot = rotate(key_raw * inv_key * gain_key, cosine, sine).astype(bf16)
    value_b = value_raw.astype(bf16)
    key_other = lax.ppermute(key_rot, "narrow", swap)
    value_other = lax.ppermute(value_b, "narrow", swap)
    attended, lse = attend(side_array, query_rot, key_rot, value_b, key_other, value_other)

    attended_own = lax.all_to_all(attended, "wide", split_axis=0, concat_axis=1, tiled=True)
    branch = dot(attended_own, w_out_all)
    hidden = stream + branch
    inv_two = lax.rsqrt(jnp.mean(hidden * hidden, -1, keepdims=True) + EPSILON)
    gain_two = norm_moe.astype(f32)
    moe_in = (hidden * inv_two * gain_two).astype(bf16)
    moe_plane = lax.all_gather(moe_in, "wide", axis=0, tiled=True)

    probs = jax.nn.softmax(dot(moe_plane, w_router), -1)
    named = jnp.any(routes_plane[:, :, None] == jnp.arange(experts, dtype=jnp.int32), 1)
    gates_dense = jnp.where(named, probs, 0.0)
    blocks = lambda a: a.reshape(wide_count, rows, -1)
    earlier = (jnp.arange(rows)[:, None] < jnp.arange(rows)[None, :]).astype(bf16)

    def pick(expert):
        chosen = jnp.take(named, expert, axis=1).reshape(wide_count, rows)
        rank = dot(chosen.astype(bf16), earlier).astype(jnp.int32)
        slot = jnp.where(chosen, rank, -1)
        onehot = (jnp.arange(capacity, dtype=jnp.int32)[None, :, None] == slot[:, None, :]).astype(bf16)
        return onehot

    def compact(onehot, values):
        return jnp.einsum(
            "wcr,wrd->wcd", onehot, blocks(values), preferred_element_type=f32
        ).astype(bf16).reshape(wide_count * capacity, -1)

    def spread(onehot, values):
        return jnp.einsum(
            "wcr,wcd->wrd", onehot, values.reshape(wide_count, capacity, -1), preferred_element_type=f32
        ).reshape(half, -1)

    moe_part = 0.0
    grad_part = 0.0
    mixing = 0.0
    expert_grads = []
    for expert, (gate_w, up_w, down_w) in (
        (place * narrow_count + side, (w_gate[0], w_up[0], w_down[0])),
        (place * narrow_count + 1 - side, other_weights),
    ):
        onehot = pick(expert)
        inputs = compact(onehot, moe_plane)
        grads = compact(onehot, grad_plane)
        gate_own = jnp.take(gates_dense, expert, axis=1)
        gate = jnp.sum(
            onehot.astype(f32) * gate_own.reshape(wide_count, 1, rows), -1
        ).reshape(wide_count * capacity, 1)
        gate_pre = dot(inputs, gate_w)
        up_pre = dot(inputs, up_w)
        back = dot_nt(grads, down_w)
        sigmoid = jax.nn.sigmoid(gate_pre)
        silu = gate_pre * sigmoid
        inner = silu * up_pre
        inner_gated = (gate * inner).astype(bf16)
        grad_gate_row = jnp.sum(inner * back, -1)
        grad_inner = gate * back
        grad_gate_pre = (grad_inner * up_pre * sigmoid * (1.0 + gate_pre * (1.0 - sigmoid))).astype(bf16)
        grad_up_pre = (grad_inner * silu).astype(bf16)
        route_in = (dot_nt(grad_gate_pre, gate_w) + dot_nt(grad_up_pre, up_w)).astype(bf16)
        grad_part = grad_part + spread(onehot, route_in)
        moe_part = moe_part + spread(onehot, dot(inner_gated, down_w).astype(bf16))
        grad_gates = jnp.sum(
            onehot.astype(f32) * grad_gate_row.reshape(wide_count, capacity, 1), 1
        ).reshape(half, 1)
        weight = gate_own[:, None] * grad_gates
        here = (jnp.arange(experts, dtype=jnp.int32) == expert).astype(f32)
        mixing = mixing + weight * (here[None, :] - probs)
        expert_grads.append(
            (dot_tn(inputs, grad_gate_pre), dot_tn(inputs, grad_up_pre), dot_tn(inner_gated, grads))
        )
    mixing = mixing.astype(bf16)
    grad_part = grad_part + dot_nt(mixing, w_router)
    grad_moe_in = lax.psum_scatter(
        grad_part.astype(bf16), "wide", scatter_dimension=0, tiled=True
    ).astype(f32)
    moe = lax.psum_scatter(moe_part.astype(bf16), "wide", scatter_dimension=0, tiled=True).astype(f32)
    grad_router = dot_tn(moe_plane, mixing)
    partner = [lax.ppermute(g.astype(bf16), "narrow", swap) for g in expert_grads[1]]
    grad_gate_w, grad_up_w, grad_down_w = (
        (own + other.astype(f32))[None] for own, other in zip(expert_grads[0], partner)
    )

    final = hidden + moe
    output = final.astype(bf16)
    grad_gain_two = jnp.sum(grad_moe_in * hidden * inv_two, 0)
    grad_hidden = (
        grad_final
        + inv_two * gain_two * grad_moe_in
        - hidden * inv_two**3 * jnp.sum(grad_moe_in * gain_two * hidden, -1, keepdims=True) / D
    )
    grad_branch = grad_hidden.astype(bf16)
    grad_attended_own = dot_nt(grad_branch, w_out_all).astype(bf16)
    grad_attended = lax.all_to_all(grad_attended_own, "wide", split_axis=1, concat_axis=0, tiled=True)
    branch_plane = lax.all_gather(grad_branch, "wide", axis=0, tiled=True)
    grad_out = dot_tn(attended, branch_plane)

    grad_query_rot, grad_key_rot, grad_value, grad_key_other, grad_value_other = attend_back(
        side_array, query_rot, key_rot, value_b, key_other, value_other, grad_attended, attended, lse
    )
    grad_key_rot = grad_key_rot + lax.ppermute(grad_key_other.astype(bf16), "narrow", swap).astype(f32)
    grad_value = grad_value + lax.ppermute(grad_value_other.astype(bf16), "narrow", swap).astype(f32)
    grad_query_normed = rotate(grad_query_rot, cosine, -sine)
    grad_key_normed = rotate(grad_key_rot, cosine, -sine)
    dots = lax.psum(
        jnp.stack(
            [
                jnp.sum(grad_query_normed * gain_query * query_raw, -1),
                jnp.sum(grad_key_normed * gain_key * key_raw, -1),
            ]
        ),
        "wide",
    )[:, :, None]
    grad_gain_query = jnp.sum(grad_query_normed * query_raw * inv_query, 0)
    grad_gain_key = jnp.sum(grad_key_normed * key_raw * inv_key, 0)
    grad_query_raw = inv_query * gain_query * grad_query_normed - query_raw * inv_query**3 * dots[0] / D
    grad_key_raw = inv_key * gain_key * grad_key_normed - key_raw * inv_key**3 * dots[1] / D
    grads_joined = jnp.concatenate([grad_query_raw, grad_key_raw, grad_value], 1).astype(bf16)
    grad_normed = lax.psum_scatter(
        dot_nt(grads_joined, joined).astype(bf16), "wide", scatter_dimension=0, tiled=True
    ).astype(f32)
    grad_weights = dot_tn(normed_plane, grads_joined)
    summed = lax.psum(
        (
            grad_weights.astype(bf16),
            grad_out.astype(bf16),
            grad_gain_query.astype(bf16),
            grad_gain_key.astype(bf16),
        ),
        "narrow",
    )
    grad_query_w, grad_key_w, grad_value_w = (
        summed[0][:, i * columns : (i + 1) * columns].astype(f32) for i in range(3)
    )
    grad_gain_one = jnp.sum(grad_normed * stream * inv_one, 0)
    grad_input = (
        grad_hidden
        + inv_one * gain_one * grad_normed
        - stream * inv_one**3 * jnp.sum(grad_normed * gain_one * stream, -1, keepdims=True) / D
    )
    stat_sums = jnp.stack([jnp.sum(v * v * mask) for v in (stream, branch, hidden, moe, final)])
    replicated = lax.psum(
        (
            grad_router.astype(bf16),
            grad_gain_one.astype(bf16),
            grad_gain_two.astype(bf16),
            stat_sums.astype(bf16),
            jnp.sum(mask).astype(bf16),
        ),
        ("wide", "narrow"),
    )
    grad_router, grad_gain_one, grad_gain_two, stat_sums, count = (v.astype(f32) for v in replicated)
    rms = jnp.sqrt(stat_sums / (jnp.maximum(count, 1.0) * D))
    return (
        output,
        grad_input,
        grad_query_w,
        grad_key_w,
        grad_value_w,
        summed[1].astype(f32),
        grad_gain_one,
        summed[2].astype(f32),
        summed[3].astype(f32),
        grad_gain_two,
        grad_router,
        grad_gate_w,
        grad_up_w,
        grad_down_w,
        rms,
    )


def solution(mesh):
    return jax.shard_map(
        shards,
        mesh=mesh,
        in_specs=(
            P(("grp", "wide", "narrow"), None),
            P(("grp", "wide", "narrow"), None),
            P(("grp", "wide", "narrow")),
            P(("grp", "wide", "narrow"), None),
            P(None, "wide"),
            P(None, "wide"),
            P(None, "wide"),
            P("wide", None),
            P(),
            P("wide"),
            P("wide"),
            P(),
            P(),
            P(("wide", "narrow"), None, None),
            P(("wide", "narrow"), None, None),
            P(("wide", "narrow"), None, None),
        ),
        out_specs=(
            P(("grp", "wide", "narrow"), None),
            P(("grp", "wide", "narrow"), None),
            P("grp", "wide"),
            P("grp", "wide"),
            P("grp", "wide"),
            P(("grp", "wide"), None),
            P("grp"),
            P(("grp", "wide")),
            P(("grp", "wide")),
            P("grp"),
            P("grp", None),
            P(("grp", "wide", "narrow"), None, None),
            P(("grp", "wide", "narrow"), None, None),
            P(("grp", "wide", "narrow"), None, None),
            P("grp"),
        ),
        check_vma=False,
    )
```

time: 2800 us -> 1680 us (0.60)
  blocking collectives: 644 us -> 205 us
  waiting for transfers between devices: 1190 us -> 948 us
  local copies, waits for them, and re-layouts: 272 us -> 42 us
  other arithmetic: 279 us -> 88.6 us
  Pallas kernels: 0 us -> 46.4 us
  matrix products: 344 us -> 308 us
  loops' own time: 28.2 us -> 0 us
    all_to_all x2 -> x1, blocking collectives: 528 us -> 57.3 us  [shards(): lax.all_to_all(grad_attended_own, 'wide', split_axis=1, concat_axis=0, ti...]
    all_to_all x2 -> x1, waiting for transfers between devices: 394 us -> 11.7 us  [shards(): lax.all_to_all(attended, 'wide', split_axis=0, concat_axis=1, tiled=True)]
    ppermute x0 -> x10, waiting for transfers between devices: none -> 326 us  [the longest x3 298 us: shards(): lax.ppermute(g.astype(bf16), 'narrow', swap)]
    psum x2, waiting for transfers between devices: 138 us -> 13.2 us  [the longest x1 13.2 us: shards(): lax.psum((grad_router.astype(bf16), grad_gain_one.astype(bf16), grad_gain...]
    dynamic_update_slice x24 -> x0, local copies, waits for them, and re-layouts: 75.2 us -> none  [the longest x8 63.1 us: add_slice(): return lax.dynamic_update_slice_in_dim(total, current + values, start, 0)]
    gather x3 -> x0, local copies, waits for them, and re-layouts: 54.5 us -> none  [the longest x1 22.1 us: shards(): jnp.take(grad_back, slot, axis=0).reshape(rows, TOP, D).astype(jnp.float32)]
    pallas_call x0 -> x2, Pallas kernels: none -> 46.4 us  [the longest x1 28.2 us: shards(): attend_back(side_array, query_rot, key_rot, value_b, key_other, value_oth...]
    dynamic_slice x45 -> x0, local copies, waits for them, and re-layouts: 45.9 us -> none  [the longest x8 14.5 us: key_span(): lax.dynamic_slice_in_dim(value_b, window_start, window, 0)]
  transfers between devices with their start and end apart: 10 -> 21, of which waited for: 9 -> 14; matrix products, arithmetic and copies ran while one was open for 6% -> 18% of each run, Pallas kernels for 0% -> 3%
where the time goes in v1:
time: 1680 us; the launch traced here: 1670 us
  waiting for transfers between devices  948 us (56%)
  matrix products  308 us (18%)
  blocking collectives  205 us (12%)
  other arithmetic  88.6 us (5%)
  Pallas kernels  46.4 us (3%)
  local copies, waits for them, and re-layouts  42 us (2%)
    ppermute x3, waiting for transfers between devices, shards(): lax.ppermute(g.astype(bf16), 'narrow', swap)  298 us
    reduce_scatter x1, waiting for transfers between devices, shards(): lax.psum_scatter(moe_part.astype(bf16), 'wide', scatter_dimension=0, tile...  153 us
    all_gather x1, waiting for transfers between devices, shards(): normed_plane = lax.all_gather(normed, 'wide', axis=0, tiled=True)  118 us
    all_gather x1, waiting for transfers between devices, shards(): moe_plane = lax.all_gather(moe_in, 'wide', axis=0, tiled=True)  115 us
    reduce_scatter x1, waiting for transfers between devices, shards(): lax.psum_scatter(grad_part.astype(bf16), 'wide', scatter_dimension=0, til...  110 us
    dot_general x9, matrix products, dot_nt(): lax.dot_general(a, b, (((1,), (1,)), ((), ())), preferred_element_type=jn...  91.3 us
    dot_general x9, matrix products, dot_tn(): lax.dot_general(a, b, (((0,), (0,)), ((), ())), preferred_element_type=jn...  78.7 us
    dot_general x11, matrix products, dot(): return jnp.dot(a, b, preferred_element_type=jnp.float32)  74.4 us
  transfers between devices with their start and end apart: 21, of which 14 were waited for; matrix products, arithmetic and copies ran while one was open for 18% of the time, Pallas kernels for 3%

profile of v1, /device:TPU:0, one launch (start us, length us, event | category | flops | bytes accessed | tf_op | source)
XLA Modules:
  0.0 1670.5 jit_solution(14110165135548733598)
XLA Ops:
  22.9 118.2 %all-gather.6.cloned.1.call-done = bf16[2048,2048]{1,0:T(8,128)(2,1)} async-done(((bf16[256,2048]{1,0:T(8,128)(2,1)}), bf16[2048,2048]{1,0:T(8,128)(2,1)}) %all-gather.6.cloned.1.call-update) | async-done | bytes 8388624 | tf_op jit(solution)/shard_map/all_gather | solution.py:245
  154.4 35.7 %psum.77 = f32[2,2048]{1,0:T(2,128)S(1)} all-reduce(f32[2,2048]{1,0:T(2,128)S(1)} %pad_maximum_fusion.5), channel_id=1, replica_groups=mesh['grp'=2,'wide'=8,'narrow'=2] {'wide'}, use_global_device_ids=true, to_apply=%region_3.0 | all-reduce | flops 4096 | bytes 32768 | tf_op jit(solution)/shard_map/psum | solution.py:256
  217.3 16.5 collective-permute-done.ko_ref
  234.8 18.3 %shard_map.271 = (bf16[2048,256]{1,0:T(8,128)(2,1)}, f32[2,2048]{1,0:T(2,128)}) custom-call(s32[1]{0:T(128)} %bitcast.side_ref, bf16[2048,256]{1,0:T(8,128)(2,1)} %get-tuple-element.113.q_ref, bf16[2048,256]{1,0:T(8,128)(2,1)} %copy-done.39, bf16[2048,256]{1,0:T(8,128)(2,1)} %slice.113.v_ref, bf16[2048,256]{1,0:T(8,128)(2,1)} %copy-done.75, ...), custom_call_target="tpu_custom_call" | custom-call | flops 4294967296 | bytes 6291456 | tf_op jit(solution)/shard_map/pallas_call | solution.py:270
  259.1 18.1 %all-gather.8.cloned.1.call-done = bf16[2048,2048]{1,0:T(8,128)(2,1)} async-done(((bf16[256,2048]{1,0:T(8,128)(2,1)}), bf16[2048,2048]{1,0:T(8,128)(2,1)}) %all-gather.8.cloned.1.call-update) | async-done | bytes 8388624 | tf_op jit(solution)/shard_map/all_gather | solution.py:249
  277.2 11.7 all-to-all-done
  303.0 31.2 %all_gather.20 = s32[2048,8]{0,1:T(8,128)S(1)} all-gather(s32[256,8]{0,1:T(8,128)S(1)} %copy-done.65), channel_id=1, replica_groups=mesh['grp'=2,'wide'=8,'narrow'=2] {'wide'}, dimensions={0}, use_global_device_ids=true | all-gather | bytes 73728 | tf_op jit(solution)/shard_map/all_gather | solution.py:248
  335.3 72.4 %all-gather.12.cloned.1.call-done = bf16[2048,2048]{1,0:T(8,128)(2,1)} async-done(((bf16[256,2048]{1,0:T(8,128)(2,1)}), bf16[2048,2048]{1,0:T(8,128)(2,1)}) %all-gather.12.cloned.1.call-update) | async-done | bytes 8388624 | tf_op jit(solution)/shard_map/all_gather | solution.py:250
  418.9 114.5 %all-gather.10.cloned.1.call-done = bf16[2048,2048]{1,0:T(8,128)(2,1)} async-done(((bf16[256,2048]{1,0:T(8,128)(2,1)}), bf16[2048,2048]{1,0:T(8,128)(2,1)}) %all-gather.10.cloned.1.call-update) | async-done | bytes 8388624 | tf_op jit(solution)/shard_map/all_gather | solution.py:278
  648.0 12.4 fusion.79
  670.3 14.0 convolution_add_fusion
  721.4 12.1 add_convert_fusion
  733.6 109.8 %reduce-scatter.6.cloned.1.call-done = bf16[256,2048]{1,0:T(8,128)(2,1)} async-done(((bf16[2048,2048]{1,0:T(8,128)(2,1)}), bf16[256,2048]{1,0:T(8,128)(2,1)}) %reduce-scatter.6.cloned.1.call-update) | async-done | bytes 1048592 | tf_op jit(solution)/shard_map/reduce_scatter | solution.py:343
  843.4 152.5 %reduce-scatter.4.cloned.1.call-done = bf16[256,2048]{1,0:T(8,128)(2,1)} async-done(((bf16[2048,2048]{1,0:T(8,128)(2,1)}), bf16[256,2048]{1,0:T(8,128)(2,1)}) %reduce-scatter.4.cloned.1.call-update) | async-done | bytes 1048592 | tf_op jit(solution)/shard_map/reduce_scatter | solution.py:346
  1009.7 57.3 %all_to_all.38 = bf16[256,8,256]{2,0,1:T(8,128)(2,1)} all-to-all(bf16[256,8,256]{2,0,1:T(8,128)(2,1)S(1)} %bitcast.209), channel_id=1, replica_groups=mesh['grp'=2,'wide'=8,'narrow'=2] {'wide'}, dimensions={1} | all-to-all | bytes 2097152 | tf_op jit(solution)/shard_map/all_to_all | solution.py:363
  1067.0 28.2 %shard_map.272 = (f32[2048,256]{1,0:T(8,128)}, f32[2048,256]{1,0:T(8,128)}, f32[2048,256]{1,0:T(8,128)}, f32[2048,256]{1,0:T(8,128)}, f32[2048,256]{1,0:T(8,128)}) custom-call(s32[1]{0:T(128)} %bitcast.side_ref, bf16[2048,256]{1,0:T(8,128)(2,1)} %get-tuple-element.113.q_ref, bf16[2048,256]{1,0:T(8,128)(2,1)} %copy-done.39, bf16[2048,256]{1,0:T(8,128)(2,1)} %slice.113.v_ref, ...), custom_call_target="tpu_custom_call" | custom-call | flops 10737418240 | bytes 20971520 | tf_op jit(solution)/shard_map/pallas_call | solution.py:367
  1112.6 11.6 collective-permute-done.5
  1142.5 34.8 %psum.78 = f32[2,2048]{1,0:T(2,128)S(1)} all-reduce(f32[2,2048]{1,0:T(2,128)S(1)} %pad_maximum_fusion.6), channel_id=1, replica_groups=mesh['grp'=2,'wide'=8,'narrow'=2] {'wide'}, use_global_device_ids=true, to_apply=%region_19.22 | all-reduce | flops 4096 | bytes 32768 | tf_op jit(solution)/shard_map/psum | solution.py:374
  1243.3 13.2 all-reduce.6.cloned.1.call-done
  1258.1 105.9 %collective-permute-done.8 = bf16[2048,1024]{1,0:T(8,128)(2,1)} collective-permute-done((bf16[2048,1024]{1,0:T(8,128)(2,1)}, bf16[2048,1024]{1,0:T(8,128)(2,1)}, u32[]{:S(2)}, u32[]{:S(2)}) %collective-permute-start.8) | collective-permute-done | bytes 4194336 | tf_op jit(solution)/shard_map/ppermute | solution.py:348
  1364.0 12.1 add_bitcast_fusion.1
  1376.1 122.9 %collective-permute-done.7 = bf16[2048,1024]{1,0:T(8,128)(2,1)} collective-permute-done((bf16[2048,1024]{1,0:T(8,128)(2,1)}, bf16[2048,1024]{1,0:T(8,128)(2,1)}, u32[]{:S(2)}, u32[]{:S(2)}) %collective-permute-start.7) | collective-permute-done | bytes 4194336 | tf_op jit(solution)/shard_map/ppermute | solution.py:348
  1508.9 69.5 %collective-permute-done.9 = bf16[1024,2048]{1,0:T(8,128)(2,1)} collective-permute-done((bf16[1024,2048]{1,0:T(8,128)(2,1)}, bf16[1024,2048]{1,0:T(8,128)(2,1)}, u32[]{:S(2)}, u32[]{:S(2)}) %collective-permute-start.9) | collective-permute-done | bytes 4194336 | tf_op jit(solution)/shard_map/ppermute | solution.py:348
  1616.3 41.5 %all-reduce = (bf16[2048]{0:T(1024)(128)(2,1)S(1)}, bf16[2048]{0:T(1024)(128)(2,1)S(1)}, bf16[5]{0:T(256)(128)(2,1)S(1)}, bf16[]{:T(256)}) all-reduce(bf16[2048]{0:T(1024)(128)(2,1)S(1)} %get-tuple-element.67, bf16[2048]{0:T(1024)(128)(2,1)S(1)} %get-tuple-element.66, ...), channel_id=1, replica_groups=mesh['grp'=2,'wide'=8,'narrow'=2] {'wide','narrow'}, use_global_device_ids=true, to_apply=%region_25.28 | all-reduce | flops 4102 | bytes 16408 | tf_op jit(solution)/shard_map/psum | solution.py:411
  (364 shorter events, 419.9 us)
Async XLA Ops:
  7.2 559.8 %copy-start = (bf16[2048,16]{0,1:T(8,128)(2,1)S(1)}, bf16[2048,16]{0,1:T(8,128)(2,1)}, u32[]{:S(2)}) copy-start(bf16[2048,16]{0,1:T(8,128)(2,1)} %param.32) | copy-start | bytes 196612
  7.2 133.8 %all-gather.6.cloned.1.call-start = ((), (), s32[]{:S(2)}) async-start(), calls=%async_computation.5 | async-start | bytes 9437184 | tf_op jit(solution)/shard_map/all_gather | solution.py:245
  13.3 263.9 %all-gather.8.cloned.1.call-start = ((), (), s32[]{:S(2)}) async-start(), calls=%async_computation.6 | async-start | bytes 9437184 | tf_op jit(solution)/shard_map/all_gather | solution.py:249
  14.0 393.7 %all-gather.12.cloned.1.call-start = ((), (), s32[]{:S(2)}) async-start(), calls=%async_computation.9 | async-start | bytes 9437184 | tf_op jit(solution)/shard_map/all_gather | solution.py:250
  152.3 65.0 %collective-permute-start.1 = (bf16[2048,256]{1,0:T(8,128)(2,1)}, bf16[2048,256]{1,0:T(8,128)(2,1)}, u32[]{:S(2)}, u32[]{:S(2)}) collective-permute-start(bf16[2048,256]{1,0:T(8,128)(2,1)} %slice.113.v_ref), channel_id=1, source_target_pairs={{0,1},{1,0},{2,3},{3,2},{4,5},{5,4},{6,7},{7,6},{8,9},{9,8},{10,11... | collective-permute-start | bytes 3145736 | tf_op jit(solution)/shard_map/ppermute | solution.py:269
  216.1 17.7 %collective-permute-start = (bf16[2048,256]{1,0:T(8,128)(2,1)S(1)}, bf16[2048,256]{1,0:T(8,128)(2,1)S(1)}, u32[]{:S(2)}, u32[]{:S(2)}) collective-permute-start(bf16[2048,256]{1,0:T(8,128)(2,1)S(1)} %get-tuple-element.112.k_ref), channel_id=1, source_target_pairs={{0,1},{1,0},{2,3},{3,2},{4,5},{5,4},{6,7},{7,6},{8,9},{9,8},{10,11... | collective-permute-start | bytes 3145736 | tf_op jit(solution)/shard_map/ppermute | solution.py:268
  255.4 33.5 %all-to-all-start = ((bf16[8,256,256]{1,2,0:T(8,128)(2,1)}), bf16[8,256,256]{1,2,0:T(8,128)(2,1)S(1)}, u32[]{:S(2)}, u32[]{:S(2)}) async-start(bf16[8,256,256]{1,2,0:T(8,128)(2,1)} %copy.45), calls=%async_computation | async-start | bytes 2097152 | tf_op jit(solution)/shard_map/all_to_all | solution.py:272
  259.0 274.4 %all-gather.10.cloned.1.call-start = ((), (), s32[]{:S(2)}) async-start(), calls=%async_computation.7 | async-start | bytes 9437184 | tf_op jit(solution)/shard_map/all_gather | solution.py:278
  299.4 544.0 %reduce-scatter.6.cloned.1.call-start = ((), (), s32[]{:S(2)}) async-start(), calls=%async_computation.10 | async-start | bytes 9437184 | tf_op jit(solution)/shard_map/reduce_scatter | solution.py:343
  299.4 294.7 %collective-permute-start.4 = (bf16[1024,2048]{1,0:T(8,128)(2,1)}, bf16[1024,2048]{1,0:T(8,128)(2,1)}, u32[]{:S(2)}, u32[]{:S(2)}) collective-permute-start(bf16[1024,2048]{1,0:T(8,128)(2,1)} %bitcast.237), channel_id=1, source_target_pairs={{0,1},{1,0},{2,3},{3,2},{4,5},{5,4},{6,7},{7,6},{8,9},{9,8},{10,11... | collective-permute-start | bytes 12582920 | tf_op jit(solution)/shard_map/ppermute | solution.py:251
  301.0 274.1 %collective-permute-start.3 = (bf16[2048,1024]{1,0:T(8,128)(2,1)}, bf16[2048,1024]{1,0:T(8,128)(2,1)}, u32[]{:S(2)}, u32[]{:S(2)}) collective-permute-start(bf16[2048,1024]{1,0:T(8,128)(2,1)} %bitcast.236), channel_id=1, source_target_pairs={{0,1},{1,0},{2,3},{3,2},{4,5},{5,4},{6,7},{7,6},{8,9},{9,8},{10,11... | collective-permute-start | bytes 12582920 | tf_op jit(solution)/shard_map/ppermute | solution.py:251
  301.5 283.3 %collective-permute-start.2 = (bf16[2048,1024]{1,0:T(8,128)(2,1)}, bf16[2048,1024]{1,0:T(8,128)(2,1)}, u32[]{:S(2)}, u32[]{:S(2)}) collective-permute-start(bf16[2048,1024]{1,0:T(8,128)(2,1)} %bitcast.235), channel_id=1, source_target_pairs={{0,1},{1,0},{2,3},{3,2},{4,5},{5,4},{6,7},{7,6},{8,9},{9,8},{10,11... | collective-permute-start | bytes 12582920 | tf_op jit(solution)/shard_map/ppermute | solution.py:251
  696.0 299.9 %reduce-scatter.4.cloned.1.call-start = ((), (), s32[]{:S(2)}) async-start(), calls=%async_computation.8 | async-start | bytes 9437184 | tf_op jit(solution)/shard_map/reduce_scatter | solution.py:346
  733.5 262.4 %copy-start.56 = (f32[256]{0:T(256)S(1)}, f32[256]{0:T(256)}, u32[]{:S(2)}) copy-start(f32[256]{0:T(256)} %copy-done.55) | copy-start | bytes 3076
  733.5 262.4 %copy-start.60 = (f32[256]{0:T(256)S(1)}, f32[256]{0:T(256)}, u32[]{:S(2)}) copy-start(f32[256]{0:T(256)} %copy-done.59) | copy-start | bytes 3076
  733.5 462.0 %all-gather.14.cloned.1.call-start = ((), (), s32[]{:S(2)}) async-start(), calls=%async_computation.12 | async-start | bytes 9437184 | tf_op jit(solution)/shard_map/all_gather | solution.py:364
  1003.5 253.0 %all-reduce.6.cloned.1.call-start = ((), (), s32[]{:S(2)}) async-start(), calls=%async_computation.13 | async-start | bytes 131072 | tf_op jit(solution)/shard_map/psum | solution.py:411
  1097.9 26.3 %collective-permute-start.5 = (bf16[2048,256]{1,0:T(8,128)(2,1)}, bf16[2048,256]{1,0:T(8,128)(2,1)S(1)}, u32[]{:S(2)}, u32[]{:S(2)}) collective-permute-start(bf16[2048,256]{1,0:T(8,128)(2,1)} %convert_element_type.289), channel_id=1, source_target_pairs={{0,1},{1,0},{2,3},{3,2},{4,5},{5,4},{6,7},{7,6},{8,9},{9,8},{10,11... | collective-permute-start | bytes 3145736 | tf_op jit(solution)/shard_map/ppermute | solution.py:370
  1104.9 489.0 %all-reduce.8.cloned.1.call-start = ((), (), s32[]{:S(2)}) async-start(), calls=%async_computation.14 | async-start | bytes 8388608 | tf_op jit(solution)/shard_map/psum | solution.py:392
  1106.1 76.3 %collective-permute-start.6 = (bf16[2048,256]{1,0:T(8,128)(2,1)}, bf16[2048,256]{1,0:T(8,128)(2,1)}, u32[]{:S(2)}, u32[]{:S(2)}) collective-permute-start(bf16[2048,256]{1,0:T(8,128)(2,1)} %convert_element_type.291), channel_id=1, source_target_pairs={{0,1},{1,0},{2,3},{3,2},{4,5},{5,4},{6,7},{7,6},{8,9},{9,8},{10,11... | collective-permute-start | bytes 3145736 | tf_op jit(solution)/shard_map/ppermute | solution.py:371
  1202.3 407.7 %reduce-scatter.8.cloned.1.call-start = ((), (), s32[]{:S(2)}) async-start(), calls=%async_computation.11 | async-start | bytes 9437184 | tf_op jit(solution)/shard_map/reduce_scatter | solution.py:388
  1224.8 139.2 %collective-permute-start.8 = (bf16[2048,1024]{1,0:T(8,128)(2,1)}, bf16[2048,1024]{1,0:T(8,128)(2,1)}, u32[]{:S(2)}, u32[]{:S(2)}) collective-permute-start(bf16[2048,1024]{1,0:T(8,128)(2,1)} %convolution_convert_fusion.8), channel_id=1, source_target_pairs={{0,1},{1,0},{2,3},{3,2},{4,5},{5,4},{6,7},{7,6},{8,9},{9,8},{10,11... | collective-permute-start | bytes 12582920 | tf_op jit(solution)/shard_map/ppermute | solution.py:348
  1233.5 265.5 %collective-permute-start.7 = (bf16[2048,1024]{1,0:T(8,128)(2,1)}, bf16[2048,1024]{1,0:T(8,128)(2,1)}, u32[]{:S(2)}, u32[]{:S(2)}) collective-permute-start(bf16[2048,1024]{1,0:T(8,128)(2,1)} %convolution_convert_fusion.9), channel_id=1, source_target_pairs={{0,1},{1,0},{2,3},{3,2},{4,5},{5,4},{6,7},{7,6},{8,9},{9,8},{10,11... | collective-permute-start | bytes 12582920 | tf_op jit(solution)/shard_map/ppermute | solution.py:348
  1241.3 337.1 %collective-permute-start.9 = (bf16[1024,2048]{1,0:T(8,128)(2,1)}, bf16[1024,2048]{1,0:T(8,128)(2,1)}, u32[]{:S(2)}, u32[]{:S(2)}) collective-permute-start(bf16[1024,2048]{1,0:T(8,128)(2,1)} %convolution_convert_fusion.7), channel_id=1, source_target_pairs={{0,1},{1,0},{2,3},{3,2},{4,5},{5,4},{6,7},{7,6},{8,9},{9,8},{10,11... | collective-permute-start | bytes 12582920 | tf_op jit(solution)/shard_map/ppermute | solution.py:348
  (95 other events, 3202.1 us)
Sparse Core Ops, SparseCore 0:
  13.4 127.6 all-gather.5
  143.2 133.9 all-gather.7
  279.9 127.7 all-gather.11
  410.3 123.1 all-gather.9
  696.2 147.1 reduce-scatter.5
  847.9 147.9 reduce-scatter.3
  1003.6 146.3 all-gather.13
  1156.1 100.3 all-reduce.5
  1259.7 197.7 all-reduce.7
  1461.0 148.9 reduce-scatter.7

commit v2 on v1

--- a/solution.py
+++ b/solution.py
@@ -61,13 +61,13 @@
     return score
 
 
-def attend_kernel(rows, prompt_blocks, paired, side_ref, q_ref, k_ref, v_ref, ko_ref, vo_ref, o_ref, lse_ref, vt_ref):
+def attend_kernel(rows, prompt_blocks, paired, side_ref, q_ref, k_ref, v_ref, ko_ref, vo_ref, o_ref, lse_ref, vt_ref, vto_ref):
     half, columns = q_ref.shape
     side = side_ref[0]
     for h in range(columns // HD):
         hs = slice(h * HD, (h + 1) * HD)
-        for plane, ref in enumerate((v_ref, vo_ref)):
-            vt_ref[plane, hs, :] = ref[:, hs].T
+        vt_ref[hs, :] = v_ref[:, hs].T
+        vto_ref[hs, :] = vo_ref[:, hs].T
 
     def one(w, w_index):
         start = w_index * rows if w is not None else pl.multiple_of(w_index * rows, rows)
@@ -90,7 +90,7 @@
                 weight = jnp.exp2(score - largest)
                 total = total + jnp.sum(weight, 0, keepdims=True)
                 mixed = mixed + jnp.dot(
-                    vt_ref[plane, hs, at], weight.astype(jnp.bfloat16), preferred_element_type=jnp.float32
+                    (vt_ref, vto_ref)[plane][hs, at], weight.astype(jnp.bfloat16), preferred_element_type=jnp.float32
                 )
             o_ref[pl.ds(start, rows), hs] = (mixed / total).T.astype(jnp.bfloat16)
             lse_ref[h : h + 1, pl.ds(start, rows)] = largest + jnp.log(total) * LOG2E
@@ -100,7 +100,7 @@
 
 def attend_back_kernel(
     rows, prompt_blocks, paired, side_ref, q_ref, k_ref, v_ref, ko_ref, vo_ref, do_ref, o_ref, lse_ref,
-    dq_ref, dk_ref, dv_ref, dko_ref, dvo_ref, kt_ref,
+    dq_ref, dk_ref, dv_ref, dkb_ref, dvb_ref, kt_ref, kto_ref, dko_ref, dvo_ref,
 ):
     half, columns = q_ref.shape
     side = side_ref[0]
@@ -108,8 +108,8 @@
         ref[...] = jnp.zeros_like(ref)
     for h in range(columns // HD):
         hs = slice(h * HD, (h + 1) * HD)
-        for plane, ref in enumerate((k_ref, ko_ref)):
-            kt_ref[plane, hs, :] = ref[:, hs].T
+        kt_ref[hs, :] = k_ref[:, hs].T
+        kto_ref[hs, :] = ko_ref[:, hs].T
 
     def one(w, w_index):
         start = w_index * rows if w is not None else pl.multiple_of(w_index * rows, rows)
@@ -134,13 +134,15 @@
                 dv[at, hs] += jnp.dot(weight.astype(jnp.bfloat16), grad, preferred_element_type=jnp.float32)
                 dk = (dk_ref, dko_ref)[plane]
                 dk[at, hs] += jnp.dot(grad_score, query, preferred_element_type=jnp.float32) * HD**-0.5
-                back = back + jnp.dot(kt_ref[plane, hs, at], grad_score, preferred_element_type=jnp.float32)
+                back = back + jnp.dot((kt_ref, kto_ref)[plane][hs, at], grad_score, preferred_element_type=jnp.float32)
             dq_ref[pl.ds(start, rows), hs] = back.T * HD**-0.5
 
     for_blocks(half // rows, prompt_blocks, one)
-
-
-def attention_calls(rows, half, columns, prompt_blocks, paired):
+    dkb_ref[...] = dko_ref[...].astype(jnp.bfloat16)
+    dvb_ref[...] = dvo_ref[...].astype(jnp.bfloat16)
+
+
+def attention_calls(rows, half, shared, columns, prompt_blocks, paired):
     smem = pl.BlockSpec(memory_space=pltpu.SMEM)
     vmem = pl.BlockSpec(memory_space=pltpu.VMEM)
     heads = columns // HD
@@ -153,20 +155,400 @@
         out_shape=(wide16, jax.ShapeDtypeStruct((heads, half), jnp.float32)),
         in_specs=[smem] + [vmem] * 5,
         out_specs=(vmem, vmem),
-        scratch_shapes=[pltpu.VMEM((2, columns, half), jnp.bfloat16)],
+        scratch_shapes=[pltpu.VMEM((columns, half), jnp.bfloat16), pltpu.VMEM((columns, shared), jnp.bfloat16)],
         compiler_params=params,
         cost_estimate=pl.CostEstimate(flops=2 * work, bytes_accessed=half * columns * 12, transcendentals=0),
     )
     backward = pl.pallas_call(
         functools.partial(attend_back_kernel, rows, prompt_blocks, paired),
-        out_shape=(wide32,) * 5,
+        out_shape=(wide32,) * 3 + (jax.ShapeDtypeStruct((shared, columns), jnp.bfloat16),) * 2,
         in_specs=[smem] + [vmem] * 8,
         out_specs=(vmem,) * 5,
-        scratch_shapes=[pltpu.VMEM((2, columns, half), jnp.bfloat16)],
+        scratch_shapes=[pltpu.VMEM((columns, half), jnp.bfloat16), pltpu.VMEM((columns, shared), jnp.bfloat16)]
+        + [pltpu.VMEM((shared, columns), jnp.float32)] * 2,
         compiler_params=params,
         cost_estimate=pl.CostEstimate(flops=5 * work, bytes_accessed=half * columns * 40, transcendentals=0),
     )
     return forward, backward
+
+
+MESH_ID = pl.DeviceIdType.MESH
+ANY = pl.BlockSpec(memory_space=pl.ANY)
+VMEM = pl.BlockSpec(memory_space=pltpu.VMEM)
+LINE = 4
+
+
+def position():
+    grp, wide, narrow = (lax.axis_index(a) for a in ("grp", "wide", "narrow"))
+    return grp, wide, narrow, wide // 2, lax.rem(wide, 2)
+
+
+def greet(targets):
+    barrier = pltpu.get_barrier_semaphore()
+    for device, when in targets:
+        def signal(device=device):
+            pl.semaphore_signal(barrier, inc=1, device_id=device, device_id_type=MESH_ID)
+
+        if when is None:
+            signal()
+        else:
+            pl.when(when)(signal)
+    peers = sum(1 if when is None else when.astype(jnp.int32) for _, when in targets)
+    pl.semaphore_wait(barrier, peers)
+
+
+def remote(src, dst, send, recv, device):
+    return pltpu.make_async_remote_copy(
+        src_ref=src, dst_ref=dst, send_sem=send, recv_sem=recv, device_id=device, device_id_type=MESH_ID
+    )
+
+
+def gather_kernel(count, *refs):
+    ins, outs = refs[:count], refs[count : 2 * count]
+    gather_body(count, ins, outs, *refs[2 * count :])
+
+
+def gather_body(count, ins, outs, send, recv, local, more=(), begin=None, finish=None):
+    grp, wide, narrow, line, cross = position()
+    across = (grp, line * 2 + 1 - cross, narrow)
+    above = (grp, wide + 2, narrow)
+    below = (grp, wide - 2, narrow)
+    has_above, has_below = line < LINE - 1, line > 0
+    greet([(across, None), (above, has_above), (below, has_below), *more])
+
+    def copy(i, source_line, way, device):
+        slot = source_line * 2 + cross
+        return remote(outs[i].at[slot], outs[i].at[slot], send.at[i, way, source_line], recv.at[i, slot], device)
+
+    def own(i, way, device):
+        return remote(ins[i], outs[i].at[wide], send.at[i, way, line], recv.at[i, wide], device)
+
+    mine = [pltpu.make_async_copy(ins[i], outs[i].at[wide], local.at[i]) for i in range(count)]
+    for i in range(count):
+        pl.when(has_above)(own(i, 1, above).start)
+        pl.when(has_below)(own(i, 2, below).start)
+        own(i, 0, across).start()
+        mine[i].start()
+    if begin is not None:
+        begin()
+    for i in range(count):
+        for distance in range(1, LINE):
+            for sign in (-1, 1):
+                source = line + sign * distance
+
+                @pl.when((source >= 0) & (source < LINE))
+                def _(i=i, source=source, sign=sign):
+                    slot = source * 2 + cross
+                    copy(i, source, 0, across).wait_recv()
+                    onward = above if sign < 0 else below
+
+                    @pl.when(has_above if sign < 0 else has_below)
+                    def _():
+                        copy(i, source, 1 if sign < 0 else 2, onward).start()
+
+                    copy(i, source, 0, across).start()
+
+    for i in range(count):
+        for source in range(LINE):
+            other = source * 2 + 1 - cross
+            remote(ins[i], outs[i].at[other], send.at[i, 0, 0], recv.at[i, other], across).wait_recv()
+        for source in range(LINE):
+            remote(ins[i], outs[i].at[0], send.at[i, 0, source], recv.at[i, 0], across).wait_send()
+
+            @pl.when(has_above & (source <= line))
+            def _(i=i, source=source):
+                remote(ins[i], outs[i].at[0], send.at[i, 1, source], recv.at[i, 0], above).wait_send()
+
+            @pl.when(has_below & (source >= line))
+            def _(i=i, source=source):
+                remote(ins[i], outs[i].at[0], send.at[i, 2, source], recv.at[i, 0], below).wait_send()
+
+        mine[i].wait()
+    if finish is not None:
+        finish()
+
+
+def gather_wide(arrays, collective_id):
+    count = len(arrays)
+    size = lax.axis_size("wide")
+    if size != 2 * LINE:
+        return [lax.all_gather(a, "wide", axis=0) for a in arrays]
+    return pl.pallas_call(
+        functools.partial(gather_kernel, count),
+        out_shape=[jax.ShapeDtypeStruct((size, *a.shape), a.dtype) for a in arrays],
+        in_specs=[ANY] * count,
+        out_specs=[ANY] * count,
+        scratch_shapes=[
+            pltpu.SemaphoreType.DMA((count, 3, LINE)),
+            pltpu.SemaphoreType.DMA((count, size)),
+            pltpu.SemaphoreType.DMA((count,)),
+        ],
+        compiler_params=pltpu.CompilerParams(collective_id=collective_id, has_side_effects=True),
+    )(*arrays)
+
+
+def scatter_kernel(part_ref, out_ref, held, from_across, from_line, load, send, recv_a, recv_l):
+    grp, wide, narrow, line, cross = position()
+    across = (grp, line * 2 + 1 - cross, narrow)
+    above = (grp, wide + 2, narrow)
+    below = (grp, wide - 2, narrow)
+    has_above, has_below = line < LINE - 1, line > 0
+    f32 = jnp.float32
+    greet([(across, None), (above, has_above), (below, has_below)])
+
+    order = []
+    for distance in range(LINE - 1, 0, -1):
+        for sign in (1, -1):
+            order.append((distance, sign))
+
+    def valid(owner):
+        return (owner >= 0) & (owner < LINE)
+
+    def across_copy(owner):
+        return remote(
+            part_ref.at[owner * 2 + 1 - cross], from_across.at[owner], send.at[0, owner], recv_a.at[owner], across
+        )
+
+    def load_copy(owner):
+        return pltpu.make_async_copy(part_ref.at[owner * 2 + cross], held.at[owner], load.at[owner])
+
+    def line_copy(owner, up):
+        return remote(
+            held.at[owner],
+            from_line.at[0 if up else 1, owner],
+            send.at[1, owner],
+            recv_l.at[0 if up else 1, owner],
+            above if up else below,
+        )
+
+    for distance, sign in order + [(0, 1)]:
+        owner = line + sign * distance
+
+        @pl.when(valid(owner))
+        def _(owner=owner):
+            across_copy(owner).start()
+            load_copy(owner).start()
+
+    for distance, sign in order:
+        owner = line + sign * distance
+
+        @pl.when(valid(owner))
+        def _(owner=owner, sign=sign):
+            load_copy(owner).wait()
+            across_copy(owner).wait_recv()
+            up = sign > 0
+            came = has_below if up else has_above
+            total = held[owner].astype(f32) + from_across[owner].astype(f32)
+
+            @pl.when(came)
+            def _():
+                line_copy(owner, up).wait_recv()
+                held[owner] = (total + from_line[0 if up else 1, owner].astype(f32)).astype(held.dtype)
+
+            @pl.when(jnp.logical_not(came))
+            def _():
+                held[owner] = total.astype(held.dtype)
+
+            line_copy(owner, up).start()
+
+    load_copy(line).wait()
+    across_copy(line).wait_recv()
+    out_ref[...] = held[line].astype(f32) + from_across[line].astype(f32)
+
+    @pl.when(has_below)
+    def _():
+        line_copy(line, True).wait_recv()
+        out_ref[...] += from_line[0, line].astype(f32)
+
+    @pl.when(has_above)
+    def _():
+        line_copy(line, False).wait_recv()
+        out_ref[...] += from_line[1, line].astype(f32)
+
+    for owner in range(LINE):
+        across_copy(owner).wait_send()
+
+        @pl.when(owner > line)
+        def _(owner=owner):
+            line_copy(owner, True).wait_send()
+
+        @pl.when(owner < line)
+        def _(owner=owner):
+            line_copy(owner, False).wait_send()
+
+
+def scatter_wide(part, collective_id):
+    size, rows, columns = part.shape
+    if size != 2 * LINE:
+        return lax.psum_scatter(part, "wide", scatter_dimension=0, tiled=False).astype(jnp.float32)
+    block = (LINE, rows, columns)
+    return pl.pallas_call(
+        scatter_kernel,
+        out_shape=jax.ShapeDtypeStruct((rows, columns), jnp.float32),
+        in_specs=[ANY],
+        out_specs=VMEM,
+        scratch_shapes=[
+            pltpu.VMEM(block, part.dtype),
+            pltpu.VMEM(block, part.dtype),
+            pltpu.VMEM((2, *block), part.dtype),
+            pltpu.SemaphoreType.DMA((LINE,)),
+            pltpu.SemaphoreType.DMA((2, LINE)),
+            pltpu.SemaphoreType.DMA((LINE,)),
+            pltpu.SemaphoreType.DMA((2, LINE)),
+        ],
+        compiler_params=pltpu.CompilerParams(
+            collective_id=collective_id, has_side_effects=True, vmem_limit_bytes=48 * 2**20
+        ),
+    )(part)
+
+
+def sum_kernel(x_ref, o_ref, held, send, recv):
+    grp, wide, narrow, _, _ = position()
+    size = held.shape[0] + 1
+    others = [(grp, lax.rem(wide + k, size), narrow) for k in range(1, size)]
+    greet([(device, None) for device in others])
+    copies = [
+        remote(x_ref, held.at[k], send.at[k], recv.at[k], device) for k, device in enumerate(others)
+    ]
+    for copy in copies:
+        copy.start()
+    for copy in copies:
+        copy.wait()
+    total = x_ref[...]
+    for k in range(size - 1):
+        total = total + held[k]
+    o_ref[...] = total
+
+
+def sum_wide(x, collective_id):
+    size = lax.axis_size("wide")
+    if size != 2 * LINE:
+        return lax.psum(x, "wide")
+    return pl.pallas_call(
+        sum_kernel,
+        out_shape=jax.ShapeDtypeStruct(x.shape, x.dtype),
+        in_specs=[VMEM],
+        out_specs=VMEM,
+        scratch_shapes=[
+            pltpu.VMEM((size - 1, *x.shape), x.dtype),
+            pltpu.SemaphoreType.DMA((size - 1,)),
+            pltpu.SemaphoreType.DMA((size - 1,)),
+        ],
+        compiler_params=pltpu.CompilerParams(collective_id=collective_id, has_side_effects=True),
+    )(x)
+
+
+def start_kernel(count, swaps, *refs):
+    ins, given = refs[:count], refs[count : count + swaps]
+    outs = refs[count + swaps : 2 * count + swaps]
+    got = refs[2 * count + swaps : 2 * (count + swaps)]
+    send, recv, local, swap_send, swap_recv, twin_send, twin_recv = refs[2 * (count + swaps) :]
+    grp, wide, narrow, line, cross = position()
+    partner = (grp, wide, 1 - narrow)
+    twin = (1 - grp, wide, narrow)
+
+    def half(ref, which):
+        size = ref.shape[0] // 2
+        return ref.at[pl.ds(pl.multiple_of(which * size, size), size)]
+
+    def swap(i):
+        return remote(half(given[i], grp), half(got[i], grp), swap_send.at[i], swap_recv.at[i], partner)
+
+    def share(i, which):
+        return remote(half(got[i], which), half(got[i], which), twin_send.at[i], twin_recv.at[i], twin)
+
+    def begin():
+        for i in range(swaps):
+            swap(i).start()
+
+    def finish():
+        for i in range(swaps):
+            swap(i).wait_recv()
+            share(i, grp).start()
+        for i in range(swaps):
+            swap(i).wait_send()
+            share(i, grp).wait_send()
+            share(i, 1 - grp).wait_recv()
+
+    gather_body(count, ins, outs, send, recv, local, [(partner, None), (twin, None)], begin, finish)
+
+
+def start_exchange(arrays, weights, collective_id):
+    size = lax.axis_size("wide")
+    if size != 2 * LINE or lax.axis_size("grp") != 2:
+        swap = [(0, 1), (1, 0)]
+        return [lax.all_gather(a, "wide", axis=0) for a in arrays], [lax.ppermute(w, "narrow", swap) for w in weights]
+    count, swaps = len(arrays), len(weights)
+    out = pl.pallas_call(
+        functools.partial(start_kernel, count, swaps),
+        out_shape=[jax.ShapeDtypeStruct((size, *a.shape), a.dtype) for a in arrays]
+        + [jax.ShapeDtypeStruct(w.shape, w.dtype) for w in weights],
+        in_specs=[ANY] * (count + swaps),
+        out_specs=[ANY] * (count + swaps),
+        scratch_shapes=[
+            pltpu.SemaphoreType.DMA((count, 3, LINE)),
+            pltpu.SemaphoreType.DMA((count, size)),
+            pltpu.SemaphoreType.DMA((count,)),
+        ]
+        + [pltpu.SemaphoreType.DMA((swaps,))] * 4,
+        compiler_params=pltpu.CompilerParams(collective_id=collective_id, has_side_effects=True),
+    )(*arrays, *weights)
+    return out[:count], out[count:]
+
+
+def sum_all_kernel(x_ref, o_ref, parts, total, send, recv, send_back, recv_back):
+    grp, wide, narrow, _, _ = position()
+    size, _, width = parts.shape
+    me = wide * 2 + narrow
+    ranks = [lax.rem(me + k, size) for k in range(size)]
+    devices = [(grp, rank // 2, lax.rem(rank, 2)) for rank in ranks]
+    greet([(device, None) for device in devices[1:]])
+
+    def columns(rank):
+        return pl.ds(pl.multiple_of(rank * width, width), width)
+
+    out = [
+        remote(x_ref.at[:, columns(ranks[k])], parts.at[k], send.at[k], recv.at[k], devices[k])
+        for k in range(1, size)
+    ]
+    for copy in out:
+        copy.start()
+    total[...] = x_ref[:, columns(me)]
+    for k, copy in enumerate(out):
+        copy.wait()
+        total[...] += parts[k + 1]
+    back = [
+        remote(total, o_ref.at[:, columns(me)], send_back.at[k], recv_back.at[k], devices[k])
+        for k in range(1, size)
+    ]
+    for copy in back:
+        copy.start()
+    o_ref[:, columns(me)] = total[...]
+    for copy in back:
+        copy.wait_send()
+    for k in range(1, size):
+        rank = lax.rem(me - k + size, size)
+        remote(total, o_ref.at[:, columns(rank)], send_back.at[k], recv_back.at[k], devices[k]).wait_recv()
+
+
+def sum_all(x, collective_id):
+    size = lax.axis_size("wide") * lax.axis_size("narrow")
+    rows, columns = x.shape
+    if size != 4 * LINE:
+        return lax.psum(x, ("wide", "narrow"))
+    width = columns // size
+    return pl.pallas_call(
+        sum_all_kernel,
+        out_shape=jax.ShapeDtypeStruct(x.shape, x.dtype),
+        in_specs=[VMEM],
+        out_specs=VMEM,
+        scratch_shapes=[
+            pltpu.VMEM((size, rows, width), x.dtype),
+            pltpu.VMEM((rows, width), x.dtype),
+        ]
+        + [pltpu.SemaphoreType.DMA((size,))] * 4,
+        compiler_params=pltpu.CompilerParams(collective_id=collective_id, has_side_effects=True),
+    )(x)
 
 
 def positions(token_ids):
@@ -229,31 +611,58 @@
     half = rows * wide_count
     columns = w_query.shape[1]
     experts = w_router.shape[1]
+    hidden_units = w_gate.shape[2]
     capacity = min(max(rows * TOP * 5 // (4 * experts), 2), rows)
     assert narrow_count == 2 and CONT in (rows, 2 * rows)
+    paired = CONT == 2 * rows
     side = lax.axis_index("narrow")
     place = lax.axis_index("wide")
+    group = lax.axis_index("grp")
     swap = [(0, 1), (1, 0)]
+    twins = lax.axis_size("grp") == 2
     prompt_blocks = PROMPT // (rows * narrow_count)
-    attend, attend_back = attention_calls(rows, half, columns, prompt_blocks, CONT == 2 * rows)
+    shared = half if paired else prompt_blocks * rows
+    attend, attend_back = attention_calls(rows, half, shared, columns, prompt_blocks, paired)
     side_array = side.astype(jnp.int32).reshape(1)
+    barrier = lax.optimization_barrier
+
+    def exchange(value):
+        return lax.ppermute(value, "narrow", swap)
 
     stream = tokens.astype(f32)
     inv_one = lax.rsqrt(jnp.mean(stream * stream, -1, keepdims=True) + EPSILON)
     gain_one = norm_attn.astype(f32)
     normed = (stream * inv_one * gain_one).astype(bf16)
-    normed_plane = lax.all_gather(normed, "wide", axis=0, tiled=True)
     mask = valid.astype(f32)[:, None]
     grad_final = cotangent.astype(f32) * mask
-    routes_plane = lax.all_gather(routes, "wide", axis=0, tiled=True)
-    w_out_all = lax.all_gather(w_out, "wide", axis=0, tiled=True)
-    grad_plane = lax.all_gather(grad_final.astype(bf16), "wide", axis=0, tiled=True)
-    other_weights = [lax.ppermute(w, "narrow", swap) for w in (w_gate[0], w_up[0], w_down[0])]
+    pieces = 2 if twins else 1
+    piece_width = D // pieces
+    piece = lax.dynamic_slice_in_dim(w_out, group * piece_width, piece_width, 1) if twins else w_out
+    (routes_plane, normed_plane, out_piece), (other_gate, other_up, other_down) = start_exchange(
+        [routes.T, normed, piece], [w_gate[0], w_up[0], w_down[0]], 0
+    )
+    normed_plane = normed_plane.reshape(half, D)
+    out_pieces = [out_piece.reshape(D, piece_width)]
+    if twins:
+        out_pieces.append(lax.ppermute(out_pieces[0], "grp", swap))
+
+    def ordered(parts):
+        if not twins:
+            return parts
+        return [jnp.where(group == 0, parts[k], parts[k ^ 1]) for k in range(2)]
+
+    def unordered(whole):
+        return ordered([whole[:, k * piece_width : (k + 1) * piece_width] for k in range(pieces)])
+
+    grad_final_b, _ = barrier((grad_final.astype(bf16), normed_plane))
+    grad_plane = lax.all_gather(grad_final_b, "wide", axis=0, tiled=True)
 
     joined = jnp.concatenate([w_query, w_key, w_value], 1)
     raw = dot(normed_plane, joined)
     query_raw, key_raw, value_raw = (raw[:, i * columns : (i + 1) * columns] for i in range(3))
-    sums = lax.psum(jnp.stack([jnp.sum(query_raw * query_raw, -1), jnp.sum(key_raw * key_raw, -1)]), "wide")
+    sums = sum_wide(
+        jnp.stack([jnp.sum(query_raw * query_raw, -1), jnp.sum(key_raw * key_raw, -1)]), 1
+    )
     inv_query, inv_key = lax.rsqrt(sums / D + EPSILON)[:, :, None]
     gain_query = norm_query.astype(f32)
     gain_key = norm_key.astype(f32)
@@ -262,33 +671,31 @@
         + jnp.arange(rows, dtype=jnp.int32)[None, :]
     ).reshape(half)
     cosine, sine = rotation(positions(plane_ids))
+    value_b = value_raw.astype(bf16)
+    value_other = exchange(value_b[:shared])
+    key_rot = rotate(key_raw * inv_key * gain_key, cosine, sine).astype(bf16)
+    key_other = exchange(key_rot[:shared])
     query_rot = rotate(query_raw * inv_query * gain_query, cosine, sine).astype(bf16)
-    key_rot = rotate(key_raw * inv_key * gain_key, cosine, sine).astype(bf16)
-    value_b = value_raw.astype(bf16)
-    key_other = lax.ppermute(key_rot, "narrow", swap)
-    value_other = lax.ppermute(value_b, "narrow", swap)
     attended, lse = attend(side_array, query_rot, key_rot, value_b, key_other, value_other)
 
     attended_own = lax.all_to_all(attended, "wide", split_axis=0, concat_axis=1, tiled=True)
-    branch = dot(attended_own, w_out_all)
+    branch = jnp.concatenate(ordered([dot(attended_own, p) for p in out_pieces]), 1)
     hidden = stream + branch
     inv_two = lax.rsqrt(jnp.mean(hidden * hidden, -1, keepdims=True) + EPSILON)
     gain_two = norm_moe.astype(f32)
     moe_in = (hidden * inv_two * gain_two).astype(bf16)
     moe_plane = lax.all_gather(moe_in, "wide", axis=0, tiled=True)
 
-    probs = jax.nn.softmax(dot(moe_plane, w_router), -1)
-    named = jnp.any(routes_plane[:, :, None] == jnp.arange(experts, dtype=jnp.int32), 1)
-    gates_dense = jnp.where(named, probs, 0.0)
+    kinds = jnp.arange(experts, dtype=jnp.int32)
+    named = jnp.any(routes_plane[:, :, :, None] == kinds, 1).reshape(half, experts)
+    earlier = (jnp.arange(rows)[:, None] < jnp.arange(rows)[None, :]).astype(bf16)
     blocks = lambda a: a.reshape(wide_count, rows, -1)
-    earlier = (jnp.arange(rows)[:, None] < jnp.arange(rows)[None, :]).astype(bf16)
 
     def pick(expert):
-        chosen = jnp.take(named, expert, axis=1).reshape(wide_count, rows)
+        chosen = jnp.any(routes_plane == expert, 1)
         rank = dot(chosen.astype(bf16), earlier).astype(jnp.int32)
         slot = jnp.where(chosen, rank, -1)
-        onehot = (jnp.arange(capacity, dtype=jnp.int32)[None, :, None] == slot[:, None, :]).astype(bf16)
-        return onehot
+        return (jnp.arange(capacity, dtype=jnp.int32)[None, :, None] == slot[:, None, :]).astype(bf16)
 
     def compact(onehot, values):
         return jnp.einsum(
@@ -300,58 +707,63 @@
             "wcr,wcd->wrd", onehot, values.reshape(wide_count, capacity, -1), preferred_element_type=f32
         ).reshape(half, -1)
 
-    moe_part = 0.0
+    ids = (place * narrow_count + 1 - side, place * narrow_count + side)
+    weights = ((other_gate, other_up, other_down), (w_gate[0], w_up[0], w_down[0]))
+    onehots = [pick(e) for e in ids]
+    grads = [compact(o, grad_plane) for o in onehots]
+    backs = [dot_nt(g, w[2]) for g, w in zip(grads, weights)]
+    probs = jax.nn.softmax(dot(moe_plane, w_router), -1)
+    gates_dense = jnp.where(named, probs, 0.0)
+    inputs = [compact(o, moe_plane) for o in onehots]
+    gates_own = [jnp.take(gates_dense, e, axis=1) for e in ids]
+    gates = [
+        jnp.sum(o.astype(f32) * g.reshape(wide_count, 1, rows), -1).reshape(wide_count * capacity, 1)
+        for o, g in zip(onehots, gates_own)
+    ]
+    gate_pres = [dot(x, w[0]) for x, w in zip(inputs, weights)]
+    up_pres = [dot(x, w[1]) for x, w in zip(inputs, weights)]
+    inners = [g * jax.nn.sigmoid(g) * u for g, u in zip(gate_pres, up_pres)]
+    inners_gated = [(g * i).astype(bf16) for g, i in zip(gates, inners)]
+    moe_part = sum(spread(o, dot(i, w[2]).astype(bf16)) for o, i, w in zip(onehots, inners_gated, weights))
+    moe_part = moe_part.astype(bf16)
+    moe = lax.psum_scatter(moe_part, "wide", scatter_dimension=0, tiled=True).astype(f32)
+
+    _, gate_pres = barrier((moe_part, gate_pres))
     grad_part = 0.0
     mixing = 0.0
-    expert_grads = []
-    for expert, (gate_w, up_w, down_w) in (
-        (place * narrow_count + side, (w_gate[0], w_up[0], w_down[0])),
-        (place * narrow_count + 1 - side, other_weights),
-    ):
-        onehot = pick(expert)
-        inputs = compact(onehot, moe_plane)
-        grads = compact(onehot, grad_plane)
-        gate_own = jnp.take(gates_dense, expert, axis=1)
-        gate = jnp.sum(
-            onehot.astype(f32) * gate_own.reshape(wide_count, 1, rows), -1
-        ).reshape(wide_count * capacity, 1)
-        gate_pre = dot(inputs, gate_w)
-        up_pre = dot(inputs, up_w)
-        back = dot_nt(grads, down_w)
+    grad_pres = []
+    for k in range(2):
+        gate_pre, up_pre, back, gate = gate_pres[k], up_pres[k], backs[k], gates[k]
         sigmoid = jax.nn.sigmoid(gate_pre)
         silu = gate_pre * sigmoid
-        inner = silu * up_pre
-        inner_gated = (gate * inner).astype(bf16)
-        grad_gate_row = jnp.sum(inner * back, -1)
+        grad_gate_row = jnp.sum(silu * up_pre * back, -1)
         grad_inner = gate * back
         grad_gate_pre = (grad_inner * up_pre * sigmoid * (1.0 + gate_pre * (1.0 - sigmoid))).astype(bf16)
         grad_up_pre = (grad_inner * silu).astype(bf16)
-        route_in = (dot_nt(grad_gate_pre, gate_w) + dot_nt(grad_up_pre, up_w)).astype(bf16)
-        grad_part = grad_part + spread(onehot, route_in)
-        moe_part = moe_part + spread(onehot, dot(inner_gated, down_w).astype(bf16))
+        grad_pres.append((grad_gate_pre, grad_up_pre))
+        route_in = (dot_nt(grad_gate_pre, weights[k][0]) + dot_nt(grad_up_pre, weights[k][1])).astype(bf16)
+        grad_part = grad_part + spread(onehots[k], route_in)
         grad_gates = jnp.sum(
-            onehot.astype(f32) * grad_gate_row.reshape(wide_count, capacity, 1), 1
+            onehots[k].astype(f32) * grad_gate_row.reshape(wide_count, capacity, 1), 1
         ).reshape(half, 1)
-        weight = gate_own[:, None] * grad_gates
-        here = (jnp.arange(experts, dtype=jnp.int32) == expert).astype(f32)
-        mixing = mixing + weight * (here[None, :] - probs)
-        expert_grads.append(
-            (dot_tn(inputs, grad_gate_pre), dot_tn(inputs, grad_up_pre), dot_tn(inner_gated, grads))
-        )
+        here = (kinds == ids[k]).astype(f32)
+        mixing = mixing + gates_own[k][:, None] * grad_gates * (here[None, :] - probs)
     mixing = mixing.astype(bf16)
-    grad_part = grad_part + dot_nt(mixing, w_router)
-    grad_moe_in = lax.psum_scatter(
-        grad_part.astype(bf16), "wide", scatter_dimension=0, tiled=True
-    ).astype(f32)
-    moe = lax.psum_scatter(moe_part.astype(bf16), "wide", scatter_dimension=0, tiled=True).astype(f32)
-    grad_router = dot_tn(moe_plane, mixing)
-    partner = [lax.ppermute(g.astype(bf16), "narrow", swap) for g in expert_grads[1]]
-    grad_gate_w, grad_up_w, grad_down_w = (
-        (own + other.astype(f32))[None] for own, other in zip(expert_grads[0], partner)
-    )
-
-    final = hidden + moe
-    output = final.astype(bf16)
+    grad_part = (grad_part + dot_nt(mixing, w_router)).astype(bf16)
+    grad_router = dot_tn(mixing, moe_plane)
+    partner_grads = [
+        dot_tn(inputs[0], grad_pres[0][0]).astype(bf16),
+        dot_tn(inputs[0], grad_pres[0][1]).astype(bf16),
+        dot_tn(inners_gated[0], grads[0]).astype(bf16),
+    ]
+    came = [exchange(g) for g in partner_grads]
+    grad_part, partner_grads = barrier((grad_part, partner_grads))
+    grad_moe_in = scatter_wide(grad_part.reshape(wide_count, rows, D), 5)
+    grad_moe_in, moe, inputs, grads = barrier((grad_moe_in, moe, inputs, grads))
+    expert_grads = [
+        dot_tn(inputs[1], grad_pres[1][0]), dot_tn(inputs[1], grad_pres[1][1]), dot_tn(inners_gated[1], grads[1])
+    ]
+
     grad_gain_two = jnp.sum(grad_moe_in * hidden * inv_two, 0)
     grad_hidden = (
         grad_final
@@ -359,47 +771,45 @@
         - hidden * inv_two**3 * jnp.sum(grad_moe_in * gain_two * hidden, -1, keepdims=True) / D
     )
     grad_branch = grad_hidden.astype(bf16)
-    grad_attended_own = dot_nt(grad_branch, w_out_all).astype(bf16)
+    grad_attended_own = sum(dot_nt(g, p) for g, p in zip(unordered(grad_branch), out_pieces)).astype(bf16)
     grad_attended = lax.all_to_all(grad_attended_own, "wide", split_axis=1, concat_axis=0, tiled=True)
     branch_plane = lax.all_gather(grad_branch, "wide", axis=0, tiled=True)
-    grad_out = dot_tn(attended, branch_plane)
 
     grad_query_rot, grad_key_rot, grad_value, grad_key_other, grad_value_other = attend_back(
         side_array, query_rot, key_rot, value_b, key_other, value_other, grad_attended, attended, lse
     )
-    grad_key_rot = grad_key_rot + lax.ppermute(grad_key_other.astype(bf16), "narrow", swap).astype(f32)
-    grad_value = grad_value + lax.ppermute(grad_value_other.astype(bf16), "narrow", swap).astype(f32)
+
+    def add_shared(own, other):
+        return jnp.concatenate([own[:shared] + other.astype(f32), own[shared:]], 0)
+
+    grad_key_rot = add_shared(grad_key_rot, exchange(grad_key_other))
+    grad_value = add_shared(grad_value, exchange(grad_value_other))
     grad_query_normed = rotate(grad_query_rot, cosine, -sine)
     grad_key_normed = rotate(grad_key_rot, cosine, -sine)
-    dots = lax.psum(
+    dots = sum_wide(
         jnp.stack(
             [
                 jnp.sum(grad_query_normed * gain_query * query_raw, -1),
                 jnp.sum(grad_key_normed * gain_key * key_raw, -1),
             ]
         ),
-        "wide",
+        2,
     )[:, :, None]
     grad_gain_query = jnp.sum(grad_query_normed * query_raw * inv_query, 0)
     grad_gain_key = jnp.sum(grad_key_normed * key_raw * inv_key, 0)
     grad_query_raw = inv_query * gain_query * grad_query_normed - query_raw * inv_query**3 * dots[0] / D
     grad_key_raw = inv_key * gain_key * grad_key_normed - key_raw * inv_key**3 * dots[1] / D
     grads_joined = jnp.concatenate([grad_query_raw, grad_key_raw, grad_value], 1).astype(bf16)
-    grad_normed = lax.psum_scatter(
-        dot_nt(grads_joined, joined).astype(bf16), "wide", scatter_dimension=0, tiled=True
-    ).astype(f32)
-    grad_weights = dot_tn(normed_plane, grads_joined)
-    summed = lax.psum(
-        (
-            grad_weights.astype(bf16),
-            grad_out.astype(bf16),
-            grad_gain_query.astype(bf16),
-            grad_gain_key.astype(bf16),
-        ),
-        "narrow",
-    )
+    grad_weights = barrier(dot_tn(normed_plane, grads_joined).astype(bf16))
+    weights_came = exchange(grad_weights)
+    normed_part, _ = barrier((dot_nt(grads_joined, joined).astype(bf16), grad_weights))
+    grad_normed = scatter_wide(normed_part.reshape(wide_count, rows, D), 3)
+    grad_out = barrier(dot_tn(attended, branch_plane).astype(bf16))
+    out_came = exchange(grad_out)
+    grad_weights = grad_weights.astype(f32) + weights_came.astype(f32)
+    grad_out = grad_out.astype(f32) + out_came.astype(f32)
     grad_query_w, grad_key_w, grad_value_w = (
-        summed[0][:, i * columns : (i + 1) * columns].astype(f32) for i in range(3)
+        grad_weights[:, i * columns : (i + 1) * columns] for i in range(3)
     )
     grad_gain_one = jnp.sum(grad_normed * stream * inv_one, 0)
     grad_input = (
@@ -407,31 +817,33 @@
         + inv_one * gain_one * grad_normed
         - stream * inv_one**3 * jnp.sum(grad_normed * gain_one * stream, -1, keepdims=True) / D
     )
-    stat_sums = jnp.stack([jnp.sum(v * v * mask) for v in (stream, branch, hidden, moe, final)])
-    replicated = lax.psum(
-        (
-            grad_router.astype(bf16),
-            grad_gain_one.astype(bf16),
-            grad_gain_two.astype(bf16),
-            stat_sums.astype(bf16),
-            jnp.sum(mask).astype(bf16),
-        ),
-        ("wide", "narrow"),
-    )
-    grad_router, grad_gain_one, grad_gain_two, stat_sums, count = (v.astype(f32) for v in replicated)
-    rms = jnp.sqrt(stat_sums / (jnp.maximum(count, 1.0) * D))
+    final = hidden + moe
+    output = final.astype(bf16)
+    grad_gate_w, grad_up_w, grad_down_w = (
+        (own + other.astype(f32))[None] for own, other in zip(expert_grads, came)
+    )
+
+    stats = jnp.stack([jnp.sum(v * v * mask) for v in (stream, branch, hidden, moe, final)] + [jnp.sum(mask)])
+    here = jnp.repeat(jnp.arange(wide_count) == place, columns)
+    spots = [jnp.where(here, jnp.tile(g, wide_count), 0.0) for g in (grad_gain_query, grad_gain_key)]
+    small = jnp.stack([grad_gain_one, grad_gain_two, *spots, jnp.pad(stats, (0, D - stats.shape[0]))])
+    small = jnp.concatenate([grad_router, small, jnp.zeros((-(experts + 5) % 8, D), f32)], 0)
+    small = sum_all(small, 4)
+    spots = lax.dynamic_slice_in_dim(small[experts + 2 : experts + 4], place * columns, columns, 1)
+    stats = small[experts + 4, :6]
+    rms = jnp.sqrt(stats[:5] / (jnp.maximum(stats[5], 1.0) * D))
     return (
         output,
         grad_input,
         grad_query_w,
         grad_key_w,
         grad_value_w,
-        summed[1].astype(f32),
-        grad_gain_one,
-        summed[2].astype(f32),
-        summed[3].astype(f32),
-        grad_gain_two,
-        grad_router,
+        grad_out,
+        small[experts],
+        spots[0],
+        spots[1],
+        small[experts + 1],
+        small[:experts].T,
         grad_gate_w,
         grad_up_w,
         grad_down_w,

time: 1680 us -> 1170 us (0.70)
  waiting for transfers between devices: 948 us -> 236 us
  Pallas kernels: 46.4 us -> 417 us
  blocking collectives: 205 us -> 0 us
  local copies, waits for them, and re-layouts: 42 us -> 78.6 us
  other arithmetic: 88.6 us -> 71.4 us
    pallas_call x0 -> x6, Pallas kernels: none -> 372 us  [the longest x2 182 us: scatter_wide(): pl.pallas_call(scatter_kernel, out_shape=jax.ShapeDtypeStruct((rows, colu...]
    reduce_scatter x3 -> x1, waiting for transfers between devices: 273 us -> 0.01 us  [shards(): lax.psum_scatter(moe_part, 'wide', scatter_dimension=0, tiled=True)]
    ppermute x10, waiting for transfers between devices: 326 us -> 87.7 us  [the longest x9 87.7 us: exchange(): return lax.ppermute(value, 'narrow', swap)]
    all_gather x3 -> x1, waiting for transfers between devices: 209 us -> 0.01 us  [shards(): grad_plane = lax.all_gather(grad_final_b, 'wide', axis=0, tiled=True)]
    psum x4 -> x0, blocking collectives: 117 us -> none  [the longest x1 41.5 us: shards(): lax.psum((grad_router.astype(bf16), grad_gain_one.astype(bf16), grad_gain...]
    all_to_all x1 -> x0, blocking collectives: 57.3 us -> none  [shards(): lax.all_to_all(grad_attended_own, 'wide', split_axis=1, concat_axis=0, ti...]
    all_gather x1 -> x0, blocking collectives: 31.2 us -> none  [shards(): routes_plane = lax.all_gather(routes, 'wide', axis=0, tiled=True)]
    all_to_all x1, waiting for transfers between devices: 11.7 us -> 39.9 us  [shards(): lax.all_to_all(attended, 'wide', split_axis=0, concat_axis=1, tiled=True)]
  transfers between devices with their start and end apart: 21 -> 16, of which waited for: 14 -> 6; matrix products, arithmetic and copies ran while one was open for 18% -> 29% of each run, Pallas kernels for 3% -> 23%
where the time goes in v2:
time: 1170 us; the launch traced here: 1160 us
  Pallas kernels  417 us (36%)
  matrix products  316 us (27%)
  waiting for transfers between devices  236 us (20%)
  local copies, waits for them, and re-layouts  78.6 us (7%)
  other arithmetic  71.4 us (6%)
  starting transfers between devices  22.6 us (2%)
  between operations  16.3 us (1%)
    pallas_call x2, Pallas kernels, scatter_wide(): pl.pallas_call(scatter_kernel, out_shape=jax.ShapeDtypeStruct((rows, colu...  182 us
    pallas_call x1, Pallas kernels, start_exchange(): pl.pallas_call(functools.partial(start_kernel, count, swaps), out_shape=[...  156 us
    all_gather x1, waiting for transfers between devices, shards(): moe_plane = lax.all_gather(moe_in, 'wide', axis=0, tiled=True)  108 us
    dot_general x10, matrix products, dot_nt(): lax.dot_general(a, b, (((1,), (1,)), ((), ())), preferred_element_type=jn...  90.8 us
    ppermute x9, waiting for transfers between devices, exchange(): return lax.ppermute(value, 'narrow', swap)  87.7 us
    dot_general x9, matrix products, dot_tn(): lax.dot_general(a, b, (((0,), (0,)), ((), ())), preferred_element_type=jn...  79.3 us
    dot_general x12, matrix products, dot(): return jnp.dot(a, b, preferred_element_type=jnp.float32)  78 us
    dot_general x4, matrix products, spread(): jnp.einsum('wcr,wcd->wrd', onehot, values.reshape(wide_count, capacity, -...  44.3 us
  transfers between devices with their start and end apart: 16, of which 6 were waited for; matrix products, arithmetic and copies ran while one was open for 29% of the time, Pallas kernels for 23%

profile of v2, /device:TPU:0, one launch (start us, length us, event | category | flops | bytes accessed | tf_op | source)
XLA Modules:
  0.0 1157.5 jit_solution(4508915505776408567)
XLA Ops:
  15.4 156.1 %shard_map.271 = (s32[8,8,256]{2,1,0:T(8,128)}, bf16[8,256,2048]{2,1,0:T(8,128)(2,1)}, bf16[8,256,1024]{2,1,0:T(8,128)(2,1)}, bf16[2048,1024]{1,0:T(8,128)(2,1)}...) custom-call(s32[8,256]{1,0:T(8,128)} %bitcast.273, bf16[256,2048]{1,0:T(8,128)(2,1)} %fusion.8.refs_1_, ...), custom_call_target="tpu_custom_call" | custom-call | tf_op jit(solution)/shard_map/pallas_call | solution.py:482
  173.2 11.4 fusion.79
  231.8 11.6 %collective-permute-done.ko_ref = bf16[1024,256]{1,0:T(8,128)(2,1)S(1)} collective-permute-done((bf16[1024,256]{1,0:T(8,128)(2,1)S(1)}, bf16[1024,256]{1,0:T(8,128)(2,1)S(1)}, u32[]{:S(2)}, u32[]{:S(2)}) %collective-permute-start) | collective-permute-done | bytes 524320 | tf_op jit(solution)/shard_map/ppermute | solution.py:630
  254.3 17.9 %shard_map.273 = (bf16[2048,256]{1,0:T(8,128)(2,1)}, f32[2,2048]{1,0:T(2,128)}) custom-call(s32[1]{0:T(128)} %bitcast.side_ref, bf16[2048,256]{1,0:T(8,128)(2,1)} %get-tuple-element.123.q_ref, bf16[2048,256]{1,0:T(8,128)(2,1)} %copy-done.30, bf16[2048,256]{1,0:T(8,128)(2,1)} %slice.153.v_ref, bf16[1024,256]{1,0:T(8,128)(2,1)} %copy-done.79, ...), custom_call_target="tpu_custom_call" | custom-call | flops 4294967296 | bytes 6291456 | tf_op jit(solution)/shard_map/pallas_call | solution.py:679
  279.6 39.9 %all-to-all-done = bf16[8,256,256]{2,1,0:T(8,128)(2,1)S(1)} async-done(((bf16[8,256,256]{2,1,0:T(8,128)(2,1)}), bf16[8,256,256]{2,1,0:T(8,128)(2,1)S(1)}, u32[]{:S(2)}, u32[]{:S(2)}) %all-to-all-start) | async-done | bytes 1048608 | tf_op jit(solution)/shard_map/all_to_all | solution.py:681
  343.5 108.3 %all-gather.4.cloned.1.call-done = bf16[2048,2048]{1,0:T(8,128)(2,1)} async-done(((bf16[256,2048]{1,0:T(8,128)(2,1)}), bf16[2048,2048]{1,0:T(8,128)(2,1)}) %all-gather.4.cloned.1.call-update) | async-done | bytes 8388624 | tf_op jit(solution)/shard_map/all_gather | solution.py:687
  465.9 10.4 fusion.65
  482.3 12.2 %multiply_convert_fusion.4 = (bf16[1280,1024]{0,1:T(8,128)(2,1)S(1)}, f32[1280,1024]{0,1:T(8,128)}) fusion(f32[1280,1024]{0,1:T(8,128)} %copy.68, f32[1280]{0:T(1024)S(1)} %mul.654, bf16[1280,2048]{1,0:T(8,128)(2,1)} %bitcast.211, bf16[1,2048,1024]{2,1,0:T(8,128)(2,1)} %param.32), kind=kOutput, calls=%fused_computation.23 | convolution fusion | flops 5377884160 | bytes 22549504 | tf_op jit(solution)/shard_map/dot_general | solution.py:578
  518.6 12.7 %multiply_convert_fusion.5 = (bf16[1280,1024]{0,1:T(8,128)(2,1)S(1)}, f32[1280,1024]{0,1:T(8,128)}) fusion(f32[1280,1024]{0,1:T(8,128)} %copy.66, f32[1280]{0:T(1024)S(1)} %mul.642, bf16[1280,2048]{1,0:T(8,128)(2,1)} %bitcast.217, bf16[2048,1024]{1,0:T(8,128)(2,1)} %get-tuple-element.44), kind=kOutput, calls=%fused_computation.24 | convolution fusion | flops 5377884160 | bytes 22549504 | tf_op jit(solution)/shard_map/dot_general | solution.py:578
  545.6 11.9 %add_convert_fusion = bf16[8,256,2048]{2,1,0:T(8,128)(2,1)} fusion(f32[8,256,2048]{2,1,0:T(8,128)} %fusion.24, bf16[8,160,2048]{2,1,0:T(8,128)(2,1)S(1)} %bitcast.234, s32[8,256]{1,0:T(8,128)S(1)} %fusion.26), kind=kOutput, calls=%fused_computation.2 | convolution fusion | flops 1350893568 | bytes 30416896 | tf_op jit(solution)/shard_map/wcr,wcd->wrd/dot_general | solution.py:706
  563.7 14.8 %multiply_reduce_fusion.1 = (f32[1280]{0:T(1024)S(1)}, bf16[1280,1024]{0,1:T(8,128)(2,1)}, bf16[1280,1024]{0,1:T(8,128)(2,1)}) fusion(f32[1280,1024]{0,1:T(8,128)} %get-tuple-element.156, f32[1280,1024]{0,1:T(8,128)} %copy.69, f32[1280]{0:T(1024)S(1)} %mul.642, bf16[1280,2048]{1,0:T(8,128)(2,1)} %bitcast.222, bf16[1024,2048]{1,0:T(8,128)(2,1)} %get-tuple-element.43), kind=kOutput, calls=%fused_computation.14 | convolution fusion | flops 5390990336 | bytes 25176064 | tf_op jit(solution)/shard_map/dot_general | solution.py:582
  584.8 14.9 %multiply_reduce_fusion = (f32[1280]{0:T(1024)S(1)}, bf16[1280,1024]{0,1:T(8,128)(2,1)}, bf16[1280,1024]{0,1:T(8,128)(2,1)}) fusion(f32[1280,1024]{0,1:T(8,128)} %get-tuple-element.158, f32[1280,1024]{0,1:T(8,128)} %copy.72, f32[1280]{0:T(1024)S(1)} %mul.654, bf16[1280,2048]{1,0:T(8,128)(2,1)} %bitcast.208, bf16[1,1024,2048]{2,1,0:T(8,128)(2,1)} %param.33), kind=kOutput, calls=%fused_computation.13 | convolution fusion | flops 5390990336 | bytes 25176064 | tf_op jit(solution)/shard_map/dot_general | solution.py:582
  600.1 10.4 convolution_convert_fusion.7
  672.9 15.9 %convolution_add_fusion = f32[8,256,2048]{2,1,0:T(8,128)} fusion(f32[8,256,2048]{2,1,0:T(8,128)} %fusion.23, bf16[8,160,2048]{2,1,0:T(8,128)(2,1)} %bitcast.235, s32[8,256]{1,0:T(8,128)S(1)} %fusion.26), kind=kOutput, calls=%fused_computation.11 | convolution fusion | flops 1346699264 | bytes 38805504 | tf_op jit(solution)/shard_map/wcr,wcd->wrd/dot_general | solution.py:706
  688.9 11.8 %fusion = bf16[2048,2048]{1,0:T(8,128)(2,1)} fusion(f32[8,256,2048]{2,1,0:T(8,128)} %convolution_add_fusion, bf16[2048,16]{0,1:T(8,128)(2,1)S(1)} %copy-done.42, f32[16]{0:T(128)S(1)} %copy-done.68, f32[2048]{0:T(1024)S(1)} %mul.684, f32[16]{0:T(128)S(1)} %copy-done.69, f32[2048]{0:T(1024)S(1)} %mul.676, f32[2048]{0:T(1024)S(1)} %copy-done.51, ...), kind=kOutput, calls=%fused_computation.1 | convolution fusion | flops 142868480 | bytes 25395328 | tf_op jit(solution)/shard_map/dot_general | solution.py:582
  700.6 92.1 %shard_map.274 = f32[256,2048]{1,0:T(8,128)S(1)} custom-call(bf16[8,256,2048]{2,1,0:T(8,128)(2,1)} %bitcast.204), custom_call_target="tpu_custom_call" | custom-call | tf_op jit(solution)/shard_map/pallas_call | solution.py:385
  815.7 11.7 %add_bitcast_fusion.1 = f32[1,2048,1024]{2,1,0:T(8,128)} fusion(bf16[2048,1024]{1,0:T(8,128)(2,1)} %collective-permute-done.8, bf16[1280,2048]{1,0:T(8,128)(2,1)} %bitcast.212, bf16[1280,1024]{0,1:T(8,128)(2,1)} %get-tuple-element.104), kind=kOutput, calls=%fused_computation.6 | convolution fusion | flops 5372903424 | bytes 20447232 | tf_op jit(solution)/shard_map/dot_general | solution.py:586
  827.4 55.2 %collective-permute-done.7 = bf16[2048,1024]{1,0:T(8,128)(2,1)} collective-permute-done((bf16[2048,1024]{1,0:T(8,128)(2,1)}, bf16[2048,1024]{1,0:T(8,128)(2,1)}, u32[]{:S(2)}, u32[]{:S(2)}) %collective-permute-start.7) | collective-permute-done | bytes 4194336 | tf_op jit(solution)/shard_map/ppermute | solution.py:630
  893.6 27.1 %shard_map.275 = (f32[2048,256]{1,0:T(8,128)}, f32[2048,256]{1,0:T(8,128)}, f32[2048,256]{1,0:T(8,128)}, bf16[1024,256]{1,0:T(8,128)(2,1)}, bf16[1024,256]{1,0:T(8,128)(2,1)}) custom-call(s32[1]{0:T(128)} %bitcast.side_ref, bf16[2048,256]{1,0:T(8,128)(2,1)} %get-tuple-element.123.q_ref, bf16[2048,256]{1,0:T(8,128)(2,1)} %copy-done.30, ...), custom_call_target="tpu_custom_call" | custom-call | flops 10737418240 | bytes 20971520 | tf_op jit(solution)/shard_map/pallas_call | solution.py:778
  922.4 11.4 add_bitcast_fusion
  976.4 10.8 convolution_convert_fusion.10
  998.1 90.3 %shard_map.277 = f32[256,2048]{1,0:T(8,128)S(1)} custom-call(bf16[8,256,2048]{2,1,0:T(8,128)(2,1)} %bitcast.224), custom_call_target="tpu_custom_call" | custom-call | tf_op jit(solution)/shard_map/pallas_call | solution.py:385
  1095.7 17.4 %shard_map.278 = f32[24,2048]{1,0:T(8,128)} custom-call(f32[24,2048]{1,0:T(8,128)} %concatenate.53.x_ref), custom_call_target="tpu_custom_call" | custom-call | tf_op jit(solution)/shard_map/pallas_call | solution.py:540
  1138.1 10.8 collective-permute-done.6
  (367 shorter events, 354.4 us)
Async XLA Ops:
  7.2 324.5 %all-gather.6.cloned.1.call-start = ((), (), s32[]{:S(2)}) async-start(), calls=%async_computation.4 | async-start | bytes 9437184 | tf_op jit(solution)/shard_map/all_gather | solution.py:658
  15.4 156.6 %copy-start.32 = (bf16[2048,256]{1,0:T(8,128)(2,1)S(1)}, bf16[2048,256]{1,0:T(8,128)(2,1)}, u32[]{:S(2)}) copy-start(bf16[2048,256]{1,0:T(8,128)(2,1)} %param.22) | copy-start | bytes 3145732
  171.6 148.5 %collective-permute-start.2 = (bf16[2048,1024]{1,0:T(8,128)(2,1)}, bf16[2048,1024]{1,0:T(8,128)(2,1)}, u32[]{:S(2)}, u32[]{:S(2)}) collective-permute-start(bf16[2048,1024]{1,0:T(8,128)(2,1)} %bitcast.280), channel_id=1, source_target_pairs={{0,16},{16,0},{1,17},{17,1},{2,18},{18,2},{3,19},{19,3},{4,20},{20... | collective-permute-start | bytes 12582920 | tf_op jit(solution)/shard_map/ppermute | solution.py:647
  197.7 133.4 %copy-start.46 = (f32[1,2048]{1,0:T(1,128)}, f32[1,2048]{1,0:T(1,128)S(1)}, u32[]{:S(2)}) copy-start(f32[1,2048]{1,0:T(1,128)S(1)} %get-tuple-element.140) | copy-start | bytes 24580
  197.7 133.3 %copy-start.48 = (f32[1,2048]{1,0:T(1,128)}, f32[1,2048]{1,0:T(1,128)S(1)}, u32[]{:S(2)}) copy-start(f32[1,2048]{1,0:T(1,128)S(1)} %get-tuple-element.141) | copy-start | bytes 24580
  228.5 14.9 %collective-permute-start = (bf16[1024,256]{1,0:T(8,128)(2,1)S(1)}, bf16[1024,256]{1,0:T(8,128)(2,1)S(1)}, u32[]{:S(2)}, u32[]{:S(2)}) collective-permute-start(bf16[1024,256]{1,0:T(8,128)(2,1)S(1)} %slice.154), channel_id=1, source_target_pairs={{0,1},{1,0},{2,3},{3,2},{4,5},{5,4},{6,7},{7,6},{8,9},{9,8},{10,11... | collective-permute-start | bytes 1572872 | tf_op jit(solution)/shard_map/ppermute | solution.py:630
  230.2 23.2 %collective-permute-start.1 = (bf16[1024,256]{1,0:T(8,128)(2,1)S(1)}, bf16[1024,256]{1,0:T(8,128)(2,1)S(1)}, u32[]{:S(2)}, u32[]{:S(2)}) collective-permute-start(bf16[1024,256]{1,0:T(8,128)(2,1)S(1)} %slice.155), channel_id=1, source_target_pairs={{0,1},{1,0},{2,3},{3,2},{4,5},{5,4},{6,7},{7,6},{8,9},{9,8},{10,11... | collective-permute-start | bytes 1572872 | tf_op jit(solution)/shard_map/ppermute | solution.py:630
  272.1 47.3 %all-to-all-start = ((bf16[8,256,256]{2,1,0:T(8,128)(2,1)}), bf16[8,256,256]{2,1,0:T(8,128)(2,1)S(1)}, u32[]{:S(2)}, u32[]{:S(2)}) async-start(bf16[8,256,256]{2,1,0:T(8,128)(2,1)} %bitcast.231), calls=%async_computation | async-start | bytes 2097152 | tf_op jit(solution)/shard_map/all_to_all | solution.py:681
  279.5 172.3 %all-gather.4.cloned.1.call-start = ((), (), s32[]{:S(2)}) async-start(), calls=%async_computation.3 | async-start | bytes 9437184 | tf_op jit(solution)/shard_map/all_gather | solution.py:687
  328.6 465.4 %reduce-scatter.2.cloned.1.call-start = ((), (), s32[]{:S(2)}) async-start(), calls=%async_computation.5 | async-start | bytes 9437184 | tf_op jit(solution)/shard_map/reduce_scatter | solution.py:729
  557.5 566.9 %all-gather.8.cloned.1.call-start = ((), (), s32[]{:S(2)}) async-start(), calls=%async_computation.6 | async-start | bytes 9437184 | tf_op jit(solution)/shard_map/all_gather | solution.py:776
  610.4 311.9 %collective-permute-start.9 = (bf16[1024,2048]{1,0:T(8,128)(2,1)}, bf16[1024,2048]{1,0:T(8,128)(2,1)}, u32[]{:S(2)}, u32[]{:S(2)}) collective-permute-start(bf16[1024,2048]{1,0:T(8,128)(2,1)} %convolution_convert_fusion.7), channel_id=1, source_target_pairs={{0,1},{1,0},{2,3},{3,2},{4,5},{5,4},{6,7},{7,6},{8,9},{9,8},{10,11... | collective-permute-start | bytes 12582920 | tf_op jit(solution)/shard_map/ppermute | solution.py:630
  622.2 193.5 %collective-permute-start.8 = (bf16[2048,1024]{1,0:T(8,128)(2,1)}, bf16[2048,1024]{1,0:T(8,128)(2,1)}, u32[]{:S(2)}, u32[]{:S(2)}) collective-permute-start(bf16[2048,1024]{1,0:T(8,128)(2,1)} %convolution_convert_fusion.8), channel_id=1, source_target_pairs={{0,1},{1,0},{2,3},{3,2},{4,5},{5,4},{6,7},{7,6},{8,9},{9,8},{10,11... | collective-permute-start | bytes 12582920 | tf_op jit(solution)/shard_map/ppermute | solution.py:630
  630.3 252.4 %collective-permute-start.7 = (bf16[2048,1024]{1,0:T(8,128)(2,1)}, bf16[2048,1024]{1,0:T(8,128)(2,1)}, u32[]{:S(2)}, u32[]{:S(2)}) collective-permute-start(bf16[2048,1024]{1,0:T(8,128)(2,1)} %convolution_convert_fusion.9), channel_id=1, source_target_pairs={{0,1},{1,0},{2,3},{3,2},{4,5},{5,4},{6,7},{7,6},{8,9},{9,8},{10,11... | collective-permute-start | bytes 12582920 | tf_op jit(solution)/shard_map/ppermute | solution.py:630
  662.6 130.2 %slice-start = ((s8[8388608]{0:T(1024)(128)(4,1)}), s8[4194304]{0:T(1024)(128)(4,1)S(1)}, s32[]{:S(2)}) async-start(s8[8388608]{0:T(1024)(128)(4,1)} %bitcast.198), calls=%async_computation.7 | async-start | bytes 8388608
  672.9 119.9 %slice-start.1 = ((s8[8388608]{0:T(1024)(128)(4,1)}), s8[4194304]{0:T(1024)(128)(4,1)S(1)}, s32[]{:S(2)}) async-start(s8[8388608]{0:T(1024)(128)(4,1)} %bitcast.198), calls=%async_computation.8 | async-start | bytes 8388608
  811.8 80.9 %all-to-all-start.1 = ((bf16[256,8,256]{2,0,1:T(8,128)(2,1)}), bf16[256,8,256]{2,0,1:T(8,128)(2,1)S(1)}, u32[]{:S(2)}, u32[]{:S(2)}) async-start(bf16[256,8,256]{2,0,1:T(8,128)(2,1)} %bitcast.195), calls=%async_computation.2 | async-start | bytes 2097152 | tf_op jit(solution)/shard_map/all_to_all | solution.py:775
  920.7 21.4 %collective-permute-start.3 = (bf16[1024,256]{1,0:T(8,128)(2,1)}, bf16[1024,256]{1,0:T(8,128)(2,1)S(1)}, u32[]{:S(2)}, u32[]{:S(2)}) collective-permute-start(bf16[1024,256]{1,0:T(8,128)(2,1)} %get-tuple-element.54), channel_id=1, source_target_pairs={{0,1},{1,0},{2,3},{3,2},{4,5},{5,4},{6,7},{7,6},{8,9},{9,8},{10,11... | collective-permute-start | bytes 1572872 | tf_op jit(solution)/shard_map/ppermute | solution.py:630
  936.1 33.6 %collective-permute-start.4 = (bf16[1024,256]{1,0:T(8,128)(2,1)}, bf16[1024,256]{1,0:T(8,128)(2,1)}, u32[]{:S(2)}, u32[]{:S(2)}) collective-permute-start(bf16[1024,256]{1,0:T(8,128)(2,1)} %get-tuple-element.56), channel_id=1, source_target_pairs={{0,1},{1,0},{2,3},{3,2},{4,5},{5,4},{6,7},{7,6},{8,9},{9,8},{10,11... | collective-permute-start | bytes 1572872 | tf_op jit(solution)/shard_map/ppermute | solution.py:630
  987.2 144.5 %collective-permute-start.5 = (bf16[2048,768]{1,0:T(8,128)(2,1)}, bf16[2048,768]{1,0:T(8,128)(2,1)}, u32[]{:S(2)}, u32[]{:S(2)}) collective-permute-start(bf16[2048,768]{1,0:T(8,128)(2,1)} %convolution_convert_fusion.10), channel_id=1, source_target_pairs={{0,1},{1,0},{2,3},{3,2},{4,5},{5,4},{6,7},{7,6},{8,9},{9,8},{10,11... | collective-permute-start | bytes 9437192 | tf_op jit(solution)/shard_map/ppermute | solution.py:630
  998.1 90.5 %copy-start.8 = (bf16[256,2048]{1,0:T(8,128)(2,1)S(1)}, bf16[256,2048]{1,0:T(8,128)(2,1)}, u32[]{:S(2)}) copy-start(bf16[256,2048]{1,0:T(8,128)(2,1)} %param.18) | copy-start | bytes 3145732
  998.1 90.5 %copy-start.53 = (f32[2048]{0:T(1024)S(1)}, f32[2048]{0:T(1024)}, u32[]{:S(2)}) copy-start(f32[2048]{0:T(1024)} %copy-done.52) | copy-start | bytes 24580
  998.1 90.5 %copy-start.61 = (f32[256]{0:T(256)S(1)}, f32[256]{0:T(256)}, u32[]{:S(2)}) copy-start(f32[256]{0:T(256)} %copy-done.60) | copy-start | bytes 3076
  1130.5 18.4 %collective-permute-start.6 = (bf16[256,2048]{1,0:T(8,128)(2,1)S(1)}, bf16[256,2048]{1,0:T(8,128)(2,1)S(1)}, u32[]{:S(2)}, u32[]{:S(2)}) collective-permute-start(bf16[256,2048]{1,0:T(8,128)(2,1)S(1)} %convolution_convert_fusion.11), channel_id=1, source_target_pairs={{0,1},{1,0},{2,3},{3,2},{4,5},{5,4},{6,7},{7,6},{8,9},{9,8},{10,11... | collective-permute-start | bytes 3145736 | tf_op jit(solution)/shard_map/ppermute | solution.py:630
  (93 other events, 1047.0 us)
Sparse Core Ops, SparseCore 0:
  171.8 144.8 all-gather.5
  328.8 122.9 all-gather.3
  557.6 147.1 reduce-scatter.1
  803.2 145.6 all-gather.7

commit v3 on v2

--- a/solution.py
+++ b/solution.py
@@ -23,29 +23,23 @@
 NT = (((1,), (1,)), ((), ()))
 
 
-def block_parts(w, rows, prompt_blocks, paired, limit):
-    def cut(plane, count):
-        return [
-            (plane, first, min(limit, count - first), None) for first in range(0, count, limit)
-        ]
-
-    if w is None:
-        parts = cut(0, prompt_blocks * rows) + cut(1, prompt_blocks * rows)
-        own = None
-        if paired:
-            parts.append((1, None, rows, "side"))
-    else:
-        own = w * rows
-        parts = cut(0, own) + cut(1, own) + [(1, own, rows, "side")]
-    return parts + [(0, own, rows, "causal")]
+def key_parts(w, plane, rows, prompt_blocks, paired, limit=512):
+    count = (prompt_blocks if w is None else w) * rows
+    parts = [(first, min(limit, count - first), None) for first in range(0, count, limit)]
+    own = None if w is None else w * rows
+    if plane == 0:
+        parts.append((own, rows, "causal"))
+    elif w is not None or paired:
+        parts.append((own, rows, "side"))
+    return parts
 
 
 def for_blocks(blocks, prompt_blocks, one):
     for w in range(prompt_blocks):
-        one(w, w)
+        one(w, w, w * one.rows)
 
     def body(w, carry):
-        one(None, w)
+        one(None, w, pl.multiple_of(w * one.rows, one.rows))
         return carry
 
     lax.fori_loop(prompt_blocks, blocks, body, 0)
@@ -61,26 +55,117 @@
     return score
 
 
-def attend_kernel(rows, prompt_blocks, paired, side_ref, q_ref, k_ref, v_ref, ko_ref, vo_ref, o_ref, lse_ref, vt_ref, vto_ref):
+def row_sums(values):
+    total = values[:, :HD]
+    for first in range(HD, values.shape[1], HD):
+        total = total + values[:, first : first + HD]
+    return jnp.sum(total.T, 0, keepdims=True)
+
+
+def turn(values, cosine, sine):
+    return values * cosine + pltpu.roll(values, HD // 2, 1) * sine
+
+
+def inverse_norms(sums_ref, at):
+    inverse = lax.rsqrt(sums_ref[:, at].T / D + EPSILON)
+    return inverse[:, 0:1], inverse[:, 1:2]
+
+
+def peer_copies(size, src, dst, send, recv, grp, wide, narrow):
+    return [
+        remote(src, dst.at[k - 1], send.at[k - 1], recv.at[k - 1], (grp, lax.rem(wide + k, size), narrow))
+        for k in range(1, size)
+    ]
+
+
+def attend_kernel(
+    rows, prompt_blocks, paired, shared, raw_ref, gains_ref, cos_ref, sin_ref,
+    q_ref, k_ref, v_ref, ko_ref, vo_ref, o_ref, own_ref, lse_ref, sums_ref,
+    vt_ref, vto_ref, came_ref, sum_send, sum_recv, pair_send, pair_recv, out_send, out_recv,
+):
     half, columns = q_ref.shape
-    side = side_ref[0]
-    for h in range(columns // HD):
+    size = half // rows
+    heads = columns // HD
+    grp, wide, narrow = (lax.axis_index(a) for a in ("grp", "wide", "narrow"))
+    partner = (grp, wide, 1 - narrow)
+    greet([((grp, lax.rem(wide + k, size), narrow), None) for k in range(1, size)] + [(partner, None)])
+    pairs = [
+        remote(src.at[pl.ds(0, shared)], dst, pair_send.at[i], pair_recv.at[i], partner)
+        for i, (src, dst) in enumerate(((k_ref, ko_ref), (v_ref, vo_ref)))
+    ]
+    v_ref[...] = raw_ref[:, 2 * columns :].astype(jnp.bfloat16)
+    pairs[1].start()
+    sums_ref[...] = jnp.zeros_like(sums_ref)
+
+    def squares(b, carry):
+        at = pl.ds(pl.multiple_of(b * rows, rows), rows)
+        for i in range(2):
+            part = raw_ref[at, i * columns : (i + 1) * columns]
+            sums_ref[i : i + 1, at] = row_sums(part * part)
+        return carry
+
+    lax.fori_loop(0, size, squares, 0)
+    copies = peer_copies(size, sums_ref, came_ref, sum_send, sum_recv, grp, wide, narrow)
+    for copy in copies:
+        copy.start()
+    for h in range(heads):
         hs = slice(h * HD, (h + 1) * HD)
         vt_ref[hs, :] = v_ref[:, hs].T
+    for copy in copies:
+        copy.wait()
+    total = sums_ref[...]
+    for k in range(size - 1):
+        total = total + came_ref[k]
+    sums_ref[...] = total
+
+    def prepare(i, ref):
+        def body(b, carry):
+            at = pl.ds(pl.multiple_of(b * rows, rows), rows)
+            inverse = inverse_norms(sums_ref, at)[i]
+            for h in range(heads):
+                hs = slice(h * HD, (h + 1) * HD)
+                values = raw_ref[at, i * columns + h * HD : i * columns + (h + 1) * HD]
+                values = values * inverse * gains_ref[i : i + 1, hs]
+                ref[at, hs] = turn(values, cos_ref[at], sin_ref[at]).astype(jnp.bfloat16)
+            return carry
+
+        return body
+
+    lax.fori_loop(0, shared // rows, prepare(1, k_ref), 0)
+    pairs[0].start()
+    lax.fori_loop(shared // rows, size, prepare(1, k_ref), 0)
+    lax.fori_loop(0, size, prepare(0, q_ref), 0)
+    pairs[1].wait()
+    for h in range(heads):
+        hs = slice(h * HD, (h + 1) * HD)
         vto_ref[hs, :] = vo_ref[:, hs].T
-
-    def one(w, w_index):
-        start = w_index * rows if w is not None else pl.multiple_of(w_index * rows, rows)
-        for h in range(columns // HD):
+    pairs[0].wait()
+
+    def mine():
+        return pl.ds(pl.multiple_of(wide * columns, columns), columns)
+
+    def hand_out(w):
+        return remote(
+            o_ref.at[pl.ds(pl.multiple_of(w * rows, rows), rows)],
+            own_ref.at[:, mine()],
+            out_send.at[w],
+            out_recv.at[wide],
+            (grp, w, narrow),
+        )
+
+    def one(w, w_index, start):
+        block = pl.ds(start, rows)
+        for h in range(heads):
             hs = slice(h * HD, (h + 1) * HD)
-            query = q_ref[pl.ds(start, rows), hs]
+            query = q_ref[block, hs]
             scores = []
-            for plane, first, count, mask in block_parts(w, rows, prompt_blocks, paired, 512):
-                at = pl.ds(start if first is None else first, count)
-                key = (k_ref, ko_ref)[plane][at, hs]
-                score = lax.dot_general(key, query, NT, preferred_element_type=jnp.float32)
-                score = score * (HD**-0.5 * LOG2E)
-                scores.append((plane, at, masked_scores(score, mask, side, rows)))
+            for plane in range(2):
+                for first, count, mask in key_parts(w, plane, rows, prompt_blocks, paired):
+                    at = pl.ds(start if first is None else first, count)
+                    key = (k_ref, ko_ref)[plane][at, hs]
+                    score = lax.dot_general(key, query, NT, preferred_element_type=jnp.float32)
+                    score = score * (HD**-0.5 * LOG2E)
+                    scores.append((plane, at, masked_scores(score, mask, narrow, rows)))
             largest = functools.reduce(
                 jnp.maximum, [jnp.max(score, 0, keepdims=True) for _, _, score in scores]
             )
@@ -89,93 +174,239 @@
             for plane, at, score in scores:
                 weight = jnp.exp2(score - largest)
                 total = total + jnp.sum(weight, 0, keepdims=True)
-                mixed = mixed + jnp.dot(
-                    (vt_ref, vto_ref)[plane][hs, at], weight.astype(jnp.bfloat16), preferred_element_type=jnp.float32
-                )
-            o_ref[pl.ds(start, rows), hs] = (mixed / total).T.astype(jnp.bfloat16)
-            lse_ref[h : h + 1, pl.ds(start, rows)] = largest + jnp.log(total) * LOG2E
-
-    for_blocks(half // rows, prompt_blocks, one)
+                mixed = mixed + dot((vt_ref, vto_ref)[plane][hs, at], weight.astype(jnp.bfloat16))
+            o_ref[block, hs] = (mixed / total).T.astype(jnp.bfloat16)
+            lse_ref[h : h + 1, block] = largest + jnp.log(total) * LOG2E
+
+        @pl.when(w_index != wide)
+        def _():
+            hand_out(w_index).start()
+
+    one.rows = rows
+    for_blocks(size, prompt_blocks, one)
+    own_ref[:, mine()] = o_ref[pl.ds(pl.multiple_of(wide * rows, rows), rows)]
+
+    def finish(w, carry):
+        @pl.when(w != wide)
+        def _():
+            hand_out(w).wait_send()
+            remote(
+                o_ref.at[pl.ds(0, rows)], own_ref.at[:, mine()], out_send.at[w], out_recv.at[w], (grp, w, narrow)
+            ).wait_recv()
+
+        return carry
+
+    lax.fori_loop(0, size, finish, 0)
 
 
 def attend_back_kernel(
-    rows, prompt_blocks, paired, side_ref, q_ref, k_ref, v_ref, ko_ref, vo_ref, do_ref, o_ref, lse_ref,
-    dq_ref, dk_ref, dv_ref, dkb_ref, dvb_ref, kt_ref, kto_ref, dko_ref, dvo_ref,
+    rows, prompt_blocks, paired, shared, raw_ref, gains_ref, cos_ref, sin_ref, sums_ref,
+    q_ref, k_ref, v_ref, ko_ref, vo_ref, grad_ref, o_ref, lse_ref,
+    joined_ref, gain_ref,
+    do_ref, dq_ref, dk_ref, dv_ref, dko_ref, dvo_ref, dkb_ref, dvb_ref, dkr_ref, dvr_ref, kt_ref, kto_ref,
+    dots_ref, came_ref, sum_send, sum_recv, pair_send, pair_recv, in_send, in_recv,
 ):
     half, columns = q_ref.shape
-    side = side_ref[0]
-    for ref in (dk_ref, dv_ref, dko_ref, dvo_ref):
+    size = half // rows
+    heads = columns // HD
+    grp, wide, narrow = (lax.axis_index(a) for a in ("grp", "wide", "narrow"))
+    partner = (grp, wide, 1 - narrow)
+    greet([((grp, lax.rem(wide + k, size), narrow), None) for k in range(1, size)] + [(partner, None)])
+    my_rows = pl.ds(pl.multiple_of(wide * rows, rows), rows)
+
+    def part_of(w):
+        return pl.ds(pl.multiple_of(w * columns, columns), columns)
+
+    def hand_in(w):
+        return remote(
+            grad_ref.at[:, part_of(w)], do_ref.at[my_rows], in_send.at[w], in_recv.at[wide], (grp, w, narrow)
+        )
+
+    def each_peer(act):
+        def body(w, carry):
+            pl.when(w != wide)(lambda: act(w))
+            return carry
+
+        lax.fori_loop(0, size, body, 0)
+
+    each_peer(lambda w: hand_in(w).start())
+    do_ref[my_rows, :] = grad_ref[:, part_of(wide)]
+    for ref in (dk_ref, dv_ref, dko_ref, dvo_ref, dots_ref, gain_ref):
         ref[...] = jnp.zeros_like(ref)
-    for h in range(columns // HD):
+    for h in range(heads):
         hs = slice(h * HD, (h + 1) * HD)
         kt_ref[hs, :] = k_ref[:, hs].T
         kto_ref[hs, :] = ko_ref[:, hs].T
-
-    def one(w, w_index):
-        start = w_index * rows if w is not None else pl.multiple_of(w_index * rows, rows)
-        for h in range(columns // HD):
-            hs = slice(h * HD, (h + 1) * HD)
-            query = q_ref[pl.ds(start, rows), hs]
-            grad = do_ref[pl.ds(start, rows), hs]
-            product = grad.astype(jnp.float32) * o_ref[pl.ds(start, rows), hs].astype(jnp.float32)
-            delta = jnp.sum(product.T, 0, keepdims=True)
-            lse = lse_ref[h : h + 1, pl.ds(start, rows)]
-            back = jnp.zeros((HD, rows), jnp.float32)
-            for plane, first, count, mask in block_parts(w, rows, prompt_blocks, paired, 512):
-                at = pl.ds(start if first is None else first, count)
-                key = (k_ref, ko_ref)[plane][at, hs]
-                value = (v_ref, vo_ref)[plane][at, hs]
-                score = lax.dot_general(key, query, NT, preferred_element_type=jnp.float32)
-                score = masked_scores(score * (HD**-0.5 * LOG2E), mask, side, rows)
-                weight = jnp.exp2(score - lse)
-                grad_weight = lax.dot_general(value, grad, NT, preferred_element_type=jnp.float32)
-                grad_score = (weight * (grad_weight - delta)).astype(jnp.bfloat16)
-                dv = (dv_ref, dvo_ref)[plane]
-                dv[at, hs] += jnp.dot(weight.astype(jnp.bfloat16), grad, preferred_element_type=jnp.float32)
-                dk = (dk_ref, dko_ref)[plane]
-                dk[at, hs] += jnp.dot(grad_score, query, preferred_element_type=jnp.float32) * HD**-0.5
-                back = back + jnp.dot((kt_ref, kto_ref)[plane][hs, at], grad_score, preferred_element_type=jnp.float32)
-            dq_ref[pl.ds(start, rows), hs] = back.T * HD**-0.5
-
-    for_blocks(half // rows, prompt_blocks, one)
+    each_peer(
+        lambda w: remote(
+            grad_ref.at[:, part_of(w)], do_ref.at[my_rows], in_send.at[w], in_recv.at[w], (grp, w, narrow)
+        ).wait_recv()
+    )
+
+    def sweep(plane):
+        keys, values = ((k_ref, v_ref), (ko_ref, vo_ref))[plane]
+        dk, dv = ((dk_ref, dv_ref), (dko_ref, dvo_ref))[plane]
+        flipped = (kt_ref, kto_ref)[plane]
+
+        def one(w, w_index, start):
+            block = pl.ds(start, rows)
+            for h in range(heads):
+                hs = slice(h * HD, (h + 1) * HD)
+                query = q_ref[block, hs]
+                grad = do_ref[block, hs]
+                delta = row_sums(grad.astype(jnp.float32) * o_ref[block, hs].astype(jnp.float32))
+                lse = lse_ref[h : h + 1, block]
+                back = jnp.zeros((HD, rows), jnp.float32)
+                for first, count, mask in key_parts(w, plane, rows, prompt_blocks, paired):
+                    at = pl.ds(start if first is None else first, count)
+                    score = lax.dot_general(keys[at, hs], query, NT, preferred_element_type=jnp.float32)
+                    score = masked_scores(score * (HD**-0.5 * LOG2E), mask, narrow, rows)
+                    weight = jnp.exp2(score - lse)
+                    grad_weight = lax.dot_general(values[at, hs], grad, NT, preferred_element_type=jnp.float32)
+                    grad_score = (weight * (grad_weight - delta)).astype(jnp.bfloat16)
+                    dv[at, hs] += dot(weight.astype(jnp.bfloat16), grad)
+                    dk[at, hs] += dot(grad_score, query) * HD**-0.5
+                    back = back + dot(flipped[hs, at], grad_score)
+                back = back.T * HD**-0.5
+                dq_ref[block, hs] = back if plane == 1 else dq_ref[block, hs] + back
+
+        one.rows = rows
+        for_blocks(size, prompt_blocks, one)
+
+    sweep(1)
     dkb_ref[...] = dko_ref[...].astype(jnp.bfloat16)
     dvb_ref[...] = dvo_ref[...].astype(jnp.bfloat16)
-
-
-def attention_calls(rows, half, shared, columns, prompt_blocks, paired):
-    smem = pl.BlockSpec(memory_space=pltpu.SMEM)
-    vmem = pl.BlockSpec(memory_space=pltpu.VMEM)
+    pairs = [
+        remote(src, dst, pair_send.at[i], pair_recv.at[i], partner)
+        for i, (src, dst) in enumerate(((dkb_ref, dkr_ref), (dvb_ref, dvr_ref)))
+    ]
+    for copy in pairs:
+        copy.start()
+    sweep(0)
+
+    def turn_back(i, ref):
+        def body(b, carry):
+            at = pl.ds(pl.multiple_of(b * rows, rows), rows)
+            inverse = inverse_norms(sums_ref, at)[i]
+            products = []
+            for h in range(heads):
+                hs = slice(h * HD, (h + 1) * HD)
+                grad = turn(ref[at, hs], cos_ref[at], -sin_ref[at])
+                ref[at, hs] = grad
+                product = grad * raw_ref[at, i * columns + h * HD : i * columns + (h + 1) * HD]
+                gain_ref[i : i + 1, hs] += jnp.sum(product * inverse, 0, keepdims=True)
+                products.append(product * gains_ref[i : i + 1, hs])
+            dots_ref[i : i + 1, at] = row_sums(sum(products[1:], products[0]))
+            return carry
+
+        lax.fori_loop(0, size, body, 0)
+
+    turn_back(0, dq_ref)
+    for copy in pairs:
+        copy.wait()
+    dk_ref[0:shared, :] += dkr_ref[...].astype(jnp.float32)
+    turn_back(1, dk_ref)
+    copies = peer_copies(size, dots_ref, came_ref, sum_send, sum_recv, grp, wide, narrow)
+    for copy in copies:
+        copy.start()
+    joined_ref[0:shared, 2 * columns :] = (dv_ref[0:shared] + dvr_ref[...].astype(jnp.float32)).astype(jnp.bfloat16)
+    if shared < half:
+        joined_ref[shared:, 2 * columns :] = dv_ref[shared:].astype(jnp.bfloat16)
+    for copy in copies:
+        copy.wait()
+    total = dots_ref[...]
+    for k in range(size - 1):
+        total = total + came_ref[k]
+    dots_ref[...] = total
+
+    def finish(b, carry):
+        at = pl.ds(pl.multiple_of(b * rows, rows), rows)
+        inverses = inverse_norms(sums_ref, at)
+        products = dots_ref[:, at].T / D
+        for i, ref in enumerate((dq_ref, dk_ref)):
+            inverse = inverses[i]
+            cubed = inverse * inverse * inverse * products[:, i : i + 1]
+            for h in range(heads):
+                hs = slice(h * HD, (h + 1) * HD)
+                there = slice(i * columns + h * HD, i * columns + (h + 1) * HD)
+                value = inverse * gains_ref[i : i + 1, hs] * ref[at, hs] - raw_ref[at, there] * cubed
+                joined_ref[at, there] = value.astype(jnp.bfloat16)
+        return carry
+
+    lax.fori_loop(0, size, finish, 0)
+    each_peer(lambda w: hand_in(w).wait_send())
+
+
+def attention_calls(rows, half, shared, columns, prompt_blocks, paired, ids):
     heads = columns // HD
-    params = pltpu.CompilerParams(vmem_limit_bytes=60 * 2**20)
-    wide16 = jax.ShapeDtypeStruct((half, columns), jnp.bfloat16)
-    wide32 = jax.ShapeDtypeStruct((half, columns), jnp.float32)
+    size = half // rows
+    bf16, f32 = jnp.bfloat16, jnp.float32
+    shape = lambda dtype, *dims: jax.ShapeDtypeStruct(dims, dtype)
+    sems = pltpu.SemaphoreType.DMA
     work = half * half * columns * 2
+    peers = [sems((size - 1,)), sems((size - 1,)), sems((2,)), sems((2,)), sems((size,)), sems((size,))]
+
+    def params(k):
+        return pltpu.CompilerParams(vmem_limit_bytes=60 * 2**20, collective_id=ids[k], has_side_effects=True)
+
     forward = pl.pallas_call(
-        functools.partial(attend_kernel, rows, prompt_blocks, paired),
-        out_shape=(wide16, jax.ShapeDtypeStruct((heads, half), jnp.float32)),
-        in_specs=[smem] + [vmem] * 5,
-        out_specs=(vmem, vmem),
-        scratch_shapes=[pltpu.VMEM((columns, half), jnp.bfloat16), pltpu.VMEM((columns, shared), jnp.bfloat16)],
-        compiler_params=params,
-        cost_estimate=pl.CostEstimate(flops=2 * work, bytes_accessed=half * columns * 12, transcendentals=0),
+        functools.partial(attend_kernel, rows, prompt_blocks, paired, shared),
+        out_shape=[shape(bf16, half, columns)] * 3
+        + [shape(bf16, shared, columns)] * 2
+        + [shape(bf16, half, columns), shape(bf16, rows, size * columns), shape(f32, heads, half), shape(f32, 8, half)],
+        in_specs=[VMEM] * 4,
+        out_specs=[VMEM] * 9,
+        scratch_shapes=[
+            pltpu.VMEM((columns, half), bf16),
+            pltpu.VMEM((columns, shared), bf16),
+            pltpu.VMEM((size - 1, 8, half), f32),
+        ]
+        + peers,
+        compiler_params=params(0),
+        cost_estimate=pl.CostEstimate(flops=2 * work, bytes_accessed=120_000_000, transcendentals=0),
     )
     backward = pl.pallas_call(
-        functools.partial(attend_back_kernel, rows, prompt_blocks, paired),
-        out_shape=(wide32,) * 3 + (jax.ShapeDtypeStruct((shared, columns), jnp.bfloat16),) * 2,
-        in_specs=[smem] + [vmem] * 8,
-        out_specs=(vmem,) * 5,
-        scratch_shapes=[pltpu.VMEM((columns, half), jnp.bfloat16), pltpu.VMEM((columns, shared), jnp.bfloat16)]
-        + [pltpu.VMEM((shared, columns), jnp.float32)] * 2,
-        compiler_params=params,
-        cost_estimate=pl.CostEstimate(flops=5 * work, bytes_accessed=half * columns * 40, transcendentals=0),
+        functools.partial(attend_back_kernel, rows, prompt_blocks, paired, shared),
+        out_shape=[shape(bf16, half, 3 * columns), shape(f32, 8, columns)],
+        in_specs=[VMEM] * 13,
+        out_specs=[VMEM] * 2,
+        scratch_shapes=[pltpu.VMEM((half, columns), bf16)]
+        + [pltpu.VMEM((half, columns), f32)] * 3
+        + [pltpu.VMEM((shared, columns), f32)] * 2
+        + [pltpu.VMEM((shared, columns), bf16)] * 4
+        + [
+            pltpu.VMEM((columns, half), bf16),
+            pltpu.VMEM((columns, shared), bf16),
+            pltpu.VMEM((8, half), f32),
+            pltpu.VMEM((size - 1, 8, half), f32),
+        ]
+        + peers,
+        compiler_params=params(1),
+        cost_estimate=pl.CostEstimate(flops=5 * work, bytes_accessed=200_000_000, transcendentals=0),
     )
     return forward, backward
+
+
+def dot(a, b):
+    return jnp.dot(a, b, preferred_element_type=jnp.float32)
+
+
+def dot_nt(a, b):
+    return lax.dot_general(a, b, NT, preferred_element_type=jnp.float32)
+
+
+def dot_tn(a, b):
+    return lax.dot_general(a, b, (((0,), (0,)), ((), ())), preferred_element_type=jnp.float32)
 
 
 MESH_ID = pl.DeviceIdType.MESH
 ANY = pl.BlockSpec(memory_space=pl.ANY)
 VMEM = pl.BlockSpec(memory_space=pltpu.VMEM)
 LINE = 4
+
+
+def lasts(microseconds):
+    return pl.CostEstimate(flops=0, bytes_accessed=microseconds * 3_000_000, transcendentals=0)
 
 
 def position():
@@ -284,6 +515,7 @@
             pltpu.SemaphoreType.DMA((count,)),
         ],
         compiler_params=pltpu.CompilerParams(collective_id=collective_id, has_side_effects=True),
+        cost_estimate=lasts(100),
     )(*arrays)
 
 
@@ -399,6 +631,7 @@
         compiler_params=pltpu.CompilerParams(
             collective_id=collective_id, has_side_effects=True, vmem_limit_bytes=48 * 2**20
         ),
+        cost_estimate=lasts(95),
     )(part)
 
 
@@ -435,6 +668,7 @@
             pltpu.SemaphoreType.DMA((size - 1,)),
         ],
         compiler_params=pltpu.CompilerParams(collective_id=collective_id, has_side_effects=True),
+        cost_estimate=lasts(8),
     )(x)
 
 
@@ -492,6 +726,7 @@
         ]
         + [pltpu.SemaphoreType.DMA((swaps,))] * 4,
         compiler_params=pltpu.CompilerParams(collective_id=collective_id, has_side_effects=True),
+        cost_estimate=lasts(150),
     )(*arrays, *weights)
     return out[:count], out[count:]
 
@@ -548,7 +783,164 @@
         ]
         + [pltpu.SemaphoreType.DMA((size,))] * 4,
         compiler_params=pltpu.CompilerParams(collective_id=collective_id, has_side_effects=True),
+        cost_estimate=lasts(15),
     )(x)
+
+
+def expert_kernel(
+    tiles, capacity, experts, first, id_ref, slot_ref, tokens_ref, grads_ref, router_ref, gate_ref, up_ref, down_ref, *refs
+):
+    if not first:
+        moe_in_ref, part_in_ref, router_in_ref = refs[:3]
+        refs = refs[3:]
+    (
+        moe_ref, part_ref, x_ref, g_ref, inner_ref, grad_gate_ref, grad_up_ref, router_grad_ref,
+        x_all, g_all, picks, moe_all, part_all, probs_all, scores_all, router_sum,
+    ) = refs
+    f32, bf16 = jnp.float32, jnp.bfloat16
+    group, step = pl.program_id(0), pl.program_id(1)
+    blocks = picks.shape[0]
+    expert = id_ref[0]
+    lane = lax.broadcasted_iota(jnp.int32, (1, 128), 1)
+
+    @pl.when(step < blocks)
+    def _():
+        rows = tokens_ref.shape[1]
+        row = lax.broadcasted_iota(jnp.int32, (capacity, rows), 0)
+        pick = jnp.where(row == slot_ref[0], 1.0, 0.0).astype(bf16)
+        picks[step] = pick
+        here = pl.ds(pl.multiple_of(step * capacity, capacity), capacity)
+        x = dot(pick, tokens_ref[0]).astype(bf16)
+        g = dot(pick, grads_ref[0]).astype(bf16)
+        x_all[here], x_ref[...] = x, x
+        g_all[here], g_ref[...] = g, g
+
+    @pl.when(step == blocks)
+    def _():
+        logits = jnp.where(lane < experts, dot(x_all[...], router_ref[...]), NEGATIVE)
+        weight = jnp.exp(logits - jnp.max(logits, -1, keepdims=True))
+        probs_all[...] = weight / jnp.sum(weight, -1, keepdims=True)
+        moe_all[...] = jnp.zeros_like(moe_all)
+        part_all[...] = jnp.zeros_like(part_all)
+        scores_all[...] = jnp.zeros_like(scores_all)
+
+    @pl.when((step >= blocks) & (step < blocks + tiles))
+    def _():
+        x, g = x_all[...], g_all[...]
+        gate = jnp.sum(jnp.where(lane == expert, probs_all[...], 0.0), -1, keepdims=True)
+        gate_pre = dot(x, gate_ref[...])
+        up_pre = dot(x, up_ref[...])
+        back = dot_nt(g, down_ref[...])
+        sigmoid = 1.0 / (1.0 + jnp.exp(-gate_pre))
+        silu = gate_pre * sigmoid
+        inner = silu * up_pre
+        scores_all[...] += jnp.sum(inner * back, -1, keepdims=True)
+        inner_gated = (gate * inner).astype(bf16)
+        back = gate * back
+        grad_gate_pre = (back * up_pre * sigmoid * (1.0 + gate_pre * (1.0 - sigmoid))).astype(bf16)
+        grad_up_pre = (back * silu).astype(bf16)
+        inner_ref[...] = inner_gated
+        grad_gate_ref[...] = grad_gate_pre
+        grad_up_ref[...] = grad_up_pre
+        moe_all[...] += dot(inner_gated, down_ref[...])
+        part_all[...] += dot_nt(grad_gate_pre, gate_ref[...]) + dot_nt(grad_up_pre, up_ref[...])
+
+    @pl.when(step == blocks + tiles)
+    def _():
+        probs = probs_all[...]
+        here = jnp.where(lane == expert, 1.0, 0.0)
+        gate = jnp.sum(probs * here, -1, keepdims=True)
+        mixing = (gate * scores_all[...] * (here - probs)).astype(bf16)
+        part_all[...] += dot_nt(mixing, router_ref[...])
+        grad = dot_tn(mixing, x_all[...])
+
+        @pl.when(group == 0)
+        def _():
+            router_sum[...] = grad if first else grad + router_in_ref[...]
+
+        @pl.when(group > 0)
+        def _():
+            router_sum[...] += grad
+
+        router_grad_ref[...] = router_sum[...]
+
+    @pl.when(step >= blocks + tiles)
+    def _():
+        block = step - blocks - tiles
+        pick = picks[block]
+        here = pl.ds(pl.multiple_of(block * capacity, capacity), capacity)
+        moe = dot_tn(pick, moe_all[here].astype(bf16))
+        part = dot_tn(pick, part_all[here].astype(bf16))
+        if not first:
+            moe = moe + moe_in_ref[0].astype(f32)
+            part = part + part_in_ref[0].astype(f32)
+        moe_ref[0] = moe.astype(bf16)
+        part_ref[0] = part.astype(bf16)
+
+
+def expert_call(expert, slots, tokens, grads, router, weights, capacity, experts, before=None):
+    wide, rows, _ = tokens.shape
+    units = weights[0].shape[1]
+    groups = 2 if wide * capacity > 1024 else 1
+    blocks, tile = wide // groups, 256
+    tiles = units // tile
+    last = blocks + tiles
+    first = before is None
+    bf16, f32 = jnp.bfloat16, jnp.float32
+
+    def picked(g, i):
+        return g * blocks + jnp.minimum(i, blocks - 1)
+
+    def tiled(i):
+        return jnp.clip(i - blocks, 0, tiles - 1)
+
+    def spread(g, i):
+        return g * blocks + jnp.clip(i - last, 0, blocks - 1)
+
+    whole = pl.BlockSpec((1, rows, D), lambda g, i: (picked(g, i), 0, 0))
+    back = pl.BlockSpec((1, rows, D), lambda g, i: (spread(g, i), 0, 0))
+    row = pl.BlockSpec((capacity, D), lambda g, i: (picked(g, i), 0))
+    column = pl.BlockSpec((D, tile), lambda g, i: (0, tiled(i)))
+    unit = pl.BlockSpec((blocks * capacity, tile), lambda g, i: (g, tiled(i)))
+    fixed = pl.BlockSpec((128, D), lambda g, i: (0, 0))
+    in_specs = [
+        pl.BlockSpec(memory_space=pltpu.SMEM),
+        pl.BlockSpec((1, 1, rows), lambda g, i: (picked(g, i), 0, 0)),
+        whole,
+        whole,
+        pl.BlockSpec((D, 128), lambda g, i: (0, 0)),
+        column,
+        column,
+        pl.BlockSpec((tile, D), lambda g, i: (tiled(i), 0)),
+    ] + ([] if first else [back, back, fixed])
+    count = wide * capacity
+    compact = jax.ShapeDtypeStruct((count, D), bf16)
+    narrow = jax.ShapeDtypeStruct((count, units), bf16)
+    held = blocks * capacity
+    return pl.pallas_call(
+        functools.partial(expert_kernel, tiles, capacity, experts, first),
+        grid=(groups, last + blocks),
+        in_specs=in_specs,
+        out_specs=[back, back, row, row, unit, unit, unit, fixed],
+        out_shape=[jax.ShapeDtypeStruct((wide, rows, D), bf16)] * 2
+        + [compact] * 2
+        + [narrow] * 3
+        + [jax.ShapeDtypeStruct((128, D), f32)],
+        scratch_shapes=[
+            pltpu.VMEM((held, D), bf16),
+            pltpu.VMEM((held, D), bf16),
+            pltpu.VMEM((blocks, capacity, rows), bf16),
+            pltpu.VMEM((held, D), f32),
+            pltpu.VMEM((held, D), f32),
+            pltpu.VMEM((held, 128), f32),
+            pltpu.VMEM((held, 1), f32),
+            pltpu.VMEM((128, D), f32),
+        ],
+        compiler_params=pltpu.CompilerParams(vmem_limit_bytes=60 * 2**20),
+        cost_estimate=pl.CostEstimate(
+            flops=12 * count * D * units, bytes_accessed=count * D * 12 + 6 * D * units, transcendentals=0
+        ),
+    )(expert.astype(jnp.int32).reshape(1), slots, tokens, grads, router, *weights, *(before or ()))
 
 
 def positions(token_ids):
@@ -561,29 +953,6 @@
     angle = place.astype(jnp.float32)[:, None] * frequency[None, :]
     cosine, sine = jnp.cos(angle), jnp.sin(angle)
     return jnp.concatenate([cosine, cosine], 1), jnp.concatenate([-sine, sine], 1)
-
-
-def swap_halves(values):
-    return jnp.concatenate([values[..., HD // 2 :], values[..., : HD // 2]], -1)
-
-
-def rotate(values, cosine, sine):
-    rows, columns = values.shape
-    heads = values.reshape(rows, columns // HD, HD)
-    turned = heads * cosine[:, None, :] + swap_halves(heads) * sine[:, None, :]
-    return turned.reshape(rows, columns)
-
-
-def dot(a, b):
-    return jnp.dot(a, b, preferred_element_type=jnp.float32)
-
-
-def dot_nt(a, b):
-    return lax.dot_general(a, b, (((1,), (1,)), ((), ())), preferred_element_type=jnp.float32)
-
-
-def dot_tn(a, b):
-    return lax.dot_general(a, b, (((0,), (0,)), ((), ())), preferred_element_type=jnp.float32)
 
 
 def shards(
@@ -622,8 +991,7 @@
     twins = lax.axis_size("grp") == 2
     prompt_blocks = PROMPT // (rows * narrow_count)
     shared = half if paired else prompt_blocks * rows
-    attend, attend_back = attention_calls(rows, half, shared, columns, prompt_blocks, paired)
-    side_array = side.astype(jnp.int32).reshape(1)
+    attend, attend_back = attention_calls(rows, half, shared, columns, prompt_blocks, paired, (1, 2))
     barrier = lax.optimization_barrier
 
     def exchange(value):
@@ -659,26 +1027,15 @@
 
     joined = jnp.concatenate([w_query, w_key, w_value], 1)
     raw = dot(normed_plane, joined)
-    query_raw, key_raw, value_raw = (raw[:, i * columns : (i + 1) * columns] for i in range(3))
-    sums = sum_wide(
-        jnp.stack([jnp.sum(query_raw * query_raw, -1), jnp.sum(key_raw * key_raw, -1)]), 1
-    )
-    inv_query, inv_key = lax.rsqrt(sums / D + EPSILON)[:, :, None]
-    gain_query = norm_query.astype(f32)
-    gain_key = norm_key.astype(f32)
+    gains = jnp.pad(jnp.stack([norm_query, norm_key]).astype(f32), ((0, 6), (0, 0)))
     plane_ids = (
         (jnp.arange(wide_count, dtype=jnp.int32)[:, None] * narrow_count + side) * rows
         + jnp.arange(rows, dtype=jnp.int32)[None, :]
     ).reshape(half)
     cosine, sine = rotation(positions(plane_ids))
-    value_b = value_raw.astype(bf16)
-    value_other = exchange(value_b[:shared])
-    key_rot = rotate(key_raw * inv_key * gain_key, cosine, sine).astype(bf16)
-    key_other = exchange(key_rot[:shared])
-    query_rot = rotate(query_raw * inv_query * gain_query, cosine, sine).astype(bf16)
-    attended, lse = attend(side_array, query_rot, key_rot, value_b, key_other, value_other)
-
-    attended_own = lax.all_to_all(attended, "wide", split_axis=0, concat_axis=1, tiled=True)
+    kept = attend(raw, gains, cosine, sine)
+    attended, attended_own, lse, sums = kept[5:]
+
     branch = jnp.concatenate(ordered([dot(attended_own, p) for p in out_pieces]), 1)
     hidden = stream + branch
     inv_two = lax.rsqrt(jnp.mean(hidden * hidden, -1, keepdims=True) + EPSILON)
@@ -686,83 +1043,39 @@
     moe_in = (hidden * inv_two * gain_two).astype(bf16)
     moe_plane = lax.all_gather(moe_in, "wide", axis=0, tiled=True)
 
-    kinds = jnp.arange(experts, dtype=jnp.int32)
-    named = jnp.any(routes_plane[:, :, :, None] == kinds, 1).reshape(half, experts)
     earlier = (jnp.arange(rows)[:, None] < jnp.arange(rows)[None, :]).astype(bf16)
-    blocks = lambda a: a.reshape(wide_count, rows, -1)
-
-    def pick(expert):
+
+    def slots_of(expert):
         chosen = jnp.any(routes_plane == expert, 1)
         rank = dot(chosen.astype(bf16), earlier).astype(jnp.int32)
-        slot = jnp.where(chosen, rank, -1)
-        return (jnp.arange(capacity, dtype=jnp.int32)[None, :, None] == slot[:, None, :]).astype(bf16)
-
-    def compact(onehot, values):
-        return jnp.einsum(
-            "wcr,wrd->wcd", onehot, blocks(values), preferred_element_type=f32
-        ).astype(bf16).reshape(wide_count * capacity, -1)
-
-    def spread(onehot, values):
-        return jnp.einsum(
-            "wcr,wcd->wrd", onehot, values.reshape(wide_count, capacity, -1), preferred_element_type=f32
-        ).reshape(half, -1)
-
-    ids = (place * narrow_count + 1 - side, place * narrow_count + side)
-    weights = ((other_gate, other_up, other_down), (w_gate[0], w_up[0], w_down[0]))
-    onehots = [pick(e) for e in ids]
-    grads = [compact(o, grad_plane) for o in onehots]
-    backs = [dot_nt(g, w[2]) for g, w in zip(grads, weights)]
-    probs = jax.nn.softmax(dot(moe_plane, w_router), -1)
-    gates_dense = jnp.where(named, probs, 0.0)
-    inputs = [compact(o, moe_plane) for o in onehots]
-    gates_own = [jnp.take(gates_dense, e, axis=1) for e in ids]
-    gates = [
-        jnp.sum(o.astype(f32) * g.reshape(wide_count, 1, rows), -1).reshape(wide_count * capacity, 1)
-        for o, g in zip(onehots, gates_own)
+        return jnp.where(chosen, rank, -1).reshape(wide_count, 1, rows)
+
+    router = jnp.pad(w_router, ((0, 0), (0, 128 - experts)))
+    tokens_in = moe_plane.reshape(wide_count, rows, D)
+    grads_in = grad_plane.reshape(wide_count, rows, D)
+
+    def run_expert(expert, weights, before):
+        return expert_call(
+            expert, slots_of(expert), tokens_in, grads_in, router, weights, capacity, experts, before
+        )
+
+    own = run_expert(place * narrow_count + side, (w_gate[0], w_up[0], w_down[0]), None)
+    other = run_expert(
+        place * narrow_count + 1 - side, (other_gate, other_up, other_down), (own[0], own[1], own[7])
+    )
+    moe_part, grad_part, grad_router = other[0], other[1], other[7][:experts]
+    inputs, grads, inners_gated = (own[2], other[2]), (own[3], other[3]), (own[4], other[4])
+    grad_pres = ((own[5], own[6]), (other[5], other[6]))
+    moe = lax.psum_scatter(moe_part.reshape(half, D), "wide", scatter_dimension=0, tiled=True).astype(f32)
+    partner_grads = [
+        dot_tn(inputs[1], grad_pres[1][0]).astype(bf16),
+        dot_tn(inputs[1], grad_pres[1][1]).astype(bf16),
+        dot_tn(inners_gated[1], grads[1]).astype(bf16),
     ]
-    gate_pres = [dot(x, w[0]) for x, w in zip(inputs, weights)]
-    up_pres = [dot(x, w[1]) for x, w in zip(inputs, weights)]
-    inners = [g * jax.nn.sigmoid(g) * u for g, u in zip(gate_pres, up_pres)]
-    inners_gated = [(g * i).astype(bf16) for g, i in zip(gates, inners)]
-    moe_part = sum(spread(o, dot(i, w[2]).astype(bf16)) for o, i, w in zip(onehots, inners_gated, weights))
-    moe_part = moe_part.astype(bf16)
-    moe = lax.psum_scatter(moe_part, "wide", scatter_dimension=0, tiled=True).astype(f32)
-
-    _, gate_pres = barrier((moe_part, gate_pres))
-    grad_part = 0.0
-    mixing = 0.0
-    grad_pres = []
-    for k in range(2):
-        gate_pre, up_pre, back, gate = gate_pres[k], up_pres[k], backs[k], gates[k]
-        sigmoid = jax.nn.sigmoid(gate_pre)
-        silu = gate_pre * sigmoid
-        grad_gate_row = jnp.sum(silu * up_pre * back, -1)
-        grad_inner = gate * back
-        grad_gate_pre = (grad_inner * up_pre * sigmoid * (1.0 + gate_pre * (1.0 - sigmoid))).astype(bf16)
-        grad_up_pre = (grad_inner * silu).astype(bf16)
-        grad_pres.append((grad_gate_pre, grad_up_pre))
-        route_in = (dot_nt(grad_gate_pre, weights[k][0]) + dot_nt(grad_up_pre, weights[k][1])).astype(bf16)
-        grad_part = grad_part + spread(onehots[k], route_in)
-        grad_gates = jnp.sum(
-            onehots[k].astype(f32) * grad_gate_row.reshape(wide_count, capacity, 1), 1
-        ).reshape(half, 1)
-        here = (kinds == ids[k]).astype(f32)
-        mixing = mixing + gates_own[k][:, None] * grad_gates * (here[None, :] - probs)
-    mixing = mixing.astype(bf16)
-    grad_part = (grad_part + dot_nt(mixing, w_router)).astype(bf16)
-    grad_router = dot_tn(mixing, moe_plane)
-    partner_grads = [
-        dot_tn(inputs[0], grad_pres[0][0]).astype(bf16),
-        dot_tn(inputs[0], grad_pres[0][1]).astype(bf16),
-        dot_tn(inners_gated[0], grads[0]).astype(bf16),
-    ]
-    came = [exchange(g) for g in partner_grads]
+    came = [exchange(g) for g in partner_grads[:2]]
     grad_part, partner_grads = barrier((grad_part, partner_grads))
-    grad_moe_in = scatter_wide(grad_part.reshape(wide_count, rows, D), 5)
-    grad_moe_in, moe, inputs, grads = barrier((grad_moe_in, moe, inputs, grads))
-    expert_grads = [
-        dot_tn(inputs[1], grad_pres[1][0]), dot_tn(inputs[1], grad_pres[1][1]), dot_tn(inners_gated[1], grads[1])
-    ]
+    grad_moe_in = scatter_wide(grad_part, 5)
+    grad_moe_in, moe, came[0] = barrier((grad_moe_in, moe, came[0]))
 
     grad_gain_two = jnp.sum(grad_moe_in * hidden * inv_two, 0)
     grad_hidden = (
@@ -772,39 +1085,22 @@
     )
     grad_branch = grad_hidden.astype(bf16)
     grad_attended_own = sum(dot_nt(g, p) for g, p in zip(unordered(grad_branch), out_pieces)).astype(bf16)
-    grad_attended = lax.all_to_all(grad_attended_own, "wide", split_axis=1, concat_axis=0, tiled=True)
     branch_plane = lax.all_gather(grad_branch, "wide", axis=0, tiled=True)
-
-    grad_query_rot, grad_key_rot, grad_value, grad_key_other, grad_value_other = attend_back(
-        side_array, query_rot, key_rot, value_b, key_other, value_other, grad_attended, attended, lse
-    )
-
-    def add_shared(own, other):
-        return jnp.concatenate([own[:shared] + other.astype(f32), own[shared:]], 0)
-
-    grad_key_rot = add_shared(grad_key_rot, exchange(grad_key_other))
-    grad_value = add_shared(grad_value, exchange(grad_value_other))
-    grad_query_normed = rotate(grad_query_rot, cosine, -sine)
-    grad_key_normed = rotate(grad_key_rot, cosine, -sine)
-    dots = sum_wide(
-        jnp.stack(
-            [
-                jnp.sum(grad_query_normed * gain_query * query_raw, -1),
-                jnp.sum(grad_key_normed * gain_key * key_raw, -1),
-            ]
-        ),
-        2,
-    )[:, :, None]
-    grad_gain_query = jnp.sum(grad_query_normed * query_raw * inv_query, 0)
-    grad_gain_key = jnp.sum(grad_key_normed * key_raw * inv_key, 0)
-    grad_query_raw = inv_query * gain_query * grad_query_normed - query_raw * inv_query**3 * dots[0] / D
-    grad_key_raw = inv_key * gain_key * grad_key_normed - key_raw * inv_key**3 * dots[1] / D
-    grads_joined = jnp.concatenate([grad_query_raw, grad_key_raw, grad_value], 1).astype(bf16)
+    grad_out = barrier(dot_tn(attended, branch_plane).astype(bf16))
+
+    grads_joined, gain_grads = attend_back(
+        raw, gains, cosine, sine, sums, *kept[:5], grad_attended_own, attended, lse
+    )
+    grads_joined, came[1], down_partner = barrier((grads_joined, came[1], partner_grads[2]))
+    came.append(exchange(down_partner))
     grad_weights = barrier(dot_tn(normed_plane, grads_joined).astype(bf16))
     weights_came = exchange(grad_weights)
     normed_part, _ = barrier((dot_nt(grads_joined, joined).astype(bf16), grad_weights))
     grad_normed = scatter_wide(normed_part.reshape(wide_count, rows, D), 3)
-    grad_out = barrier(dot_tn(attended, branch_plane).astype(bf16))
+    grad_normed, came[2] = barrier((grad_normed, came[2]))
+    expert_grads = [
+        dot_tn(inputs[0], grad_pres[0][0]), dot_tn(inputs[0], grad_pres[0][1]), dot_tn(inners_gated[0], grads[0])
+    ]
     out_came = exchange(grad_out)
     grad_weights = grad_weights.astype(f32) + weights_came.astype(f32)
     grad_out = grad_out.astype(f32) + out_came.astype(f32)
@@ -825,7 +1121,7 @@
 
     stats = jnp.stack([jnp.sum(v * v * mask) for v in (stream, branch, hidden, moe, final)] + [jnp.sum(mask)])
     here = jnp.repeat(jnp.arange(wide_count) == place, columns)
-    spots = [jnp.where(here, jnp.tile(g, wide_count), 0.0) for g in (grad_gain_query, grad_gain_key)]
+    spots = [jnp.where(here, jnp.tile(g, wide_count), 0.0) for g in gain_grads[:2]]
     small = jnp.stack([grad_gain_one, grad_gain_two, *spots, jnp.pad(stats, (0, D - stats.shape[0]))])
     small = jnp.concatenate([grad_router, small, jnp.zeros((-(experts + 5) % 8, D), f32)], 0)
     small = sum_all(small, 4)

time: 1170 us -> 1200 us (1.026)
  Pallas kernels: 417 us -> 778 us
  matrix products: 316 us -> 109 us
  local copies, waits for them, and re-layouts: 78.6 us -> 22.2 us
  waiting for transfers between devices: 236 us -> 198 us
  starting transfers between devices: 22.6 us -> 6.12 us
    pallas_call x4, Pallas kernels: 61.3 us -> 315 us  [the longest x2 147 us: expert_call(): pl.pallas_call(functools.partial(expert_kernel, tiles, capacity, experts,...]
    dot_general x18 -> x3, matrix products: 158 us -> 15 us  [dot_nt(): return lax.dot_general(a, b, NT, preferred_element_type=jnp.float32)]
    pallas_call x2, Pallas kernels: 182 us -> 266 us  [scatter_wide(): pl.pallas_call(scatter_kernel, out_shape=jax.ShapeDtypeStruct((rows, colu...]
    ppermute x9 -> x5, waiting for transfers between devices: 87.7 us -> 23.9 us  [exchange(): return lax.ppermute(value, 'narrow', swap)]
    dot_general x12 -> x5, matrix products: 78 us -> 16.3 us  [dot(): return jnp.dot(a, b, preferred_element_type=jnp.float32)]
    all_gather x1, waiting for transfers between devices: 0.01 us -> 45.4 us  [shards(): grad_plane = lax.all_gather(grad_final_b, 'wide', axis=0, tiled=True)]
    all_to_all x2 -> x0, waiting for transfers between devices: 39.9 us -> none  [the longest x1 39.9 us: shards(): lax.all_to_all(attended, 'wide', split_axis=0, concat_axis=1, tiled=True)]
    broadcast_in_dim x0 -> x3, other arithmetic: none -> 27.3 us  [shards(): (own + other.astype(f32))[None]]
  transfers between devices with their start and end apart: 16 -> 10, of which waited for: 6 -> 4; matrix products, arithmetic and copies ran while one was open for 29% -> 15% of each run, Pallas kernels for 23% -> 40%
where the time goes in v3:
time: 1200 us; the launch traced here: 1190 us
  Pallas kernels  778 us (65%)
  waiting for transfers between devices  198 us (16%)
  matrix products  109 us (9%)
  other arithmetic  61 us (5%)
  local copies, waits for them, and re-layouts  22.2 us (2%)
  between operations  15.5 us (1%)
    pallas_call x2, Pallas kernels, scatter_wide(): pl.pallas_call(scatter_kernel, out_shape=jax.ShapeDtypeStruct((rows, colu...  266 us
    pallas_call x1, Pallas kernels, start_exchange(): pl.pallas_call(functools.partial(start_kernel, count, swaps), out_shape=[...  156 us
    pallas_call x2, Pallas kernels, expert_call(): pl.pallas_call(functools.partial(expert_kernel, tiles, capacity, experts,...  147 us
    all_gather x1, waiting for transfers between devices, shards(): moe_plane = lax.all_gather(moe_in, 'wide', axis=0, tiled=True)  129 us
    pallas_call x1, Pallas kernels, shards(): attend_back(raw, gains, cosine, sine, sums, *kept[:5], grad_attended_own,...  91.8 us
    dot_general x8, matrix products, dot_tn(): lax.dot_general(a, b, (((0,), (0,)), ((), ())), preferred_element_type=jn...  77.9 us
    pallas_call x1, Pallas kernels, shards(): kept = attend(raw, gains, cosine, sine)  76.5 us
    all_gather x1, waiting for transfers between devices, shards(): grad_plane = lax.all_gather(grad_final_b, 'wide', axis=0, tiled=True)  45.4 us
  transfers between devices with their start and end apart: 10, of which 4 were waited for; matrix products, arithmetic and copies ran while one was open for 15% of the time, Pallas kernels for 40%

profile of v3, /device:TPU:0, one launch (start us, length us, event | category | flops | bytes accessed | tf_op | source)
XLA Modules:
  0.0 1190.1 jit_solution(8922173130396258010)
XLA Ops:
  14.3 156.1 %shard_map.271 = (s32[8,8,256]{2,1,0:T(8,128)}, bf16[8,256,2048]{2,1,0:T(8,128)(2,1)}, bf16[8,256,1024]{2,1,0:T(8,128)(2,1)}, bf16[2048,1024]{1,0:T(8,128)(2,1)}...) custom-call(s32[8,256]{1,0:T(8,128)} %bitcast.95, bf16[256,2048]{1,0:T(8,128)(2,1)} %fusion.5.refs_1_, ...), custom_call_target="tpu_custom_call" | custom-call | bytes 450000000 | tf_op jit(solution)/shard_map/pallas_call | solution.py:716
  178.0 8.6 fusion.40.raw_ref
  186.6 76.5 %shard_map.272 = (bf16[2048,256]{1,0:T(8,128)(2,1)}, bf16[2048,256]{1,0:T(8,128)(2,1)}, bf16[2048,256]{1,0:T(8,128)(2,1)}, bf16[1024,256]{1,0:T(8,128)(2,1)}, bf...) custom-call(f32[2048,768]{1,0:T(8,128)} %fusion.40.raw_ref, ...), custom_call_target="tpu_custom_call" | custom-call | flops 4294967296 | bytes 120000000 | tf_op jit(solution)/shard_map/pallas_call | solution.py:1036
  276.9 45.4 %all-gather.6.cloned.1.call-done = bf16[2048,2048]{1,0:T(8,128)(2,1)} async-done(((bf16[256,2048]{1,0:T(8,128)(2,1)}), bf16[2048,2048]{1,0:T(8,128)(2,1)}) %all-gather.6.cloned.1.call-update) | async-done | bytes 8388624 | tf_op jit(solution)/shard_map/all_gather | solution.py:1026
  322.4 128.9 %all-gather.4.cloned.1.call-done = bf16[2048,2048]{1,0:T(8,128)(2,1)} async-done(((bf16[256,2048]{1,0:T(8,128)(2,1)}), bf16[2048,2048]{1,0:T(8,128)(2,1)}) %all-gather.4.cloned.1.call-update) | async-done | bytes 8388624 | tf_op jit(solution)/shard_map/all_gather | solution.py:1044
  451.2 70.5 %shard_map.273 = (bf16[8,256,2048]{2,1,0:T(8,128)(2,1)}, bf16[8,256,2048]{2,1,0:T(8,128)(2,1)}, bf16[1280,2048]{1,0:T(8,128)(2,1)}, bf16[1280,2048]{1,0:T(8,128)...) custom-call(s32[1]{0:T(128)} %bitcast.9.id_ref, ...), custom_call_target="tpu_custom_call" | custom-call | flops 32212254720 | bytes 44040192 | tf_op jit(solution)/shard_map/pallas_call | solution.py:920
  521.7 76.3 %shard_map.274 = (bf16[8,256,2048]{2,1,0:T(8,128)(2,1)}, bf16[8,256,2048]{2,1,0:T(8,128)(2,1)}, bf16[1280,2048]{1,0:T(8,128)(2,1)}, bf16[1280,2048]{1,0:T(8,128)...) custom-call(s32[1]{0:T(128)} %bitcast.6.id_ref, ...), custom_call_target="tpu_custom_call" | custom-call | flops 32212254720 | bytes 44040192 | tf_op jit(solution)/shard_map/pallas_call | solution.py:920
  598.1 10.3 convolution_convert_fusion.3
  610.5 10.3 convolution_convert_fusion.2
  621.4 9.8 convolution_convert_fusion.1
  631.3 156.8 %shard_map.275 = f32[256,2048]{1,0:T(8,128)S(1)} custom-call(bf16[8,256,2048]{2,1,0:T(8,128)(2,1)} %get-tuple-element.77.part_ref), custom_call_target="tpu_custom_call" | custom-call | bytes 285000000 | tf_op jit(solution)/shard_map/pallas_call | solution.py:617
  795.7 10.9 fusion.43
  807.7 10.6 fusion.42
  818.3 8.2 fusion.44
  832.3 91.8 %shard_map.276 = (bf16[2048,768]{1,0:T(8,128)(2,1)}, f32[8,256]{1,0:T(8,128)}) custom-call(f32[2048,768]{1,0:T(8,128)} %fusion.40.raw_ref, f32[8,256]{1,0:T(8,128)} %fusion.34.gains_ref, f32[2048,128]{1,0:T(8,128)} %get-tuple-element.143.cos_ref, f32[2048,128]{1,0:T(8,128)} %get-tuple-element.144.sin_ref, f32[8,2048]{1,0:T(8,128)} %get-tuple-element.81.sums_ref, ...), custom_call_target="tpu_custom_call" | custom-call | flops 10737418240 | bytes 200000000 | tf_op jit(solution)/shard_map/pallas_call | solution.py:1091
  924.2 11.6 convolution_convert_fusion.4
  937.8 9.2 convolution_convert_fusion
  947.0 109.5 %shard_map.277 = f32[256,2048]{1,0:T(8,128)S(1)} custom-call(bf16[8,256,2048]{2,1,0:T(8,128)(2,1)} %bitcast.79), custom_call_target="tpu_custom_call" | custom-call | bytes 285000000 | tf_op jit(solution)/shard_map/pallas_call | solution.py:617
  1057.4 6.9 add_bitcast_fusion.1
  1064.3 10.2 add_bitcast_fusion.2
  1074.5 15.9 %collective-permute-done.4 = bf16[2048,768]{1,0:T(8,128)(2,1)} collective-permute-done((bf16[2048,768]{1,0:T(8,128)(2,1)}, bf16[2048,768]{1,0:T(8,128)(2,1)}, u32[]{:S(2)}, u32[]{:S(2)}) %collective-permute-start.4) | collective-permute-done | bytes 3145760 | tf_op jit(solution)/shard_map/ppermute | solution.py:998
  1104.0 40.4 %shard_map.278 = f32[24,2048]{1,0:T(8,128)} custom-call(f32[24,2048]{1,0:T(8,128)} %concatenate.19.x_ref), custom_call_target="tpu_custom_call" | custom-call | bytes 45000000 | tf_op jit(solution)/shard_map/pallas_call | solution.py:775
  1163.2 10.2 add_bitcast_fusion
  1173.4 8.0 collective-permute-done.5
  (159 shorter events, 81.6 us)
Async XLA Ops:
  7.2 315.1 %all-gather.6.cloned.1.call-start = ((), (), s32[]{:S(2)}) async-start(), calls=%async_computation.2 | async-start | bytes 9437184 | tf_op jit(solution)/shard_map/all_gather | solution.py:1026
  14.2 156.8 %copy-start.28 = (bf16[256]{0:T(256)(128)(2,1)S(1)}, bf16[256]{0:T(256)(128)(2,1)}, u32[]{:S(2)}) copy-start(bf16[256]{0:T(256)(128)(2,1)} %param.25) | copy-start | bytes 1540
  14.2 156.8 %copy-start.29 = (bf16[256]{0:T(256)(128)(2,1)S(1)}, bf16[256]{0:T(256)(128)(2,1)}, u32[]{:S(2)}) copy-start(bf16[256]{0:T(256)(128)(2,1)} %param.26) | copy-start | bytes 1540
  14.2 156.8 %copy-start.24 = (bf16[2048]{0:T(1024)(128)(2,1)S(1)}, bf16[2048]{0:T(1024)(128)(2,1)}, u32[]{:S(2)}) copy-start(bf16[2048]{0:T(1024)(128)(2,1)} %param.27) | copy-start | bytes 12292
  14.3 157.5 %copy-start.12 = (bf16[2048,256]{1,0:T(8,128)(2,1)S(1)}, bf16[2048,256]{1,0:T(8,128)(2,1)}, u32[]{:S(2)}) copy-start(bf16[2048,256]{1,0:T(8,128)(2,1)} %param.20) | copy-start | bytes 3145732
  170.4 280.8 %all-gather.4.cloned.1.call-start = ((), (), s32[]{:S(2)}) async-start(), calls=%async_computation.1 | async-start | bytes 9437184 | tf_op jit(solution)/shard_map/all_gather | solution.py:1044
  170.5 96.6 %collective-permute-start = (bf16[2048,1024]{1,0:T(8,128)(2,1)}, bf16[2048,1024]{1,0:T(8,128)(2,1)}, u32[]{:S(2)}, u32[]{:S(2)}) collective-permute-start(bf16[2048,1024]{1,0:T(8,128)(2,1)} %bitcast.108), channel_id=1, source_target_pairs={{0,16},{16,0},{1,17},{17,1},{2,18},{18,2},{3,19},{19,3},{4,20},{20... | collective-permute-start | bytes 12582920 | tf_op jit(solution)/shard_map/ppermute | solution.py:1015
  274.1 514.0 %reduce-scatter.2.cloned.1.call-start = ((), (), s32[]{:S(2)}) async-start(), calls=%async_computation.3 | async-start | bytes 9437184 | tf_op jit(solution)/shard_map/reduce_scatter | solution.py:1069
  598.0 557.0 %all-gather.8.cloned.1.call-start = ((), (), s32[]{:S(2)}) async-start(), calls=%async_computation.4 | async-start | bytes 9437184 | tf_op jit(solution)/shard_map/all_gather | solution.py:1088
  598.1 11.8 copy-start.25
  608.4 181.4 %collective-permute-start.1 = (bf16[2048,1024]{1,0:T(8,128)(2,1)}, bf16[2048,1024]{1,0:T(8,128)(2,1)}, u32[]{:S(2)}, u32[]{:S(2)}) collective-permute-start(bf16[2048,1024]{1,0:T(8,128)(2,1)} %convolution_convert_fusion.3), channel_id=1, source_target_pairs={{0,1},{1,0},{2,3},{3,2},{4,5},{5,4},{6,7},{7,6},{8,9},{9,8},{10,11... | collective-permute-start | bytes 12582920 | tf_op jit(solution)/shard_map/ppermute | solution.py:998
  620.9 303.3 %collective-permute-start.2 = (bf16[2048,1024]{1,0:T(8,128)(2,1)}, bf16[2048,1024]{1,0:T(8,128)(2,1)}, u32[]{:S(2)}, u32[]{:S(2)}) collective-permute-start(bf16[2048,1024]{1,0:T(8,128)(2,1)} %convolution_convert_fusion.2), channel_id=1, source_target_pairs={{0,1},{1,0},{2,3},{3,2},{4,5},{5,4},{6,7},{7,6},{8,9},{9,8},{10,11... | collective-permute-start | bytes 12582920 | tf_op jit(solution)/shard_map/ppermute | solution.py:998
  795.7 12.0 %copy-start.32 = (bf16[1280,1024]{1,0:T(8,128)(2,1)S(1)}, bf16[1280,1024]{1,0:T(8,128)(2,1)}, u32[]{:S(2)}) copy-start(bf16[1280,1024]{1,0:T(8,128)(2,1)} %get-tuple-element.98) | copy-start | bytes 7864324
  795.7 22.5 %slice-start.2 = ((s8[5242880]{0:T(1024)(128)(4,1)}), s8[4194304]{0:T(1024)(128)(4,1)S(1)}, s32[]{:S(2)}) async-start(s8[5242880]{0:T(1024)(128)(4,1)} %bitcast.111), calls=%async_computation.7 | async-start | bytes 8388608
  806.6 11.6 slice-start.3
  924.1 13.7 %copy-start.16 = (bf16[2048,768]{1,0:T(8,128)(2,1)S(1)}, bf16[2048,768]{1,0:T(8,128)(2,1)}, u32[]{:S(2)}) copy-start(bf16[2048,768]{1,0:T(8,128)(2,1)} %copy-done.15) | copy-start | bytes 9437188
  924.1 13.7 %copy-start.33 = (bf16[2048,768]{1,0:T(8,128)(2,1)S(1)}, bf16[2048,768]{1,0:T(8,128)(2,1)}, u32[]{:S(2)}) copy-start(bf16[2048,768]{1,0:T(8,128)(2,1)} %get-tuple-element.91) | copy-start | bytes 9437188
  924.1 133.2 %slice-start = ((s8[8388608]{0:T(1024)(128)(4,1)}), s8[4194304]{0:T(1024)(128)(4,1)S(1)}, s32[]{:S(2)}) async-start(s8[8388608]{0:T(1024)(128)(4,1)} %bitcast.80), calls=%async_computation.5 | async-start | bytes 8388608
  935.8 121.6 %slice-start.1 = ((s8[8388608]{0:T(1024)(128)(4,1)}), s8[4194304]{0:T(1024)(128)(4,1)S(1)}, s32[]{:S(2)}) async-start(s8[8388608]{0:T(1024)(128)(4,1)} %bitcast.80), calls=%async_computation.6 | async-start | bytes 8388608
  935.8 161.1 %collective-permute-start.3 = (bf16[1024,2048]{1,0:T(8,128)(2,1)}, bf16[1024,2048]{1,0:T(8,128)(2,1)}, u32[]{:S(2)}, u32[]{:S(2)}) collective-permute-start(bf16[1024,2048]{1,0:T(8,128)(2,1)} %convolution_convert_fusion.1), channel_id=1, source_target_pairs={{0,1},{1,0},{2,3},{3,2},{4,5},{5,4},{6,7},{7,6},{8,9},{9,8},{10,11... | collective-permute-start | bytes 12582920 | tf_op jit(solution)/shard_map/ppermute | solution.py:998
  936.2 154.2 %collective-permute-start.4 = (bf16[2048,768]{1,0:T(8,128)(2,1)}, bf16[2048,768]{1,0:T(8,128)(2,1)}, u32[]{:S(2)}, u32[]{:S(2)}) collective-permute-start(bf16[2048,768]{1,0:T(8,128)(2,1)} %convolution_convert_fusion.4), channel_id=1, source_target_pairs={{0,1},{1,0},{2,3},{3,2},{4,5},{5,4},{6,7},{7,6},{8,9},{9,8},{10,11... | collective-permute-start | bytes 9437192 | tf_op jit(solution)/shard_map/ppermute | solution.py:998
  1096.8 54.7 %copy-start.23 = (f32[256]{0:T(256)S(1)}, f32[256]{0:T(256)}, u32[]{:S(2)}) copy-start(f32[256]{0:T(256)} %get-tuple-element.137) | copy-start | bytes 3076
  1161.1 20.3 %collective-permute-start.5 = (bf16[256,2048]{1,0:T(8,128)(2,1)S(1)}, bf16[256,2048]{1,0:T(8,128)(2,1)S(1)}, u32[]{:S(2)}, u32[]{:S(2)}) collective-permute-start(bf16[256,2048]{1,0:T(8,128)(2,1)S(1)} %convolution_convert_fusion.5), channel_id=1, source_target_pairs={{0,1},{1,0},{2,3},{3,2},{4,5},{5,4},{6,7},{7,6},{8,9},{9,8},{10,11... | collective-permute-start | bytes 3145736 | tf_op jit(solution)/shard_map/ppermute | solution.py:998
  1163.2 19.9 %copy-start.1 = (bf16[256,2048]{1,0:T(8,128)(2,1)S(1)}, bf16[256,2048]{1,0:T(8,128)(2,1)}, u32[]{:S(2)}) copy-start(bf16[256,2048]{1,0:T(8,128)(2,1)} %param.23) | copy-start | bytes 3145732
  (24 other events, 103.4 us)
Sparse Core Ops, SparseCore 0:
  170.6 151.7 all-gather.5
  325.1 126.1 all-gather.3
  598.2 188.8 reduce-scatter.1
  795.8 149.5 all-gather.7

commit v4 on v3

--- a/solution.py
+++ b/solution.py
@@ -17,6 +17,308 @@
 EPSILON = 1e-05
 THETA = 10000.0
 NEGATIVE = -1e30
+
+
+MESH_ID = pl.DeviceIdType.MESH
+ANY = pl.BlockSpec(memory_space=pl.ANY)
+VMEM = pl.BlockSpec(memory_space=pltpu.VMEM)
+LINE = 4
+
+
+def lasts(microseconds):
+    return pl.CostEstimate(flops=0, bytes_accessed=microseconds * 3_000_000, transcendentals=0)
+
+
+def position():
+    grp, wide, narrow = (lax.axis_index(a) for a in ("grp", "wide", "narrow"))
+    return grp, wide, narrow, wide // 2, lax.rem(wide, 2)
+
+
+def greet(targets):
+    barrier = pltpu.get_barrier_semaphore()
+    for device, when in targets:
+        def signal(device=device):
+            pl.semaphore_signal(barrier, inc=1, device_id=device, device_id_type=MESH_ID)
+
+        if when is None:
+            signal()
+        else:
+            pl.when(when)(signal)
+    peers = sum(1 if when is None else when.astype(jnp.int32) for _, when in targets)
+    pl.semaphore_wait(barrier, peers)
+
+
+def remote(src, dst, send, recv, device):
+    return pltpu.make_async_remote_copy(
+        src_ref=src, dst_ref=dst, send_sem=send, recv_sem=recv, device_id=device, device_id_type=MESH_ID
+    )
+
+
+def gather_kernel(count, *refs):
+    ins, outs = refs[:count], refs[count : 2 * count]
+    gather_body(count, ins, outs, *refs[2 * count :])
+
+
+class Gather:
+    def __init__(self, ins, outs, send, recv, local):
+        self.ins, self.outs, self.send, self.recv, self.local = ins, outs, send, recv, local
+        grp, wide, narrow, self.line, self.cross = position()
+        self.wide = wide
+        self.across = (grp, self.line * 2 + 1 - self.cross, narrow)
+        self.above = (grp, wide + 2, narrow)
+        self.below = (grp, wide - 2, narrow)
+        self.has_above, self.has_below = self.line < LINE - 1, self.line > 0
+        self.targets = [(self.across, None), (self.above, self.has_above), (self.below, self.has_below)]
+
+    def copy(self, i, source_line, way, device):
+        slot = source_line * 2 + self.cross
+        out = self.outs[i].at[slot]
+        return remote(out, out, self.send.at[i, way, source_line], self.recv.at[i, slot], device)
+
+    def own(self, i, way, device):
+        return remote(
+            self.ins[i], self.outs[i].at[self.wide], self.send.at[i, way, self.line], self.recv.at[i, self.wide], device
+        )
+
+    def mine(self, i):
+        return pltpu.make_async_copy(self.ins[i], self.outs[i].at[self.wide], self.local.at[i])
+
+    def start(self):
+        for i in range(len(self.ins)):
+            pl.when(self.has_above)(self.own(i, 1, self.above).start)
+            pl.when(self.has_below)(self.own(i, 2, self.below).start)
+            self.own(i, 0, self.across).start()
+            self.mine(i).start()
+
+    def forward(self, distance, only=None):
+        for i in range(len(self.ins)) if only is None else (only,):
+            for sign in (-1, 1):
+                source = self.line + sign * distance
+
+                @pl.when((source >= 0) & (source < LINE))
+                def _(i=i, source=source, sign=sign):
+                    self.copy(i, source, 0, self.across).wait_recv()
+                    onward = self.above if sign < 0 else self.below
+
+                    @pl.when(self.has_above if sign < 0 else self.has_below)
+                    def _():
+                        self.copy(i, source, 1 if sign < 0 else 2, onward).start()
+
+                    self.copy(i, source, 0, self.across).start()
+
+    def finish(self):
+        for i in range(len(self.ins)):
+            send, recv, src, out = self.send, self.recv, self.ins[i], self.outs[i]
+            for source in range(LINE):
+                other = source * 2 + 1 - self.cross
+                remote(src, out.at[other], send.at[i, 0, 0], recv.at[i, other], self.across).wait_recv()
+            for source in range(LINE):
+                remote(src, out.at[0], send.at[i, 0, source], recv.at[i, 0], self.across).wait_send()
+
+                @pl.when(self.has_above & (source <= self.line))
+                def _(source=source):
+                    remote(src, out.at[0], send.at[i, 1, source], recv.at[i, 0], self.above).wait_send()
+
+                @pl.when(self.has_below & (source >= self.line))
+                def _(source=source):
+                    remote(src, out.at[0], send.at[i, 2, source], recv.at[i, 0], self.below).wait_send()
+
+            self.mine(i).wait()
+
+
+def gather_sems(count):
+    return [
+        pltpu.SemaphoreType.DMA((count, 3, LINE)),
+        pltpu.SemaphoreType.DMA((count, 2 * LINE)),
+        pltpu.SemaphoreType.DMA((count,)),
+    ]
+
+
+def gather_body(count, ins, outs, send, recv, local, more=(), begin=None, finish=None):
+    gather = Gather(ins, outs, send, recv, local)
+    greet([*gather.targets, *more])
+    gather.start()
+    if begin is not None:
+        begin()
+    for i in range(count):
+        for distance in range(1, LINE):
+            gather.forward(distance, i)
+    gather.finish()
+    if finish is not None:
+        finish()
+
+
+def gather_wide(arrays, collective_id):
+    count = len(arrays)
+    size = lax.axis_size("wide")
+    if size != 2 * LINE:
+        return [lax.all_gather(a, "wide", axis=0) for a in arrays]
+    return pl.pallas_call(
+        functools.partial(gather_kernel, count),
+        out_shape=[jax.ShapeDtypeStruct((size, *a.shape), a.dtype) for a in arrays],
+        in_specs=[ANY] * count,
+        out_specs=[ANY] * count,
+        scratch_shapes=[
+            pltpu.SemaphoreType.DMA((count, 3, LINE)),
+            pltpu.SemaphoreType.DMA((count, size)),
+            pltpu.SemaphoreType.DMA((count,)),
+        ],
+        compiler_params=pltpu.CompilerParams(collective_id=collective_id, has_side_effects=True),
+        cost_estimate=lasts(100),
+    )(*arrays)
+
+
+def scatter_kernel(part_ref, out_ref, held, from_across, from_line, load, send, recv_a, recv_l):
+    grp, wide, narrow, line, cross = position()
+    across = (grp, line * 2 + 1 - cross, narrow)
+    above = (grp, wide + 2, narrow)
+    below = (grp, wide - 2, narrow)
+    has_above, has_below = line < LINE - 1, line > 0
+    f32 = jnp.float32
+    greet([(across, None), (above, has_above), (below, has_below)])
+
+    order = []
+    for distance in range(LINE - 1, 0, -1):
+        for sign in (1, -1):
+            order.append((distance, sign))
+
+    def valid(owner):
+        return (owner >= 0) & (owner < LINE)
+
+    def across_copy(owner):
+        return remote(
+            part_ref.at[owner * 2 + 1 - cross], from_across.at[owner], send.at[0, owner], recv_a.at[owner], across
+        )
+
+    def load_copy(owner):
+        return pltpu.make_async_copy(part_ref.at[owner * 2 + cross], held.at[owner], load.at[owner])
+
+    def line_copy(owner, up):
+        return remote(
+            held.at[owner],
+            from_line.at[0 if up else 1, owner],
+            send.at[1, owner],
+            recv_l.at[0 if up else 1, owner],
+            above if up else below,
+        )
+
+    for distance, sign in order + [(0, 1)]:
+        owner = line + sign * distance
+
+        @pl.when(valid(owner))
+        def _(owner=owner):
+            across_copy(owner).start()
+            load_copy(owner).start()
+
+    for distance, sign in order:
+        owner = line + sign * distance
+
+        @pl.when(valid(owner))
+        def _(owner=owner, sign=sign):
+            load_copy(owner).wait()
+            across_copy(owner).wait_recv()
+            up = sign > 0
+            came = has_below if up else has_above
+            total = held[owner].astype(f32) + from_across[owner].astype(f32)
+
+            @pl.when(came)
+            def _():
+                line_copy(owner, up).wait_recv()
+                held[owner] = (total + from_line[0 if up else 1, owner].astype(f32)).astype(held.dtype)
+
+            @pl.when(jnp.logical_not(came))
+            def _():
+                held[owner] = total.astype(held.dtype)
+
+            line_copy(owner, up).start()
+
+    load_copy(line).wait()
+    across_copy(line).wait_recv()
+    out_ref[...] = held[line].astype(f32) + from_across[line].astype(f32)
+
+    @pl.when(has_below)
+    def _():
+        line_copy(line, True).wait_recv()
+        out_ref[...] += from_line[0, line].astype(f32)
+
+    @pl.when(has_above)
+    def _():
+        line_copy(line, False).wait_recv()
+        out_ref[...] += from_line[1, line].astype(f32)
+
+    for owner in range(LINE):
+        across_copy(owner).wait_send()
+
+        @pl.when(owner > line)
+        def _(owner=owner):
+            line_copy(owner, True).wait_send()
+
+        @pl.when(owner < line)
+        def _(owner=owner):
+            line_copy(owner, False).wait_send()
+
+
+def scatter_wide(part, collective_id):
+    size, rows, columns = part.shape
+    if size != 2 * LINE:
+        return lax.psum_scatter(part, "wide", scatter_dimension=0, tiled=False).astype(jnp.float32)
+    block = (LINE, rows, columns)
+    return pl.pallas_call(
+        scatter_kernel,
+        out_shape=jax.ShapeDtypeStruct((rows, columns), jnp.float32),
+        in_specs=[ANY],
+        out_specs=VMEM,
+        scratch_shapes=[
+            pltpu.VMEM(block, part.dtype),
+            pltpu.VMEM(block, part.dtype),
+            pltpu.VMEM((2, *block), part.dtype),
+            pltpu.SemaphoreType.DMA((LINE,)),
+            pltpu.SemaphoreType.DMA((2, LINE)),
+            pltpu.SemaphoreType.DMA((LINE,)),
+            pltpu.SemaphoreType.DMA((2, LINE)),
+        ],
+        compiler_params=pltpu.CompilerParams(
+            collective_id=collective_id, has_side_effects=True, vmem_limit_bytes=48 * 2**20
+        ),
+        cost_estimate=lasts(95),
+    )(part)
+
+
+def sum_kernel(x_ref, o_ref, held, send, recv):
+    grp, wide, narrow, _, _ = position()
+    size = held.shape[0] + 1
+    others = [(grp, lax.rem(wide + k, size), narrow) for k in range(1, size)]
+    greet([(device, None) for device in others])
+    copies = [
+        remote(x_ref, held.at[k], send.at[k], recv.at[k], device) for k, device in enumerate(others)
+    ]
+    for copy in copies:
+        copy.start()
+    for copy in copies:
+        copy.wait()
+    total = x_ref[...]
+    for k in range(size - 1):
+        total = total + held[k]
+    o_ref[...] = total
+
+
+def sum_wide(x, collective_id):
+    size = lax.axis_size("wide")
+    if size != 2 * LINE:
+        return lax.psum(x, "wide")
+    return pl.pallas_call(
+        sum_kernel,
+        out_shape=jax.ShapeDtypeStruct(x.shape, x.dtype),
+        in_specs=[VMEM],
+        out_specs=VMEM,
+        scratch_shapes=[
+            pltpu.VMEM((size - 1, *x.shape), x.dtype),
+            pltpu.SemaphoreType.DMA((size - 1,)),
+            pltpu.SemaphoreType.DMA((size - 1,)),
+        ],
+        compiler_params=pltpu.CompilerParams(collective_id=collective_id, has_side_effects=True),
+        cost_estimate=lasts(8),
+    )(x)
 
 
 LOG2E = 1.4426950408889634
@@ -79,16 +381,21 @@
 
 
 def attend_kernel(
-    rows, prompt_blocks, paired, shared, raw_ref, gains_ref, cos_ref, sin_ref,
-    q_ref, k_ref, v_ref, ko_ref, vo_ref, o_ref, own_ref, lse_ref, sums_ref,
-    vt_ref, vto_ref, came_ref, sum_send, sum_recv, pair_send, pair_recv, out_send, out_recv,
+    rows, prompt_blocks, paired, shared, carried, raw_ref, gains_ref, cos_ref, sin_ref, *refs
 ):
+    carry_in, refs = refs[:carried], refs[carried:]
+    q_ref, k_ref, v_ref, ko_ref, vo_ref, o_ref, own_ref, lse_ref, sums_ref = refs[:9]
+    carry_out, refs = refs[9 : 9 + carried], refs[9 + carried :]
+    vt_ref, vto_ref, came_ref, sum_send, sum_recv, pair_send, pair_recv, out_send, out_recv = refs[:9]
+    gather = Gather(carry_in, carry_out, *refs[9:]) if carried else None
     half, columns = q_ref.shape
     size = half // rows
     heads = columns // HD
     grp, wide, narrow = (lax.axis_index(a) for a in ("grp", "wide", "narrow"))
     partner = (grp, wide, 1 - narrow)
     greet([((grp, lax.rem(wide + k, size), narrow), None) for k in range(1, size)] + [(partner, None)])
+    if carried:
+        gather.start()
     pairs = [
         remote(src.at[pl.ds(0, shared)], dst, pair_send.at[i], pair_recv.at[i], partner)
         for i, (src, dst) in enumerate(((k_ref, ko_ref), (v_ref, vo_ref)))
@@ -140,6 +447,8 @@
         hs = slice(h * HD, (h + 1) * HD)
         vto_ref[hs, :] = vo_ref[:, hs].T
     pairs[0].wait()
+    if carried:
+        gather.forward(1)
 
     def mine():
         return pl.ds(pl.multiple_of(wide * columns, columns), columns)
@@ -184,6 +493,9 @@
 
     one.rows = rows
     for_blocks(size, prompt_blocks, one)
+    if carried:
+        for distance in range(2, LINE):
+            gather.forward(distance)
     own_ref[:, mine()] = o_ref[pl.ds(pl.multiple_of(wide * rows, rows), rows)]
 
     def finish(w, carry):
@@ -197,6 +509,8 @@
         return carry
 
     lax.fori_loop(0, size, finish, 0)
+    if carried:
+        gather.finish()
 
 
 def attend_back_kernel(
@@ -349,22 +663,31 @@
     def params(k):
         return pltpu.CompilerParams(vmem_limit_bytes=60 * 2**20, collective_id=ids[k], has_side_effects=True)
 
-    forward = pl.pallas_call(
-        functools.partial(attend_kernel, rows, prompt_blocks, paired, shared),
+    carried = 1 if size == 2 * LINE else 0
+    forward_call = pl.pallas_call(
+        functools.partial(attend_kernel, rows, prompt_blocks, paired, shared, carried),
         out_shape=[shape(bf16, half, columns)] * 3
         + [shape(bf16, shared, columns)] * 2
-        + [shape(bf16, half, columns), shape(bf16, rows, size * columns), shape(f32, heads, half), shape(f32, 8, half)],
-        in_specs=[VMEM] * 4,
-        out_specs=[VMEM] * 9,
+        + [shape(bf16, half, columns), shape(bf16, rows, size * columns), shape(f32, heads, half), shape(f32, 8, half)]
+        + [shape(bf16, size, rows, D)] * carried,
+        in_specs=[VMEM] * 4 + [ANY] * carried,
+        out_specs=[VMEM] * 9 + [ANY] * carried,
         scratch_shapes=[
             pltpu.VMEM((columns, half), bf16),
             pltpu.VMEM((columns, shared), bf16),
             pltpu.VMEM((size - 1, 8, half), f32),
         ]
-        + peers,
+        + peers
+        + gather_sems(carried) * carried,
         compiler_params=params(0),
         cost_estimate=pl.CostEstimate(flops=2 * work, bytes_accessed=120_000_000, transcendentals=0),
     )
+
+    def forward(raw, gains, cosine, sine, carry):
+        if carried:
+            return forward_call(raw, gains, cosine, sine, carry)
+        return [*forward_call(raw, gains, cosine, sine), lax.all_gather(carry, "wide", axis=0)]
+
     backward = pl.pallas_call(
         functools.partial(attend_back_kernel, rows, prompt_blocks, paired, shared),
         out_shape=[shape(bf16, half, 3 * columns), shape(f32, 8, columns)],
@@ -397,279 +720,6 @@
 
 def dot_tn(a, b):
     return lax.dot_general(a, b, (((0,), (0,)), ((), ())), preferred_element_type=jnp.float32)
-
-
-MESH_ID = pl.DeviceIdType.MESH
-ANY = pl.BlockSpec(memory_space=pl.ANY)
-VMEM = pl.BlockSpec(memory_space=pltpu.VMEM)
-LINE = 4
-
-
-def lasts(microseconds):
-    return pl.CostEstimate(flops=0, bytes_accessed=microseconds * 3_000_000, transcendentals=0)
-
-
-def position():
-    grp, wide, narrow = (lax.axis_index(a) for a in ("grp", "wide", "narrow"))
-    return grp, wide, narrow, wide // 2, lax.rem(wide, 2)
-
-
-def greet(targets):
-    barrier = pltpu.get_barrier_semaphore()
-    for device, when in targets:
-        def signal(device=device):
-            pl.semaphore_signal(barrier, inc=1, device_id=device, device_id_type=MESH_ID)
-
-        if when is None:
-            signal()
-        else:
-            pl.when(when)(signal)
-    peers = sum(1 if when is None else when.astype(jnp.int32) for _, when in targets)
-    pl.semaphore_wait(barrier, peers)
-
-
-def remote(src, dst, send, recv, device):
-    return pltpu.make_async_remote_copy(
-        src_ref=src, dst_ref=dst, send_sem=send, recv_sem=recv, device_id=device, device_id_type=MESH_ID
-    )
-
-
-def gather_kernel(count, *refs):
-    ins, outs = refs[:count], refs[count : 2 * count]
-    gather_body(count, ins, outs, *refs[2 * count :])
-
-
-def gather_body(count, ins, outs, send, recv, local, more=(), begin=None, finish=None):
-    grp, wide, narrow, line, cross = position()
-    across = (grp, line * 2 + 1 - cross, narrow)
-    above = (grp, wide + 2, narrow)
-    below = (grp, wide - 2, narrow)
-    has_above, has_below = line < LINE - 1, line > 0
-    greet([(across, None), (above, has_above), (below, has_below), *more])
-
-    def copy(i, source_line, way, device):
-        slot = source_line * 2 + cross
-        return remote(outs[i].at[slot], outs[i].at[slot], send.at[i, way, source_line], recv.at[i, slot], device)
-
-    def own(i, way, device):
-        return remote(ins[i], outs[i].at[wide], send.at[i, way, line], recv.at[i, wide], device)
-
-    mine = [pltpu.make_async_copy(ins[i], outs[i].at[wide], local.at[i]) for i in range(count)]
-    for i in range(count):
-        pl.when(has_above)(own(i, 1, above).start)
-        pl.when(has_below)(own(i, 2, below).start)
-        own(i, 0, across).start()
-        mine[i].start()
-    if begin is not None:
-        begin()
-    for i in range(count):
-        for distance in range(1, LINE):
-            for sign in (-1, 1):
-                source = line + sign * distance
-
-                @pl.when((source >= 0) & (source < LINE))
-                def _(i=i, source=source, sign=sign):
-                    slot = source * 2 + cross
-                    copy(i, source, 0, across).wait_recv()
-                    onward = above if sign < 0 else below
-
-                    @pl.when(has_above if sign < 0 else has_below)
-                    def _():
-                        copy(i, source, 1 if sign < 0 else 2, onward).start()
-
-                    copy(i, source, 0, across).start()
-
-    for i in range(count):
-        for source in range(LINE):
-            other = source * 2 + 1 - cross
-            remote(ins[i], outs[i].at[other], send.at[i, 0, 0], recv.at[i, other], across).wait_recv()
-        for source in range(LINE):
-            remote(ins[i], outs[i].at[0], send.at[i, 0, source], recv.at[i, 0], across).wait_send()
-
-            @pl.when(has_above & (source <= line))
-            def _(i=i, source=source):
-                remote(ins[i], outs[i].at[0], send.at[i, 1, source], recv.at[i, 0], above).wait_send()
-
-            @pl.when(has_below & (source >= line))
-            def _(i=i, source=source):
-                remote(ins[i], outs[i].at[0], send.at[i, 2, source], recv.at[i, 0], below).wait_send()
-
-        mine[i].wait()
-    if finish is not None:
-        finish()
-
-
-def gather_wide(arrays, collective_id):
-    count = len(arrays)
-    size = lax.axis_size("wide")
-    if size != 2 * LINE:
-        return [lax.all_gather(a, "wide", axis=0) for a in arrays]
-    return pl.pallas_call(
-        functools.partial(gather_kernel, count),
-        out_shape=[jax.ShapeDtypeStruct((size, *a.shape), a.dtype) for a in arrays],
-        in_specs=[ANY] * count,
-        out_specs=[ANY] * count,
-        scratch_shapes=[
-            pltpu.SemaphoreType.DMA((count, 3, LINE)),
-            pltpu.SemaphoreType.DMA((count, size)),
-            pltpu.SemaphoreType.DMA((count,)),
-        ],
-        compiler_params=pltpu.CompilerParams(collective_id=collective_id, has_side_effects=True),
-        cost_estimate=lasts(100),
-    )(*arrays)
-
-
-def scatter_kernel(part_ref, out_ref, held, from_across, from_line, load, send, recv_a, recv_l):
-    grp, wide, narrow, line, cross = position()
-    across = (grp, line * 2 + 1 - cross, narrow)
-    above = (grp, wide + 2, narrow)
-    below = (grp, wide - 2, narrow)
-    has_above, has_below = line < LINE - 1, line > 0
-    f32 = jnp.float32
-    greet([(across, None), (above, has_above), (below, has_below)])
-
-    order = []
-    for distance in range(LINE - 1, 0, -1):
-        for sign in (1, -1):
-            order.append((distance, sign))
-
-    def valid(owner):
-        return (owner >= 0) & (owner < LINE)
-
-    def across_copy(owner):
-        return remote(
-            part_ref.at[owner * 2 + 1 - cross], from_across.at[owner], send.at[0, owner], recv_a.at[owner], across
-        )
-
-    def load_copy(owner):
-        return pltpu.make_async_copy(part_ref.at[owner * 2 + cross], held.at[owner], load.at[owner])
-
-    def line_copy(owner, up):
-        return remote(
-            held.at[owner],
-            from_line.at[0 if up else 1, owner],
-            send.at[1, owner],
-            recv_l.at[0 if up else 1, owner],
-            above if up else below,
-        )
-
-    for distance, sign in order + [(0, 1)]:
-        owner = line + sign * distance
-
-        @pl.when(valid(owner))
-        def _(owner=owner):
-            across_copy(owner).start()
-            load_copy(owner).start()
-
-    for distance, sign in order:
-        owner = line + sign * distance
-
-        @pl.when(valid(owner))
-        def _(owner=owner, sign=sign):
-            load_copy(owner).wait()
-            across_copy(owner).wait_recv()
-            up = sign > 0
-            came = has_below if up else has_above
-            total = held[owner].astype(f32) + from_across[owner].astype(f32)
-
-            @pl.when(came)
-            def _():
-                line_copy(owner, up).wait_recv()
-                held[owner] = (total + from_line[0 if up else 1, owner].astype(f32)).astype(held.dtype)
-
-            @pl.when(jnp.logical_not(came))
-            def _():
-                held[owner] = total.astype(held.dtype)
-
-            line_copy(owner, up).start()
-
-    load_copy(line).wait()
-    across_copy(line).wait_recv()
-    out_ref[...] = held[line].astype(f32) + from_across[line].astype(f32)
-
-    @pl.when(has_below)
-    def _():
-        line_copy(line, True).wait_recv()
-        out_ref[...] += from_line[0, line].astype(f32)
-
-    @pl.when(has_above)
-    def _():
-        line_copy(line, False).wait_recv()
-        out_ref[...] += from_line[1, line].astype(f32)
-
-    for owner in range(LINE):
-        across_copy(owner).wait_send()
-
-        @pl.when(owner > line)
-        def _(owner=owner):
-            line_copy(owner, True).wait_send()
-
-        @pl.when(owner < line)
-        def _(owner=owner):
-            line_copy(owner, False).wait_send()
-
-
-def scatter_wide(part, collective_id):
-    size, rows, columns = part.shape
-    if size != 2 * LINE:
-        return lax.psum_scatter(part, "wide", scatter_dimension=0, tiled=False).astype(jnp.float32)
-    block = (LINE, rows, columns)
-    return pl.pallas_call(
-        scatter_kernel,
-        out_shape=jax.ShapeDtypeStruct((rows, columns), jnp.float32),
-        in_specs=[ANY],
-        out_specs=VMEM,
-        scratch_shapes=[
-            pltpu.VMEM(block, part.dtype),
-            pltpu.VMEM(block, part.dtype),
-            pltpu.VMEM((2, *block), part.dtype),
-            pltpu.SemaphoreType.DMA((LINE,)),
-            pltpu.SemaphoreType.DMA((2, LINE)),
-            pltpu.SemaphoreType.DMA((LINE,)),
-            pltpu.SemaphoreType.DMA((2, LINE)),
-        ],
-        compiler_params=pltpu.CompilerParams(
-            collective_id=collective_id, has_side_effects=True, vmem_limit_bytes=48 * 2**20
-        ),
-        cost_estimate=lasts(95),
-    )(part)
-
-
-def sum_kernel(x_ref, o_ref, held, send, recv):
-    grp, wide, narrow, _, _ = position()
-    size = held.shape[0] + 1
-    others = [(grp, lax.rem(wide + k, size), narrow) for k in range(1, size)]
-    greet([(device, None) for device in others])
-    copies = [
-        remote(x_ref, held.at[k], send.at[k], recv.at[k], device) for k, device in enumerate(others)
-    ]
-    for copy in copies:
-        copy.start()
-    for copy in copies:
-        copy.wait()
-    total = x_ref[...]
-    for k in range(size - 1):
-        total = total + held[k]
-    o_ref[...] = total
-
-
-def sum_wide(x, collective_id):
-    size = lax.axis_size("wide")
-    if size != 2 * LINE:
-        return lax.psum(x, "wide")
-    return pl.pallas_call(
-        sum_kernel,
-        out_shape=jax.ShapeDtypeStruct(x.shape, x.dtype),
-        in_specs=[VMEM],
-        out_specs=VMEM,
-        scratch_shapes=[
-            pltpu.VMEM((size - 1, *x.shape), x.dtype),
-            pltpu.SemaphoreType.DMA((size - 1,)),
-            pltpu.SemaphoreType.DMA((size - 1,)),
-        ],
-        compiler_params=pltpu.CompilerParams(collective_id=collective_id, has_side_effects=True),
-        cost_estimate=lasts(8),
-    )(x)
 
 
 def start_kernel(count, swaps, *refs):
@@ -731,60 +781,187 @@
     return out[:count], out[count:]
 
 
-def sum_all_kernel(x_ref, o_ref, parts, total, send, recv, send_back, recv_back):
-    grp, wide, narrow, _, _ = position()
-    size, _, width = parts.shape
-    me = wide * 2 + narrow
-    ranks = [lax.rem(me + k, size) for k in range(size)]
-    devices = [(grp, rank // 2, lax.rem(rank, 2)) for rank in ranks]
-    greet([(device, None) for device in devices[1:]])
-
-    def columns(rank):
-        return pl.ds(pl.multiple_of(rank * width, width), width)
-
-    out = [
-        remote(x_ref.at[:, columns(ranks[k])], parts.at[k], send.at[k], recv.at[k], devices[k])
-        for k in range(1, size)
-    ]
-    for copy in out:
-        copy.start()
-    total[...] = x_ref[:, columns(me)]
-    for k, copy in enumerate(out):
-        copy.wait()
-        total[...] += parts[k + 1]
-    back = [
-        remote(total, o_ref.at[:, columns(me)], send_back.at[k], recv_back.at[k], devices[k])
-        for k in range(1, size)
-    ]
-    for copy in back:
-        copy.start()
-    o_ref[:, columns(me)] = total[...]
-    for copy in back:
-        copy.wait_send()
-    for k in range(1, size):
-        rank = lax.rem(me - k + size, size)
-        remote(total, o_ref.at[:, columns(rank)], send_back.at[k], recv_back.at[k], devices[k]).wait_recv()
-
-
-def sum_all(x, collective_id):
-    size = lax.axis_size("wide") * lax.axis_size("narrow")
-    rows, columns = x.shape
-    if size != 4 * LINE:
-        return lax.psum(x, ("wide", "narrow"))
-    width = columns // size
+class SmallSum:
+    def __init__(self, x_ref, o_ref, parts, total, send, recv, send_back, recv_back):
+        self.refs = x_ref, o_ref, parts, total, send, recv, send_back, recv_back
+        grp, wide, narrow, _, _ = position()
+        self.size, _, self.width = parts.shape
+        self.me = wide * 2 + narrow
+        self.ranks = [lax.rem(self.me + k, self.size) for k in range(self.size)]
+        self.devices = [(grp, rank // 2, lax.rem(rank, 2)) for rank in self.ranks]
+        self.targets = [(device, None) for device in self.devices[1:]]
+
+    def columns(self, rank):
+        return pl.ds(pl.multiple_of(rank * self.width, self.width), self.width)
+
+    def run(self):
+        x_ref, o_ref, parts, total, send, recv, send_back, recv_back = self.refs
+        devices, size, mine = self.devices, self.size, self.columns(self.me)
+        out = [
+            remote(x_ref.at[:, self.columns(self.ranks[k])], parts.at[k], send.at[k], recv.at[k], devices[k])
+            for k in range(1, size)
+        ]
+        for copy in out:
+            copy.start()
+        total[...] = x_ref[:, mine]
+        for k, copy in enumerate(out):
+            copy.wait()
+            total[...] += parts[k + 1]
+        back = [
+            remote(total, o_ref.at[:, mine], send_back.at[k], recv_back.at[k], devices[k]) for k in range(1, size)
+        ]
+        for copy in back:
+            copy.start()
+        o_ref[:, mine] = total[...]
+        for copy in back:
+            copy.wait_send()
+        for k in range(1, size):
+            rank = lax.rem(self.me - k + size, size)
+            remote(total, o_ref.at[:, self.columns(rank)], send_back.at[k], recv_back.at[k], devices[k]).wait_recv()
+
+
+def input_grad_kernel(
+    gain_row, joined_ref, weights_ref, tokens_ref, hidden_ref, gain_ref, small_ref, out_ref, sums_ref,
+    held, from_across, from_line, x_ref, parts, total_ref, send, recv_a, recv_l, *small_sems
+):
+    rows = tokens_ref.shape[0]
+    f32 = jnp.float32
+    small = SmallSum(x_ref, sums_ref, parts, total_ref, *small_sems)
+    grp, wide, narrow, line, cross = position()
+    across = (grp, line * 2 + 1 - cross, narrow)
+    above = (grp, wide + 2, narrow)
+    below = (grp, wide - 2, narrow)
+    has_above, has_below = line < LINE - 1, line > 0
+    greet(small.targets)
+    order = [(distance, sign) for distance in range(LINE - 1, 0, -1) for sign in (1, -1)] + [(0, 1)]
+
+    def valid(owner):
+        return (owner >= 0) & (owner < LINE)
+
+    def part(owner, column):
+        at = pl.ds(pl.multiple_of((owner * 2 + column) * rows, rows), rows)
+        return dot_nt(joined_ref[at], weights_ref[...])
+
+    def across_copy(owner):
+        return remote(held.at[0, owner], from_across.at[owner], send.at[0, owner], recv_a.at[owner], across)
+
+    def line_copy(owner, up):
+        slot = 0 if up else 1
+        return remote(
+            held.at[1, owner], from_line.at[slot, owner], send.at[1, owner], recv_l.at[slot, owner], above if up else below
+        )
+
+    for distance, sign in order:
+        owner = line + sign * distance
+
+        @pl.when(valid(owner))
+        def _(owner=owner):
+            held[0, owner] = part(owner, 1 - cross).astype(held.dtype)
+            across_copy(owner).start()
+
+    for distance, sign in order[:-1]:
+        owner = line + sign * distance
+
+        @pl.when(valid(owner))
+        def _(owner=owner, sign=sign):
+            up = sign > 0
+            came = has_below if up else has_above
+            total = part(owner, cross)
+            across_copy(owner).wait_recv()
+            total = total + from_across[owner].astype(f32)
+
+            @pl.when(came)
+            def _():
+                line_copy(owner, up).wait_recv()
+                held[1, owner] = (total + from_line[0 if up else 1, owner].astype(f32)).astype(held.dtype)
+
+            @pl.when(jnp.logical_not(came))
+            def _():
+                held[1, owner] = total.astype(held.dtype)
+
+            line_copy(owner, up).start()
+
+    out_ref[...] = part(line, cross)
+    across_copy(line).wait_recv()
+    out_ref[...] += from_across[line].astype(f32)
+
+    @pl.when(has_below)
+    def _():
+        line_copy(line, True).wait_recv()
+        out_ref[...] += from_line[0, line].astype(f32)
+
+    @pl.when(has_above)
+    def _():
+        line_copy(line, False).wait_recv()
+        out_ref[...] += from_line[1, line].astype(f32)
+
+    x_ref[...] = small_ref[...]
+    x_ref[gain_row : gain_row + 1, :] = jnp.zeros((1, D), f32)
+    chunk = min(rows, 64)
+
+    def finish(i, carry):
+        at = pl.ds(pl.multiple_of(i * chunk, chunk), chunk)
+        grad = out_ref[at]
+        stream = tokens_ref[at].astype(f32)
+        inverse = lax.rsqrt(jnp.mean(stream * stream, -1, keepdims=True) + EPSILON)
+        product = grad * stream
+        x_ref[gain_row : gain_row + 1, :] += jnp.sum(product * inverse, 0, keepdims=True)
+        slope = inverse * inverse * inverse * jnp.sum(product * gain_ref[...], -1, keepdims=True) / D
+        out_ref[at] = hidden_ref[at] + inverse * gain_ref[...] * grad - stream * slope
+        return carry
+
+    lax.fori_loop(0, rows // chunk, finish, 0)
+    small.run()
+
+    for owner in range(LINE):
+        across_copy(owner).wait_send()
+
+        @pl.when(owner > line)
+        def _(owner=owner):
+            line_copy(owner, True).wait_send()
+
+        @pl.when(owner < line)
+        def _(owner=owner):
+            line_copy(owner, False).wait_send()
+
+
+def input_grad(joined, weights, tokens, grad_hidden, gain, small, gain_row, ids):
+    size = lax.axis_size("wide")
+    rows = tokens.shape[0]
+    f32, bf16 = jnp.float32, jnp.bfloat16
+    if size != 2 * LINE:
+        part = dot_nt(joined, weights).astype(bf16).reshape(size, rows, D)
+        grad = lax.psum_scatter(part, "wide", scatter_dimension=0, tiled=False).astype(f32)
+        stream = tokens.astype(f32)
+        inverse = lax.rsqrt(jnp.mean(stream * stream, -1, keepdims=True) + EPSILON)
+        small = small.at[gain_row].set(jnp.sum(grad * stream * inverse, 0))
+        slope = inverse**3 * jnp.sum(grad * gain * stream, -1, keepdims=True) / D
+        return grad_hidden + inverse * gain * grad - stream * slope, lax.psum(small, ("wide", "narrow"))
+    devices = 4 * LINE
+    block = (LINE, rows, D)
+    dma = pltpu.SemaphoreType.DMA
     return pl.pallas_call(
-        sum_all_kernel,
-        out_shape=jax.ShapeDtypeStruct(x.shape, x.dtype),
-        in_specs=[VMEM],
-        out_specs=VMEM,
+        functools.partial(input_grad_kernel, gain_row),
+        out_shape=[jax.ShapeDtypeStruct((rows, D), f32), jax.ShapeDtypeStruct(small.shape, f32)],
+        in_specs=[VMEM] * 6,
+        out_specs=[VMEM] * 2,
         scratch_shapes=[
-            pltpu.VMEM((size, rows, width), x.dtype),
-            pltpu.VMEM((rows, width), x.dtype),
+            pltpu.VMEM((2, *block), bf16),
+            pltpu.VMEM(block, bf16),
+            pltpu.VMEM((2, *block), bf16),
+            pltpu.VMEM(small.shape, f32),
+            pltpu.VMEM((devices, small.shape[0], D // devices), f32),
+            pltpu.VMEM((small.shape[0], D // devices), f32),
+            dma((2, LINE)),
+            dma((LINE,)),
+            dma((2, LINE)),
         ]
-        + [pltpu.SemaphoreType.DMA((size,))] * 4,
-        compiler_params=pltpu.CompilerParams(collective_id=collective_id, has_side_effects=True),
-        cost_estimate=lasts(15),
-    )(x)
+        + [dma((devices,))] * 4,
+        compiler_params=pltpu.CompilerParams(
+            collective_id=ids, has_side_effects=True, vmem_limit_bytes=56 * 2**20
+        ),
+        cost_estimate=lasts(110),
+    )(joined, weights, tokens, grad_hidden, gain, small)
 
 
 def expert_kernel(
@@ -1022,9 +1199,6 @@
     def unordered(whole):
         return ordered([whole[:, k * piece_width : (k + 1) * piece_width] for k in range(pieces)])
 
-    grad_final_b, _ = barrier((grad_final.astype(bf16), normed_plane))
-    grad_plane = lax.all_gather(grad_final_b, "wide", axis=0, tiled=True)
-
     joined = jnp.concatenate([w_query, w_key, w_value], 1)
     raw = dot(normed_plane, joined)
     gains = jnp.pad(jnp.stack([norm_query, norm_key]).astype(f32), ((0, 6), (0, 0)))
@@ -1033,15 +1207,15 @@
         + jnp.arange(rows, dtype=jnp.int32)[None, :]
     ).reshape(half)
     cosine, sine = rotation(positions(plane_ids))
-    kept = attend(raw, gains, cosine, sine)
-    attended, attended_own, lse, sums = kept[5:]
+    kept = attend(raw, gains, cosine, sine, grad_final.astype(bf16))
+    attended, attended_own, lse, sums, grads_in = kept[5:]
 
     branch = jnp.concatenate(ordered([dot(attended_own, p) for p in out_pieces]), 1)
     hidden = stream + branch
     inv_two = lax.rsqrt(jnp.mean(hidden * hidden, -1, keepdims=True) + EPSILON)
     gain_two = norm_moe.astype(f32)
     moe_in = (hidden * inv_two * gain_two).astype(bf16)
-    moe_plane = lax.all_gather(moe_in, "wide", axis=0, tiled=True)
+    (tokens_in,) = gather_wide([moe_in], 6)
 
     earlier = (jnp.arange(rows)[:, None] < jnp.arange(rows)[None, :]).astype(bf16)
 
@@ -1051,8 +1225,6 @@
         return jnp.where(chosen, rank, -1).reshape(wide_count, 1, rows)
 
     router = jnp.pad(w_router, ((0, 0), (0, 128 - experts)))
-    tokens_in = moe_plane.reshape(wide_count, rows, D)
-    grads_in = grad_plane.reshape(wide_count, rows, D)
 
     def run_expert(expert, weights, before):
         return expert_call(
@@ -1095,23 +1267,25 @@
     came.append(exchange(down_partner))
     grad_weights = barrier(dot_tn(normed_plane, grads_joined).astype(bf16))
     weights_came = exchange(grad_weights)
-    normed_part, _ = barrier((dot_nt(grads_joined, joined).astype(bf16), grad_weights))
-    grad_normed = scatter_wide(normed_part.reshape(wide_count, rows, D), 3)
-    grad_normed, came[2] = barrier((grad_normed, came[2]))
+    out_came = exchange(grad_out)
+    stats = jnp.stack([jnp.sum(v * v * mask) for v in (stream, branch, hidden, moe, hidden + moe)] + [jnp.sum(mask)])
+    here = jnp.repeat(jnp.arange(wide_count) == place, columns)
+    spots = [jnp.where(here, jnp.tile(g, wide_count), 0.0) for g in gain_grads[:2]]
+    zeros = jnp.zeros((D,), f32)
+    small = jnp.stack([zeros, grad_gain_two, *spots, jnp.pad(stats, (0, D - stats.shape[0]))])
+    small = jnp.concatenate([grad_router, small, jnp.zeros((-(experts + 5) % 8, D), f32)], 0)
+    small, _ = barrier((small, grad_weights))
+    grad_input, small = input_grad(
+        grads_joined, joined, tokens, grad_hidden, gain_one.reshape(1, D), small, experts, 3
+    )
+    grad_input, came[2] = barrier((grad_input, came[2]))
     expert_grads = [
         dot_tn(inputs[0], grad_pres[0][0]), dot_tn(inputs[0], grad_pres[0][1]), dot_tn(inners_gated[0], grads[0])
     ]
-    out_came = exchange(grad_out)
     grad_weights = grad_weights.astype(f32) + weights_came.astype(f32)
     grad_out = grad_out.astype(f32) + out_came.astype(f32)
     grad_query_w, grad_key_w, grad_value_w = (
         grad_weights[:, i * columns : (i + 1) * columns] for i in range(3)
-    )
-    grad_gain_one = jnp.sum(grad_normed * stream * inv_one, 0)
-    grad_input = (
-        grad_hidden
-        + inv_one * gain_one * grad_normed
-        - stream * inv_one**3 * jnp.sum(grad_normed * gain_one * stream, -1, keepdims=True) / D
     )
     final = hidden + moe
     output = final.astype(bf16)
@@ -1119,12 +1293,6 @@
         (own + other.astype(f32))[None] for own, other in zip(expert_grads, came)
     )
 
-    stats = jnp.stack([jnp.sum(v * v * mask) for v in (stream, branch, hidden, moe, final)] + [jnp.sum(mask)])
-    here = jnp.repeat(jnp.arange(wide_count) == place, columns)
-    spots = [jnp.where(here, jnp.tile(g, wide_count), 0.0) for g in gain_grads[:2]]
-    small = jnp.stack([grad_gain_one, grad_gain_two, *spots, jnp.pad(stats, (0, D - stats.shape[0]))])
-    small = jnp.concatenate([grad_router, small, jnp.zeros((-(experts + 5) % 8, D), f32)], 0)
-    small = sum_all(small, 4)
     spots = lax.dynamic_slice_in_dim(small[experts + 2 : experts + 4], place * columns, columns, 1)
     stats = small[experts + 4, :6]
     rms = jnp.sqrt(stats[:5] / (jnp.maximum(stats[5], 1.0) * D))

time: 1200 us -> 1190 us (level)
  Pallas kernels: 778 us -> 900 us
  waiting for transfers between devices: 198 us -> 81.7 us
  matrix products: 109 us -> 94 us
    pallas_call x2 -> x3, Pallas kernels: 117 us -> 361 us  [the longest x1 144 us: forward(): return forward_call(raw, gains, cosine, sine, carry)]
    all_gather x2 -> x0, waiting for transfers between devices: 174 us -> none  [the longest x1 129 us: shards(): moe_plane = lax.all_gather(moe_in, 'wide', axis=0, tiled=True)]
    pallas_call x2 -> x1, Pallas kernels: 266 us -> 133 us  [scatter_wide(): pl.pallas_call(scatter_kernel, out_shape=jax.ShapeDtypeStruct((rows, colu...]
    ppermute x5, waiting for transfers between devices: 23.9 us -> 57.5 us  [exchange(): return lax.ppermute(value, 'narrow', swap)]
    reduce_scatter x1, waiting for transfers between devices: 0.02 us -> 24.2 us  [shards(): lax.psum_scatter(moe_part.reshape(half, D), 'wide', scatter_dimension=0,...]
  transfers between devices with their start and end apart: 10 -> 8, of which waited for: 4 -> 3; matrix products, arithmetic and copies ran while one was open for 15% -> 13% of each run, Pallas kernels for 40% -> 43%
where the time goes in v4:
time: 1190 us; the launch traced here: 1180 us
  Pallas kernels  900 us (76%)
  matrix products  94 us (8%)
  waiting for transfers between devices  81.7 us (7%)
  other arithmetic  59.7 us (5%)
  local copies, waits for them, and re-layouts  27 us (2%)
  between operations  15.7 us (1%)
    pallas_call x1, Pallas kernels, start_exchange(): pl.pallas_call(functools.partial(start_kernel, count, swaps), out_shape=[...  156 us
    pallas_call x2, Pallas kernels, expert_call(): pl.pallas_call(functools.partial(expert_kernel, tiles, capacity, experts,...  147 us
    pallas_call x1, Pallas kernels, forward(): return forward_call(raw, gains, cosine, sine, carry)  144 us
    pallas_call x1, Pallas kernels, scatter_wide(): pl.pallas_call(scatter_kernel, out_shape=jax.ShapeDtypeStruct((rows, colu...  133 us
    pallas_call x1, Pallas kernels, input_grad(): pl.pallas_call(functools.partial(input_grad_kernel, gain_row), out_shape=...  127 us
    pallas_call x1, Pallas kernels, shards(): attend_back(raw, gains, cosine, sine, sums, *kept[:5], grad_attended_own,...  102 us
    pallas_call x1, Pallas kernels, gather_wide(): pl.pallas_call(functools.partial(gather_kernel, count), out_shape=[jax.Sh...  91 us
    dot_general x8, matrix products, dot_tn(): lax.dot_general(a, b, (((0,), (0,)), ((), ())), preferred_element_type=jn...  72 us
  transfers between devices with their start and end apart: 8, of which 3 were waited for; matrix products, arithmetic and copies ran while one was open for 13% of the time, Pallas kernels for 43%

profile of v4, /device:TPU:0, one launch (start us, length us, event | category | flops | bytes accessed | tf_op | source)
XLA Modules:
  0.0 1184.0 jit_solution(11174595049437584174)
XLA Ops:
  14.0 156.1 %shard_map.271 = (s32[8,8,256]{2,1,0:T(8,128)}, bf16[8,256,2048]{2,1,0:T(8,128)(2,1)}, bf16[8,256,1024]{2,1,0:T(8,128)(2,1)}, bf16[2048,1024]{1,0:T(8,128)(2,1)}...) custom-call(s32[8,256]{1,0:T(8,128)} %bitcast.89, bf16[256,2048]{1,0:T(8,128)(2,1)} %fusion.5.refs_1_, ...), custom_call_target="tpu_custom_call" | custom-call | bytes 450000000 | tf_op jit(solution)/shard_map/pallas_call | solution.py:766
  184.8 8.7 fusion.34.raw_ref
  193.4 143.7 %shard_map.272 = (bf16[2048,256]{1,0:T(8,128)(2,1)}, bf16[2048,256]{1,0:T(8,128)(2,1)}, bf16[2048,256]{1,0:T(8,128)(2,1)}, bf16[1024,256]{1,0:T(8,128)(2,1)}, bf...) custom-call(f32[2048,768]{1,0:T(8,128)} %fusion.34.raw_ref, ...), custom_call_target="tpu_custom_call" | custom-call | flops 4294967296 | bytes 120000000 | tf_op jit(solution)/shard_map/pallas_call | solution.py:688
  348.0 91.0 %shard_map.273.tokens_ref = bf16[8,256,2048]{2,1,0:T(8,128)(2,1)} custom-call(bf16[256,2048]{1,0:T(8,128)(2,1)} %multiply_convert_fusion.refs_0_), custom_call_target="tpu_custom_call" | custom-call | bytes 300000000 | tf_op jit(solution)/shard_map/pallas_call | solution.py:156
  439.0 70.5 %shard_map.274 = (bf16[8,256,2048]{2,1,0:T(8,128)(2,1)}, bf16[8,256,2048]{2,1,0:T(8,128)(2,1)}, bf16[1280,2048]{1,0:T(8,128)(2,1)}, bf16[1280,2048]{1,0:T(8,128)...) custom-call(s32[1]{0:T(128)} %bitcast.7.id_ref, ...), custom_call_target="tpu_custom_call" | custom-call | flops 32212254720 | bytes 44040192 | tf_op jit(solution)/shard_map/pallas_call | solution.py:1097
  509.5 76.3 %shard_map.275 = (bf16[8,256,2048]{2,1,0:T(8,128)(2,1)}, bf16[8,256,2048]{2,1,0:T(8,128)(2,1)}, bf16[1280,2048]{1,0:T(8,128)(2,1)}, bf16[1280,2048]{1,0:T(8,128)...) custom-call(s32[1]{0:T(128)} %bitcast.6.id_ref, ...), custom_call_target="tpu_custom_call" | custom-call | flops 32212254720 | bytes 44040192 | tf_op jit(solution)/shard_map/pallas_call | solution.py:1097
  585.9 10.5 convolution_convert_fusion.2
  597.0 7.2 convolution_convert_fusion.1
  604.2 7.3 convolution_convert_fusion
  611.5 132.9 %shard_map.276 = f32[256,2048]{1,0:T(8,128)S(1)} custom-call(bf16[8,256,2048]{2,1,0:T(8,128)(2,1)} %get-tuple-element.79.part_ref), custom_call_target="tpu_custom_call" | custom-call | bytes 285000000 | tf_op jit(solution)/shard_map/pallas_call | solution.py:266
  744.4 24.2 %reduce-scatter.2.cloned.1.call-done = bf16[256,2048]{1,0:T(8,128)(2,1)} async-done(((bf16[2048,2048]{1,0:T(8,128)(2,1)}), bf16[256,2048]{1,0:T(8,128)(2,1)}) %reduce-scatter.2.cloned.1.call-update) | async-done | bytes 1048592 | tf_op jit(solution)/shard_map/reduce_scatter | solution.py:1241
  779.4 10.9 fusion.37
  790.3 10.6 fusion.36
  801.0 8.2 fusion.38
  815.0 102.3 %shard_map.277 = (bf16[2048,768]{1,0:T(8,128)(2,1)}, f32[8,256]{1,0:T(8,128)}) custom-call(f32[2048,768]{1,0:T(8,128)} %fusion.34.raw_ref, f32[8,256]{1,0:T(8,128)} %fusion.28.gains_ref, f32[2048,128]{1,0:T(8,128)} %get-tuple-element.145.cos_ref, f32[2048,128]{1,0:T(8,128)} %get-tuple-element.146.sin_ref, f32[8,2048]{1,0:T(8,128)} %get-tuple-element.82.sums_ref, ...), custom_call_target="tpu_custom_call" | custom-call | flops 10737418240 | bytes 200000000 | tf_op jit(solution)/shard_map/pallas_call | solution.py:1263
  917.3 11.3 convolution_convert_fusion.3
  936.6 126.7 %shard_map.278 = (f32[256,2048]{1,0:T(8,128)}, f32[24,2048]{1,0:T(8,128)}) custom-call(bf16[2048,768]{1,0:T(8,128)(2,1)} %get-tuple-element.93.joined_ref, bf16[2048,768]{1,0:T(8,128)(2,1)} %constant_dynamic-update-slice_fusion.weights_ref, bf16[256,2048]{1,0:T(8,128)(2,1)} %tokens_ref.1, f32[256,2048]{1,0:T(8,128)} %get-tuple-element.122.hidden_ref, ...), custom_call_target="tpu_custom_call" | custom-call | bytes 330000000 | tf_op jit(solution)/shard_map/pallas_call | solution.py:943
  1071.6 10.3 add_bitcast_fusion.1
  1082.0 7.8 add_bitcast_fusion.2
  1089.8 6.3 convert_add_fusion
  1096.1 5.9 convolution_convert_fusion.4
  1106.2 53.0 %collective-permute-done.3 = bf16[1024,2048]{1,0:T(8,128)(2,1)} collective-permute-done((bf16[1024,2048]{1,0:T(8,128)(2,1)}, bf16[1024,2048]{1,0:T(8,128)(2,1)}, u32[]{:S(2)}, u32[]{:S(2)}) %collective-permute-start.3) | collective-permute-done | bytes 4194336 | tf_op jit(solution)/shard_map/ppermute | solution.py:1175
  1159.2 10.1 add_bitcast_fusion
  1169.3 4.5 collective-permute-done.5
  (153 shorter events, 72.0 us)
Async XLA Ops:
  7.2 761.4 %reduce-scatter.2.cloned.1.call-start = ((), (), s32[]{:S(2)}) async-start(), calls=%async_computation.1 | async-start | bytes 9437184 | tf_op jit(solution)/shard_map/reduce_scatter | solution.py:1241
  14.0 156.6 %copy-start.14 = (bf16[2048,256]{1,0:T(8,128)(2,1)S(1)}, bf16[2048,256]{1,0:T(8,128)(2,1)}, u32[]{:S(2)}) copy-start(bf16[2048,256]{1,0:T(8,128)(2,1)} %param.20) | copy-start | bytes 3145732
  14.0 157.9 %copy-start.24 = (bf16[256]{0:T(256)(128)(2,1)S(1)}, bf16[256]{0:T(256)(128)(2,1)}, u32[]{:S(2)}) copy-start(bf16[256]{0:T(256)(128)(2,1)} %param.25) | copy-start | bytes 1540
  14.0 157.9 %copy-start.25 = (bf16[256]{0:T(256)(128)(2,1)S(1)}, bf16[256]{0:T(256)(128)(2,1)}, u32[]{:S(2)}) copy-start(bf16[256]{0:T(256)(128)(2,1)} %param.26) | copy-start | bytes 1540
  14.0 157.9 %copy-start.20 = (bf16[2048]{0:T(1024)(128)(2,1)S(1)}, bf16[2048]{0:T(1024)(128)(2,1)}, u32[]{:S(2)}) copy-start(bf16[2048]{0:T(1024)(128)(2,1)} %param.27) | copy-start | bytes 12292
  14.0 159.6 %copy-start.18 = (bf16[2048,16]{0,1:T(8,128)(2,1)S(1)}, bf16[2048,16]{0,1:T(8,128)(2,1)}, u32[]{:S(2)}) copy-start(bf16[2048,16]{0,1:T(8,128)(2,1)} %param.28) | copy-start | bytes 196612
  170.2 170.8 %collective-permute-start = (bf16[2048,1024]{1,0:T(8,128)(2,1)}, bf16[2048,1024]{1,0:T(8,128)(2,1)}, u32[]{:S(2)}, u32[]{:S(2)}) collective-permute-start(bf16[2048,1024]{1,0:T(8,128)(2,1)} %bitcast.98), channel_id=1, source_target_pairs={{0,16},{16,0},{1,17},{17,1},{2,18},{18,2},{3,19},{19,3},{4,20},{20... | collective-permute-start | bytes 12582920 | tf_op jit(solution)/shard_map/ppermute | solution.py:1192
  585.8 11.1 slice-start.6
  585.9 510.2 %all-gather.2.cloned.1.call-start = ((), (), s32[]{:S(2)}) async-start(), calls=%async_computation.2 | async-start | bytes 9437184 | tf_op jit(solution)/shard_map/all_gather | solution.py:1260
  585.9 11.1 slice-start.7
  585.9 11.1 copy-start.29
  585.9 18.3 %slice-start.4 = ((s8[5242880]{0:T(1024)(128)(4,1)}), s8[4194304]{0:T(1024)(128)(4,1)S(1)}, s32[]{:S(2)}) async-start(s8[5242880]{0:T(1024)(128)(4,1)} %bitcast.103), calls=%async_computation.7 | async-start | bytes 8388608
  596.5 173.8 %collective-permute-start.1 = (bf16[2048,1024]{1,0:T(8,128)(2,1)}, bf16[2048,1024]{1,0:T(8,128)(2,1)}, u32[]{:S(2)}, u32[]{:S(2)}) collective-permute-start(bf16[2048,1024]{1,0:T(8,128)(2,1)} %convolution_convert_fusion.2), channel_id=1, source_target_pairs={{0,1},{1,0},{2,3},{3,2},{4,5},{5,4},{6,7},{7,6},{8,9},{9,8},{10,11... | collective-permute-start | bytes 12582920 | tf_op jit(solution)/shard_map/ppermute | solution.py:1175
  776.9 140.4 %collective-permute-start.2 = (bf16[2048,1024]{1,0:T(8,128)(2,1)}, bf16[2048,1024]{1,0:T(8,128)(2,1)}, u32[]{:S(2)}, u32[]{:S(2)}) collective-permute-start(bf16[2048,1024]{1,0:T(8,128)(2,1)} %convolution_convert_fusion.1), channel_id=1, source_target_pairs={{0,1},{1,0},{2,3},{3,2},{4,5},{5,4},{6,7},{7,6},{8,9},{9,8},{10,11... | collective-permute-start | bytes 12582920 | tf_op jit(solution)/shard_map/ppermute | solution.py:1175
  779.4 10.9 copy-start.28
  779.4 21.5 %slice-start.2 = ((s8[5242880]{0:T(1024)(128)(4,1)}), s8[4194304]{0:T(1024)(128)(4,1)S(1)}, s32[]{:S(2)}) async-start(s8[5242880]{0:T(1024)(128)(4,1)} %bitcast.101), calls=%async_computation.5 | async-start | bytes 8388608
  790.3 10.6 slice-start.3
  790.3 10.6 copy-start.26
  800.9 8.3 copy-start.10
  929.5 160.2 %collective-permute-start.4 = (bf16[2048,768]{1,0:T(8,128)(2,1)}, bf16[2048,768]{1,0:T(8,128)(2,1)}, u32[]{:S(2)}, u32[]{:S(2)}) collective-permute-start(bf16[2048,768]{1,0:T(8,128)(2,1)} %convolution_convert_fusion.3), channel_id=1, source_target_pairs={{0,1},{1,0},{2,3},{3,2},{4,5},{5,4},{6,7},{7,6},{8,9},{9,8},{10,11... | collective-permute-start | bytes 9437192 | tf_op jit(solution)/shard_map/ppermute | solution.py:1175
  936.6 145.4 %slice-start = ((s8[8388608]{0:T(1024)(128)(4,1)}), s8[4194304]{0:T(1024)(128)(4,1)S(1)}, s32[]{:S(2)}) async-start(s8[8388608]{0:T(1024)(128)(4,1)} %bitcast.74), calls=%async_computation.3 | async-start | bytes 8388608
  1065.4 93.8 %collective-permute-start.3 = (bf16[1024,2048]{1,0:T(8,128)(2,1)}, bf16[1024,2048]{1,0:T(8,128)(2,1)}, u32[]{:S(2)}, u32[]{:S(2)}) collective-permute-start(bf16[1024,2048]{1,0:T(8,128)(2,1)} %convolution_convert_fusion), channel_id=1, source_target_pairs={{0,1},{1,0},{2,3},{3,2},{4,5},{5,4},{6,7},{7,6},{8,9},{9,8},{10,11... | collective-permute-start | bytes 12582920 | tf_op jit(solution)/shard_map/ppermute | solution.py:1175
  1071.6 10.3 slice-start.1
  1102.0 71.8 %collective-permute-start.5 = (bf16[256,2048]{1,0:T(8,128)(2,1)S(1)}, bf16[256,2048]{1,0:T(8,128)(2,1)S(1)}, u32[]{:S(2)}, u32[]{:S(2)}) collective-permute-start(bf16[256,2048]{1,0:T(8,128)(2,1)S(1)} %convolution_convert_fusion.4), channel_id=1, source_target_pairs={{0,1},{1,0},{2,3},{3,2},{4,5},{5,4},{6,7},{7,6},{8,9},{9,8},{10,11... | collective-permute-start | bytes 3145736 | tf_op jit(solution)/shard_map/ppermute | solution.py:1175
  (22 other events, 96.9 us)
Sparse Core Ops, SparseCore 0:
  586.0 182.6 reduce-scatter.1
  776.4 149.7 all-gather.1

commit v5 on v4

--- a/solution.py
+++ b/solution.py
@@ -336,9 +336,11 @@
     return parts
 
 
-def for_blocks(blocks, prompt_blocks, one):
+def for_blocks(blocks, prompt_blocks, one, between=None):
     for w in range(prompt_blocks):
         one(w, w, w * one.rows)
+    if between is not None:
+        between()
 
     def body(w, carry):
         one(None, w, pl.multiple_of(w * one.rows, one.rows))
@@ -442,13 +444,13 @@
     pairs[0].start()
     lax.fori_loop(shared // rows, size, prepare(1, k_ref), 0)
     lax.fori_loop(0, size, prepare(0, q_ref), 0)
+    if carried:
+        gather.forward(1)
     pairs[1].wait()
     for h in range(heads):
         hs = slice(h * HD, (h + 1) * HD)
         vto_ref[hs, :] = vo_ref[:, hs].T
     pairs[0].wait()
-    if carried:
-        gather.forward(1)
 
     def mine():
         return pl.ds(pl.multiple_of(wide * columns, columns), columns)
@@ -492,10 +494,9 @@
             hand_out(w_index).start()
 
     one.rows = rows
-    for_blocks(size, prompt_blocks, one)
+    for_blocks(size, prompt_blocks, one, (lambda: gather.forward(2)) if carried else None)
     if carried:
-        for distance in range(2, LINE):
-            gather.forward(distance)
+        gather.forward(3)
     own_ref[:, mine()] = o_ref[pl.ds(pl.multiple_of(wide * rows, rows), rows)]
 
     def finish(w, carry):
@@ -514,12 +515,15 @@
 
 
 def attend_back_kernel(
-    rows, prompt_blocks, paired, shared, raw_ref, gains_ref, cos_ref, sin_ref, sums_ref,
-    q_ref, k_ref, v_ref, ko_ref, vo_ref, grad_ref, o_ref, lse_ref,
-    joined_ref, gain_ref,
-    do_ref, dq_ref, dk_ref, dv_ref, dko_ref, dvo_ref, dkb_ref, dvb_ref, dkr_ref, dvr_ref, kt_ref, kto_ref,
-    dots_ref, came_ref, sum_send, sum_recv, pair_send, pair_recv, in_send, in_recv,
+    rows, prompt_blocks, paired, shared, carried, raw_ref, gains_ref, cos_ref, sin_ref, sums_ref,
+    q_ref, k_ref, v_ref, ko_ref, vo_ref, grad_ref, o_ref, lse_ref, *refs
 ):
+    carry_in, refs = refs[:carried], refs[carried:]
+    joined_ref, gain_ref = refs[:2]
+    carry_out, refs = refs[2 : 2 + carried], refs[2 + carried :]
+    do_ref, dq_ref, dk_ref, dv_ref, dko_ref, dvo_ref, dkb_ref, dvb_ref, dkr_ref, dvr_ref, kt_ref, kto_ref = refs[:12]
+    dots_ref, came_ref, sum_send, sum_recv, pair_send, pair_recv, in_send, in_recv = refs[12:20]
+    gather = Gather(carry_in, carry_out, *refs[20:]) if carried else None
     half, columns = q_ref.shape
     size = half // rows
     heads = columns // HD
@@ -544,6 +548,8 @@
         lax.fori_loop(0, size, body, 0)
 
     each_peer(lambda w: hand_in(w).start())
+    if carried:
+        gather.start()
     do_ref[my_rows, :] = grad_ref[:, part_of(wide)]
     for ref in (dk_ref, dv_ref, dko_ref, dvo_ref, dots_ref, gain_ref):
         ref[...] = jnp.zeros_like(ref)
@@ -585,7 +591,7 @@
                 dq_ref[block, hs] = back if plane == 1 else dq_ref[block, hs] + back
 
         one.rows = rows
-        for_blocks(size, prompt_blocks, one)
+        for_blocks(size, prompt_blocks, one, (lambda: gather.forward(2 - plane)) if carried else None)
 
     sweep(1)
     dkb_ref[...] = dko_ref[...].astype(jnp.bfloat16)
@@ -616,6 +622,8 @@
         lax.fori_loop(0, size, body, 0)
 
     turn_back(0, dq_ref)
+    if carried:
+        gather.forward(3)
     for copy in pairs:
         copy.wait()
     dk_ref[0:shared, :] += dkr_ref[...].astype(jnp.float32)
@@ -649,6 +657,8 @@
 
     lax.fori_loop(0, size, finish, 0)
     each_peer(lambda w: hand_in(w).wait_send())
+    if carried:
+        gather.finish()
 
 
 def attention_calls(rows, half, shared, columns, prompt_blocks, paired, ids):
@@ -657,7 +667,6 @@
     bf16, f32 = jnp.bfloat16, jnp.float32
     shape = lambda dtype, *dims: jax.ShapeDtypeStruct(dims, dtype)
     sems = pltpu.SemaphoreType.DMA
-    work = half * half * columns * 2
     peers = [sems((size - 1,)), sems((size - 1,)), sems((2,)), sems((2,)), sems((size,)), sems((size,))]
 
     def params(k):
@@ -680,7 +689,7 @@
         + peers
         + gather_sems(carried) * carried,
         compiler_params=params(0),
-        cost_estimate=pl.CostEstimate(flops=2 * work, bytes_accessed=120_000_000, transcendentals=0),
+        cost_estimate=pl.CostEstimate(flops=0, bytes_accessed=300_000_000, transcendentals=0),
     )
 
     def forward(raw, gains, cosine, sine, carry):
@@ -688,11 +697,12 @@
             return forward_call(raw, gains, cosine, sine, carry)
         return [*forward_call(raw, gains, cosine, sine), lax.all_gather(carry, "wide", axis=0)]
 
-    backward = pl.pallas_call(
-        functools.partial(attend_back_kernel, rows, prompt_blocks, paired, shared),
-        out_shape=[shape(bf16, half, 3 * columns), shape(f32, 8, columns)],
-        in_specs=[VMEM] * 13,
-        out_specs=[VMEM] * 2,
+    backward_call = pl.pallas_call(
+        functools.partial(attend_back_kernel, rows, prompt_blocks, paired, shared, carried),
+        out_shape=[shape(bf16, half, 3 * columns), shape(f32, 8, columns)]
+        + [shape(bf16, size, rows, D)] * carried,
+        in_specs=[VMEM] * 13 + [ANY] * carried,
+        out_specs=[VMEM] * 2 + [ANY] * carried,
         scratch_shapes=[pltpu.VMEM((half, columns), bf16)]
         + [pltpu.VMEM((half, columns), f32)] * 3
         + [pltpu.VMEM((shared, columns), f32)] * 2
@@ -703,10 +713,16 @@
             pltpu.VMEM((8, half), f32),
             pltpu.VMEM((size - 1, 8, half), f32),
         ]
-        + peers,
+        + peers
+        + gather_sems(carried) * carried,
         compiler_params=params(1),
-        cost_estimate=pl.CostEstimate(flops=5 * work, bytes_accessed=200_000_000, transcendentals=0),
+        cost_estimate=pl.CostEstimate(flops=0, bytes_accessed=300_000_000, transcendentals=0),
     )
+    def backward(*args):
+        if carried:
+            return backward_call(*args)
+        return [*backward_call(*args[:-1]), lax.all_gather(args[-1], "wide", axis=0)]
+
     return forward, backward
 
 
@@ -779,6 +795,200 @@
         cost_estimate=lasts(150),
     )(*arrays, *weights)
     return out[:count], out[count:]
+
+
+def expert_grad_kernel(
+    part_ref, *refs
+):
+    operands = refs[0:5]
+    out_ref, gate_out, up_out, down_out = refs[5:9]
+    held, from_across, from_line, x_buf, g_buf, inner_buf, gate_buf, up_buf, stage = refs[9:18]
+    load, send, recv_a, recv_l, fetch, put = refs[18:]
+    grp, wide, narrow, line, cross = position()
+    across = (grp, line * 2 + 1 - cross, narrow)
+    above = (grp, wide + 2, narrow)
+    below = (grp, wide - 2, narrow)
+    has_above, has_below = line < LINE - 1, line > 0
+    f32, bf16 = jnp.float32, jnp.bfloat16
+    greet([(across, None), (above, has_above), (below, has_below)])
+    order = [(distance, sign) for distance in range(LINE - 1, 0, -1) for sign in (1, -1)]
+
+    def valid(owner):
+        return (owner >= 0) & (owner < LINE)
+
+    def across_copy(owner):
+        return remote(
+            part_ref.at[owner * 2 + 1 - cross], from_across.at[owner], send.at[0, owner], recv_a.at[owner], across
+        )
+
+    def load_copy(owner):
+        return pltpu.make_async_copy(part_ref.at[owner * 2 + cross], held.at[owner], load.at[owner])
+
+    def line_copy(owner, up):
+        slot = 0 if up else 1
+        return remote(
+            held.at[owner], from_line.at[slot, owner], send.at[1, owner], recv_l.at[slot, owner], above if up else below
+        )
+
+    for distance, sign in order + [(0, 1)]:
+        owner = line + sign * distance
+
+        @pl.when(valid(owner))
+        def _(owner=owner):
+            across_copy(owner).start()
+            load_copy(owner).start()
+
+    bufs = (x_buf, g_buf, inner_buf, gate_buf, up_buf)
+
+    fetches = [pltpu.make_async_copy(src, dst, fetch.at[i]) for i, (src, dst) in enumerate(zip(operands, bufs))]
+    for copy in fetches:
+        copy.start()
+
+    tiles = stage.shape[0]
+    width = gate_buf.shape[1] // tiles
+
+    def tile(n, size):
+        return pl.ds(pl.multiple_of(n * size, size), size)
+
+    def column_job(values, result):
+        def put_copy(n):
+            return pltpu.make_async_copy(stage.at[n], result.at[:, tile(n, width)], put.at[n])
+
+        def run():
+            @pl.loop(0, tiles)
+            def _(n):
+                stage[n] = dot_tn(x_buf[...], values[:, tile(n, width)]).astype(bf16)
+                put_copy(n).start()
+
+            @pl.loop(0, tiles)
+            def _(n):
+                put_copy(n).wait()
+
+        return run
+
+    def down_job(result):
+        units = inner_buf.shape[1] // tiles
+
+        def run():
+            for n in range(tiles):
+                at = slice(n * units, (n + 1) * units)
+                product = dot_tn(inner_buf[:, at], g_buf[...]).astype(bf16)
+                for c in range(product.shape[1] // width):
+                    stage[n, c * units : (c + 1) * units, :] = product[:, c * width : (c + 1) * width]
+            copies = [
+                pltpu.make_async_copy(
+                    stage.at[n, pl.ds(c * units, units)],
+                    result.at[pl.ds(n * units, units), pl.ds(c * width, width)],
+                    put.at[n * (g_buf.shape[1] // width) + c],
+                )
+                for n in range(tiles)
+                for c in range(g_buf.shape[1] // width)
+            ]
+            for copy in copies:
+                copy.start()
+            for copy in copies:
+                copy.wait()
+
+        return run
+
+    def first_job():
+        for copy in fetches:
+            copy.wait()
+        column_job(gate_buf, gate_out)()
+
+    jobs = [first_job, None, column_job(up_buf, up_out), None, down_job(down_out), None]
+    for job, (distance, sign) in zip(jobs, order):
+        if job is not None:
+            job()
+        owner = line + sign * distance
+
+        @pl.when(valid(owner))
+        def _(owner=owner, sign=sign):
+            load_copy(owner).wait()
+            across_copy(owner).wait_recv()
+            up = sign > 0
+            came = has_below if up else has_above
+            total = held[owner].astype(f32) + from_across[owner].astype(f32)
+
+            @pl.when(came)
+            def _():
+                line_copy(owner, up).wait_recv()
+                held[owner] = (total + from_line[0 if up else 1, owner].astype(f32)).astype(held.dtype)
+
+            @pl.when(jnp.logical_not(came))
+            def _():
+                held[owner] = total.astype(held.dtype)
+
+            line_copy(owner, up).start()
+
+    load_copy(line).wait()
+    across_copy(line).wait_recv()
+    out_ref[...] = held[line].astype(f32) + from_across[line].astype(f32)
+
+    @pl.when(has_below)
+    def _():
+        line_copy(line, True).wait_recv()
+        out_ref[...] += from_line[0, line].astype(f32)
+
+    @pl.when(has_above)
+    def _():
+        line_copy(line, False).wait_recv()
+        out_ref[...] += from_line[1, line].astype(f32)
+
+    for owner in range(LINE):
+        across_copy(owner).wait_send()
+
+        @pl.when(owner > line)
+        def _(owner=owner):
+            line_copy(owner, True).wait_send()
+
+        @pl.when(owner < line)
+        def _(owner=owner):
+            line_copy(owner, False).wait_send()
+
+
+def plain_grads(x, g, inner, gate, up):
+    return [dot_tn(a, b).astype(jnp.bfloat16) for a, b in ((x, gate), (x, up), (inner, g))]
+
+
+def expert_grad(part, own, collective_id):
+    size, rows, columns = part.shape
+    f32, bf16 = jnp.float32, jnp.bfloat16
+    if size != 2 * LINE:
+        return lax.psum_scatter(part, "wide", scatter_dimension=0, tiled=False).astype(f32), *plain_grads(*own)
+    count, units = own[2].shape
+    tiles = 4
+    block = (LINE, rows, columns)
+    gate = jax.ShapeDtypeStruct((D, units), bf16)
+    down = jax.ShapeDtypeStruct((units, D), bf16)
+    dma = pltpu.SemaphoreType.DMA
+    return pl.pallas_call(
+        expert_grad_kernel,
+        out_shape=[jax.ShapeDtypeStruct((rows, columns), f32), gate, gate, down],
+        in_specs=[ANY] * 6,
+        out_specs=[VMEM] + [ANY] * 3,
+        scratch_shapes=[
+            pltpu.VMEM(block, bf16),
+            pltpu.VMEM(block, bf16),
+            pltpu.VMEM((2, *block), bf16),
+            pltpu.VMEM((count, D), bf16),
+            pltpu.VMEM((count, D), bf16),
+            pltpu.VMEM((count, units), bf16),
+            pltpu.VMEM((count, units), bf16),
+            pltpu.VMEM((count, units), bf16),
+            pltpu.VMEM((tiles, D, units // tiles), bf16),
+            dma((LINE,)),
+            dma((2, LINE)),
+            dma((LINE,)),
+            dma((2, LINE)),
+            dma((5,)),
+            dma((tiles * D // (units // tiles),)),
+        ],
+        compiler_params=pltpu.CompilerParams(
+            collective_id=collective_id, has_side_effects=True, vmem_limit_bytes=60 * 2**20
+        ),
+        cost_estimate=lasts(1),
+    )(part, *own)
 
 
 class SmallSum:
@@ -960,7 +1170,7 @@
         compiler_params=pltpu.CompilerParams(
             collective_id=ids, has_side_effects=True, vmem_limit_bytes=56 * 2**20
         ),
-        cost_estimate=lasts(110),
+        cost_estimate=lasts(100),
     )(joined, weights, tokens, grad_hidden, gain, small)
 
 
@@ -1115,7 +1325,7 @@
         ],
         compiler_params=pltpu.CompilerParams(vmem_limit_bytes=60 * 2**20),
         cost_estimate=pl.CostEstimate(
-            flops=12 * count * D * units, bytes_accessed=count * D * 12 + 6 * D * units, transcendentals=0
+            flops=0, bytes_accessed=250_000_000, transcendentals=0
         ),
     )(expert.astype(jnp.int32).reshape(1), slots, tokens, grads, router, *weights, *(before or ()))
 
@@ -1180,21 +1390,22 @@
     normed = (stream * inv_one * gain_one).astype(bf16)
     mask = valid.astype(f32)[:, None]
     grad_final = cotangent.astype(f32) * mask
-    pieces = 2 if twins else 1
+    pieces = 2 * narrow_count if twins else 1
     piece_width = D // pieces
-    piece = lax.dynamic_slice_in_dim(w_out, group * piece_width, piece_width, 1) if twins else w_out
-    (routes_plane, normed_plane, out_piece), (other_gate, other_up, other_down) = start_exchange(
-        [routes.T, normed, piece], [w_gate[0], w_up[0], w_down[0]], 0
-    )
+    piece_id = group * narrow_count + side if twins else 0
+    piece = lax.dynamic_slice_in_dim(w_out, piece_id * piece_width, piece_width, 1)
+    (routes_plane, normed_plane, out_piece), (other_up,) = start_exchange([routes.T, normed, piece], [w_up[0]], 0)
     normed_plane = normed_plane.reshape(half, D)
     out_pieces = [out_piece.reshape(D, piece_width)]
     if twins:
-        out_pieces.append(lax.ppermute(out_pieces[0], "grp", swap))
+        out_pieces.append(exchange(out_pieces[0]))
+        out_pieces += [lax.ppermute(p, "grp", swap) for p in out_pieces]
 
     def ordered(parts):
         if not twins:
             return parts
-        return [jnp.where(group == 0, parts[k], parts[k ^ 1]) for k in range(2)]
+        parts = [jnp.where(side == 0, parts[k], parts[k ^ 1]) for k in range(4)]
+        return [jnp.where(group == 0, parts[k], parts[k ^ 2]) for k in range(4)]
 
     def unordered(whole):
         return ordered([whole[:, k * piece_width : (k + 1) * piece_width] for k in range(pieces)])
@@ -1215,7 +1426,7 @@
     inv_two = lax.rsqrt(jnp.mean(hidden * hidden, -1, keepdims=True) + EPSILON)
     gain_two = norm_moe.astype(f32)
     moe_in = (hidden * inv_two * gain_two).astype(bf16)
-    (tokens_in,) = gather_wide([moe_in], 6)
+    (tokens_in,), (other_gate, other_down) = start_exchange([moe_in], [w_gate[0], w_down[0]], 6)
 
     earlier = (jnp.arange(rows)[:, None] < jnp.arange(rows)[None, :]).astype(bf16)
 
@@ -1231,23 +1442,16 @@
             expert, slots_of(expert), tokens_in, grads_in, router, weights, capacity, experts, before
         )
 
-    own = run_expert(place * narrow_count + side, (w_gate[0], w_up[0], w_down[0]), None)
-    other = run_expert(
-        place * narrow_count + 1 - side, (other_gate, other_up, other_down), (own[0], own[1], own[7])
-    )
-    moe_part, grad_part, grad_router = other[0], other[1], other[7][:experts]
-    inputs, grads, inners_gated = (own[2], other[2]), (own[3], other[3]), (own[4], other[4])
-    grad_pres = ((own[5], own[6]), (other[5], other[6]))
+    other = run_expert(place * narrow_count + 1 - side, (other_gate, other_up, other_down), None)
+    partner_grads = plain_grads(*other[2:7])
+    came = [exchange(g) for g in partner_grads[:2]]
+    before, partner_grads = barrier(((other[0], other[1], other[7]), partner_grads))
+    own = run_expert(place * narrow_count + side, (w_gate[0], w_up[0], w_down[0]), before)
+    moe_part, grad_part, grad_router = own[0], own[1], own[7][:experts]
     moe = lax.psum_scatter(moe_part.reshape(half, D), "wide", scatter_dimension=0, tiled=True).astype(f32)
-    partner_grads = [
-        dot_tn(inputs[1], grad_pres[1][0]).astype(bf16),
-        dot_tn(inputs[1], grad_pres[1][1]).astype(bf16),
-        dot_tn(inners_gated[1], grads[1]).astype(bf16),
-    ]
-    came = [exchange(g) for g in partner_grads[:2]]
-    grad_part, partner_grads = barrier((grad_part, partner_grads))
-    grad_moe_in = scatter_wide(grad_part, 5)
-    grad_moe_in, moe, came[0] = barrier((grad_moe_in, moe, came[0]))
+    grad_moe_in, *own_grads = expert_grad(grad_part, own[2:7], 5)
+    grad_moe_in, moe, down_grad = barrier((grad_moe_in, moe, partner_grads[2]))
+    came.append(exchange(down_grad))
 
     grad_gain_two = jnp.sum(grad_moe_in * hidden * inv_two, 0)
     grad_hidden = (
@@ -1257,14 +1461,12 @@
     )
     grad_branch = grad_hidden.astype(bf16)
     grad_attended_own = sum(dot_nt(g, p) for g, p in zip(unordered(grad_branch), out_pieces)).astype(bf16)
-    branch_plane = lax.all_gather(grad_branch, "wide", axis=0, tiled=True)
-    grad_out = barrier(dot_tn(attended, branch_plane).astype(bf16))
-
-    grads_joined, gain_grads = attend_back(
-        raw, gains, cosine, sine, sums, *kept[:5], grad_attended_own, attended, lse
+    grad_attended_own, came[0], came[1] = barrier((grad_attended_own, came[0], came[1]))
+    grads_joined, gain_grads, branch_plane = attend_back(
+        raw, gains, cosine, sine, sums, *kept[:5], grad_attended_own, attended, lse, grad_branch
     )
-    grads_joined, came[1], down_partner = barrier((grads_joined, came[1], partner_grads[2]))
-    came.append(exchange(down_partner))
+    grads_joined, came[2] = barrier((grads_joined, came[2]))
+    grad_out = barrier(dot_tn(attended, branch_plane.reshape(half, D)).astype(bf16))
     grad_weights = barrier(dot_tn(normed_plane, grads_joined).astype(bf16))
     weights_came = exchange(grad_weights)
     out_came = exchange(grad_out)
@@ -1274,14 +1476,10 @@
     zeros = jnp.zeros((D,), f32)
     small = jnp.stack([zeros, grad_gain_two, *spots, jnp.pad(stats, (0, D - stats.shape[0]))])
     small = jnp.concatenate([grad_router, small, jnp.zeros((-(experts + 5) % 8, D), f32)], 0)
-    small, _ = barrier((small, grad_weights))
+    small, _, _ = barrier((small, grad_weights, grad_out))
     grad_input, small = input_grad(
         grads_joined, joined, tokens, grad_hidden, gain_one.reshape(1, D), small, experts, 3
     )
-    grad_input, came[2] = barrier((grad_input, came[2]))
-    expert_grads = [
-        dot_tn(inputs[0], grad_pres[0][0]), dot_tn(inputs[0], grad_pres[0][1]), dot_tn(inners_gated[0], grads[0])
-    ]
     grad_weights = grad_weights.astype(f32) + weights_came.astype(f32)
     grad_out = grad_out.astype(f32) + out_came.astype(f32)
     grad_query_w, grad_key_w, grad_value_w = (
@@ -1290,7 +1488,7 @@
     final = hidden + moe
     output = final.astype(bf16)
     grad_gate_w, grad_up_w, grad_down_w = (
-        (own + other.astype(f32))[None] for own, other in zip(expert_grads, came)
+        (own.astype(f32) + other.astype(f32))[None] for own, other in zip(own_grads, came)
     )
 
     spots = lax.dynamic_slice_in_dim(small[experts + 2 : experts + 4], place * columns, columns, 1)

time: 1190 us -> 1170 us (0.983)
  matrix products: 94 us -> 69.3 us
  Pallas kernels: 900 us -> 921 us
    pallas_call x1 -> x2, Pallas kernels: 156 us -> 228 us  [start_exchange(): pl.pallas_call(functools.partial(start_kernel, count, swaps), out_shape=[...]
    pallas_call x3 -> x2, Pallas kernels: 326 us -> 285 us  [the longest x1 152 us: expert_grad(): pl.pallas_call(expert_grad_kernel, out_shape=[jax.ShapeDtypeStruct((rows,...]
    dot_general x8 -> x5, matrix products: 72 us -> 41.6 us  [dot_tn(): lax.dot_general(a, b, (((0,), (0,)), ((), ())), preferred_element_type=jn...]
    ppermute x5 -> x6, waiting for transfers between devices: 57.5 us -> 31.1 us  [exchange(): return lax.ppermute(value, 'narrow', swap)]
    reduce_scatter x1, waiting for transfers between devices: 24.2 us -> 39.5 us  [shards(): lax.psum_scatter(moe_part.reshape(half, D), 'wide', scatter_dimension=0,...]
    pallas_call x1, Pallas kernels: 127 us -> 112 us  [input_grad(): pl.pallas_call(functools.partial(input_grad_kernel, gain_row), out_shape=...]
  transfers between devices with their start and end apart: 8 -> 9, of which waited for: 3 -> 2; matrix products, arithmetic and copies ran while one was open for 13% -> 9% of each run, Pallas kernels for 43% -> 46%
where the time goes in v5:
time: 1170 us; the launch traced here: 1160 us
  Pallas kernels  921 us (79%)
  waiting for transfers between devices  70.6 us (6%)
  matrix products  69.3 us (6%)
  other arithmetic  52.8 us (5%)
  local copies, waits for them, and re-layouts  25.8 us (2%)
  between operations  15.5 us (1%)
    pallas_call x2, Pallas kernels, start_exchange(): pl.pallas_call(functools.partial(start_kernel, count, swaps), out_shape=[...  228 us
    pallas_call x2, Pallas kernels, expert_call(): pl.pallas_call(functools.partial(expert_kernel, tiles, capacity, experts,...  158 us
    pallas_call x1, Pallas kernels, expert_grad(): pl.pallas_call(expert_grad_kernel, out_shape=[jax.ShapeDtypeStruct((rows,...  152 us
    pallas_call x1, Pallas kernels, forward(): return forward_call(raw, gains, cosine, sine, carry)  138 us
    pallas_call x1, Pallas kernels, backward(): return backward_call(*args)  133 us
    pallas_call x1, Pallas kernels, input_grad(): pl.pallas_call(functools.partial(input_grad_kernel, gain_row), out_shape=...  112 us
    dot_general x5, matrix products, dot_tn(): lax.dot_general(a, b, (((0,), (0,)), ((), ())), preferred_element_type=jn...  41.6 us
    reduce_scatter x1, waiting for transfers between devices, shards(): lax.psum_scatter(moe_part.reshape(half, D), 'wide', scatter_dimension=0,...  39.5 us
  transfers between devices with their start and end apart: 9, of which 2 were waited for; matrix products, arithmetic and copies ran while one was open for 9% of the time, Pallas kernels for 46%

profile of v5, /device:TPU:0, one launch (start us, length us, event | category | flops | bytes accessed | tf_op | source)
XLA Modules:
  0.0 1163.1 jit_solution(1778887107879477141)
XLA Ops:
  8.1 3.7 fusion.3
  13.9 127.5 %shard_map.271 = (s32[8,8,256]{2,1,0:T(8,128)}, bf16[8,256,2048]{2,1,0:T(8,128)(2,1)}, bf16[8,256,512]{2,1,0:T(8,128)(2,1)}, bf16[2048,1024]{1,0:T(8,128)(2,1)}) custom-call(s32[8,256]{1,0:T(8,128)} %bitcast.93, bf16[256,2048]{1,0:T(8,128)(2,1)} %fusion.5.refs_1_, bf16[256,512]{1,0:T(8,128)(2,1)} %constant_dynamic-slice_fusion.1.refs_2_, ...), custom_call_target="tpu_custom_call" | custom-call | bytes 450000000 | tf_op jit(solution)/shard_map/pallas_call | solution.py:782
  146.9 11.7 %fusion.34.raw_ref = f32[2048,768]{1,0:T(8,128)} fusion(bf16[2048,2048]{1,0:T(8,128)(2,1)} %bitcast.100, bf16[2048,768]{1,0:T(8,128)(2,1)} %constant_dynamic-update-slice_fusion.weights_ref), kind=kOutput, calls=%fused_computation.108 | convolution fusion | flops 6442450944 | bytes 17825792 | tf_op jit(solution)/shard_map/dot_general | solution.py:730
  158.6 31.1 %collective-permute-done = bf16[2048,512]{1,0:T(8,128)(2,1)} collective-permute-done((bf16[2048,512]{1,0:T(8,128)(2,1)}, bf16[2048,512]{1,0:T(8,128)(2,1)}, u32[]{:S(2)}, u32[]{:S(2)}) %collective-permute-start) | collective-permute-done | bytes 2097184 | tf_op jit(solution)/shard_map/ppermute | solution.py:1385
  192.8 3.7 fusion.10
  198.5 137.9 %shard_map.272 = (bf16[2048,256]{1,0:T(8,128)(2,1)}, bf16[2048,256]{1,0:T(8,128)(2,1)}, bf16[2048,256]{1,0:T(8,128)(2,1)}, bf16[1024,256]{1,0:T(8,128)(2,1)}, bf...) custom-call(f32[2048,768]{1,0:T(8,128)} %fusion.34.raw_ref, ...), custom_call_target="tpu_custom_call" | custom-call | bytes 300000000 | tf_op jit(solution)/shard_map/pallas_call | solution.py:697
  347.7 100.5 %shard_map.273 = (bf16[8,256,2048]{2,1,0:T(8,128)(2,1)}, bf16[2048,1024]{1,0:T(8,128)(2,1)}, bf16[1024,2048]{1,0:T(8,128)(2,1)}) custom-call(bf16[256,2048]{1,0:T(8,128)(2,1)} %multiply_convert_fusion.refs_0_, bf16[2048,1024]{1,0:T(8,128)(2,1)} %bitcast.78, bf16[1024,2048]{1,0:T(8,128)(2,1)} %bitcast.80), custom_call_target="tpu_custom_call" | custom-call | bytes 450000000 | tf_op jit(solution)/shard_map/pallas_call | solution.py:782
  448.2 81.9 %shard_map.274 = (bf16[8,256,2048]{2,1,0:T(8,128)(2,1)}, bf16[8,256,2048]{2,1,0:T(8,128)(2,1)}, bf16[1280,2048]{1,0:T(8,128)(2,1)}, bf16[1280,2048]{1,0:T(8,128)...) custom-call(s32[1]{0:T(128)} %bitcast.7.id_ref, ...), custom_call_target="tpu_custom_call" | custom-call | bytes 250000000 | tf_op jit(solution)/shard_map/pallas_call | solution.py:1307
  530.1 10.4 convolution_convert_fusion.1
  540.5 7.3 convolution_convert_fusion.2
  547.8 7.3 convolution_convert_fusion
  555.1 76.3 %shard_map.275 = (bf16[8,256,2048]{2,1,0:T(8,128)(2,1)}, bf16[8,256,2048]{2,1,0:T(8,128)(2,1)}, bf16[1280,2048]{1,0:T(8,128)(2,1)}, bf16[1280,2048]{1,0:T(8,128)...) custom-call(s32[1]{0:T(128)} %bitcast.4.id_ref, ...), custom_call_target="tpu_custom_call" | custom-call | bytes 250000000 | tf_op jit(solution)/shard_map/pallas_call | solution.py:1307
  635.5 151.8 %shard_map.276 = (f32[256,2048]{1,0:T(8,128)}, bf16[2048,1024]{1,0:T(8,128)(2,1)}, bf16[2048,1024]{1,0:T(8,128)(2,1)}, bf16[1024,2048]{1,0:T(8,128)(2,1)}) custom-call(bf16[8,256,2048]{2,1,0:T(8,128)(2,1)} %get-tuple-element.90.part_ref, bf16[1280,2048]{1,0:T(8,128)(2,1)} %get-tuple-element.91.refs_0_, bf16[1280,2048]{1,0:T(8,128)(2,1)} %get-tuple-element.92.refs_1_, ...), custom_call_target="tpu_custom_call" | custom-call | bytes 3000000 | tf_op jit(solution)/shard_map/pallas_call | solution.py:965
  787.3 39.5 %reduce-scatter.2.cloned.1.call-done = bf16[256,2048]{1,0:T(8,128)(2,1)} async-done(((bf16[2048,2048]{1,0:T(8,128)(2,1)}), bf16[256,2048]{1,0:T(8,128)(2,1)}) %reduce-scatter.2.cloned.1.call-update) | async-done | bytes 1048592 | tf_op jit(solution)/shard_map/reduce_scatter | solution.py:1451
  830.0 4.2 multiply_reduce_fusion
  843.9 133.3 %shard_map.277 = (bf16[2048,768]{1,0:T(8,128)(2,1)}, f32[8,256]{1,0:T(8,128)}, bf16[8,256,2048]{2,1,0:T(8,128)(2,1)}) custom-call(f32[2048,768]{1,0:T(8,128)} %fusion.34.raw_ref, f32[8,256]{1,0:T(8,128)} %fusion.28.gains_ref, f32[2048,128]{1,0:T(8,128)} %get-tuple-element.163.cos_ref, f32[2048,128]{1,0:T(8,128)} %get-tuple-element.164.sin_ref, ...), custom_call_target="tpu_custom_call" | custom-call | bytes 300000000 | tf_op jit(solution)/shard_map/pallas_call | solution.py:723
  977.2 5.7 convolution_convert_fusion.4
  984.5 4.0 stack.48
  989.8 9.0 add_bitcast_fusion.1
  998.8 10.8 convolution_convert_fusion.3
  1011.1 7.6 add_bitcast_fusion.2
  1020.3 112.1 %shard_map.278 = (f32[256,2048]{1,0:T(8,128)}, f32[24,2048]{1,0:T(8,128)}) custom-call(bf16[2048,768]{1,0:T(8,128)(2,1)} %get-tuple-element.112.joined_ref, bf16[2048,768]{1,0:T(8,128)(2,1)} %constant_dynamic-update-slice_fusion.weights_ref, bf16[256,2048]{1,0:T(8,128)(2,1)} %tokens_ref.1, f32[256,2048]{1,0:T(8,128)} %get-tuple-element.138.hidden_ref, ...), custom_call_target="tpu_custom_call" | custom-call | bytes 300000000 | tf_op jit(solution)/shard_map/pallas_call | solution.py:1153
  1140.2 7.5 add_bitcast_fusion
  1147.7 3.5 convert_add_fusion
  (152 shorter events, 59.2 us)
Async XLA Ops:
  7.2 819.6 %reduce-scatter.2.cloned.1.call-start = ((), (), s32[]{:S(2)}) async-start(), calls=%async_computation.1 | async-start | bytes 9437184 | tf_op jit(solution)/shard_map/reduce_scatter | solution.py:1451
  11.8 129.6 %copy-start.25 = (f32[2048]{0:T(1024)}, f32[2048]{0:T(1024)S(1)}, u32[]{:S(2)}) copy-start(f32[2048]{0:T(1024)S(1)} %convert_element_type.105) | copy-start | bytes 24580
  13.8 129.3 %copy-start.21 = (bf16[2048,256]{1,0:T(8,128)(2,1)S(1)}, bf16[2048,256]{1,0:T(8,128)(2,1)}, u32[]{:S(2)}) copy-start(bf16[2048,256]{1,0:T(8,128)(2,1)} %param.20) | copy-start | bytes 3145732
  141.4 48.3 %collective-permute-start = (bf16[2048,512]{1,0:T(8,128)(2,1)}, bf16[2048,512]{1,0:T(8,128)(2,1)}, u32[]{:S(2)}, u32[]{:S(2)}) collective-permute-start(bf16[2048,512]{1,0:T(8,128)(2,1)} %bitcast.83), channel_id=1, source_target_pairs={{0,1},{1,0},{2,3},{3,2},{4,5},{5,4},{6,7},{7,6},{8,9},{9,8},{10,11... | collective-permute-start | bytes 6291464 | tf_op jit(solution)/shard_map/ppermute | solution.py:1385
  143.0 198.4 %collective-permute-start.1 = (bf16[2048,512]{1,0:T(8,128)(2,1)}, bf16[2048,512]{1,0:T(8,128)(2,1)}, u32[]{:S(2)}, u32[]{:S(2)}) collective-permute-start(bf16[2048,512]{1,0:T(8,128)(2,1)} %bitcast.84), channel_id=1, source_target_pairs={{0,16},{16,0},{1,17},{17,1},{2,18},{18,2},{3,19},{19,3},{4,20},{20... | collective-permute-start | bytes 6291464 | tf_op jit(solution)/shard_map/ppermute | solution.py:1402
  146.8 42.9 %copy-start.34 = (bf16[256]{0:T(256)(128)(2,1)S(1)}, bf16[256]{0:T(256)(128)(2,1)}, u32[]{:S(2)}) copy-start(bf16[256]{0:T(256)(128)(2,1)} %param.25) | copy-start | bytes 1540
  146.8 42.9 %copy-start.35 = (bf16[256]{0:T(256)(128)(2,1)S(1)}, bf16[256]{0:T(256)(128)(2,1)}, u32[]{:S(2)}) copy-start(bf16[256]{0:T(256)(128)(2,1)} %param.26) | copy-start | bytes 1540
  146.8 42.9 %copy-start.29 = (bf16[2048]{0:T(1024)(128)(2,1)S(1)}, bf16[2048]{0:T(1024)(128)(2,1)}, u32[]{:S(2)}) copy-start(bf16[2048]{0:T(1024)(128)(2,1)} %param.27) | copy-start | bytes 12292
  146.8 43.6 %copy-start.26 = (bf16[2048,16]{0,1:T(8,128)(2,1)S(1)}, bf16[2048,16]{0,1:T(8,128)(2,1)}, u32[]{:S(2)}) copy-start(bf16[2048,16]{0,1:T(8,128)(2,1)} %param.28) | copy-start | bytes 196612
  189.7 154.0 %collective-permute-start.2 = (bf16[2048,512]{1,0:T(8,128)(2,1)}, bf16[2048,512]{1,0:T(8,128)(2,1)S(1)}, u32[]{:S(2)}, u32[]{:S(2)}) collective-permute-start(bf16[2048,512]{1,0:T(8,128)(2,1)} %collective-permute-done), channel_id=1, source_target_pairs={{0,16},{16,0},{1,17},{17,1},{2,18},{18,2},{3,19},{19,3},{4,20},{20... | collective-permute-start | bytes 6291464 | tf_op jit(solution)/shard_map/ppermute | solution.py:1402
  530.0 10.5 copy-start.31
  530.1 10.5 copy-start.33
  530.1 17.8 %slice-start = ((s8[5242880]{0:T(1024)(128)(4,1)}), s8[4194304]{0:T(1024)(128)(4,1)S(1)}, s32[]{:S(2)}) async-start(s8[5242880]{0:T(1024)(128)(4,1)} %bitcast.102), calls=%async_computation.2 | async-start | bytes 8388608
  631.5 212.4 %collective-permute-start.4 = (bf16[2048,1024]{1,0:T(8,128)(2,1)}, bf16[2048,1024]{1,0:T(8,128)(2,1)}, u32[]{:S(2)}, u32[]{:S(2)}) collective-permute-start(bf16[2048,1024]{1,0:T(8,128)(2,1)} %convolution_convert_fusion.1), channel_id=1, source_target_pairs={{0,1},{1,0},{2,3},{3,2},{4,5},{5,4},{6,7},{7,6},{8,9},{9,8},{10,11... | collective-permute-start | bytes 12582920 | tf_op jit(solution)/shard_map/ppermute | solution.py:1385
  633.9 210.0 %collective-permute-start.3 = (bf16[2048,1024]{1,0:T(8,128)(2,1)}, bf16[2048,1024]{1,0:T(8,128)(2,1)}, u32[]{:S(2)}, u32[]{:S(2)}) collective-permute-start(bf16[2048,1024]{1,0:T(8,128)(2,1)} %convolution_convert_fusion.2), channel_id=1, source_target_pairs={{0,1},{1,0},{2,3},{3,2},{4,5},{5,4},{6,7},{7,6},{8,9},{9,8},{10,11... | collective-permute-start | bytes 12582920 | tf_op jit(solution)/shard_map/ppermute | solution.py:1385
  787.3 42.7 %copy-start.10 = (f32[256,512]{1,0:T(8,128)S(1)}, f32[256,512]{1,0:T(8,128)}, u32[]{:S(2)}) copy-start(f32[256,512]{1,0:T(8,128)} %copy-done.9) | copy-start | bytes 1572868
  787.3 42.7 %copy-start.12 = (f32[256,512]{1,0:T(8,128)S(1)}, f32[256,512]{1,0:T(8,128)}, u32[]{:S(2)}) copy-start(f32[256,512]{1,0:T(8,128)} %copy-done.11) | copy-start | bytes 1572868
  828.4 170.4 %collective-permute-start.5 = (bf16[1024,2048]{1,0:T(8,128)(2,1)}, bf16[1024,2048]{1,0:T(8,128)(2,1)}, u32[]{:S(2)}, u32[]{:S(2)}) collective-permute-start(bf16[1024,2048]{1,0:T(8,128)(2,1)} %convolution_convert_fusion), channel_id=1, source_target_pairs={{0,1},{1,0},{2,3},{3,2},{4,5},{5,4},{6,7},{7,6},{8,9},{9,8},{10,11... | collective-permute-start | bytes 12582920 | tf_op jit(solution)/shard_map/ppermute | solution.py:1385
  843.9 133.3 %copy-start.8 = (bf16[2048,256]{1,0:T(8,128)(2,1)S(1)}, bf16[2048,256]{1,0:T(8,128)(2,1)}, u32[]{:S(2)}) copy-start(bf16[2048,256]{1,0:T(8,128)(2,1)} %get-tuple-element.108.o_ref) | copy-start | bytes 3145732
  983.8 34.8 %collective-permute-start.7 = (bf16[256,2048]{1,0:T(8,128)(2,1)S(1)}, bf16[256,2048]{1,0:T(8,128)(2,1)S(1)}, u32[]{:S(2)}, u32[]{:S(2)}) collective-permute-start(bf16[256,2048]{1,0:T(8,128)(2,1)S(1)} %convolution_convert_fusion.4), channel_id=1, source_target_pairs={{0,1},{1,0},{2,3},{3,2},{4,5},{5,4},{6,7},{7,6},{8,9},{9,8},{10,11... | collective-permute-start | bytes 3145736 | tf_op jit(solution)/shard_map/ppermute | solution.py:1385
  989.8 9.0 copy-start.18
  998.8 12.3 %copy-start.17 = (bf16[2048,1024]{1,0:T(8,128)(2,1)S(1)}, bf16[2048,1024]{1,0:T(8,128)(2,1)}, u32[]{:S(2)}) copy-start(bf16[2048,1024]{1,0:T(8,128)(2,1)} %get-tuple-element.119) | copy-start | bytes 12582916
  1009.6 138.0 %collective-permute-start.6 = (bf16[2048,768]{1,0:T(8,128)(2,1)}, bf16[2048,768]{1,0:T(8,128)(2,1)}, u32[]{:S(2)}, u32[]{:S(2)}) collective-permute-start(bf16[2048,768]{1,0:T(8,128)(2,1)} %convolution_convert_fusion.3), channel_id=1, source_target_pairs={{0,1},{1,0},{2,3},{3,2},{4,5},{5,4},{6,7},{7,6},{8,9},{9,8},{10,11... | collective-permute-start | bytes 9437192 | tf_op jit(solution)/shard_map/ppermute | solution.py:1385
  1020.3 119.8 %copy-start.16 = (bf16[1024,2048]{1,0:T(8,128)(2,1)S(1)}, bf16[1024,2048]{1,0:T(8,128)(2,1)}, u32[]{:S(2)}) copy-start(bf16[1024,2048]{1,0:T(8,128)(2,1)} %get-tuple-element.123) | copy-start | bytes 12582916
  (23 other events, 75.0 us)
Sparse Core Ops, SparseCore 0:
  631.7 195.0 reduce-scatter.1

commit v6 on v5

--- a/solution.py
+++ b/solution.py
@@ -69,6 +69,7 @@
         self.below = (grp, wide - 2, narrow)
         self.has_above, self.has_below = self.line < LINE - 1, self.line > 0
         self.targets = [(self.across, None), (self.above, self.has_above), (self.below, self.has_below)]
+        self.arrived = lambda i, slot: None
 
     def copy(self, i, source_line, way, device):
         slot = source_line * 2 + self.cross
@@ -89,6 +90,7 @@
             pl.when(self.has_below)(self.own(i, 2, self.below).start)
             self.own(i, 0, self.across).start()
             self.mine(i).start()
+            self.arrived(i, None)
 
     def forward(self, distance, only=None):
         for i in range(len(self.ins)) if only is None else (only,):
@@ -105,6 +107,7 @@
                         self.copy(i, source, 1 if sign < 0 else 2, onward).start()
 
                     self.copy(i, source, 0, self.across).start()
+                    self.arrived(i, source * 2 + self.cross)
 
     def finish(self):
         for i in range(len(self.ins)):
@@ -112,6 +115,7 @@
             for source in range(LINE):
                 other = source * 2 + 1 - self.cross
                 remote(src, out.at[other], send.at[i, 0, 0], recv.at[i, other], self.across).wait_recv()
+                self.arrived(i, other)
             for source in range(LINE):
                 remote(src, out.at[0], send.at[i, 0, source], recv.at[i, 0], self.across).wait_send()
 
@@ -134,8 +138,10 @@
     ]
 
 
-def gather_body(count, ins, outs, send, recv, local, more=(), begin=None, finish=None):
+def gather_body(count, ins, outs, send, recv, local, more=(), begin=None, finish=None, arrived=None):
     gather = Gather(ins, outs, send, recv, local)
+    if arrived is not None:
+        gather.arrived = arrived
     greet([*gather.targets, *more])
     gather.start()
     if begin is not None:
@@ -673,29 +679,22 @@
         return pltpu.CompilerParams(vmem_limit_bytes=60 * 2**20, collective_id=ids[k], has_side_effects=True)
 
     carried = 1 if size == 2 * LINE else 0
-    forward_call = pl.pallas_call(
-        functools.partial(attend_kernel, rows, prompt_blocks, paired, shared, carried),
+    forward = pl.pallas_call(
+        functools.partial(attend_kernel, rows, prompt_blocks, paired, shared, 0),
         out_shape=[shape(bf16, half, columns)] * 3
         + [shape(bf16, shared, columns)] * 2
-        + [shape(bf16, half, columns), shape(bf16, rows, size * columns), shape(f32, heads, half), shape(f32, 8, half)]
-        + [shape(bf16, size, rows, D)] * carried,
-        in_specs=[VMEM] * 4 + [ANY] * carried,
-        out_specs=[VMEM] * 9 + [ANY] * carried,
+        + [shape(bf16, half, columns), shape(bf16, rows, size * columns), shape(f32, heads, half), shape(f32, 8, half)],
+        in_specs=[VMEM] * 4,
+        out_specs=[VMEM] * 9,
         scratch_shapes=[
             pltpu.VMEM((columns, half), bf16),
             pltpu.VMEM((columns, shared), bf16),
             pltpu.VMEM((size - 1, 8, half), f32),
         ]
-        + peers
-        + gather_sems(carried) * carried,
+        + peers,
         compiler_params=params(0),
         cost_estimate=pl.CostEstimate(flops=0, bytes_accessed=300_000_000, transcendentals=0),
     )
-
-    def forward(raw, gains, cosine, sine, carry):
-        if carried:
-            return forward_call(raw, gains, cosine, sine, carry)
-        return [*forward_call(raw, gains, cosine, sine), lax.all_gather(carry, "wide", axis=0)]
 
     backward_call = pl.pallas_call(
         functools.partial(attend_back_kernel, rows, prompt_blocks, paired, shared, carried),
@@ -738,14 +737,16 @@
     return lax.dot_general(a, b, (((0,), (0,)), ((), ())), preferred_element_type=jnp.float32)
 
 
-def start_kernel(count, swaps, *refs):
+def start_kernel(count, swaps, spread, *refs):
     ins, given = refs[:count], refs[count : count + swaps]
-    outs = refs[count + swaps : 2 * count + swaps]
-    got = refs[2 * count + swaps : 2 * (count + swaps)]
-    send, recv, local, swap_send, swap_recv, twin_send, twin_recv = refs[2 * (count + swaps) :]
+    refs = refs[count + swaps :]
+    outs, got, pieces = refs[:count], refs[count : count + swaps], refs[count + swaps : count + swaps + 3 * spread]
+    refs = refs[count + swaps + 3 * spread :]
+    send, recv, local, swap_send, swap_recv, twin_send, twin_recv = refs[:7]
     grp, wide, narrow, line, cross = position()
     partner = (grp, wide, 1 - narrow)
     twin = (1 - grp, wide, narrow)
+    size = 2 * LINE
 
     def half(ref, which):
         size = ref.shape[0] // 2
@@ -757,11 +758,34 @@
     def share(i, which):
         return remote(half(got[i], which), half(got[i], which), twin_send.at[i], twin_recv.at[i], twin)
 
+    def piece(k, slot):
+        piece_send, piece_recv = refs[7:]
+        src = pieces[0] if k == 2 else outs[-1]
+        device = twin if k else partner
+        return remote(src.at[slot], pieces[k].at[slot], piece_send.at[k, slot], piece_recv.at[k, slot], device)
+
+    def own_piece(k):
+        piece_send, piece_recv = refs[7:]
+        device = twin if k else partner
+        return remote(ins[-1], pieces[k].at[wide], piece_send.at[k, wide], piece_recv.at[k, wide], device)
+
+    def arrived(i, slot):
+        if i == count - 1:
+            for k in range(2):
+                if slot is None:
+                    own_piece(k).start()
+                else:
+                    piece(k, slot).start()
+
     def begin():
         for i in range(swaps):
             swap(i).start()
 
     def finish():
+        if spread:
+            for slot in range(size):
+                piece(0, slot).wait_recv()
+                piece(2, slot).start()
         for i in range(swaps):
             swap(i).wait_recv()
             share(i, grp).start()
@@ -769,32 +793,34 @@
             swap(i).wait_send()
             share(i, grp).wait_send()
             share(i, 1 - grp).wait_recv()
-
-    gather_body(count, ins, outs, send, recv, local, [(partner, None), (twin, None)], begin, finish)
-
-
-def start_exchange(arrays, weights, collective_id):
+        if spread:
+            for slot in range(size):
+                piece(0, slot).wait_send()
+                piece(1, slot).wait()
+                piece(2, slot).wait()
+
+    more = [(partner, None), (twin, None)]
+    gather_body(count, ins, outs, send, recv, local, more, begin, finish, arrived if spread else None)
+
+
+def start_exchange(arrays, weights, collective_id, spread=False):
     size = lax.axis_size("wide")
+    swap = [(0, 1), (1, 0)]
     if size != 2 * LINE or lax.axis_size("grp") != 2:
-        swap = [(0, 1), (1, 0)]
-        return [lax.all_gather(a, "wide", axis=0) for a in arrays], [lax.ppermute(w, "narrow", swap) for w in weights]
-    count, swaps = len(arrays), len(weights)
+        return [lax.all_gather(a, "wide", axis=0) for a in arrays], [lax.ppermute(w, "narrow", swap) for w in weights], []
+    count, swaps, spread = len(arrays), len(weights), int(spread)
+    gathered = [jax.ShapeDtypeStruct((size, *a.shape), a.dtype) for a in arrays]
+    dma = pltpu.SemaphoreType.DMA
     out = pl.pallas_call(
-        functools.partial(start_kernel, count, swaps),
-        out_shape=[jax.ShapeDtypeStruct((size, *a.shape), a.dtype) for a in arrays]
-        + [jax.ShapeDtypeStruct(w.shape, w.dtype) for w in weights],
+        functools.partial(start_kernel, count, swaps, spread),
+        out_shape=gathered + [jax.ShapeDtypeStruct(w.shape, w.dtype) for w in weights] + gathered[-1:] * 3 * spread,
         in_specs=[ANY] * (count + swaps),
-        out_specs=[ANY] * (count + swaps),
-        scratch_shapes=[
-            pltpu.SemaphoreType.DMA((count, 3, LINE)),
-            pltpu.SemaphoreType.DMA((count, size)),
-            pltpu.SemaphoreType.DMA((count,)),
-        ]
-        + [pltpu.SemaphoreType.DMA((swaps,))] * 4,
+        out_specs=[ANY] * (count + swaps + 3 * spread),
+        scratch_shapes=gather_sems(count) + [dma((swaps,))] * 4 + [dma((3, size))] * 2 * spread,
         compiler_params=pltpu.CompilerParams(collective_id=collective_id, has_side_effects=True),
-        cost_estimate=lasts(150),
+        cost_estimate=lasts(120),
     )(*arrays, *weights)
-    return out[:count], out[count:]
+    return out[:count], out[count : count + swaps], out[count + swaps :]
 
 
 def expert_grad_kernel(
@@ -1174,72 +1200,106 @@
     )(joined, weights, tokens, grad_hidden, gain, small)
 
 
-def expert_kernel(
-    tiles, capacity, experts, first, id_ref, slot_ref, tokens_ref, grads_ref, router_ref, gate_ref, up_ref, down_ref, *refs
+def pick_rows(step, capacity, slot_ref, source_ref, picks, held, out_ref):
+    row = lax.broadcasted_iota(jnp.int32, (capacity, source_ref.shape[1]), 0)
+    pick = jnp.where(row == slot_ref[0], 1.0, 0.0).astype(jnp.bfloat16)
+    picks[step] = pick
+    values = dot(pick, source_ref[0]).astype(jnp.bfloat16)
+    held[pl.ds(pl.multiple_of(step * capacity, capacity), capacity)] = values
+    out_ref[...] = values
+
+
+def spread_rows(block, capacity, picks, total, before_ref, out_ref):
+    here = pl.ds(pl.multiple_of(block * capacity, capacity), capacity)
+    values = dot_tn(picks[block], total[here].astype(jnp.bfloat16))
+    if before_ref is not None:
+        values = values + before_ref[0].astype(jnp.float32)
+    out_ref[0] = values.astype(jnp.bfloat16)
+
+
+def expert_forward_kernel(
+    tiles, capacity, experts, first, id_ref, slot_ref, tokens_ref, router_ref, gate_ref, up_ref, down_ref, *refs
 ):
-    if not first:
-        moe_in_ref, part_in_ref, router_in_ref = refs[:3]
-        refs = refs[3:]
-    (
-        moe_ref, part_ref, x_ref, g_ref, inner_ref, grad_gate_ref, grad_up_ref, router_grad_ref,
-        x_all, g_all, picks, moe_all, part_all, probs_all, scores_all, router_sum,
-    ) = refs
-    f32, bf16 = jnp.float32, jnp.bfloat16
-    group, step = pl.program_id(0), pl.program_id(1)
+    before_ref = None if first else refs[0]
+    moe_ref, x_ref, inner_ref, gate_pre_ref, up_pre_ref, probs_ref, x_all, picks, moe_all = refs[0 if first else 1 :]
+    step = pl.program_id(1)
     blocks = picks.shape[0]
-    expert = id_ref[0]
     lane = lax.broadcasted_iota(jnp.int32, (1, 128), 1)
 
     @pl.when(step < blocks)
     def _():
-        rows = tokens_ref.shape[1]
-        row = lax.broadcasted_iota(jnp.int32, (capacity, rows), 0)
-        pick = jnp.where(row == slot_ref[0], 1.0, 0.0).astype(bf16)
-        picks[step] = pick
-        here = pl.ds(pl.multiple_of(step * capacity, capacity), capacity)
-        x = dot(pick, tokens_ref[0]).astype(bf16)
-        g = dot(pick, grads_ref[0]).astype(bf16)
-        x_all[here], x_ref[...] = x, x
-        g_all[here], g_ref[...] = g, g
+        pick_rows(step, capacity, slot_ref, tokens_ref, picks, x_all, x_ref)
 
     @pl.when(step == blocks)
     def _():
         logits = jnp.where(lane < experts, dot(x_all[...], router_ref[...]), NEGATIVE)
         weight = jnp.exp(logits - jnp.max(logits, -1, keepdims=True))
-        probs_all[...] = weight / jnp.sum(weight, -1, keepdims=True)
+        probs_ref[...] = weight / jnp.sum(weight, -1, keepdims=True)
         moe_all[...] = jnp.zeros_like(moe_all)
+
+    @pl.when((step >= blocks) & (step < blocks + tiles))
+    def _():
+        x = x_all[...]
+        gate = jnp.sum(jnp.where(lane == id_ref[0], probs_ref[...], 0.0), -1, keepdims=True)
+        gate_pre = dot(x, gate_ref[...])
+        up_pre = dot(x, up_ref[...])
+        gate_pre_ref[...] = gate_pre
+        up_pre_ref[...] = up_pre
+        inner_gated = (gate * (gate_pre / (1.0 + jnp.exp(-gate_pre))) * up_pre).astype(jnp.bfloat16)
+        inner_ref[...] = inner_gated
+        moe_all[...] += dot(inner_gated, down_ref[...])
+
+    @pl.when(step >= blocks + tiles)
+    def _():
+        spread_rows(step - blocks - tiles, capacity, picks, moe_all, before_ref, moe_ref)
+
+
+def expert_backward_kernel(
+    tiles, capacity, first, id_ref, slot_ref, grads_ref, x_ref, probs_ref, gate_pre_ref, up_pre_ref,
+    router_ref, gate_ref, up_ref, down_ref, *refs
+):
+    before_ref, router_in_ref = (None, None) if first else refs[:2]
+    (
+        part_ref, g_ref, grad_gate_ref, grad_up_ref, router_grad_ref,
+        g_all, picks, part_all, scores_all, router_sum,
+    ) = refs[0 if first else 2 :]
+    bf16 = jnp.bfloat16
+    group, step = pl.program_id(0), pl.program_id(1)
+    blocks = picks.shape[0]
+    lane = lax.broadcasted_iota(jnp.int32, (1, 128), 1)
+    here = jnp.where(lane == id_ref[0], 1.0, 0.0)
+
+    @pl.when(step < blocks)
+    def _():
+        pick_rows(step, capacity, slot_ref, grads_ref, picks, g_all, g_ref)
+
+    @pl.when(step == blocks)
+    def _():
         part_all[...] = jnp.zeros_like(part_all)
         scores_all[...] = jnp.zeros_like(scores_all)
 
     @pl.when((step >= blocks) & (step < blocks + tiles))
     def _():
-        x, g = x_all[...], g_all[...]
-        gate = jnp.sum(jnp.where(lane == expert, probs_all[...], 0.0), -1, keepdims=True)
-        gate_pre = dot(x, gate_ref[...])
-        up_pre = dot(x, up_ref[...])
-        back = dot_nt(g, down_ref[...])
+        gate = jnp.sum(probs_ref[...] * here, -1, keepdims=True)
+        gate_pre, up_pre = gate_pre_ref[...], up_pre_ref[...]
+        back = dot_nt(g_all[...], down_ref[...])
         sigmoid = 1.0 / (1.0 + jnp.exp(-gate_pre))
         silu = gate_pre * sigmoid
-        inner = silu * up_pre
-        scores_all[...] += jnp.sum(inner * back, -1, keepdims=True)
-        inner_gated = (gate * inner).astype(bf16)
+        scores_all[...] += jnp.sum(silu * up_pre * back, -1, keepdims=True)
         back = gate * back
         grad_gate_pre = (back * up_pre * sigmoid * (1.0 + gate_pre * (1.0 - sigmoid))).astype(bf16)
         grad_up_pre = (back * silu).astype(bf16)
-        inner_ref[...] = inner_gated
         grad_gate_ref[...] = grad_gate_pre
         grad_up_ref[...] = grad_up_pre
-        moe_all[...] += dot(inner_gated, down_ref[...])
         part_all[...] += dot_nt(grad_gate_pre, gate_ref[...]) + dot_nt(grad_up_pre, up_ref[...])
 
     @pl.when(step == blocks + tiles)
     def _():
-        probs = probs_all[...]
-        here = jnp.where(lane == expert, 1.0, 0.0)
+        probs = probs_ref[...]
         gate = jnp.sum(probs * here, -1, keepdims=True)
         mixing = (gate * scores_all[...] * (here - probs)).astype(bf16)
         part_all[...] += dot_nt(mixing, router_ref[...])
-        grad = dot_tn(mixing, x_all[...])
+        grad = dot_tn(mixing, x_ref[...])
 
         @pl.when(group == 0)
         def _():
@@ -1253,81 +1313,97 @@
 
     @pl.when(step >= blocks + tiles)
     def _():
-        block = step - blocks - tiles
-        pick = picks[block]
-        here = pl.ds(pl.multiple_of(block * capacity, capacity), capacity)
-        moe = dot_tn(pick, moe_all[here].astype(bf16))
-        part = dot_tn(pick, part_all[here].astype(bf16))
-        if not first:
-            moe = moe + moe_in_ref[0].astype(f32)
-            part = part + part_in_ref[0].astype(f32)
-        moe_ref[0] = moe.astype(bf16)
-        part_ref[0] = part.astype(bf16)
-
-
-def expert_call(expert, slots, tokens, grads, router, weights, capacity, experts, before=None):
-    wide, rows, _ = tokens.shape
-    units = weights[0].shape[1]
-    groups = 2 if wide * capacity > 1024 else 1
-    blocks, tile = wide // groups, 256
-    tiles = units // tile
-    last = blocks + tiles
-    first = before is None
-    bf16, f32 = jnp.bfloat16, jnp.float32
-
-    def picked(g, i):
-        return g * blocks + jnp.minimum(i, blocks - 1)
-
-    def tiled(i):
-        return jnp.clip(i - blocks, 0, tiles - 1)
-
-    def spread(g, i):
-        return g * blocks + jnp.clip(i - last, 0, blocks - 1)
-
-    whole = pl.BlockSpec((1, rows, D), lambda g, i: (picked(g, i), 0, 0))
-    back = pl.BlockSpec((1, rows, D), lambda g, i: (spread(g, i), 0, 0))
-    row = pl.BlockSpec((capacity, D), lambda g, i: (picked(g, i), 0))
-    column = pl.BlockSpec((D, tile), lambda g, i: (0, tiled(i)))
-    unit = pl.BlockSpec((blocks * capacity, tile), lambda g, i: (g, tiled(i)))
-    fixed = pl.BlockSpec((128, D), lambda g, i: (0, 0))
-    in_specs = [
-        pl.BlockSpec(memory_space=pltpu.SMEM),
-        pl.BlockSpec((1, 1, rows), lambda g, i: (picked(g, i), 0, 0)),
-        whole,
-        whole,
-        pl.BlockSpec((D, 128), lambda g, i: (0, 0)),
-        column,
-        column,
-        pl.BlockSpec((tile, D), lambda g, i: (tiled(i), 0)),
-    ] + ([] if first else [back, back, fixed])
-    count = wide * capacity
-    compact = jax.ShapeDtypeStruct((count, D), bf16)
-    narrow = jax.ShapeDtypeStruct((count, units), bf16)
-    held = blocks * capacity
-    return pl.pallas_call(
-        functools.partial(expert_kernel, tiles, capacity, experts, first),
-        grid=(groups, last + blocks),
-        in_specs=in_specs,
-        out_specs=[back, back, row, row, unit, unit, unit, fixed],
-        out_shape=[jax.ShapeDtypeStruct((wide, rows, D), bf16)] * 2
-        + [compact] * 2
-        + [narrow] * 3
-        + [jax.ShapeDtypeStruct((128, D), f32)],
-        scratch_shapes=[
-            pltpu.VMEM((held, D), bf16),
-            pltpu.VMEM((held, D), bf16),
-            pltpu.VMEM((blocks, capacity, rows), bf16),
-            pltpu.VMEM((held, D), f32),
-            pltpu.VMEM((held, D), f32),
-            pltpu.VMEM((held, 128), f32),
-            pltpu.VMEM((held, 1), f32),
-            pltpu.VMEM((128, D), f32),
-        ],
-        compiler_params=pltpu.CompilerParams(vmem_limit_bytes=60 * 2**20),
-        cost_estimate=pl.CostEstimate(
-            flops=0, bytes_accessed=250_000_000, transcendentals=0
-        ),
-    )(expert.astype(jnp.int32).reshape(1), slots, tokens, grads, router, *weights, *(before or ()))
+        spread_rows(step - blocks - tiles, capacity, picks, part_all, before_ref, part_ref)
+
+
+class Expert:
+    def __init__(self, expert, slots, router, weights, capacity, experts):
+        self.scalars = expert.astype(jnp.int32).reshape(1), slots
+        self.router, self.weights, self.capacity, self.experts = router, weights, capacity, experts
+        wide, _, rows = slots.shape
+        units = weights[0].shape[1]
+        groups = 2 if wide * capacity > 1024 else 1
+        blocks, tile = wide // groups, 256
+        tiles = units // tile
+        last = blocks + tiles
+        self.tiles, self.grid = tiles, (groups, last + blocks)
+        self.held, self.blocks, self.rows = blocks * capacity, blocks, rows
+        count = wide * capacity
+
+        def picked(g, i):
+            return g * blocks + jnp.minimum(i, blocks - 1)
+
+        def tiled(i):
+            return jnp.clip(i - blocks, 0, tiles - 1)
+
+        self.whole = pl.BlockSpec((1, rows, D), lambda g, i: (picked(g, i), 0, 0))
+        self.back = pl.BlockSpec((1, rows, D), lambda g, i: (g * blocks + jnp.clip(i - last, 0, blocks - 1), 0, 0))
+        self.row = pl.BlockSpec((capacity, D), lambda g, i: (picked(g, i), 0))
+        column = pl.BlockSpec((D, tile), lambda g, i: (0, tiled(i)))
+        self.unit = pl.BlockSpec((self.held, tile), lambda g, i: (g, tiled(i)))
+        self.fixed = pl.BlockSpec((128, D), lambda g, i: (0, 0))
+        self.rows_all = pl.BlockSpec((self.held, D), lambda g, i: (g, 0))
+        self.probs = pl.BlockSpec((self.held, 128), lambda g, i: (g, 0))
+        self.heads = [
+            pl.BlockSpec(memory_space=pltpu.SMEM), pl.BlockSpec((1, 1, rows), lambda g, i: (picked(g, i), 0, 0))
+        ]
+        self.weight_specs = [
+            pl.BlockSpec((D, 128), lambda g, i: (0, 0)), column, column,
+            pl.BlockSpec((tile, D), lambda g, i: (tiled(i), 0)),
+        ]
+        shape = jax.ShapeDtypeStruct
+        self.blocks_shape = shape((wide, rows, D), jnp.bfloat16)
+        self.compact = shape((count, D), jnp.bfloat16)
+        self.narrow = shape((count, units), jnp.bfloat16)
+        self.narrow32 = shape((count, units), jnp.float32)
+        self.probs_shape = shape((count, 128), jnp.float32)
+        self.common = dict(
+            grid=self.grid,
+            compiler_params=pltpu.CompilerParams(vmem_limit_bytes=60 * 2**20),
+            cost_estimate=pl.CostEstimate(flops=0, bytes_accessed=120_000_000, transcendentals=0),
+        )
+
+    def forward(self, tokens, before):
+        first = before is None
+        f32, bf16 = jnp.float32, jnp.bfloat16
+        return pl.pallas_call(
+            functools.partial(expert_forward_kernel, self.tiles, self.capacity, self.experts, first),
+            in_specs=self.heads + [self.whole] + self.weight_specs + ([] if first else [self.back]),
+            out_specs=[self.back, self.row, self.unit, self.unit, self.unit, self.probs],
+            out_shape=[
+                self.blocks_shape, self.compact, self.narrow, self.narrow32, self.narrow32, self.probs_shape
+            ],
+            scratch_shapes=[
+                pltpu.VMEM((self.held, D), bf16),
+                pltpu.VMEM((self.blocks, self.capacity, self.rows), bf16),
+                pltpu.VMEM((self.held, D), f32),
+            ],
+            **self.common,
+        )(*self.scalars, tokens, self.router, *self.weights, *(() if first else (before,)))
+
+    def backward(self, grads, kept, before):
+        first = before is None
+        f32, bf16 = jnp.float32, jnp.bfloat16
+        _, x, _, gate_pre, up_pre, probs = kept
+        return pl.pallas_call(
+            functools.partial(expert_backward_kernel, self.tiles, self.capacity, first),
+            in_specs=self.heads
+            + [self.whole, self.rows_all, self.probs, self.unit, self.unit]
+            + self.weight_specs
+            + ([] if first else [self.back, self.fixed]),
+            out_specs=[self.back, self.row, self.unit, self.unit, self.fixed],
+            out_shape=[
+                self.blocks_shape, self.compact, self.narrow, self.narrow, jax.ShapeDtypeStruct((128, D), f32)
+            ],
+            scratch_shapes=[
+                pltpu.VMEM((self.held, D), bf16),
+                pltpu.VMEM((self.blocks, self.capacity, self.rows), bf16),
+                pltpu.VMEM((self.held, D), f32),
+                pltpu.VMEM((self.held, 1), f32),
+                pltpu.VMEM((128, D), f32),
+            ],
+            **self.common,
+        )(*self.scalars, grads, x, probs, gate_pre, up_pre, self.router, *self.weights, *(before or ()))
 
 
 def positions(token_ids):
@@ -1394,12 +1470,11 @@
     piece_width = D // pieces
     piece_id = group * narrow_count + side if twins else 0
     piece = lax.dynamic_slice_in_dim(w_out, piece_id * piece_width, piece_width, 1)
-    (routes_plane, normed_plane, out_piece), (other_up,) = start_exchange([routes.T, normed, piece], [w_up[0]], 0)
+    (routes_plane, normed_plane, out_piece), (other_up,), others = start_exchange(
+        [routes.T, normed, piece], [w_up[0]], 0, twins
+    )
     normed_plane = normed_plane.reshape(half, D)
-    out_pieces = [out_piece.reshape(D, piece_width)]
-    if twins:
-        out_pieces.append(exchange(out_pieces[0]))
-        out_pieces += [lax.ppermute(p, "grp", swap) for p in out_pieces]
+    out_pieces = [p.reshape(D, piece_width) for p in (out_piece, *others)]
 
     def ordered(parts):
         if not twins:
@@ -1410,6 +1485,8 @@
     def unordered(whole):
         return ordered([whole[:, k * piece_width : (k + 1) * piece_width] for k in range(pieces)])
 
+    grad_final_b, _ = barrier((grad_final.astype(bf16), normed_plane))
+    grads_in = lax.all_gather(grad_final_b, "wide", axis=0, tiled=True).reshape(wide_count, rows, D)
     joined = jnp.concatenate([w_query, w_key, w_value], 1)
     raw = dot(normed_plane, joined)
     gains = jnp.pad(jnp.stack([norm_query, norm_key]).astype(f32), ((0, 6), (0, 0)))
@@ -1418,15 +1495,15 @@
         + jnp.arange(rows, dtype=jnp.int32)[None, :]
     ).reshape(half)
     cosine, sine = rotation(positions(plane_ids))
-    kept = attend(raw, gains, cosine, sine, grad_final.astype(bf16))
-    attended, attended_own, lse, sums, grads_in = kept[5:]
+    kept = attend(raw, gains, cosine, sine)
+    attended, attended_own, lse, sums = kept[5:]
 
     branch = jnp.concatenate(ordered([dot(attended_own, p) for p in out_pieces]), 1)
     hidden = stream + branch
     inv_two = lax.rsqrt(jnp.mean(hidden * hidden, -1, keepdims=True) + EPSILON)
     gain_two = norm_moe.astype(f32)
     moe_in = (hidden * inv_two * gain_two).astype(bf16)
-    (tokens_in,), (other_gate, other_down) = start_exchange([moe_in], [w_gate[0], w_down[0]], 6)
+    (tokens_in,), (other_gate, other_down), _ = start_exchange([moe_in], [w_gate[0], w_down[0]], 6)
 
     earlier = (jnp.arange(rows)[:, None] < jnp.arange(rows)[None, :]).astype(bf16)
 
@@ -1437,20 +1514,27 @@
 
     router = jnp.pad(w_router, ((0, 0), (0, 128 - experts)))
 
-    def run_expert(expert, weights, before):
-        return expert_call(
-            expert, slots_of(expert), tokens_in, grads_in, router, weights, capacity, experts, before
+    own, other = (
+        Expert(e, slots_of(e), router, w, capacity, experts)
+        for e, w in (
+            (place * narrow_count + side, (w_gate[0], w_up[0], w_down[0])),
+            (place * narrow_count + 1 - side, (other_gate, other_up, other_down)),
         )
-
-    other = run_expert(place * narrow_count + 1 - side, (other_gate, other_up, other_down), None)
-    partner_grads = plain_grads(*other[2:7])
+    )
+    kept_own = own.forward(tokens_in, None)
+    kept_other = other.forward(tokens_in, kept_own[0])
+    moe_part = kept_other[0]
+    moe = lax.psum_scatter(moe_part.reshape(half, D), "wide", scatter_dimension=0, tiled=True).astype(f32)
+    kept_other, grads_in, _ = barrier((kept_other, grads_in, moe_part))
+    back_other = other.backward(grads_in, kept_other, None)
+    partner_grads = plain_grads(kept_other[1], back_other[1], kept_other[2], back_other[2], back_other[3])
     came = [exchange(g) for g in partner_grads[:2]]
-    before, partner_grads = barrier(((other[0], other[1], other[7]), partner_grads))
-    own = run_expert(place * narrow_count + side, (w_gate[0], w_up[0], w_down[0]), before)
-    moe_part, grad_part, grad_router = own[0], own[1], own[7][:experts]
-    moe = lax.psum_scatter(moe_part.reshape(half, D), "wide", scatter_dimension=0, tiled=True).astype(f32)
-    grad_moe_in, *own_grads = expert_grad(grad_part, own[2:7], 5)
-    grad_moe_in, moe, down_grad = barrier((grad_moe_in, moe, partner_grads[2]))
+    before, partner_grads = barrier(((back_other[0], back_other[4]), partner_grads))
+    back_own = own.backward(grads_in, kept_own, before)
+    grad_part, grad_router = back_own[0], back_own[4][:experts]
+    own_operands = (kept_own[1], back_own[1], kept_own[2], back_own[2], back_own[3])
+    grad_moe_in, *own_grads = expert_grad(grad_part, own_operands, 5)
+    grad_moe_in, moe, came[0], down_grad = barrier((grad_moe_in, moe, came[0], partner_grads[2]))
     came.append(exchange(down_grad))
 
     grad_gain_two = jnp.sum(grad_moe_in * hidden * inv_two, 0)
@@ -1461,11 +1545,10 @@
     )
     grad_branch = grad_hidden.astype(bf16)
     grad_attended_own = sum(dot_nt(g, p) for g, p in zip(unordered(grad_branch), out_pieces)).astype(bf16)
-    grad_attended_own, came[0], came[1] = barrier((grad_attended_own, came[0], came[1]))
     grads_joined, gain_grads, branch_plane = attend_back(
         raw, gains, cosine, sine, sums, *kept[:5], grad_attended_own, attended, lse, grad_branch
     )
-    grads_joined, came[2] = barrier((grads_joined, came[2]))
+    grads_joined, came[1], came[2] = barrier((grads_joined, came[1], came[2]))
     grad_out = barrier(dot_tn(attended, branch_plane.reshape(half, D)).astype(bf16))
     grad_weights = barrier(dot_tn(normed_plane, grads_joined).astype(bf16))
     weights_came = exchange(grad_weights)

time: 1170 us -> 1090 us (0.932)
  waiting for transfers between devices: 70.6 us -> 0.09 us
    pallas_call x1, Pallas kernels: 152 us -> 97.8 us  [expert_grad(): pl.pallas_call(expert_grad_kernel, out_shape=[jax.ShapeDtypeStruct((rows,...]
    pallas_call x5 -> x7, Pallas kernels: 524 us -> 578 us  [the longest x2 285 us: start_exchange(): pl.pallas_call(functools.partial(start_kernel, count, swaps, spread), out...]
    reduce_scatter x1, waiting for transfers between devices: 39.5 us -> 0.02 us  [shards(): lax.psum_scatter(moe_part.reshape(half, D), 'wide', scatter_dimension=0,...]
    ppermute x6 -> x5, waiting for transfers between devices: 31.1 us -> 0.01 us  [exchange(): return lax.ppermute(value, 'narrow', swap)]
  transfers between devices with their start and end apart: 9 -> 7, of which waited for: 2 -> 0; matrix products, arithmetic and copies ran while one was open for 9% -> 11% of each run, Pallas kernels for 46% -> 72%
where the time goes in v6:
time: 1090 us; the launch traced here: 1080 us
  Pallas kernels  918 us (84%)
  matrix products  62 us (6%)
  other arithmetic  54.2 us (5%)
  local copies, waits for them, and re-layouts  26.9 us (2%)
  between operations  15.7 us (1%)
    pallas_call x2, Pallas kernels, start_exchange(): pl.pallas_call(functools.partial(start_kernel, count, swaps, spread), out...  285 us
    pallas_call x1, Pallas kernels, backward(): return backward_call(*args)  130 us
    pallas_call x2, Pallas kernels, backward(): pl.pallas_call(functools.partial(expert_backward_kernel, self.tiles, self...  117 us
    pallas_call x1, Pallas kernels, input_grad(): pl.pallas_call(functools.partial(input_grad_kernel, gain_row), out_shape=...  112 us
    pallas_call x1, Pallas kernels, expert_grad(): pl.pallas_call(expert_grad_kernel, out_shape=[jax.ShapeDtypeStruct((rows,...  97.8 us
    pallas_call x1, Pallas kernels, shards(): kept = attend(raw, gains, cosine, sine)  91.6 us
    pallas_call x2, Pallas kernels, forward(): pl.pallas_call(functools.partial(expert_forward_kernel, self.tiles, self....  84.8 us
    dot_general x5, matrix products, dot_tn(): lax.dot_general(a, b, (((0,), (0,)), ((), ())), preferred_element_type=jn...  44.5 us
  transfers between devices with their start and end apart: 7, of which 0 were waited for; matrix products, arithmetic and copies ran while one was open for 11% of the time, Pallas kernels for 72%

profile of v6, /device:TPU:0, one launch (start us, length us, event | category | flops | bytes accessed | tf_op | source)
XLA Modules:
  0.0 1081.9 jit_solution(17905901784697109120)
XLA Ops:
  8.1 3.7 fusion.3
  13.9 137.0 %shard_map.271 = (s32[8,8,256]{2,1,0:T(8,128)}, bf16[8,256,2048]{2,1,0:T(8,128)(2,1)}, bf16[8,256,512]{2,1,0:T(8,128)(2,1)}, bf16[2048,1024]{1,0:T(8,128)(2,1)},...) custom-call(s32[8,256]{1,0:T(8,128)} %bitcast.106, ...), custom_call_target="tpu_custom_call" | custom-call | bytes 360000000 | tf_op jit(solution)/shard_map/pallas_call | solution.py:814
  156.8 3.7 fusion.10
  162.5 8.7 fusion.34.raw_ref
  171.2 91.6 %shard_map.272 = (bf16[2048,256]{1,0:T(8,128)(2,1)}, bf16[2048,256]{1,0:T(8,128)(2,1)}, bf16[2048,256]{1,0:T(8,128)(2,1)}, bf16[1024,256]{1,0:T(8,128)(2,1)}, bf...) custom-call(f32[2048,768]{1,0:T(8,128)} %fusion.34.raw_ref, ...), custom_call_target="tpu_custom_call" | custom-call | bytes 300000000 | tf_op jit(solution)/shard_map/pallas_call | solution.py:1498
  270.7 147.8 %shard_map.273 = (bf16[8,256,2048]{2,1,0:T(8,128)(2,1)}, bf16[2048,1024]{1,0:T(8,128)(2,1)}, bf16[1024,2048]{1,0:T(8,128)(2,1)}) custom-call(bf16[256,2048]{1,0:T(8,128)(2,1)} %multiply_convert_fusion.refs_0_, bf16[2048,1024]{1,0:T(8,128)(2,1)} %bitcast.82, bf16[1024,2048]{1,0:T(8,128)(2,1)} %bitcast.85), custom_call_target="tpu_custom_call" | custom-call | bytes 360000000 | tf_op jit(solution)/shard_map/pallas_call | solution.py:814
  418.5 41.0 %shard_map.274 = (bf16[8,256,2048]{2,1,0:T(8,128)(2,1)}, bf16[1280,2048]{1,0:T(8,128)(2,1)}, bf16[1280,1024]{1,0:T(8,128)(2,1)}, f32[1280,1024]{1,0:T(8,128)}, f...) custom-call(s32[1]{0:T(128)} %bitcast.7.id_ref, s32[8,1,256]{2,1,0:T(1,128)} %reshape.202.slot_ref, ...), custom_call_target="tpu_custom_call" | custom-call | bytes 120000000 | tf_op jit(solution)/shard_map/pallas_call | solution.py:1369
  459.5 43.8 %shard_map.275 = (bf16[8,256,2048]{2,1,0:T(8,128)(2,1)}, bf16[1280,2048]{1,0:T(8,128)(2,1)}, bf16[1280,1024]{1,0:T(8,128)(2,1)}, f32[1280,1024]{1,0:T(8,128)}, f...) custom-call(s32[1]{0:T(128)} %bitcast.8.id_ref, s32[8,1,256]{2,1,0:T(1,128)} %copy.32.slot_ref, ...), custom_call_target="tpu_custom_call" | custom-call | bytes 120000000 | tf_op jit(solution)/shard_map/pallas_call | solution.py:1369
  503.4 57.4 %shard_map.276 = (bf16[8,256,2048]{2,1,0:T(8,128)(2,1)}, bf16[1280,2048]{1,0:T(8,128)(2,1)}, bf16[1280,1024]{1,0:T(8,128)(2,1)}, bf16[1280,1024]{1,0:T(8,128)(2,1)}, f32[128,2048]{1,0:T(8,128)}) custom-call(s32[1]{0:T(128)} %bitcast.8.id_ref, s32[8,1,256]{2,1,0:T(1,128)} %copy.32.slot_ref, bf16[8,256,2048]{2,1,0:T(8,128)(2,1)} %bitcast.88, ...), custom_call_target="tpu_custom_call" | custom-call | bytes 120000000 | tf_op jit(solution)/shard_map/pallas_call | solution.py:1388
  560.9 10.2 convolution_convert_fusion.2
  573.6 10.4 convolution_convert_fusion.1
  584.1 7.4 convolution_convert_fusion
  591.5 59.3 %shard_map.277 = (bf16[8,256,2048]{2,1,0:T(8,128)(2,1)}, bf16[1280,2048]{1,0:T(8,128)(2,1)}, bf16[1280,1024]{1,0:T(8,128)(2,1)}, bf16[1280,1024]{1,0:T(8,128)(2,1)}, f32[128,2048]{1,0:T(8,128)}) custom-call(s32[1]{0:T(128)} %bitcast.7.id_ref, s32[8,1,256]{2,1,0:T(1,128)} %reshape.202.slot_ref, bf16[8,256,2048]{2,1,0:T(8,128)(2,1)} %bitcast.89, ...), custom_call_target="tpu_custom_call" | custom-call | bytes 120000000 | tf_op jit(solution)/shard_map/pallas_call | solution.py:1388
  651.8 97.8 %shard_map.278 = (f32[256,2048]{1,0:T(8,128)}, bf16[2048,1024]{1,0:T(8,128)(2,1)}, bf16[2048,1024]{1,0:T(8,128)(2,1)}, bf16[1024,2048]{1,0:T(8,128)(2,1)}) custom-call(bf16[8,256,2048]{2,1,0:T(8,128)(2,1)} %get-tuple-element.119.part_ref, bf16[1280,2048]{1,0:T(8,128)(2,1)} %get-tuple-element.103.x_ref.refs_0_, ...), custom_call_target="tpu_custom_call" | custom-call | bytes 3000000 | tf_op jit(solution)/shard_map/pallas_call | solution.py:991
  752.0 4.4 multiply_reduce_fusion
  765.5 130.4 %shard_map.279 = (bf16[2048,768]{1,0:T(8,128)(2,1)}, f32[8,256]{1,0:T(8,128)}, bf16[8,256,2048]{2,1,0:T(8,128)(2,1)}) custom-call(f32[2048,768]{1,0:T(8,128)} %fusion.34.raw_ref, f32[8,256]{1,0:T(8,128)} %fusion.28.gains_ref, f32[2048,128]{1,0:T(8,128)} %get-tuple-element.189.cos_ref, f32[2048,128]{1,0:T(8,128)} %get-tuple-element.190.sin_ref, ...), custom_call_target="tpu_custom_call" | custom-call | bytes 300000000 | tf_op jit(solution)/shard_map/pallas_call | solution.py:722
  896.0 5.7 convolution_convert_fusion.4
  903.9 3.9 stack.48
  909.3 9.0 add_bitcast_fusion.2
  918.3 10.7 convolution_convert_fusion.3
  931.4 111.9 %shard_map.280 = (f32[256,2048]{1,0:T(8,128)}, f32[24,2048]{1,0:T(8,128)}) custom-call(bf16[2048,768]{1,0:T(8,128)(2,1)} %get-tuple-element.138.joined_ref, bf16[2048,768]{1,0:T(8,128)(2,1)} %copy-done.9, bf16[256,2048]{1,0:T(8,128)(2,1)} %tokens_ref.1, f32[256,2048]{1,0:T(8,128)} %get-tuple-element.164.hidden_ref, f32[1,2048]{1,0:T(1,128)} %bitcast.100, ...), custom_call_target="tpu_custom_call" | custom-call | bytes 300000000 | tf_op jit(solution)/shard_map/pallas_call | solution.py:1179
  1051.1 7.7 add_bitcast_fusion
  1058.7 7.6 add_bitcast_fusion.1
  1066.3 3.5 convert_add_fusion
  (156 shorter events, 51.4 us)
Async XLA Ops:
  7.2 5.4 copy-start.2
  7.2 496.2 %all-gather.2.cloned.1.call-start = ((), (), s32[]{:S(2)}) async-start(), calls=%async_computation.1 | async-start | bytes 9437184 | tf_op jit(solution)/shard_map/all_gather | solution.py:1489
  11.8 139.0 %copy-start.31 = (f32[2048]{0:T(1024)}, f32[2048]{0:T(1024)S(1)}, u32[]{:S(2)}) copy-start(f32[2048]{0:T(1024)S(1)} %convert_element_type.105) | copy-start | bytes 24580
  13.8 137.2 %copy-start.39 = (bf16[256]{0:T(256)(128)(2,1)S(1)}, bf16[256]{0:T(256)(128)(2,1)}, u32[]{:S(2)}) copy-start(bf16[256]{0:T(256)(128)(2,1)} %param.25) | copy-start | bytes 1540
  13.9 137.2 %copy-start.40 = (bf16[256]{0:T(256)(128)(2,1)S(1)}, bf16[256]{0:T(256)(128)(2,1)}, u32[]{:S(2)}) copy-start(bf16[256]{0:T(256)(128)(2,1)} %param.26) | copy-start | bytes 1540
  13.9 137.2 %copy-start.34 = (bf16[2048]{0:T(1024)(128)(2,1)S(1)}, bf16[2048]{0:T(1024)(128)(2,1)}, u32[]{:S(2)}) copy-start(bf16[2048]{0:T(1024)(128)(2,1)} %param.27) | copy-start | bytes 12292
  13.9 139.0 %copy-start.32 = (bf16[2048,16]{0,1:T(8,128)(2,1)S(1)}, bf16[2048,16]{0,1:T(8,128)(2,1)}, u32[]{:S(2)}) copy-start(bf16[2048,16]{0,1:T(8,128)(2,1)} %param.28) | copy-start | bytes 196612
  150.9 598.7 %reduce-scatter.2.cloned.1.call-start = ((), (), s32[]{:S(2)}) async-start(), calls=%async_computation.2 | async-start | bytes 9437184 | tf_op jit(solution)/shard_map/reduce_scatter | solution.py:1527
  156.8 5.7 copy-start.9
  156.8 5.7 copy-start.36
  171.2 91.6 %copy-start.20 = (bf16[8,256,512]{2,1,0:T(8,128)(2,1)S(1)}, bf16[8,256,512]{2,1,0:T(8,128)(2,1)}, u32[]{:S(2)}) copy-start(bf16[8,256,512]{2,1,0:T(8,128)(2,1)} %get-tuple-element.88) | copy-start | bytes 6291460
  560.8 12.2 %copy-start.35 = (s32[256]{0:T(256)S(1)}, s32[256]{0:T(256)}, u32[]{:S(2)}) copy-start(s32[256]{0:T(256)} %param.18) | copy-start | bytes 3076
  571.0 180.2 %collective-permute-start = (bf16[2048,1024]{1,0:T(8,128)(2,1)}, bf16[2048,1024]{1,0:T(8,128)(2,1)}, u32[]{:S(2)}, u32[]{:S(2)}) collective-permute-start(bf16[2048,1024]{1,0:T(8,128)(2,1)} %convolution_convert_fusion.2), channel_id=1, source_target_pairs={{0,1},{1,0},{2,3},{3,2},{4,5},{5,4},{6,7},{7,6},{8,9},{9,8},{10,11... | collective-permute-start | bytes 12582920 | tf_op jit(solution)/shard_map/ppermute | solution.py:1461
  573.6 10.4 copy-start.37
  573.6 10.4 copy-start.38
  584.0 334.2 %collective-permute-start.1 = (bf16[2048,1024]{1,0:T(8,128)(2,1)}, bf16[2048,1024]{1,0:T(8,128)(2,1)}, u32[]{:S(2)}, u32[]{:S(2)}) collective-permute-start(bf16[2048,1024]{1,0:T(8,128)(2,1)} %convolution_convert_fusion.1), channel_id=1, source_target_pairs={{0,1},{1,0},{2,3},{3,2},{4,5},{5,4},{6,7},{7,6},{8,9},{9,8},{10,11... | collective-permute-start | bytes 12582920 | tf_op jit(solution)/shard_map/ppermute | solution.py:1461
  751.2 5.3 copy-start.16
  751.2 167.0 %collective-permute-start.2 = (bf16[1024,2048]{1,0:T(8,128)(2,1)}, bf16[1024,2048]{1,0:T(8,128)(2,1)}, u32[]{:S(2)}, u32[]{:S(2)}) collective-permute-start(bf16[1024,2048]{1,0:T(8,128)(2,1)} %convolution_convert_fusion), channel_id=1, source_target_pairs={{0,1},{1,0},{2,3},{3,2},{4,5},{5,4},{6,7},{7,6},{8,9},{9,8},{10,11... | collective-permute-start | bytes 12582920 | tf_op jit(solution)/shard_map/ppermute | solution.py:1461
  765.5 130.4 %copy-start.8 = (bf16[2048,256]{1,0:T(8,128)(2,1)S(1)}, bf16[2048,256]{1,0:T(8,128)(2,1)}, u32[]{:S(2)}) copy-start(bf16[2048,256]{1,0:T(8,128)(2,1)} %get-tuple-element.134.o_ref) | copy-start | bytes 3145732
  902.6 27.2 %collective-permute-start.4 = (bf16[256,2048]{1,0:T(8,128)(2,1)S(1)}, bf16[256,2048]{1,0:T(8,128)(2,1)S(1)}, u32[]{:S(2)}, u32[]{:S(2)}) collective-permute-start(bf16[256,2048]{1,0:T(8,128)(2,1)S(1)} %convolution_convert_fusion.4), channel_id=1, source_target_pairs={{0,1},{1,0},{2,3},{3,2},{4,5},{5,4},{6,7},{7,6},{8,9},{9,8},{10,11... | collective-permute-start | bytes 3145736 | tf_op jit(solution)/shard_map/ppermute | solution.py:1461
  909.3 9.0 copy-start.19
  929.0 137.3 %collective-permute-start.3 = (bf16[2048,768]{1,0:T(8,128)(2,1)}, bf16[2048,768]{1,0:T(8,128)(2,1)}, u32[]{:S(2)}, u32[]{:S(2)}) collective-permute-start(bf16[2048,768]{1,0:T(8,128)(2,1)} %convolution_convert_fusion.3), channel_id=1, source_target_pairs={{0,1},{1,0},{2,3},{3,2},{4,5},{5,4},{6,7},{7,6},{8,9},{9,8},{10,11... | collective-permute-start | bytes 9437192 | tf_op jit(solution)/shard_map/ppermute | solution.py:1461
  931.4 119.6 %copy-start.18 = (bf16[1024,2048]{1,0:T(8,128)(2,1)S(1)}, bf16[1024,2048]{1,0:T(8,128)(2,1)}, u32[]{:S(2)}) copy-start(bf16[1024,2048]{1,0:T(8,128)(2,1)} %get-tuple-element.149) | copy-start | bytes 12582916
  1051.1 7.7 copy-start.17
  (24 other events, 56.8 us)
Sparse Core Ops, SparseCore 0:
  151.0 174.9 all-gather.1
  503.5 146.9 reduce-scatter.1

commit v7 on v6

--- a/solution.py
+++ b/solution.py
@@ -342,13 +342,14 @@
     return parts
 
 
-def for_blocks(blocks, prompt_blocks, one, between=None):
+def for_blocks(blocks, prompt_blocks, one, between=None, first=0):
     for w in range(prompt_blocks):
         one(w, w, w * one.rows)
     if between is not None:
         between()
 
-    def body(w, carry):
+    def body(i, carry):
+        w = prompt_blocks + lax.rem(i - prompt_blocks + first, blocks - prompt_blocks)
         one(None, w, pl.multiple_of(w * one.rows, one.rows))
         return carry
 
@@ -500,7 +501,7 @@
             hand_out(w_index).start()
 
     one.rows = rows
-    for_blocks(size, prompt_blocks, one, (lambda: gather.forward(2)) if carried else None)
+    for_blocks(size, prompt_blocks, one, (lambda: gather.forward(2)) if carried else None, wide)
     if carried:
         gather.forward(3)
     own_ref[:, mine()] = o_ref[pl.ds(pl.multiple_of(wide * rows, rows), rows)]
@@ -554,8 +555,6 @@
         lax.fori_loop(0, size, body, 0)
 
     each_peer(lambda w: hand_in(w).start())
-    if carried:
-        gather.start()
     do_ref[my_rows, :] = grad_ref[:, part_of(wide)]
     for ref in (dk_ref, dv_ref, dko_ref, dvo_ref, dots_ref, gain_ref):
         ref[...] = jnp.zeros_like(ref)
@@ -568,6 +567,8 @@
             grad_ref.at[:, part_of(w)], do_ref.at[my_rows], in_send.at[w], in_recv.at[w], (grp, w, narrow)
         ).wait_recv()
     )
+    if carried:
+        gather.start()
 
     def sweep(plane):
         keys, values = ((k_ref, v_ref), (ko_ref, vo_ref))[plane]
@@ -1200,11 +1201,13 @@
     )(joined, weights, tokens, grad_hidden, gain, small)
 
 
-def pick_rows(step, capacity, slot_ref, source_ref, picks, held, out_ref):
-    row = lax.broadcasted_iota(jnp.int32, (capacity, source_ref.shape[1]), 0)
+def pick_rows(step, capacity, slot_ref, source_refs, picks, held, out_ref):
+    row = lax.broadcasted_iota(jnp.int32, (capacity, slot_ref.shape[2]), 0)
     pick = jnp.where(row == slot_ref[0], 1.0, 0.0).astype(jnp.bfloat16)
     picks[step] = pick
-    values = dot(pick, source_ref[0]).astype(jnp.bfloat16)
+    part = pick.shape[1] // len(source_refs)
+    values = sum(dot(pick[:, k * part : (k + 1) * part], ref[0]) for k, ref in enumerate(source_refs))
+    values = values.astype(jnp.bfloat16)
     held[pl.ds(pl.multiple_of(step * capacity, capacity), capacity)] = values
     out_ref[...] = values
 
@@ -1228,7 +1231,7 @@
 
     @pl.when(step < blocks)
     def _():
-        pick_rows(step, capacity, slot_ref, tokens_ref, picks, x_all, x_ref)
+        pick_rows(step, capacity, slot_ref, [tokens_ref], picks, x_all, x_ref)
 
     @pl.when(step == blocks)
     def _():
@@ -1255,7 +1258,7 @@
 
 
 def expert_backward_kernel(
-    tiles, capacity, first, id_ref, slot_ref, grads_ref, x_ref, probs_ref, gate_pre_ref, up_pre_ref,
+    tiles, capacity, first, id_ref, slot_ref, low_ref, high_ref, x_ref, probs_ref, gate_pre_ref, up_pre_ref,
     router_ref, gate_ref, up_ref, down_ref, *refs
 ):
     before_ref, router_in_ref = (None, None) if first else refs[:2]
@@ -1271,7 +1274,7 @@
 
     @pl.when(step < blocks)
     def _():
-        pick_rows(step, capacity, slot_ref, grads_ref, picks, g_all, g_ref)
+        pick_rows(step, capacity, slot_ref, [low_ref, high_ref], picks, g_all, g_ref)
 
     @pl.when(step == blocks)
     def _():
@@ -1337,6 +1340,7 @@
             return jnp.clip(i - blocks, 0, tiles - 1)
 
         self.whole = pl.BlockSpec((1, rows, D), lambda g, i: (picked(g, i), 0, 0))
+        self.part = pl.BlockSpec((1, rows // 2, D), lambda g, i: (picked(g, i), 0, 0))
         self.back = pl.BlockSpec((1, rows, D), lambda g, i: (g * blocks + jnp.clip(i - last, 0, blocks - 1), 0, 0))
         self.row = pl.BlockSpec((capacity, D), lambda g, i: (picked(g, i), 0))
         column = pl.BlockSpec((D, tile), lambda g, i: (0, tiled(i)))
@@ -1388,7 +1392,7 @@
         return pl.pallas_call(
             functools.partial(expert_backward_kernel, self.tiles, self.capacity, first),
             in_specs=self.heads
-            + [self.whole, self.rows_all, self.probs, self.unit, self.unit]
+            + [self.part, self.part, self.rows_all, self.probs, self.unit, self.unit]
             + self.weight_specs
             + ([] if first else [self.back, self.fixed]),
             out_specs=[self.back, self.row, self.unit, self.unit, self.fixed],
@@ -1403,7 +1407,7 @@
                 pltpu.VMEM((128, D), f32),
             ],
             **self.common,
-        )(*self.scalars, grads, x, probs, gate_pre, up_pre, self.router, *self.weights, *(before or ()))
+        )(*self.scalars, *grads, x, probs, gate_pre, up_pre, self.router, *self.weights, *(before or ()))
 
 
 def positions(token_ids):
@@ -1485,8 +1489,9 @@
     def unordered(whole):
         return ordered([whole[:, k * piece_width : (k + 1) * piece_width] for k in range(pieces)])
 
-    grad_final_b, _ = barrier((grad_final.astype(bf16), normed_plane))
-    grads_in = lax.all_gather(grad_final_b, "wide", axis=0, tiled=True).reshape(wide_count, rows, D)
+    grad_final_b = grad_final.astype(bf16)
+    low, _ = barrier((grad_final_b[: rows // 2], normed_plane))
+    grads_low = lax.all_gather(low, "wide", axis=0, tiled=True).reshape(wide_count, rows // 2, D)
     joined = jnp.concatenate([w_query, w_key, w_value], 1)
     raw = dot(normed_plane, joined)
     gains = jnp.pad(jnp.stack([norm_query, norm_key]).astype(f32), ((0, 6), (0, 0)))
@@ -1504,6 +1509,9 @@
     gain_two = norm_moe.astype(f32)
     moe_in = (hidden * inv_two * gain_two).astype(bf16)
     (tokens_in,), (other_gate, other_down), _ = start_exchange([moe_in], [w_gate[0], w_down[0]], 6)
+
+    high, tokens_in, grads_low = barrier((grad_final_b[rows // 2 :], tokens_in, grads_low))
+    grads_high = lax.all_gather(high, "wide", axis=0, tiled=True).reshape(wide_count, rows // 2, D)
 
     earlier = (jnp.arange(rows)[:, None] < jnp.arange(rows)[None, :]).astype(bf16)
 
@@ -1525,7 +1533,8 @@
     kept_other = other.forward(tokens_in, kept_own[0])
     moe_part = kept_other[0]
     moe = lax.psum_scatter(moe_part.reshape(half, D), "wide", scatter_dimension=0, tiled=True).astype(f32)
-    kept_other, grads_in, _ = barrier((kept_other, grads_in, moe_part))
+    kept_other, grads_high, _ = barrier((kept_other, grads_high, moe_part))
+    grads_in = (grads_low, grads_high)
     back_other = other.backward(grads_in, kept_other, None)
     partner_grads = plain_grads(kept_other[1], back_other[1], kept_other[2], back_other[2], back_other[3])
     came = [exchange(g) for g in partner_grads[:2]]

time: 1090 us -> 1050 us (0.963)
  Pallas kernels: 918 us -> 884 us
    pallas_call x2, Pallas kernels: 285 us -> 256 us  [start_exchange(): pl.pallas_call(functools.partial(start_kernel, count, swaps, spread), out...]
    pallas_call x1, Pallas kernels: 91.6 us -> 79.9 us  [shards(): kept = attend(raw, gains, cosine, sine)]
  transfers between devices with their start and end apart: 7 -> 8, of which waited for: 0 -> 0; matrix products, arithmetic and copies ran while one was open for 11% -> 12% of each run, Pallas kernels for 72% -> 71%
where the time goes in v7:
time: 1050 us
  Pallas kernels  884 us (84%)
  matrix products  62.1 us (6%)
  other arithmetic  52.6 us (5%)
  local copies, waits for them, and re-layouts  28.1 us (3%)
  between operations  15.4 us (1%)
    pallas_call x2, Pallas kernels, start_exchange(): pl.pallas_call(functools.partial(start_kernel, count, swaps, spread), out...  256 us
    pallas_call x1, Pallas kernels, backward(): return backward_call(*args)  132 us
    pallas_call x2, Pallas kernels, backward(): pl.pallas_call(functools.partial(expert_backward_kernel, self.tiles, self...  118 us
    pallas_call x1, Pallas kernels, input_grad(): pl.pallas_call(functools.partial(input_grad_kernel, gain_row), out_shape=...  114 us
    pallas_call x1, Pallas kernels, expert_grad(): pl.pallas_call(expert_grad_kernel, out_shape=[jax.ShapeDtypeStruct((rows,...  98.4 us
    pallas_call x2, Pallas kernels, forward(): pl.pallas_call(functools.partial(expert_forward_kernel, self.tiles, self....  85 us
    pallas_call x1, Pallas kernels, shards(): kept = attend(raw, gains, cosine, sine)  79.9 us
    dot_general x5, matrix products, dot_tn(): lax.dot_general(a, b, (((0,), (0,)), ((), ())), preferred_element_type=jn...  44.6 us
  transfers between devices with their start and end apart: 8, of which 0 were waited for; matrix products, arithmetic and copies ran while one was open for 12% of the time, Pallas kernels for 71%

profile of v7, /device:TPU:0, one launch (start us, length us, event | category | flops | bytes accessed | tf_op | source)
XLA Modules:
  0.0 1047.8 jit_solution(14404149273742365419)
XLA Ops:
  8.0 3.1 fusion.3
  14.3 137.0 %shard_map.271 = (s32[8,8,256]{2,1,0:T(8,128)}, bf16[8,256,2048]{2,1,0:T(8,128)(2,1)}, bf16[8,256,512]{2,1,0:T(8,128)(2,1)}, bf16[2048,1024]{1,0:T(8,128)(2,1)},...) custom-call(s32[8,256]{1,0:T(8,128)} %bitcast.109, ...), custom_call_target="tpu_custom_call" | custom-call | bytes 360000000 | tf_op jit(solution)/shard_map/pallas_call | solution.py:815
  153.5 3.7 fusion.10
  159.2 8.7 fusion.35.raw_ref
  167.9 79.9 %shard_map.272 = (bf16[2048,256]{1,0:T(8,128)(2,1)}, bf16[2048,256]{1,0:T(8,128)(2,1)}, bf16[2048,256]{1,0:T(8,128)(2,1)}, bf16[1024,256]{1,0:T(8,128)(2,1)}, bf...) custom-call(f32[2048,768]{1,0:T(8,128)} %fusion.35.raw_ref, ...), custom_call_target="tpu_custom_call" | custom-call | bytes 300000000 | tf_op jit(solution)/shard_map/pallas_call | solution.py:1503
  255.8 118.9 %shard_map.273 = (bf16[8,256,2048]{2,1,0:T(8,128)(2,1)}, bf16[2048,1024]{1,0:T(8,128)(2,1)}, bf16[1024,2048]{1,0:T(8,128)(2,1)}) custom-call(bf16[256,2048]{1,0:T(8,128)(2,1)} %multiply_convert_fusion.refs_0_, bf16[2048,1024]{1,0:T(8,128)(2,1)} %bitcast.83, bf16[1024,2048]{1,0:T(8,128)(2,1)} %bitcast.86), custom_call_target="tpu_custom_call" | custom-call | bytes 360000000 | tf_op jit(solution)/shard_map/pallas_call | solution.py:815
  377.6 41.2 %shard_map.274 = (bf16[8,256,2048]{2,1,0:T(8,128)(2,1)}, bf16[1280,2048]{1,0:T(8,128)(2,1)}, bf16[1280,1024]{1,0:T(8,128)(2,1)}, f32[1280,1024]{1,0:T(8,128)}, f...) custom-call(s32[1]{0:T(128)} %bitcast.7.id_ref, s32[8,1,256]{2,1,0:T(1,128)} %reshape.205.slot_ref, ...), custom_call_target="tpu_custom_call" | custom-call | bytes 120000000 | tf_op jit(solution)/shard_map/pallas_call | solution.py:1373
  418.8 43.8 %shard_map.275 = (bf16[8,256,2048]{2,1,0:T(8,128)(2,1)}, bf16[1280,2048]{1,0:T(8,128)(2,1)}, bf16[1280,1024]{1,0:T(8,128)(2,1)}, f32[1280,1024]{1,0:T(8,128)}, f...) custom-call(s32[1]{0:T(128)} %bitcast.11.id_ref, s32[8,1,256]{2,1,0:T(1,128)} %copy.32.slot_ref, ...), custom_call_target="tpu_custom_call" | custom-call | bytes 120000000 | tf_op jit(solution)/shard_map/pallas_call | solution.py:1373
  462.7 58.0 %shard_map.276 = (bf16[8,256,2048]{2,1,0:T(8,128)(2,1)}, bf16[1280,2048]{1,0:T(8,128)(2,1)}, bf16[1280,1024]{1,0:T(8,128)(2,1)}, bf16[1280,1024]{1,0:T(8,128)(2,1)}, f32[128,2048]{1,0:T(8,128)}) custom-call(s32[1]{0:T(128)} %bitcast.11.id_ref, s32[8,1,256]{2,1,0:T(1,128)} %copy.32.slot_ref, bf16[8,128,2048]{2,1,0:T(8,128)(2,1)} %bitcast.90, ...), custom_call_target="tpu_custom_call" | custom-call | bytes 120000000 | tf_op jit(solution)/shard_map/pallas_call | solution.py:1392
  520.8 10.3 convolution_convert_fusion.2
  534.5 10.4 convolution_convert_fusion.1
  544.9 7.4 convolution_convert_fusion
  552.4 59.8 %shard_map.277 = (bf16[8,256,2048]{2,1,0:T(8,128)(2,1)}, bf16[1280,2048]{1,0:T(8,128)(2,1)}, bf16[1280,1024]{1,0:T(8,128)(2,1)}, bf16[1280,1024]{1,0:T(8,128)(2,1)}, f32[128,2048]{1,0:T(8,128)}) custom-call(s32[1]{0:T(128)} %bitcast.7.id_ref, s32[8,1,256]{2,1,0:T(1,128)} %reshape.205.slot_ref, bf16[8,128,2048]{2,1,0:T(8,128)(2,1)} %bitcast.91, ...), custom_call_target="tpu_custom_call" | custom-call | bytes 120000000 | tf_op jit(solution)/shard_map/pallas_call | solution.py:1392
  613.1 98.4 %shard_map.278 = (f32[256,2048]{1,0:T(8,128)}, bf16[2048,1024]{1,0:T(8,128)(2,1)}, bf16[2048,1024]{1,0:T(8,128)(2,1)}, bf16[1024,2048]{1,0:T(8,128)(2,1)}) custom-call(bf16[8,256,2048]{2,1,0:T(8,128)(2,1)} %get-tuple-element.125.part_ref, bf16[1280,2048]{1,0:T(8,128)(2,1)} %get-tuple-element.109.x_ref.refs_0_, ...), custom_call_target="tpu_custom_call" | custom-call | bytes 3000000 | tf_op jit(solution)/shard_map/pallas_call | solution.py:992
  713.9 4.4 multiply_reduce_fusion
  727.4 132.4 %shard_map.279 = (bf16[2048,768]{1,0:T(8,128)(2,1)}, f32[8,256]{1,0:T(8,128)}, bf16[8,256,2048]{2,1,0:T(8,128)(2,1)}) custom-call(f32[2048,768]{1,0:T(8,128)} %fusion.35.raw_ref, f32[8,256]{1,0:T(8,128)} %fusion.28.gains_ref, f32[2048,128]{1,0:T(8,128)} %get-tuple-element.197.cos_ref, f32[2048,128]{1,0:T(8,128)} %get-tuple-element.198.sin_ref, ...), custom_call_target="tpu_custom_call" | custom-call | bytes 300000000 | tf_op jit(solution)/shard_map/pallas_call | solution.py:723
  859.8 5.7 convolution_convert_fusion.4
  867.6 3.9 stack.48
  872.9 9.0 add_bitcast_fusion.2
  881.9 10.7 %convolution_convert_fusion.3 = bf16[2048,768]{1,0:T(8,128)(2,1)} fusion(bf16[2048,2048]{1,0:T(8,128)(2,1)} %bitcast.116, bf16[2048,768]{1,0:T(8,128)(2,1)S(1)} %copy-done.19), kind=kOutput, calls=%fused_computation.7 | convolution fusion | flops 6444023808 | bytes 14680064 | tf_op jit(solution)/shard_map/dot_general | solution.py:738
  895.2 114.3 %shard_map.280 = (f32[256,2048]{1,0:T(8,128)}, f32[24,2048]{1,0:T(8,128)}) custom-call(bf16[2048,768]{1,0:T(8,128)(2,1)} %get-tuple-element.144.joined_ref, bf16[2048,768]{1,0:T(8,128)(2,1)} %copy-done.9, bf16[256,2048]{1,0:T(8,128)(2,1)} %tokens_ref.1, f32[256,2048]{1,0:T(8,128)} %get-tuple-element.170.hidden_ref, f32[1,2048]{1,0:T(1,128)} %bitcast.103, ...), custom_call_target="tpu_custom_call" | custom-call | bytes 300000000 | tf_op jit(solution)/shard_map/pallas_call | solution.py:1180
  1017.3 7.7 add_bitcast_fusion
  1024.9 7.6 add_bitcast_fusion.1
  1032.5 3.5 convert_add_fusion
  (162 shorter events, 52.4 us)
Async XLA Ops:
  7.2 367.6 %all-gather.3.cloned.1.call-start = ((), (), s32[]{:S(2)}) async-start(), calls=%async_computation.1 | async-start | bytes 4718592 | tf_op jit(solution)/shard_map/all_gather | solution.py:1494
  14.2 137.2 %copy-start.40 = (bf16[256]{0:T(256)(128)(2,1)S(1)}, bf16[256]{0:T(256)(128)(2,1)}, u32[]{:S(2)}) copy-start(bf16[256]{0:T(256)(128)(2,1)} %param.25) | copy-start | bytes 1540
  14.2 137.2 %copy-start.41 = (bf16[256]{0:T(256)(128)(2,1)S(1)}, bf16[256]{0:T(256)(128)(2,1)}, u32[]{:S(2)}) copy-start(bf16[256]{0:T(256)(128)(2,1)} %param.26) | copy-start | bytes 1540
  14.2 137.2 %copy-start.35 = (bf16[2048]{0:T(1024)(128)(2,1)S(1)}, bf16[2048]{0:T(1024)(128)(2,1)}, u32[]{:S(2)}) copy-start(bf16[2048]{0:T(1024)(128)(2,1)} %param.27) | copy-start | bytes 12292
  14.3 137.9 %copy-start.27 = (bf16[2048,256]{1,0:T(8,128)(2,1)S(1)}, bf16[2048,256]{1,0:T(8,128)(2,1)}, u32[]{:S(2)}) copy-start(bf16[2048,256]{1,0:T(8,128)(2,1)} %param.20) | copy-start | bytes 3145732
  151.3 311.5 %all-gather.5.cloned.1.call-start = ((), (), s32[]{:S(2)}) async-start(), calls=%async_computation.2 | async-start | bytes 4718592 | tf_op jit(solution)/shard_map/all_gather | solution.py:1514
  153.5 5.7 copy-start.9
  153.5 5.7 copy-start.37
  167.9 79.9 %copy-start.20 = (bf16[8,256,512]{2,1,0:T(8,128)(2,1)S(1)}, bf16[8,256,512]{2,1,0:T(8,128)(2,1)}, u32[]{:S(2)}) copy-start(bf16[8,256,512]{2,1,0:T(8,128)(2,1)} %get-tuple-element.91) | copy-start | bytes 6291460
  255.8 119.1 %copy-start.33 = (s32[8,8,256]{2,1,0:T(8,128)S(1)}, s32[8,8,256]{2,1,0:T(8,128)}, u32[]{:S(2)}) copy-start(s32[8,8,256]{2,1,0:T(8,128)} %get-tuple-element.92) | copy-start | bytes 196612
  255.8 119.9 %copy-start.32 = (bf16[2048,16]{0,1:T(8,128)(2,1)S(1)}, bf16[2048,16]{0,1:T(8,128)(2,1)}, u32[]{:S(2)}) copy-start(bf16[2048,16]{0,1:T(8,128)(2,1)} %param.28) | copy-start | bytes 196612
  374.8 336.7 %reduce-scatter.2.cloned.1.call-start = ((), (), s32[]{:S(2)}) async-start(), calls=%async_computation.3 | async-start | bytes 9437184 | tf_op jit(solution)/shard_map/reduce_scatter | solution.py:1535
  520.7 13.1 %copy-start.36 = (s32[256]{0:T(256)S(1)}, s32[256]{0:T(256)}, u32[]{:S(2)}) copy-start(s32[256]{0:T(256)} %param.18) | copy-start | bytes 3076
  531.1 182.1 %collective-permute-start = (bf16[2048,1024]{1,0:T(8,128)(2,1)}, bf16[2048,1024]{1,0:T(8,128)(2,1)}, u32[]{:S(2)}, u32[]{:S(2)}) collective-permute-start(bf16[2048,1024]{1,0:T(8,128)(2,1)} %convolution_convert_fusion.2), channel_id=1, source_target_pairs={{0,1},{1,0},{2,3},{3,2},{4,5},{5,4},{6,7},{7,6},{8,9},{9,8},{10,11... | collective-permute-start | bytes 12582920 | tf_op jit(solution)/shard_map/ppermute | solution.py:1465
  534.5 10.4 copy-start.38
  534.5 10.4 copy-start.39
  544.9 337.0 %collective-permute-start.1 = (bf16[2048,1024]{1,0:T(8,128)(2,1)}, bf16[2048,1024]{1,0:T(8,128)(2,1)}, u32[]{:S(2)}, u32[]{:S(2)}) collective-permute-start(bf16[2048,1024]{1,0:T(8,128)(2,1)} %convolution_convert_fusion.1), channel_id=1, source_target_pairs={{0,1},{1,0},{2,3},{3,2},{4,5},{5,4},{6,7},{7,6},{8,9},{9,8},{10,11... | collective-permute-start | bytes 12582920 | tf_op jit(solution)/shard_map/ppermute | solution.py:1465
  713.2 168.8 %collective-permute-start.2 = (bf16[1024,2048]{1,0:T(8,128)(2,1)}, bf16[1024,2048]{1,0:T(8,128)(2,1)}, u32[]{:S(2)}, u32[]{:S(2)}) collective-permute-start(bf16[1024,2048]{1,0:T(8,128)(2,1)} %convolution_convert_fusion), channel_id=1, source_target_pairs={{0,1},{1,0},{2,3},{3,2},{4,5},{5,4},{6,7},{7,6},{8,9},{9,8},{10,11... | collective-permute-start | bytes 12582920 | tf_op jit(solution)/shard_map/ppermute | solution.py:1465
  727.4 132.4 %copy-start.8 = (bf16[2048,256]{1,0:T(8,128)(2,1)S(1)}, bf16[2048,256]{1,0:T(8,128)(2,1)}, u32[]{:S(2)}) copy-start(bf16[2048,256]{1,0:T(8,128)(2,1)} %get-tuple-element.140.o_ref) | copy-start | bytes 3145732
  866.4 27.2 %collective-permute-start.4 = (bf16[256,2048]{1,0:T(8,128)(2,1)S(1)}, bf16[256,2048]{1,0:T(8,128)(2,1)S(1)}, u32[]{:S(2)}, u32[]{:S(2)}) collective-permute-start(bf16[256,2048]{1,0:T(8,128)(2,1)S(1)} %convolution_convert_fusion.4), channel_id=1, source_target_pairs={{0,1},{1,0},{2,3},{3,2},{4,5},{5,4},{6,7},{7,6},{8,9},{9,8},{10,11... | collective-permute-start | bytes 3145736 | tf_op jit(solution)/shard_map/ppermute | solution.py:1465
  872.9 9.0 copy-start.19
  892.7 139.8 %collective-permute-start.3 = (bf16[2048,768]{1,0:T(8,128)(2,1)}, bf16[2048,768]{1,0:T(8,128)(2,1)}, u32[]{:S(2)}, u32[]{:S(2)}) collective-permute-start(bf16[2048,768]{1,0:T(8,128)(2,1)} %convolution_convert_fusion.3), channel_id=1, source_target_pairs={{0,1},{1,0},{2,3},{3,2},{4,5},{5,4},{6,7},{7,6},{8,9},{9,8},{10,11... | collective-permute-start | bytes 9437192 | tf_op jit(solution)/shard_map/ppermute | solution.py:1465
  895.2 122.0 %copy-start.18 = (bf16[1024,2048]{1,0:T(8,128)(2,1)S(1)}, bf16[1024,2048]{1,0:T(8,128)(2,1)}, u32[]{:S(2)}) copy-start(bf16[1024,2048]{1,0:T(8,128)(2,1)} %get-tuple-element.155) | copy-start | bytes 12582916
  1017.3 7.7 copy-start.17
  (26 other events, 58.4 us)
Sparse Core Ops, SparseCore 0:
  151.4 109.4 all-gather.2
  374.9 72.1 all-gather.4
  462.8 148.0 reduce-scatter.1

commit v8 on v7

--- a/solution.py
+++ b/solution.py
@@ -679,7 +679,7 @@
     def params(k):
         return pltpu.CompilerParams(vmem_limit_bytes=60 * 2**20, collective_id=ids[k], has_side_effects=True)
 
-    carried = 1 if size == 2 * LINE else 0
+    carried = 0
     forward = pl.pallas_call(
         functools.partial(attend_kernel, rows, prompt_blocks, paired, shared, 0),
         out_shape=[shape(bf16, half, columns)] * 3
@@ -697,7 +697,7 @@
         cost_estimate=pl.CostEstimate(flops=0, bytes_accessed=300_000_000, transcendentals=0),
     )
 
-    backward_call = pl.pallas_call(
+    backward = pl.pallas_call(
         functools.partial(attend_back_kernel, rows, prompt_blocks, paired, shared, carried),
         out_shape=[shape(bf16, half, 3 * columns), shape(f32, 8, columns)]
         + [shape(bf16, size, rows, D)] * carried,
@@ -718,11 +718,6 @@
         compiler_params=params(1),
         cost_estimate=pl.CostEstimate(flops=0, bytes_accessed=300_000_000, transcendentals=0),
     )
-    def backward(*args):
-        if carried:
-            return backward_call(*args)
-        return [*backward_call(*args[:-1]), lax.all_gather(args[-1], "wide", axis=0)]
-
     return forward, backward
 
 
@@ -1325,7 +1320,7 @@
         self.router, self.weights, self.capacity, self.experts = router, weights, capacity, experts
         wide, _, rows = slots.shape
         units = weights[0].shape[1]
-        groups = 2 if wide * capacity > 1024 else 1
+        groups = 1 if wide * capacity <= 1280 else 2
         blocks, tile = wide // groups, 256
         tiles = units // tile
         last = blocks + tiles
@@ -1543,7 +1538,7 @@
     grad_part, grad_router = back_own[0], back_own[4][:experts]
     own_operands = (kept_own[1], back_own[1], kept_own[2], back_own[2], back_own[3])
     grad_moe_in, *own_grads = expert_grad(grad_part, own_operands, 5)
-    grad_moe_in, moe, came[0], down_grad = barrier((grad_moe_in, moe, came[0], partner_grads[2]))
+    grad_moe_in, moe, came[0], came[1], down_grad = barrier((grad_moe_in, moe, *came, partner_grads[2]))
     came.append(exchange(down_grad))
 
     grad_gain_two = jnp.sum(grad_moe_in * hidden * inv_two, 0)
@@ -1554,11 +1549,12 @@
     )
     grad_branch = grad_hidden.astype(bf16)
     grad_attended_own = sum(dot_nt(g, p) for g, p in zip(unordered(grad_branch), out_pieces)).astype(bf16)
-    grads_joined, gain_grads, branch_plane = attend_back(
-        raw, gains, cosine, sine, sums, *kept[:5], grad_attended_own, attended, lse, grad_branch
+    branch_plane = lax.all_gather(grad_branch, "wide", axis=0, tiled=True)
+    grads_joined, gain_grads = attend_back(
+        raw, gains, cosine, sine, sums, *kept[:5], grad_attended_own, attended, lse
     )
-    grads_joined, came[1], came[2] = barrier((grads_joined, came[1], came[2]))
-    grad_out = barrier(dot_tn(attended, branch_plane.reshape(half, D)).astype(bf16))
+    grads_joined, came[2] = barrier((grads_joined, came[2]))
+    grad_out = barrier(dot_tn(attended, branch_plane).astype(bf16))
     grad_weights = barrier(dot_tn(normed_plane, grads_joined).astype(bf16))
     weights_came = exchange(grad_weights)
     out_came = exchange(grad_out)
@@ -1568,7 +1564,7 @@
     zeros = jnp.zeros((D,), f32)
     small = jnp.stack([zeros, grad_gain_two, *spots, jnp.pad(stats, (0, D - stats.shape[0]))])
     small = jnp.concatenate([grad_router, small, jnp.zeros((-(experts + 5) % 8, D), f32)], 0)
-    small, _, _ = barrier((small, grad_weights, grad_out))
+    small, _ = barrier((small, grad_weights))
     grad_input, small = input_grad(
         grads_joined, joined, tokens, grad_hidden, gain_one.reshape(1, D), small, experts, 3
     )

time: 1050 us -> 1070 us (1.019)
  waiting for transfers between devices: 0.13 us -> 28.7 us
  Pallas kernels: 884 us -> 872 us
    ppermute x5, waiting for transfers between devices: 0.01 us -> 28.6 us  [exchange(): return lax.ppermute(value, 'narrow', swap)]
    pallas_call x1, Pallas kernels: 114 us -> 125 us  [input_grad(): pl.pallas_call(functools.partial(input_grad_kernel, gain_row), out_shape=...]
  transfers between devices with their start and end apart: 8 -> 9, of which waited for: 0 -> 2; matrix products, arithmetic and copies ran while one was open for 12% -> 11% of each run, Pallas kernels for 71% -> 69%
where the time goes in v8:
time: 1070 us; the launch traced here: 1060 us
  Pallas kernels  872 us (81%)
  matrix products  59.5 us (6%)
  other arithmetic  52.7 us (5%)
  waiting for transfers between devices  28.7 us (3%)
  local copies, waits for them, and re-layouts  27.6 us (3%)
  between operations  15.3 us (1%)
    pallas_call x2, Pallas kernels, start_exchange(): pl.pallas_call(functools.partial(start_kernel, count, swaps, spread), out...  256 us
    pallas_call x1, Pallas kernels, input_grad(): pl.pallas_call(functools.partial(input_grad_kernel, gain_row), out_shape=...  125 us
    pallas_call x1, Pallas kernels, shards(): attend_back(raw, gains, cosine, sine, sums, *kept[:5], grad_attended_own,...  123 us
    pallas_call x2, Pallas kernels, backward(): pl.pallas_call(functools.partial(expert_backward_kernel, self.tiles, self...  110 us
    pallas_call x1, Pallas kernels, expert_grad(): pl.pallas_call(expert_grad_kernel, out_shape=[jax.ShapeDtypeStruct((rows,...  97.7 us
    pallas_call x2, Pallas kernels, forward(): pl.pallas_call(functools.partial(expert_forward_kernel, self.tiles, self....  80.3 us
    pallas_call x1, Pallas kernels, shards(): kept = attend(raw, gains, cosine, sine)  79.9 us
    dot_general x5, matrix products, dot_tn(): lax.dot_general(a, b, (((0,), (0,)), ((), ())), preferred_element_type=jn...  39.6 us
  transfers between devices with their start and end apart: 9, of which 2 were waited for; matrix products, arithmetic and copies ran while one was open for 11% of the time, Pallas kernels for 69%

profile of v8, /device:TPU:0, one launch (start us, length us, event | category | flops | bytes accessed | tf_op | source)
XLA Modules:
  0.0 1062.9 jit_solution(257868200502894806)
XLA Ops:
  14.3 137.0 %shard_map.271 = (s32[8,8,256]{2,1,0:T(8,128)}, bf16[8,256,2048]{2,1,0:T(8,128)(2,1)}, bf16[8,256,512]{2,1,0:T(8,128)(2,1)}, bf16[2048,1024]{1,0:T(8,128)(2,1)},...) custom-call(s32[8,256]{1,0:T(8,128)} %bitcast.107, ...), custom_call_target="tpu_custom_call" | custom-call | bytes 360000000 | tf_op jit(solution)/shard_map/pallas_call | solution.py:810
  153.5 3.7 fusion.10
  159.2 8.7 fusion.35.raw_ref
  167.9 79.9 %shard_map.272 = (bf16[2048,256]{1,0:T(8,128)(2,1)}, bf16[2048,256]{1,0:T(8,128)(2,1)}, bf16[2048,256]{1,0:T(8,128)(2,1)}, bf16[1024,256]{1,0:T(8,128)(2,1)}, bf...) custom-call(f32[2048,768]{1,0:T(8,128)} %fusion.35.raw_ref, ...), custom_call_target="tpu_custom_call" | custom-call | bytes 300000000 | tf_op jit(solution)/shard_map/pallas_call | solution.py:1498
  255.8 119.0 %shard_map.273 = (bf16[8,256,2048]{2,1,0:T(8,128)(2,1)}, bf16[2048,1024]{1,0:T(8,128)(2,1)}, bf16[1024,2048]{1,0:T(8,128)(2,1)}) custom-call(bf16[256,2048]{1,0:T(8,128)(2,1)} %multiply_convert_fusion.refs_0_, bf16[2048,1024]{1,0:T(8,128)(2,1)} %bitcast.82, bf16[1024,2048]{1,0:T(8,128)(2,1)} %bitcast.85), custom_call_target="tpu_custom_call" | custom-call | bytes 360000000 | tf_op jit(solution)/shard_map/pallas_call | solution.py:810
  377.7 38.4 %shard_map.274 = (bf16[8,256,2048]{2,1,0:T(8,128)(2,1)}, bf16[1280,2048]{1,0:T(8,128)(2,1)}, bf16[1280,1024]{1,0:T(8,128)(2,1)}, f32[1280,1024]{1,0:T(8,128)}, f...) custom-call(s32[1]{0:T(128)} %bitcast.7.id_ref, s32[8,1,256]{2,1,0:T(1,128)} %reshape.202.slot_ref, ...), custom_call_target="tpu_custom_call" | custom-call | bytes 120000000 | tf_op jit(solution)/shard_map/pallas_call | solution.py:1368
  416.1 41.9 %shard_map.275 = (bf16[8,256,2048]{2,1,0:T(8,128)(2,1)}, bf16[1280,2048]{1,0:T(8,128)(2,1)}, bf16[1280,1024]{1,0:T(8,128)(2,1)}, f32[1280,1024]{1,0:T(8,128)}, f...) custom-call(s32[1]{0:T(128)} %bitcast.11.id_ref, s32[8,1,256]{2,1,0:T(1,128)} %copy.32.slot_ref, ...), custom_call_target="tpu_custom_call" | custom-call | bytes 120000000 | tf_op jit(solution)/shard_map/pallas_call | solution.py:1368
  458.1 53.2 %shard_map.276 = (bf16[8,256,2048]{2,1,0:T(8,128)(2,1)}, bf16[1280,2048]{1,0:T(8,128)(2,1)}, bf16[1280,1024]{1,0:T(8,128)(2,1)}, bf16[1280,1024]{1,0:T(8,128)(2,1)}, f32[128,2048]{1,0:T(8,128)}) custom-call(s32[1]{0:T(128)} %bitcast.11.id_ref, s32[8,1,256]{2,1,0:T(1,128)} %copy.32.slot_ref, bf16[8,128,2048]{2,1,0:T(8,128)(2,1)} %bitcast.88, ...), custom_call_target="tpu_custom_call" | custom-call | bytes 120000000 | tf_op jit(solution)/shard_map/pallas_call | solution.py:1387
  511.4 10.7 %convolution_convert_fusion.1 = bf16[2048,1024]{1,0:T(8,128)(2,1)} fusion(bf16[1280,2048]{1,0:T(8,128)(2,1)} %get-tuple-element.112.x_ref, bf16[1280,1024]{1,0:T(8,128)(2,1)} %get-tuple-element.119), kind=kOutput, calls=%fused_computation.5 | convolution fusion | flops 5370806272 | bytes 12058624 | tf_op jit(solution)/shard_map/dot_general | solution.py:733
  522.1 7.2 convolution_convert_fusion.2
  532.6 7.3 convolution_convert_fusion
  540.0 56.7 %shard_map.277 = (bf16[8,256,2048]{2,1,0:T(8,128)(2,1)}, bf16[1280,2048]{1,0:T(8,128)(2,1)}, bf16[1280,1024]{1,0:T(8,128)(2,1)}, bf16[1280,1024]{1,0:T(8,128)(2,1)}, f32[128,2048]{1,0:T(8,128)}) custom-call(s32[1]{0:T(128)} %bitcast.7.id_ref, s32[8,1,256]{2,1,0:T(1,128)} %reshape.202.slot_ref, bf16[8,128,2048]{2,1,0:T(8,128)(2,1)} %bitcast.89, ...), custom_call_target="tpu_custom_call" | custom-call | bytes 120000000 | tf_op jit(solution)/shard_map/pallas_call | solution.py:1387
  596.7 97.7 %shard_map.278 = (f32[256,2048]{1,0:T(8,128)}, bf16[2048,1024]{1,0:T(8,128)(2,1)}, bf16[2048,1024]{1,0:T(8,128)(2,1)}, bf16[1024,2048]{1,0:T(8,128)(2,1)}) custom-call(bf16[8,256,2048]{2,1,0:T(8,128)(2,1)} %get-tuple-element.124.part_ref, bf16[1280,2048]{1,0:T(8,128)(2,1)} %get-tuple-element.108.x_ref.refs_0_, ...), custom_call_target="tpu_custom_call" | custom-call | bytes 3000000 | tf_op jit(solution)/shard_map/pallas_call | solution.py:987
  696.1 17.8 %collective-permute-done = bf16[2048,1024]{1,0:T(8,128)(2,1)} collective-permute-done((bf16[2048,1024]{1,0:T(8,128)(2,1)}, bf16[2048,1024]{1,0:T(8,128)(2,1)}, u32[]{:S(2)}, u32[]{:S(2)}) %collective-permute-start) | collective-permute-done | bytes 4194336 | tf_op jit(solution)/shard_map/ppermute | solution.py:1460
  714.0 4.1 multiply_reduce_fusion
  732.6 122.5 %shard_map.279 = (bf16[2048,768]{1,0:T(8,128)(2,1)}, f32[8,256]{1,0:T(8,128)}) custom-call(f32[2048,768]{1,0:T(8,128)} %fusion.35.raw_ref, f32[8,256]{1,0:T(8,128)} %fusion.28.gains_ref, f32[2048,128]{1,0:T(8,128)} %get-tuple-element.195.cos_ref, f32[2048,128]{1,0:T(8,128)} %get-tuple-element.196.sin_ref, f32[8,2048]{1,0:T(8,128)} %get-tuple-element.132.sums_ref, ...), custom_call_target="tpu_custom_call" | custom-call | bytes 300000000 | tf_op jit(solution)/shard_map/pallas_call | solution.py:1553
  855.2 9.1 add_bitcast_fusion.1
  864.3 7.7 add_bitcast_fusion.2
  872.0 8.7 convolution_convert_fusion.3
  882.3 4.0 stack.48
  887.6 125.3 %shard_map.280 = (f32[256,2048]{1,0:T(8,128)}, f32[24,2048]{1,0:T(8,128)}) custom-call(bf16[2048,768]{1,0:T(8,128)(2,1)} %get-tuple-element.143.joined_ref, bf16[2048,768]{1,0:T(8,128)(2,1)} %copy-done.8, bf16[256,2048]{1,0:T(8,128)(2,1)} %tokens_ref.1, f32[256,2048]{1,0:T(8,128)} %get-tuple-element.168.hidden_ref, f32[1,2048]{1,0:T(1,128)} %bitcast.101, ...), custom_call_target="tpu_custom_call" | custom-call | bytes 300000000 | tf_op jit(solution)/shard_map/pallas_call | solution.py:1175
  1020.6 7.6 add_bitcast_fusion
  1028.2 5.7 convolution_convert_fusion.4
  1041.7 10.8 %collective-permute-done.4 = bf16[256,2048]{1,0:T(8,128)(2,1)S(1)} collective-permute-done((bf16[256,2048]{1,0:T(8,128)(2,1)S(1)}, bf16[256,2048]{1,0:T(8,128)(2,1)S(1)}, u32[]{:S(2)}, u32[]{:S(2)}) %collective-permute-start.4) | collective-permute-done | bytes 1048608 | tf_op jit(solution)/shard_map/ppermute | solution.py:1460
  (175 shorter events, 62.9 us)
Async XLA Ops:
  7.2 367.7 %all-gather.4.cloned.1.call-start = ((), (), s32[]{:S(2)}) async-start(), calls=%async_computation.1 | async-start | bytes 4718592 | tf_op jit(solution)/shard_map/all_gather | solution.py:1489
  14.3 137.2 %copy-start.40 = (bf16[256]{0:T(256)(128)(2,1)S(1)}, bf16[256]{0:T(256)(128)(2,1)}, u32[]{:S(2)}) copy-start(bf16[256]{0:T(256)(128)(2,1)} %param.25) | copy-start | bytes 1540
  14.3 137.2 %copy-start.41 = (bf16[256]{0:T(256)(128)(2,1)S(1)}, bf16[256]{0:T(256)(128)(2,1)}, u32[]{:S(2)}) copy-start(bf16[256]{0:T(256)(128)(2,1)} %param.26) | copy-start | bytes 1540
  14.3 137.2 %copy-start.35 = (bf16[2048]{0:T(1024)(128)(2,1)S(1)}, bf16[2048]{0:T(1024)(128)(2,1)}, u32[]{:S(2)}) copy-start(bf16[2048]{0:T(1024)(128)(2,1)} %param.27) | copy-start | bytes 12292
  14.3 137.9 %copy-start.27 = (bf16[2048,256]{1,0:T(8,128)(2,1)S(1)}, bf16[2048,256]{1,0:T(8,128)(2,1)}, u32[]{:S(2)}) copy-start(bf16[2048,256]{1,0:T(8,128)(2,1)} %param.20) | copy-start | bytes 3145732
  151.3 306.8 %all-gather.6.cloned.1.call-start = ((), (), s32[]{:S(2)}) async-start(), calls=%async_computation.2 | async-start | bytes 4718592 | tf_op jit(solution)/shard_map/all_gather | solution.py:1509
  167.9 79.9 %copy-start.20 = (bf16[8,256,512]{2,1,0:T(8,128)(2,1)S(1)}, bf16[8,256,512]{2,1,0:T(8,128)(2,1)}, u32[]{:S(2)}) copy-start(bf16[8,256,512]{2,1,0:T(8,128)(2,1)} %get-tuple-element.90) | copy-start | bytes 6291460
  255.8 119.1 %copy-start.33 = (s32[8,8,256]{2,1,0:T(8,128)S(1)}, s32[8,8,256]{2,1,0:T(8,128)}, u32[]{:S(2)}) copy-start(s32[8,8,256]{2,1,0:T(8,128)} %get-tuple-element.91) | copy-start | bytes 196612
  255.8 119.9 %copy-start.32 = (bf16[2048,16]{0,1:T(8,128)(2,1)S(1)}, bf16[2048,16]{0,1:T(8,128)(2,1)}, u32[]{:S(2)}) copy-start(bf16[2048,16]{0,1:T(8,128)(2,1)} %param.28) | copy-start | bytes 196612
  374.9 319.5 %reduce-scatter.2.cloned.1.call-start = ((), (), s32[]{:S(2)}) async-start(), calls=%async_computation.3 | async-start | bytes 9437184 | tf_op jit(solution)/shard_map/reduce_scatter | solution.py:1530
  458.0 570.2 %all-gather.8.cloned.1.call-start = ((), (), s32[]{:S(2)}) async-start(), calls=%async_computation.4 | async-start | bytes 9437184 | tf_op jit(solution)/shard_map/all_gather | solution.py:1552
  511.4 10.7 %copy-start.9 = (bf16[1280,2048]{1,0:T(8,128)(2,1)S(1)}, bf16[1280,2048]{1,0:T(8,128)(2,1)}, u32[]{:S(2)}) copy-start(bf16[1280,2048]{1,0:T(8,128)(2,1)} %get-tuple-element.112.x_ref) | copy-start | bytes 15728644
  511.4 21.2 %slice-start.2 = ((s8[5242880]{0:T(1024)(128)(4,1)}), s8[4194304]{0:T(1024)(128)(4,1)S(1)}, s32[]{:S(2)}) async-start(s8[5242880]{0:T(1024)(128)(4,1)} %bitcast.118), calls=%async_computation.7 | async-start | bytes 8388608
  529.3 166.8 %collective-permute-start.1 = (bf16[2048,1024]{1,0:T(8,128)(2,1)}, bf16[2048,1024]{1,0:T(8,128)(2,1)}, u32[]{:S(2)}, u32[]{:S(2)}) collective-permute-start(bf16[2048,1024]{1,0:T(8,128)(2,1)} %convolution_convert_fusion.1), channel_id=1, source_target_pairs={{0,1},{1,0},{2,3},{3,2},{4,5},{5,4},{6,7},{7,6},{8,9},{9,8},{10,11... | collective-permute-start | bytes 12582920 | tf_op jit(solution)/shard_map/ppermute | solution.py:1460
  532.6 181.4 %collective-permute-start = (bf16[2048,1024]{1,0:T(8,128)(2,1)}, bf16[2048,1024]{1,0:T(8,128)(2,1)}, u32[]{:S(2)}, u32[]{:S(2)}) collective-permute-start(bf16[2048,1024]{1,0:T(8,128)(2,1)} %convolution_convert_fusion.2), channel_id=1, source_target_pairs={{0,1},{1,0},{2,3},{3,2},{4,5},{5,4},{6,7},{7,6},{8,9},{9,8},{10,11... | collective-permute-start | bytes 12582920 | tf_op jit(solution)/shard_map/ppermute | solution.py:1460
  694.4 19.5 %copy-start.11 = (f32[256,512]{1,0:T(8,128)S(1)}, f32[256,512]{1,0:T(8,128)}, u32[]{:S(2)}) copy-start(f32[256,512]{1,0:T(8,128)} %copy-done.10) | copy-start | bytes 1572868
  694.4 19.5 %copy-start.13 = (f32[256,512]{1,0:T(8,128)S(1)}, f32[256,512]{1,0:T(8,128)}, u32[]{:S(2)}) copy-start(f32[256,512]{1,0:T(8,128)} %copy-done.12) | copy-start | bytes 1572868
  694.5 19.5 %copy-start.6 = (f32[256,2048]{1,0:T(8,128)S(1)}, f32[256,2048]{1,0:T(8,128)}, u32[]{:S(2)}) copy-start(f32[256,2048]{1,0:T(8,128)} %get-tuple-element.138) | copy-start | bytes 6291460
  720.5 151.4 %collective-permute-start.2 = (bf16[1024,2048]{1,0:T(8,128)(2,1)}, bf16[1024,2048]{1,0:T(8,128)(2,1)}, u32[]{:S(2)}, u32[]{:S(2)}) collective-permute-start(bf16[1024,2048]{1,0:T(8,128)(2,1)} %convolution_convert_fusion), channel_id=1, source_target_pairs={{0,1},{1,0},{2,3},{3,2},{4,5},{5,4},{6,7},{7,6},{8,9},{9,8},{10,11... | collective-permute-start | bytes 12582920 | tf_op jit(solution)/shard_map/ppermute | solution.py:1460
  855.2 16.8 %slice-start = ((s8[8388608]{0:T(1024)(128)(4,1)}), s8[4194304]{0:T(1024)(128)(4,1)S(1)}, s32[]{:S(2)}) async-start(s8[8388608]{0:T(1024)(128)(4,1)} %bitcast.115), calls=%async_computation.5 | async-start | bytes 8388608
  880.7 154.6 %collective-permute-start.3 = (bf16[2048,768]{1,0:T(8,128)(2,1)}, bf16[2048,768]{1,0:T(8,128)(2,1)}, u32[]{:S(2)}, u32[]{:S(2)}) collective-permute-start(bf16[2048,768]{1,0:T(8,128)(2,1)} %convolution_convert_fusion.3), channel_id=1, source_target_pairs={{0,1},{1,0},{2,3},{3,2},{4,5},{5,4},{6,7},{7,6},{8,9},{9,8},{10,11... | collective-permute-start | bytes 9437192 | tf_op jit(solution)/shard_map/ppermute | solution.py:1460
  887.6 133.0 %copy-start.17 = (bf16[1024,2048]{1,0:T(8,128)(2,1)S(1)}, bf16[1024,2048]{1,0:T(8,128)(2,1)}, u32[]{:S(2)}) copy-start(bf16[1024,2048]{1,0:T(8,128)(2,1)} %get-tuple-element.153) | copy-start | bytes 12582916
  1033.9 18.5 %collective-permute-start.4 = (bf16[256,2048]{1,0:T(8,128)(2,1)S(1)}, bf16[256,2048]{1,0:T(8,128)(2,1)S(1)}, u32[]{:S(2)}, u32[]{:S(2)}) collective-permute-start(bf16[256,2048]{1,0:T(8,128)(2,1)S(1)} %convolution_convert_fusion.4), channel_id=1, source_target_pairs={{0,1},{1,0},{2,3},{3,2},{4,5},{5,4},{6,7},{7,6},{8,9},{9,8},{10,11... | collective-permute-start | bytes 3145736 | tf_op jit(solution)/shard_map/ppermute | solution.py:1460
  1041.7 12.4 %copy-start.26 = (f32[256,2048]{1,0:T(8,128)S(1)}, f32[256,2048]{1,0:T(8,128)}, u32[]{:S(2)}) copy-start(f32[256,2048]{1,0:T(8,128)} %get-tuple-element.213) | copy-start | bytes 6291460
  (31 other events, 125.5 us)
Sparse Core Ops, SparseCore 0:
  151.4 109.4 all-gather.3
  375.0 72.2 all-gather.5
  458.2 147.9 reduce-scatter.1
  720.6 153.5 all-gather.7

commit v9 on v7

--- a/solution.py
+++ b/solution.py
@@ -1325,7 +1325,7 @@
         self.router, self.weights, self.capacity, self.experts = router, weights, capacity, experts
         wide, _, rows = slots.shape
         units = weights[0].shape[1]
-        groups = 2 if wide * capacity > 1024 else 1
+        groups = 1 if wide * capacity <= 1280 else 2
         blocks, tile = wide // groups, 256
         tiles = units // tile
         last = blocks + tiles

time: 1050 us -> 1040 us (level)
  Pallas kernels: 884 us -> 868 us
where the time goes in v9:
time: 1040 us; the launch traced here: 1030 us
  Pallas kernels  868 us (83%)
  matrix products  61.9 us (6%)
  other arithmetic  52.2 us (5%)
  local copies, waits for them, and re-layouts  28.3 us (3%)
  between operations  15.2 us (1%)
    pallas_call x2, Pallas kernels, start_exchange(): pl.pallas_call(functools.partial(start_kernel, count, swaps, spread), out...  256 us
    pallas_call x1, Pallas kernels, backward(): return backward_call(*args)  132 us
    pallas_call x1, Pallas kernels, input_grad(): pl.pallas_call(functools.partial(input_grad_kernel, gain_row), out_shape=...  113 us
    pallas_call x2, Pallas kernels, backward(): pl.pallas_call(functools.partial(expert_backward_kernel, self.tiles, self...  110 us
    pallas_call x1, Pallas kernels, expert_grad(): pl.pallas_call(expert_grad_kernel, out_shape=[jax.ShapeDtypeStruct((rows,...  98 us
    pallas_call x2, Pallas kernels, forward(): pl.pallas_call(functools.partial(expert_forward_kernel, self.tiles, self....  80.2 us
    pallas_call x1, Pallas kernels, shards(): kept = attend(raw, gains, cosine, sine)  79.9 us
    dot_general x5, matrix products, dot_tn(): lax.dot_general(a, b, (((0,), (0,)), ((), ())), preferred_element_type=jn...  44.4 us
  transfers between devices with their start and end apart: 8, of which 0 were waited for; matrix products, arithmetic and copies ran while one was open for 12% of the time, Pallas kernels for 71%

profile of v9, /device:TPU:0, one launch (start us, length us, event | category | flops | bytes accessed | tf_op | source)
XLA Modules:
  0.0 1031.7 jit_solution(3375363797376664136)
XLA Ops:
  14.3 137.0 %shard_map.271 = (s32[8,8,256]{2,1,0:T(8,128)}, bf16[8,256,2048]{2,1,0:T(8,128)(2,1)}, bf16[8,256,512]{2,1,0:T(8,128)(2,1)}, bf16[2048,1024]{1,0:T(8,128)(2,1)},...) custom-call(s32[8,256]{1,0:T(8,128)} %bitcast.109, ...), custom_call_target="tpu_custom_call" | custom-call | bytes 360000000 | tf_op jit(solution)/shard_map/pallas_call | solution.py:815
  153.5 3.7 fusion.10
  159.2 8.7 fusion.35.raw_ref
  167.9 79.9 %shard_map.272 = (bf16[2048,256]{1,0:T(8,128)(2,1)}, bf16[2048,256]{1,0:T(8,128)(2,1)}, bf16[2048,256]{1,0:T(8,128)(2,1)}, bf16[1024,256]{1,0:T(8,128)(2,1)}, bf...) custom-call(f32[2048,768]{1,0:T(8,128)} %fusion.35.raw_ref, ...), custom_call_target="tpu_custom_call" | custom-call | bytes 300000000 | tf_op jit(solution)/shard_map/pallas_call | solution.py:1503
  255.8 118.9 %shard_map.273 = (bf16[8,256,2048]{2,1,0:T(8,128)(2,1)}, bf16[2048,1024]{1,0:T(8,128)(2,1)}, bf16[1024,2048]{1,0:T(8,128)(2,1)}) custom-call(bf16[256,2048]{1,0:T(8,128)(2,1)} %multiply_convert_fusion.refs_0_, bf16[2048,1024]{1,0:T(8,128)(2,1)} %bitcast.83, bf16[1024,2048]{1,0:T(8,128)(2,1)} %bitcast.86), custom_call_target="tpu_custom_call" | custom-call | bytes 360000000 | tf_op jit(solution)/shard_map/pallas_call | solution.py:815
  377.6 38.3 %shard_map.274 = (bf16[8,256,2048]{2,1,0:T(8,128)(2,1)}, bf16[1280,2048]{1,0:T(8,128)(2,1)}, bf16[1280,1024]{1,0:T(8,128)(2,1)}, f32[1280,1024]{1,0:T(8,128)}, f...) custom-call(s32[1]{0:T(128)} %bitcast.7.id_ref, s32[8,1,256]{2,1,0:T(1,128)} %reshape.205.slot_ref, ...), custom_call_target="tpu_custom_call" | custom-call | bytes 120000000 | tf_op jit(solution)/shard_map/pallas_call | solution.py:1373
  416.0 41.9 %shard_map.275 = (bf16[8,256,2048]{2,1,0:T(8,128)(2,1)}, bf16[1280,2048]{1,0:T(8,128)(2,1)}, bf16[1280,1024]{1,0:T(8,128)(2,1)}, f32[1280,1024]{1,0:T(8,128)}, f...) custom-call(s32[1]{0:T(128)} %bitcast.11.id_ref, s32[8,1,256]{2,1,0:T(1,128)} %copy.32.slot_ref, ...), custom_call_target="tpu_custom_call" | custom-call | bytes 120000000 | tf_op jit(solution)/shard_map/pallas_call | solution.py:1373
  457.9 53.3 %shard_map.276 = (bf16[8,256,2048]{2,1,0:T(8,128)(2,1)}, bf16[1280,2048]{1,0:T(8,128)(2,1)}, bf16[1280,1024]{1,0:T(8,128)(2,1)}, bf16[1280,1024]{1,0:T(8,128)(2,1)}, f32[128,2048]{1,0:T(8,128)}) custom-call(s32[1]{0:T(128)} %bitcast.11.id_ref, s32[8,1,256]{2,1,0:T(1,128)} %copy.32.slot_ref, bf16[8,128,2048]{2,1,0:T(8,128)(2,1)} %bitcast.90, ...), custom_call_target="tpu_custom_call" | custom-call | bytes 120000000 | tf_op jit(solution)/shard_map/pallas_call | solution.py:1392
  511.2 10.5 %convolution_convert_fusion.2 = bf16[2048,1024]{1,0:T(8,128)(2,1)} fusion(bf16[1280,2048]{1,0:T(8,128)(2,1)} %get-tuple-element.113.x_ref, bf16[1280,1024]{1,0:T(8,128)(2,1)} %get-tuple-element.119), kind=kOutput, calls=%fused_computation.6 | convolution fusion | flops 5370806272 | bytes 12058624 | tf_op jit(solution)/shard_map/dot_general | solution.py:738
  521.7 3.2 collective-permute-start
  525.6 10.3 convolution_convert_fusion.1
  535.9 7.2 convolution_convert_fusion
  543.1 56.7 %shard_map.277 = (bf16[8,256,2048]{2,1,0:T(8,128)(2,1)}, bf16[1280,2048]{1,0:T(8,128)(2,1)}, bf16[1280,1024]{1,0:T(8,128)(2,1)}, bf16[1280,1024]{1,0:T(8,128)(2,1)}, f32[128,2048]{1,0:T(8,128)}) custom-call(s32[1]{0:T(128)} %bitcast.7.id_ref, s32[8,1,256]{2,1,0:T(1,128)} %reshape.205.slot_ref, bf16[8,128,2048]{2,1,0:T(8,128)(2,1)} %bitcast.91, ...), custom_call_target="tpu_custom_call" | custom-call | bytes 120000000 | tf_op jit(solution)/shard_map/pallas_call | solution.py:1392
  600.8 98.0 %shard_map.278 = (f32[256,2048]{1,0:T(8,128)}, bf16[2048,1024]{1,0:T(8,128)(2,1)}, bf16[2048,1024]{1,0:T(8,128)(2,1)}, bf16[1024,2048]{1,0:T(8,128)(2,1)}) custom-call(bf16[8,256,2048]{2,1,0:T(8,128)(2,1)} %get-tuple-element.125.part_ref, bf16[1280,2048]{1,0:T(8,128)(2,1)} %get-tuple-element.109.x_ref.refs_0_, ...), custom_call_target="tpu_custom_call" | custom-call | bytes 3000000 | tf_op jit(solution)/shard_map/pallas_call | solution.py:992
  701.0 4.0 multiply_reduce_fusion
  714.0 131.6 %shard_map.279 = (bf16[2048,768]{1,0:T(8,128)(2,1)}, f32[8,256]{1,0:T(8,128)}, bf16[8,256,2048]{2,1,0:T(8,128)(2,1)}) custom-call(f32[2048,768]{1,0:T(8,128)} %fusion.35.raw_ref, f32[8,256]{1,0:T(8,128)} %fusion.28.gains_ref, f32[2048,128]{1,0:T(8,128)} %get-tuple-element.197.cos_ref, f32[2048,128]{1,0:T(8,128)} %get-tuple-element.198.sin_ref, ...), custom_call_target="tpu_custom_call" | custom-call | bytes 300000000 | tf_op jit(solution)/shard_map/pallas_call | solution.py:723
  845.6 5.7 convolution_convert_fusion.4
  853.6 3.9 stack.48
  858.9 9.0 add_bitcast_fusion.2
  867.9 10.7 %convolution_convert_fusion.3 = bf16[2048,768]{1,0:T(8,128)(2,1)} fusion(bf16[2048,2048]{1,0:T(8,128)(2,1)} %bitcast.116, bf16[2048,768]{1,0:T(8,128)(2,1)S(1)} %copy-done.19), kind=kOutput, calls=%fused_computation.7 | convolution fusion | flops 6444023808 | bytes 14680064 | tf_op jit(solution)/shard_map/dot_general | solution.py:738
  881.0 112.6 %shard_map.280 = (f32[256,2048]{1,0:T(8,128)}, f32[24,2048]{1,0:T(8,128)}) custom-call(bf16[2048,768]{1,0:T(8,128)(2,1)} %get-tuple-element.144.joined_ref, bf16[2048,768]{1,0:T(8,128)(2,1)} %copy-done.9, bf16[256,2048]{1,0:T(8,128)(2,1)} %tokens_ref.1, f32[256,2048]{1,0:T(8,128)} %get-tuple-element.170.hidden_ref, f32[1,2048]{1,0:T(1,128)} %bitcast.103, ...), custom_call_target="tpu_custom_call" | custom-call | bytes 300000000 | tf_op jit(solution)/shard_map/pallas_call | solution.py:1180
  1001.4 7.7 add_bitcast_fusion
  1009.1 7.6 add_bitcast_fusion.1
  1016.6 3.5 convert_add_fusion
  (162 shorter events, 52.6 us)
Async XLA Ops:
  7.2 367.6 %all-gather.3.cloned.1.call-start = ((), (), s32[]{:S(2)}) async-start(), calls=%async_computation.1 | async-start | bytes 4718592 | tf_op jit(solution)/shard_map/all_gather | solution.py:1494
  14.2 137.2 %copy-start.40 = (bf16[256]{0:T(256)(128)(2,1)S(1)}, bf16[256]{0:T(256)(128)(2,1)}, u32[]{:S(2)}) copy-start(bf16[256]{0:T(256)(128)(2,1)} %param.25) | copy-start | bytes 1540
  14.2 137.2 %copy-start.41 = (bf16[256]{0:T(256)(128)(2,1)S(1)}, bf16[256]{0:T(256)(128)(2,1)}, u32[]{:S(2)}) copy-start(bf16[256]{0:T(256)(128)(2,1)} %param.26) | copy-start | bytes 1540
  14.2 137.2 %copy-start.35 = (bf16[2048]{0:T(1024)(128)(2,1)S(1)}, bf16[2048]{0:T(1024)(128)(2,1)}, u32[]{:S(2)}) copy-start(bf16[2048]{0:T(1024)(128)(2,1)} %param.27) | copy-start | bytes 12292
  14.3 137.9 %copy-start.27 = (bf16[2048,256]{1,0:T(8,128)(2,1)S(1)}, bf16[2048,256]{1,0:T(8,128)(2,1)}, u32[]{:S(2)}) copy-start(bf16[2048,256]{1,0:T(8,128)(2,1)} %param.20) | copy-start | bytes 3145732
  151.3 306.6 %all-gather.5.cloned.1.call-start = ((), (), s32[]{:S(2)}) async-start(), calls=%async_computation.2 | async-start | bytes 4718592 | tf_op jit(solution)/shard_map/all_gather | solution.py:1514
  153.5 5.7 copy-start.9
  153.5 5.7 copy-start.37
  167.9 79.9 %copy-start.20 = (bf16[8,256,512]{2,1,0:T(8,128)(2,1)S(1)}, bf16[8,256,512]{2,1,0:T(8,128)(2,1)}, u32[]{:S(2)}) copy-start(bf16[8,256,512]{2,1,0:T(8,128)(2,1)} %get-tuple-element.91) | copy-start | bytes 6291460
  255.8 119.1 %copy-start.33 = (s32[8,8,256]{2,1,0:T(8,128)S(1)}, s32[8,8,256]{2,1,0:T(8,128)}, u32[]{:S(2)}) copy-start(s32[8,8,256]{2,1,0:T(8,128)} %get-tuple-element.92) | copy-start | bytes 196612
  255.8 119.9 %copy-start.32 = (bf16[2048,16]{0,1:T(8,128)(2,1)S(1)}, bf16[2048,16]{0,1:T(8,128)(2,1)}, u32[]{:S(2)}) copy-start(bf16[2048,16]{0,1:T(8,128)(2,1)} %param.28) | copy-start | bytes 196612
  374.8 324.0 %reduce-scatter.2.cloned.1.call-start = ((), (), s32[]{:S(2)}) async-start(), calls=%async_computation.3 | async-start | bytes 9437184 | tf_op jit(solution)/shard_map/reduce_scatter | solution.py:1535
  511.2 13.7 %copy-start.36 = (s32[256]{0:T(256)S(1)}, s32[256]{0:T(256)}, u32[]{:S(2)}) copy-start(s32[256]{0:T(256)} %param.18) | copy-start | bytes 3076
  521.7 178.7 %collective-permute-start = (bf16[2048,1024]{1,0:T(8,128)(2,1)}, bf16[2048,1024]{1,0:T(8,128)(2,1)}, u32[]{:S(2)}, u32[]{:S(2)}) collective-permute-start(bf16[2048,1024]{1,0:T(8,128)(2,1)} %convolution_convert_fusion.2), channel_id=1, source_target_pairs={{0,1},{1,0},{2,3},{3,2},{4,5},{5,4},{6,7},{7,6},{8,9},{9,8},{10,11... | collective-permute-start | bytes 12582920 | tf_op jit(solution)/shard_map/ppermute | solution.py:1465
  525.6 10.3 %copy-start.38 = (bf16[1280,2048]{1,0:T(8,128)(2,1)S(1)}, bf16[1280,2048]{1,0:T(8,128)(2,1)}, u32[]{:S(2)}) copy-start(bf16[1280,2048]{1,0:T(8,128)(2,1)} %get-tuple-element.122) | copy-start | bytes 15728644
  525.6 10.3 %copy-start.39 = (bf16[1280,1024]{1,0:T(8,128)(2,1)S(1)}, bf16[1280,1024]{1,0:T(8,128)(2,1)}, u32[]{:S(2)}) copy-start(bf16[1280,1024]{1,0:T(8,128)(2,1)} %get-tuple-element.121) | copy-start | bytes 7864324
  535.9 332.0 %collective-permute-start.1 = (bf16[2048,1024]{1,0:T(8,128)(2,1)}, bf16[2048,1024]{1,0:T(8,128)(2,1)}, u32[]{:S(2)}, u32[]{:S(2)}) collective-permute-start(bf16[2048,1024]{1,0:T(8,128)(2,1)} %convolution_convert_fusion.1), channel_id=1, source_target_pairs={{0,1},{1,0},{2,3},{3,2},{4,5},{5,4},{6,7},{7,6},{8,9},{9,8},{10,11... | collective-permute-start | bytes 12582920 | tf_op jit(solution)/shard_map/ppermute | solution.py:1465
  700.4 167.5 %collective-permute-start.2 = (bf16[1024,2048]{1,0:T(8,128)(2,1)}, bf16[1024,2048]{1,0:T(8,128)(2,1)}, u32[]{:S(2)}, u32[]{:S(2)}) collective-permute-start(bf16[1024,2048]{1,0:T(8,128)(2,1)} %convolution_convert_fusion), channel_id=1, source_target_pairs={{0,1},{1,0},{2,3},{3,2},{4,5},{5,4},{6,7},{7,6},{8,9},{9,8},{10,11... | collective-permute-start | bytes 12582920 | tf_op jit(solution)/shard_map/ppermute | solution.py:1465
  714.0 131.6 %copy-start.8 = (bf16[2048,256]{1,0:T(8,128)(2,1)S(1)}, bf16[2048,256]{1,0:T(8,128)(2,1)}, u32[]{:S(2)}) copy-start(bf16[2048,256]{1,0:T(8,128)(2,1)} %get-tuple-element.140.o_ref) | copy-start | bytes 3145732
  852.3 27.1 %collective-permute-start.4 = (bf16[256,2048]{1,0:T(8,128)(2,1)S(1)}, bf16[256,2048]{1,0:T(8,128)(2,1)S(1)}, u32[]{:S(2)}, u32[]{:S(2)}) collective-permute-start(bf16[256,2048]{1,0:T(8,128)(2,1)S(1)} %convolution_convert_fusion.4), channel_id=1, source_target_pairs={{0,1},{1,0},{2,3},{3,2},{4,5},{5,4},{6,7},{7,6},{8,9},{9,8},{10,11... | collective-permute-start | bytes 3145736 | tf_op jit(solution)/shard_map/ppermute | solution.py:1465
  858.9 9.0 copy-start.19
  878.6 138.0 %collective-permute-start.3 = (bf16[2048,768]{1,0:T(8,128)(2,1)}, bf16[2048,768]{1,0:T(8,128)(2,1)}, u32[]{:S(2)}, u32[]{:S(2)}) collective-permute-start(bf16[2048,768]{1,0:T(8,128)(2,1)} %convolution_convert_fusion.3), channel_id=1, source_target_pairs={{0,1},{1,0},{2,3},{3,2},{4,5},{5,4},{6,7},{7,6},{8,9},{9,8},{10,11... | collective-permute-start | bytes 9437192 | tf_op jit(solution)/shard_map/ppermute | solution.py:1465
  881.0 120.3 %copy-start.18 = (bf16[1024,2048]{1,0:T(8,128)(2,1)S(1)}, bf16[1024,2048]{1,0:T(8,128)(2,1)}, u32[]{:S(2)}) copy-start(bf16[1024,2048]{1,0:T(8,128)(2,1)} %get-tuple-element.155) | copy-start | bytes 12582916
  1001.4 7.7 copy-start.17
  (26 other events, 57.0 us)
Sparse Core Ops, SparseCore 0:
  151.4 109.4 all-gather.2
  374.9 72.1 all-gather.4
  458.0 147.9 reduce-scatter.1
